TPU v7x, 512 devices: a whole 4x4x16 slice. The times are simulated.
512 devices in a mesh: gx: 4 (over x), gy: 16 (over z_lo, core), gz: 8 (over y, z_hi).
Axes of the slice: x: 4, y: 4, z: 16 (z_hi: 2, z_lo: 8; z = z_hi * 8 + z_lo), core: 2. Of those that a mesh axis runs over, the one named last changes fastest.
Arguments:
- fractions: float32 [2, 3, 524288], P(None, None, ('gx', 'gy', 'gz')), may hold values from -0.5 to 0.5
- centers: int32 [2, 524288], P(None, ('gx', 'gy', 'gz')), may hold values from 0 to 2047, as said below
- deform: float32 [2, 9, 524288], P(None, None, ('gx', 'gy', 'gz')), may hold values from -0.12 to 1.4, as said below
- next_affine: float32 [2, 9, 524288], P(None, None, ('gx', 'gy', 'gz')), may hold values from -3 to 3
- cell_mass: float32 [2, 16, 64, 1024], P(None, 'gx', 'gy', 'gz'), may hold values from 0.25 to 4
- final_adjoint: float32 [21, 524288], P(None, ('gx', 'gy', 'gz')), may hold values from -6 to 6
- live_count: int32 [512, 2], P(('gx', 'gy', 'gz')), may hold values from 128 to 1024, as said below
- send_slot: int32 [512, 26, 32], P(('gx', 'gy', 'gz')), may hold values from 0 to 1023, as said below
- receive_slot: int32 [512, 26, 32], P(('gx', 'gy', 'gz')), may hold values from 0 to 1023, as said below
- receive_count: int32 [512, 26], P(('gx', 'gy', 'gz')), may hold values from 0 to 32, as said below
- prior_slot: int32 [524288], P(('gx', 'gy', 'gz')), may hold values from 0 to 1024, as said below
Outputs:
- initial_adjoint: float32 [21, 524288], P(None, ('gx', 'gy', 'gz'))
Inputs may be any that keep to these rules, and one draw needn't show every extreme that they name: `live_count`: particles in use occupy the slots below the count; the counts differ between tiles. `receive_count`: zero toward offsets that leave the grid of tiles. For j below receive_count[t, d], receive_slot[t, d, j] are distinct in-use second-step slots of tile t; no slot is named both here and by a prior_slot entry below 1024, and together they name every in-use second-step slot once; later entries are arbitrary slots. send_slot[u, 25 - d, j] is the first-step slot on tile u of the particle named by receive_slot[t, d, j], u the tile at offset d from t; together with prior_slot these name every in-use first-step slot once; entries past the count are arbitrary slots. `prior_slot`: 1024 marks a second-step slot whose particle did not stay on the tile, or that is not in use. `centers`: the global node is at least one cell away from the grid's faces; within each tile and step the values do not fall from slot to slot. `deform`: each 3 x 3 matrix has diagonal entries in [0.7, 1.4] and other entries in [-0.12, 0.12].
All inputs are finite; a program needn't handle non-finite values.
Results may differ from a plain program's by a relative error of at most 0.0003.
Values sent between devices are 32-bit elements; how exact they have to be, the bound alone decides.
No kernel may reach another device: no remote copies, remote signals or barrier semaphores. Data moves between devices by JAX's collectives and lax.ppermute only.
A program may use at most 128 MiB of HBM per device.

v0:
```python
import jax
import jax.numpy as jnp
from jax import lax
from jax.sharding import PartitionSpec as P

TIME_STEP = 0.2
APIC_SCALE = 4.0
STRESS_SCALE = 0.3
SHEAR = 1.0
BULK = 1.0
stencil_rows = [
    [along_x, along_y, along_z]
    for along_x in (-1, 0, 1)
    for along_y in (-1, 0, 1)
    for along_z in (-1, 0, 1)
]


def with_halo(cells, sides, width):
    for axis, dim in sides:
        count = lax.axis_size(axis)
        ends = count - 1
        head = lax.slice_in_dim(cells, 0, width, axis=dim)
        tail = lax.slice_in_dim(cells, cells.shape[dim] - width, cells.shape[dim], axis=dim)
        cells = jnp.concatenate(
            [
                lax.ppermute(tail, axis, [(i, (i + 1) % count) for i in range(ends)]),
                cells,
                lax.ppermute(head, axis, [((i + 1) % count, i) for i in range(ends)]),
            ],
            axis=dim,
        )
    return cells


def spline_table(fraction):
    lower = 0.5 * (0.5 - fraction) * (0.5 - fraction)
    middle = 0.75 - fraction * fraction
    upper = 0.5 * (0.5 + fraction) * (0.5 + fraction)
    return jnp.stack([lower, middle, upper])


def transfer_rule(adjoint, deform_now, affine_next):
    count = adjoint.shape[1]
    velocity = adjoint[0:3]
    affine = adjoint[3:12].reshape(3, 3, count)
    gradient = adjoint[12:21].reshape(3, 3, count)
    deformation = deform_now.reshape(3, 3, count)
    successor = affine_next.reshape(3, 3, count)
    back_deform = gradient + TIME_STEP * jnp.sum(successor[:, :, None] * gradient[:, None], axis=0)
    back_affine = affine + TIME_STEP * jnp.sum(gradient[:, None] * deformation[None], axis=2)
    return (velocity, back_affine, back_deform, deformation)


def cofactors(deformation):
    rows = []
    for row in range(3):
        entries = []
        for column in range(3):
            entries.append(
                deformation[(row + 1) % 3, (column + 1) % 3]
                * deformation[(row + 2) % 3, (column + 2) % 3]
                - deformation[(row + 1) % 3, (column + 2) % 3]
                * deformation[(row + 2) % 3, (column + 1) % 3]
            )
        rows.append(jnp.stack(entries))
    return jnp.stack(rows)


def particle_rule(gathered, area, back_deform, deformation):
    count = gathered.shape[1]
    stress = -STRESS_SCALE * area
    symmetric = stress + jnp.swapaxes(stress, 0, 1)
    shear_term = jnp.sum(symmetric[:, :, None] * deformation[None], axis=1)
    cofactor = cofactors(deformation)
    determinant = jnp.sum(deformation[0] * cofactor[0], axis=0)
    trace_value = stress[0, 0] + stress[1, 1] + stress[2, 2]
    new_deform = (
        back_deform + SHEAR * shear_term + BULK * (trace_value / determinant)[None, None] * cofactor
    )
    return jnp.concatenate([gathered, area.reshape(9, count), new_deform.reshape(9, count)])


def fold_margins(extended, width):
    for direction in (1, 2, 3):
        length = extended.shape[direction]
        core = lax.slice_in_dim(extended, 2, length - 2, axis=direction)
        head = lax.slice_in_dim(extended, 0, width, axis=direction)
        tail = lax.slice_in_dim(extended, length - width, length, axis=direction)
        inner = core.shape[direction]
        extended = jnp.concatenate(
            [
                lax.slice_in_dim(core, 0, width, axis=direction) + head,
                lax.slice_in_dim(core, width, inner - width, axis=direction),
                lax.slice_in_dim(core, inner - width, inner, axis=direction) + tail,
            ],
            axis=direction,
        )
    return extended


def axis_keep(anchor, extent, count, margin):
    coords = anchor - margin + jnp.arange(count + 2 * margin, dtype=jnp.int32)
    return ((coords >= 1) & (coords <= extent - 2)).astype(jnp.float32)


def body(
    fractions,
    centers,
    deform,
    next_affine,
    cell_mass,
    final_adjoint,
    live_count,
    send_slot,
    receive_slot,
    receive_count,
    prior_slot,
):
    size_x, size_y, size_z = (cell_mass.shape[1], cell_mass.shape[2], cell_mass.shape[3])
    slots = final_adjoint.shape[1]
    capacity = receive_slot.shape[2]
    pad_x, pad_y, pad_z = (size_x + 2, size_y + 2, size_z + 2)
    anchor_x = lax.axis_index("gx") * size_x
    anchor_y = lax.axis_index("gy") * size_y
    anchor_z = lax.axis_index("gz") * size_z
    extent_x = lax.axis_size("gx") * size_x
    extent_y = lax.axis_size("gy") * size_y
    extent_z = lax.axis_size("gz") * size_z
    inner_keep = (
        axis_keep(anchor_x, extent_x, size_x, 0)[:, None, None]
        * axis_keep(anchor_y, extent_y, size_y, 0)[None, :, None]
        * axis_keep(anchor_z, extent_z, size_z, 0)[None, None, :]
    )

    def reverse_step(adjoint, which):
        in_use = (jnp.arange(slots, dtype=jnp.int32) < live_count[0, which]).astype(jnp.float32)
        adjoint = adjoint * in_use[None]
        velocity, back_affine, back_deform, deformation = transfer_rule(
            adjoint, deform[which], next_affine[which]
        )
        fraction = fractions[which]
        table = spline_table(fraction)
        shifted_base = velocity - APIC_SCALE * jnp.sum(back_affine * fraction[None], axis=1)
        centre = centers[which]
        local_x = centre // (size_y * size_z)
        local_y = centre // size_z % size_y
        local_z = centre % size_z
        base = ((local_x + 1) * pad_y + local_y + 1) * pad_z + local_z + 1
        partial_value = jnp.zeros((3, pad_x * pad_y * pad_z), jnp.float32)
        for offset in stencil_rows:
            weight = table[offset[0] + 1, 0] * table[offset[1] + 1, 1] * table[offset[2] + 1, 2]
            lifted = shifted_base + APIC_SCALE * (
                offset[0] * back_affine[:, 0]
                + offset[1] * back_affine[:, 1]
                + offset[2] * back_affine[:, 2]
            )
            target = base + (offset[0] * pad_y * pad_z + offset[1] * pad_z + offset[2])
            partial_value = partial_value.at[:, target].add(weight[None] * lifted)
        partial_value = partial_value.reshape(3, pad_x, pad_y, pad_z)
        extended = with_halo(partial_value, (("gx", 1), ("gy", 2), ("gz", 3)), 1)
        totals = fold_margins(extended, 1)
        settled = totals / cell_mass[which][None] * inner_keep[None]
        values = with_halo(settled, (("gx", 1), ("gy", 2), ("gz", 3)), 1)
        flat_values = values.reshape(3, -1)
        gathered = jnp.zeros((3, slots), jnp.float32)
        moment_x = jnp.zeros((3, slots), jnp.float32)
        moment_y = jnp.zeros((3, slots), jnp.float32)
        moment_z = jnp.zeros((3, slots), jnp.float32)
        for offset in stencil_rows:
            weight = table[offset[0] + 1, 0] * table[offset[1] + 1, 1] * table[offset[2] + 1, 2]
            target = base + (offset[0] * pad_y * pad_z + offset[1] * pad_z + offset[2])
            weighted = weight[None] * flat_values[:, target]
            gathered = gathered + weighted
            if offset[0] != 0:
                moment_x = moment_x + offset[0] * weighted
            if offset[1] != 0:
                moment_y = moment_y + offset[1] * weighted
            if offset[2] != 0:
                moment_z = moment_z + offset[2] * weighted
        moments = jnp.stack([moment_x, moment_y, moment_z], axis=1)
        area = moments - gathered[:, None] * fraction[None]
        return particle_rule(gathered, area, back_deform, deformation) * in_use[None]

    second = reverse_step(final_adjoint, 1)
    carried = jnp.zeros((21, slots + 1), jnp.float32).at[:, prior_slot].add(second)
    picked = second[:, receive_slot[0].reshape(-1)].reshape(21, 26, capacity)
    valid = (jnp.arange(capacity, dtype=jnp.int32)[None] < receive_count[0][:, None]).astype(
        jnp.float32
    )
    packed = jnp.moveaxis(picked * valid[None], 1, 0)
    boxed = jnp.concatenate(
        [packed[:13], jnp.zeros((1, 21, capacity), jnp.float32), packed[13:]]
    ).reshape(3, 3, 3, 21, capacity)
    arrived = with_halo(boxed, (("gx", 0), ("gy", 1), ("gz", 2)), 1)[0::2, 0::2, 0::2]
    arrived = arrived.reshape(27, 21, capacity)
    arrived = jnp.concatenate([arrived[:13], arrived[14:]])
    spread = jnp.moveaxis(arrived, 1, 0).reshape(21, 26 * capacity)
    carried = carried[:, :slots].at[:, send_slot[0].reshape(-1)].add(spread)
    return reverse_step(carried, 0)


def solution(mesh):
    in_specs = (
        P(None, None, ("gx", "gy", "gz")),
        P(None, ("gx", "gy", "gz")),
        P(None, None, ("gx", "gy", "gz")),
        P(None, None, ("gx", "gy", "gz")),
        P(None, "gx", "gy", "gz"),
        P(None, ("gx", "gy", "gz")),
        P(("gx", "gy", "gz"), None),
        P(("gx", "gy", "gz"), None, None),
        P(("gx", "gy", "gz"), None, None),
        P(("gx", "gy", "gz"), None),
        P(("gx", "gy", "gz")),
    )
    out_specs = P(None, ("gx", "gy", "gz"))
    return jax.shard_map(body, mesh=mesh, in_specs=in_specs, out_specs=out_specs, check_vma=False)
```

profile of v0, /device:TPU:158, one launch (start us, length us, event | category | flops | bytes accessed | tf_op | source)
XLA Modules:
  0.0 961.2 jit_solution(1693644711420984382)
XLA Ops:
  52.1 7.2 scatter_fusion.1
  59.4 7.5 scatter_fusion.2
  66.8 7.2 scatter_fusion.3
  81.3 7.2 scatter_fusion.5
  95.8 7.2 scatter_fusion.7
  103.1 7.6 scatter_fusion.8
  110.7 7.2 scatter_fusion.9
  118.0 7.2 scatter_fusion.10
  125.2 7.2 scatter_fusion.11
  132.4 7.2 scatter_fusion.12
  139.7 7.2 scatter_fusion.13
  146.9 7.4 scatter_fusion.14
  154.4 7.2 scatter_fusion.15
  168.8 7.2 scatter_fusion.17
  176.1 7.2 scatter_fusion.18
  183.3 7.2 scatter_fusion.19
  190.6 7.5 scatter_fusion.20
  198.1 7.2 scatter_fusion.21
  205.3 7.2 scatter_fusion.22
  212.6 7.2 scatter_fusion.23
  280.5 12.2 %collective-permute-start.5 = (f32[3,8,8,1]{3,2,1,0:T(8,128)S(1)}, f32[3,8,8,1]{3,2,1,0:T(8,128)S(1)}, u32[]{:S(2)}, u32[]{:S(2)}) collective-permute-start(f32[3,8,8,1]{3,2,1,0:T(8,128)S(1)} %get-tuple-element.48), channel_id=1, source_target_pairs={{1,0},{2,1},{3,2},{4,3},{5,4},{6,5},{7,6},{9,8},{10,9},{11,10},{12... | collective-permute-start | bytes 2312 | tf_op jit(solution)/shard_map/ppermute | solution.py:29
  298.1 15.3 %collective-permute-done.4 = f32[3,8,8,1]{3,2,1,0:T(8,128)S(1)} collective-permute-done((f32[3,8,8,1]{3,2,1,0:T(8,128)S(1)}, f32[3,8,8,1]{3,2,1,0:T(8,128)S(1)}, u32[]{:S(2)}, u32[]{:S(2)}) %collective-permute-start.4) | collective-permute-done | bytes 800 | tf_op jit(solution)/shard_map/ppermute | solution.py:27
  337.4 7.8 collective-permute-start.10
  346.9 7.5 collective-permute-done.10
  472.1 61.4 %collective-permute-start.17 = (f32[5,5,1,21,32]{3,4,2,1,0:T(8,128)S(1)}, f32[5,5,1,21,32]{3,4,2,1,0:T(8,128)}, u32[]{:S(2)}, u32[]{:S(2)}) collective-permute-start(f32[5,5,1,21,32]{3,4,2,1,0:T(8,128)S(1)} %get-tuple-element.34), channel_id=1, source_target_pairs={{1,0},{2,1},{3,2},{4,3},{5,4},{6,5},{7,6},{9,8},{10,9},{11,10},{12... | collective-permute-start | bytes 201608 | tf_op jit(solution)/shard_map/ppermute | solution.py:29
  543.0 10.1 %collective-permute-done.16 = f32[5,5,1,21,32]{3,4,2,1,0:T(8,128)} collective-permute-done((f32[5,5,1,21,32]{3,4,2,1,0:T(8,128)S(1)}, f32[5,5,1,21,32]{3,4,2,1,0:T(8,128)}, u32[]{:S(2)}, u32[]{:S(2)}) %collective-permute-start.16) | collective-permute-done | bytes 67232 | tf_op jit(solution)/shard_map/ppermute | solution.py:27
  596.3 7.5 scatter_fusion.27
  603.7 7.2 scatter_fusion.28
  611.0 7.2 scatter_fusion.29
  618.3 7.2 scatter_fusion.30
  632.8 7.2 scatter_fusion.32
  640.1 7.6 scatter_fusion.33
  647.7 7.2 scatter_fusion.34
  655.0 7.2 scatter_fusion.35
  662.3 7.2 scatter_fusion.36
  669.5 7.2 scatter_fusion.37
  676.8 7.2 scatter_fusion.38
  684.0 7.4 scatter_fusion.39
  691.5 7.2 scatter_fusion.40
  706.0 7.2 scatter_fusion.42
  720.5 7.2 scatter_fusion.44
  727.7 7.5 scatter_fusion.45
  735.2 7.2 scatter_fusion.46
  749.3 7.2 scatter_fusion.48
  771.1 7.5 scatter_fusion.51
  811.6 12.6 %collective-permute-start.22 = (f32[3,8,8,1]{3,2,1,0:T(8,128)S(1)}, f32[3,8,8,1]{3,2,1,0:T(8,128)S(1)}, u32[]{:S(2)}, u32[]{:S(2)}) collective-permute-start(f32[3,8,8,1]{3,2,1,0:T(8,128)S(1)} %get-tuple-element.43), channel_id=1, source_target_pairs={{0,1},{1,2},{2,3},{3,4},{4,5},{5,6},{6,7},{8,9},{9,10},{10,11},{11... | collective-permute-start | bytes 2312 | tf_op jit(solution)/shard_map/ppermute | solution.py:27
  852.8 8.3 collective-permute-start.28
  861.2 7.4 collective-permute-done.28
  (799 shorter events, 529.8 us)
Async XLA Ops:
  38.1 223.0 %copy-start.67 = (s32[1024,1]{0,1:T(1,128)}, s32[1024,1]{0,1:T(1,128)S(1)}, u32[]{:S(2)}) copy-start(s32[1024,1]{0,1:T(1,128)S(1)} %get-tuple-element.226) | copy-start | bytes 12292
  38.1 223.5 %copy-start.69 = (s32[1024,1]{0,1:T(1,128)}, s32[1024,1]{0,1:T(1,128)S(1)}, u32[]{:S(2)}) copy-start(s32[1024,1]{0,1:T(1,128)S(1)} %get-tuple-element.234) | copy-start | bytes 12292
  38.1 224.1 %copy-start.71 = (s32[1024,1]{0,1:T(1,128)}, s32[1024,1]{0,1:T(1,128)S(1)}, u32[]{:S(2)}) copy-start(s32[1024,1]{0,1:T(1,128)S(1)} %get-tuple-element.216) | copy-start | bytes 12292
  38.1 224.7 %copy-start.73 = (s32[1024,1]{0,1:T(1,128)}, s32[1024,1]{0,1:T(1,128)S(1)}, u32[]{:S(2)}) copy-start(s32[1024,1]{0,1:T(1,128)S(1)} %get-tuple-element.220) | copy-start | bytes 12292
  38.2 225.3 %copy-start.75 = (s32[1024,1]{0,1:T(1,128)}, s32[1024,1]{0,1:T(1,128)S(1)}, u32[]{:S(2)}) copy-start(s32[1024,1]{0,1:T(1,128)S(1)} %get-tuple-element.224) | copy-start | bytes 12292
  38.2 225.9 %copy-start.77 = (s32[1024,1]{0,1:T(1,128)}, s32[1024,1]{0,1:T(1,128)S(1)}, u32[]{:S(2)}) copy-start(s32[1024,1]{0,1:T(1,128)S(1)} %get-tuple-element.228) | copy-start | bytes 12292
  38.2 226.5 %copy-start.79 = (s32[1024,1]{0,1:T(1,128)}, s32[1024,1]{0,1:T(1,128)S(1)}, u32[]{:S(2)}) copy-start(s32[1024,1]{0,1:T(1,128)S(1)} %get-tuple-element.232) | copy-start | bytes 12292
  38.2 227.1 %copy-start.81 = (s32[1024,1]{0,1:T(1,128)}, s32[1024,1]{0,1:T(1,128)S(1)}, u32[]{:S(2)}) copy-start(s32[1024,1]{0,1:T(1,128)S(1)} %get-tuple-element.214) | copy-start | bytes 12292
  38.2 227.7 %copy-start.83 = (s32[1024,1]{0,1:T(1,128)}, s32[1024,1]{0,1:T(1,128)S(1)}, u32[]{:S(2)}) copy-start(s32[1024,1]{0,1:T(1,128)S(1)} %get-tuple-element.215) | copy-start | bytes 12292
  38.2 228.2 %copy-start.85 = (s32[1024,1]{0,1:T(1,128)}, s32[1024,1]{0,1:T(1,128)S(1)}, u32[]{:S(2)}) copy-start(s32[1024,1]{0,1:T(1,128)S(1)} %get-tuple-element.217) | copy-start | bytes 12292
  38.2 228.8 %copy-start.87 = (s32[1024,1]{0,1:T(1,128)}, s32[1024,1]{0,1:T(1,128)S(1)}, u32[]{:S(2)}) copy-start(s32[1024,1]{0,1:T(1,128)S(1)} %get-tuple-element.219) | copy-start | bytes 12292
  38.2 229.4 %copy-start.89 = (s32[1024,1]{0,1:T(1,128)}, s32[1024,1]{0,1:T(1,128)S(1)}, u32[]{:S(2)}) copy-start(s32[1024,1]{0,1:T(1,128)S(1)} %get-tuple-element.221) | copy-start | bytes 12292
  38.2 230.0 %copy-start.91 = (s32[1024,1]{0,1:T(1,128)}, s32[1024,1]{0,1:T(1,128)S(1)}, u32[]{:S(2)}) copy-start(s32[1024,1]{0,1:T(1,128)S(1)} %get-tuple-element.223) | copy-start | bytes 12292
  38.2 230.6 %copy-start.93 = (s32[1024,1]{0,1:T(1,128)}, s32[1024,1]{0,1:T(1,128)S(1)}, u32[]{:S(2)}) copy-start(s32[1024,1]{0,1:T(1,128)S(1)} %get-tuple-element.225) | copy-start | bytes 12292
  38.3 231.2 %copy-start.95 = (s32[1024,1]{0,1:T(1,128)}, s32[1024,1]{0,1:T(1,128)S(1)}, u32[]{:S(2)}) copy-start(s32[1024,1]{0,1:T(1,128)S(1)} %get-tuple-element.227) | copy-start | bytes 12292
  38.3 231.8 %copy-start.97 = (s32[1024,1]{0,1:T(1,128)}, s32[1024,1]{0,1:T(1,128)S(1)}, u32[]{:S(2)}) copy-start(s32[1024,1]{0,1:T(1,128)S(1)} %get-tuple-element.229) | copy-start | bytes 12292
  38.3 233.1 %copy-start.99 = (s32[1024,1]{0,1:T(1,128)}, s32[1024,1]{0,1:T(1,128)S(1)}, u32[]{:S(2)}) copy-start(s32[1024,1]{0,1:T(1,128)S(1)} %get-tuple-element.231) | copy-start | bytes 12292
  38.3 238.1 %copy-start.101 = (s32[1024,1]{0,1:T(1,128)}, s32[1024,1]{0,1:T(1,128)S(1)}, u32[]{:S(2)}) copy-start(s32[1024,1]{0,1:T(1,128)S(1)} %get-tuple-element.233) | copy-start | bytes 12292
  235.3 36.7 %collective-permute-start = (f32[3,1,6,130]{3,2,1,0:T(8,128)S(1)}, f32[3,1,6,130]{3,2,1,0:T(8,128)S(1)}, u32[]{:S(2)}, u32[]{:S(2)}) collective-permute-start(f32[3,1,6,130]{3,2,1,0:T(8,128)S(1)} %get-tuple-element.54), channel_id=1, source_target_pairs={{0,128},{128,256},{256,384},{1,129},{129,257},{257,385},{2,130},{1... | collective-permute-start | bytes 28088 | tf_op jit(solution)/shard_map/ppermute | solution.py:27
  236.6 35.4 %collective-permute-start.1 = (f32[3,1,6,130]{3,2,1,0:T(8,128)S(1)}, f32[3,1,6,130]{3,2,1,0:T(8,128)S(1)}, u32[]{:S(2)}, u32[]{:S(2)}) collective-permute-start(f32[3,1,6,130]{3,2,1,0:T(8,128)S(1)} %get-tuple-element.53), channel_id=1, source_target_pairs={{128,0},{256,128},{384,256},{129,1},{257,129},{385,257},{130,2},{2... | collective-permute-start | bytes 28088 | tf_op jit(solution)/shard_map/ppermute | solution.py:29
  272.1 4.9 collective-permute-start.3
  274.0 6.4 collective-permute-start.2
  280.5 17.5 %collective-permute-start.5 = (f32[3,8,8,1]{3,2,1,0:T(8,128)S(1)}, f32[3,8,8,1]{3,2,1,0:T(8,128)S(1)}, u32[]{:S(2)}, u32[]{:S(2)}) collective-permute-start(f32[3,8,8,1]{3,2,1,0:T(8,128)S(1)} %get-tuple-element.48), channel_id=1, source_target_pairs={{1,0},{2,1},{3,2},{4,3},{5,4},{6,5},{7,6},{9,8},{10,9},{11,10},{12... | collective-permute-start | bytes 2312 | tf_op jit(solution)/shard_map/ppermute | solution.py:29
  292.7 20.6 %collective-permute-start.4 = (f32[3,8,8,1]{3,2,1,0:T(8,128)S(1)}, f32[3,8,8,1]{3,2,1,0:T(8,128)S(1)}, u32[]{:S(2)}, u32[]{:S(2)}) collective-permute-start(f32[3,8,8,1]{3,2,1,0:T(8,128)S(1)} %get-tuple-element.47), channel_id=1, source_target_pairs={{0,1},{1,2},{2,3},{3,4},{4,5},{5,6},{6,7},{8,9},{9,10},{10,11},{11... | collective-permute-start | bytes 2312 | tf_op jit(solution)/shard_map/ppermute | solution.py:27
  314.1 4.1 collective-permute-start.7
  316.9 5.5 collective-permute-start.6
  322.4 4.4 collective-permute-start.9
  324.4 6.2 collective-permute-start.8
  330.7 16.2 %collective-permute-start.11 = (f32[3,6,6,1]{3,2,1,0:T(8,128)S(1)}, f32[3,6,6,1]{3,2,1,0:T(8,128)S(1)}, u32[]{:S(2)}, u32[]{:S(2)}) collective-permute-start(f32[3,6,6,1]{3,2,1,0:T(8,128)S(1)} %get-tuple-element.68), channel_id=1, source_target_pairs={{1,0},{2,1},{3,2},{4,3},{5,4},{6,5},{7,6},{9,8},{10,9},{11,10},{12... | collective-permute-start | bytes 1304 | tf_op jit(solution)/shard_map/ppermute | solution.py:29
  337.4 16.9 %collective-permute-start.10 = (f32[3,6,6,1]{3,2,1,0:T(8,128)S(1)}, f32[3,6,6,1]{3,2,1,0:T(8,128)S(1)}, u32[]{:S(2)}, u32[]{:S(2)}) collective-permute-start(f32[3,6,6,1]{3,2,1,0:T(8,128)S(1)} %get-tuple-element.67), channel_id=1, source_target_pairs={{0,1},{1,2},{2,3},{3,4},{4,5},{5,6},{6,7},{8,9},{9,10},{10,11},{11... | collective-permute-start | bytes 1304 | tf_op jit(solution)/shard_map/ppermute | solution.py:27
  451.8 5.1 collective-permute-start.13
  454.3 7.0 collective-permute-start.12
  461.4 5.6 collective-permute-start.15
  463.3 8.7 collective-permute-start.14
  472.1 70.9 %collective-permute-start.17 = (f32[5,5,1,21,32]{3,4,2,1,0:T(8,128)S(1)}, f32[5,5,1,21,32]{3,4,2,1,0:T(8,128)}, u32[]{:S(2)}, u32[]{:S(2)}) collective-permute-start(f32[5,5,1,21,32]{3,4,2,1,0:T(8,128)S(1)} %get-tuple-element.34), channel_id=1, source_target_pairs={{1,0},{2,1},{3,2},{4,3},{5,4},{6,5},{7,6},{9,8},{10,9},{11,10},{12... | collective-permute-start | bytes 201608 | tf_op jit(solution)/shard_map/ppermute | solution.py:29
  533.5 19.6 %collective-permute-start.16 = (f32[5,5,1,21,32]{3,4,2,1,0:T(8,128)S(1)}, f32[5,5,1,21,32]{3,4,2,1,0:T(8,128)}, u32[]{:S(2)}, u32[]{:S(2)}) collective-permute-start(f32[5,5,1,21,32]{3,4,2,1,0:T(8,128)S(1)} %get-tuple-element.33), channel_id=1, source_target_pairs={{0,1},{1,2},{2,3},{3,4},{4,5},{5,6},{6,7},{8,9},{9,10},{10,11},{11... | collective-permute-start | bytes 201608 | tf_op jit(solution)/shard_map/ppermute | solution.py:27
  786.8 6.4 collective-permute-start.18
  788.7 6.0 collective-permute-start.19
  794.8 7.5 collective-permute-start.21
  799.8 9.8 %collective-permute-start.20 = (f32[3,8,1,130]{3,2,1,0:T(1,128)S(1)}, f32[3,8,1,130]{3,2,1,0:T(1,128)S(1)}, u32[]{:S(2)}, u32[]{:S(2)}) collective-permute-start(f32[3,8,1,130]{3,2,1,0:T(1,128)S(1)} %get-tuple-element.45), channel_id=1, source_target_pairs={{0,8},{8,16},{16,24},{24,32},{32,40},{40,48},{48,56},{56,64},{64,7... | collective-permute-start | bytes 37448 | tf_op jit(solution)/shard_map/ppermute | solution.py:27
  809.7 15.3 %collective-permute-start.23 = (f32[3,8,8,1]{3,2,1,0:T(8,128)S(1)}, f32[3,8,8,1]{3,2,1,0:T(8,128)S(1)}, u32[]{:S(2)}, u32[]{:S(2)}) collective-permute-start(f32[3,8,8,1]{3,2,1,0:T(8,128)S(1)} %get-tuple-element.44), channel_id=1, source_target_pairs={{1,0},{2,1},{3,2},{4,3},{5,4},{6,5},{7,6},{9,8},{10,9},{11,10},{12... | collective-permute-start | bytes 2312 | tf_op jit(solution)/shard_map/ppermute | solution.py:29
  811.6 16.1 %collective-permute-start.22 = (f32[3,8,8,1]{3,2,1,0:T(8,128)S(1)}, f32[3,8,8,1]{3,2,1,0:T(8,128)S(1)}, u32[]{:S(2)}, u32[]{:S(2)}) collective-permute-start(f32[3,8,8,1]{3,2,1,0:T(8,128)S(1)} %get-tuple-element.43), channel_id=1, source_target_pairs={{0,1},{1,2},{2,3},{3,4},{4,5},{5,6},{6,7},{8,9},{9,10},{10,11},{11... | collective-permute-start | bytes 2312 | tf_op jit(solution)/shard_map/ppermute | solution.py:27
  828.6 5.3 collective-permute-start.25
  832.5 5.5 collective-permute-start.24
  838.0 4.4 collective-permute-start.27
  840.0 6.2 collective-permute-start.26
  846.3 15.0 %collective-permute-start.29 = (f32[3,6,6,1]{3,2,1,0:T(8,128)S(1)}, f32[3,6,6,1]{3,2,1,0:T(8,128)S(1)}, u32[]{:S(2)}, u32[]{:S(2)}) collective-permute-start(f32[3,6,6,1]{3,2,1,0:T(8,128)S(1)} %get-tuple-element.66), channel_id=1, source_target_pairs={{1,0},{2,1},{3,2},{4,3},{5,4},{6,5},{7,6},{9,8},{10,9},{11,10},{12... | collective-permute-start | bytes 1304 | tf_op jit(solution)/shard_map/ppermute | solution.py:29
  852.8 15.9 %collective-permute-start.28 = (f32[3,6,6,1]{3,2,1,0:T(8,128)S(1)}, f32[3,6,6,1]{3,2,1,0:T(8,128)S(1)}, u32[]{:S(2)}, u32[]{:S(2)}) collective-permute-start(f32[3,6,6,1]{3,2,1,0:T(8,128)S(1)} %get-tuple-element.65), channel_id=1, source_target_pairs={{0,1},{1,2},{2,3},{3,4},{4,5},{5,6},{6,7},{8,9},{9,10},{10,11},{11... | collective-permute-start | bytes 1304 | tf_op jit(solution)/shard_map/ppermute | solution.py:27
  (151 other events, 6013.5 us)
where the time goes:
time: 972 us; the launch traced here: 961 us
  other arithmetic  458 us (47%)
  local copies, waits for them, and re-layouts  243 us (25%)
  starting transfers between devices  171 us (18%)
  waiting for transfers between devices  84.6 us (9%)
    scatter-add x54, other arithmetic, reverse_step(): partial_value = partial_value.at[:, target].add(weight[None] * lifted)  392 us
    gather x108, local copies, waits for them, and re-layouts, reverse_step(): weighted = weight[None] * flat_values[:, target]  174 us
    ppermute x15, starting transfers between devices, with_halo(): lax.ppermute(head, axis, [((i + 1) % count, i) for i in range(ends)])  120 us
    ppermute x15, waiting for transfers between devices, with_halo(): lax.ppermute(tail, axis, [(i, (i + 1) % count) for i in range(ends)])  78.7 us
    mul x54, local copies, waits for them, and re-layouts, reverse_step(): partial_value = partial_value.at[:, target].add(weight[None] * lifted)  54.3 us
    ppermute x15, starting transfers between devices, with_halo(): lax.ppermute(tail, axis, [(i, (i + 1) % count) for i in range(ends)])  51.2 us
    gather x53, other arithmetic, reverse_step(): weighted = weight[None] * flat_values[:, target]  23.9 us
  transfers between devices with their start and end apart: 30, of which 19 were waited for; matrix products, arithmetic and copies ran while one was open for 4% of the time, Pallas kernels for 0%

commit v1 on v0

v1 whole, which is shorter than its diff:
```python
import functools

import jax
import jax.numpy as jnp
from jax import lax
from jax.experimental import pallas as pl
from jax.experimental.pallas import tpu as pltpu
from jax.sharding import PartitionSpec as P

TIME_STEP = 0.2
APIC_SCALE = 4.0
STRESS_SCALE = 0.3
F32 = jnp.float32
BF16 = jnp.bfloat16
I32 = jnp.int32
AXES = ("gx", "gy", "gz")
VMEM = pl.BlockSpec(memory_space=pltpu.VMEM)
SMEM = pl.BlockSpec(memory_space=pltpu.SMEM)
CHUNKS = 8
ZROWS = 144


def contract(a, b, da, db, precision=None):
    return lax.dot_general(
        a, b, (((da,), (db,)), ((), ())), preferred_element_type=F32, precision=precision
    )


def nt(a, b):
    return contract(a, b, 1, 1)


def nn(a, b):
    return contract(a, b, 1, 0)


def split(x):
    hi = x.astype(BF16)
    return hi, (x - hi.astype(F32)).astype(BF16)


def rounded(x):
    hi = x.astype(BF16).astype(F32)
    return hi, x - hi


def spline(f):
    return 0.5 * (0.5 - f) * (0.5 - f), 0.75 - f * f, 0.5 * (0.5 + f) * (0.5 + f)


def iota(shape, axis):
    return lax.broadcasted_iota(I32, shape, axis)


def dense(ref, lead, rows):
    value = ref[lead] if lead is not None else ref[...]
    value = value.reshape(rows, CHUNKS, 128)
    return [value[i] for i in range(rows)]


def axis_tables(fx, cell_x, count):
    low, mid, high = spline(fx)
    plain, signed = [], []
    for plane in range(count):
        is_low, is_mid, is_high = cell_x == plane, cell_x + 1 == plane, cell_x + 2 == plane
        plain.append(jnp.where(is_low, low, jnp.where(is_mid, mid, jnp.where(is_high, high, 0.0))))
        signed.append(jnp.where(is_low, -low, jnp.where(is_high, high, 0.0)))
    return plain, signed


def y_tables(fy, cell_y, chunk):
    low, mid, high = (v[chunk : chunk + 1] for v in spline(fy))
    away = iota((8, 128), 0) - (cell_y[chunk : chunk + 1] + 1)
    plain = jnp.where(away == -1, low, jnp.where(away == 0, mid, jnp.where(away == 1, high, 0.0)))
    signed = jnp.where(away == -1, -low, jnp.where(away == 1, high, 0.0))
    return plain, signed


def build_z(fz, cell_z, w_hi, w_lo, d_hi, d_lo):
    low, mid, high = spline(fz)
    low_h, low_l = rounded(low)
    mid_h, mid_l = rounded(mid)
    high_h, high_l = rounded(high)
    to_low = jnp.where(cell_z == 0, 129, cell_z - 1)
    to_high = cell_z + 1
    inner = iota((128, 128), 0)
    edge = iota((16, 128), 0)
    edge = jnp.where(edge < 2, edge + 128, jnp.where(edge == 2, 0, jnp.where(edge == 3, 127, 999)))
    for chunk in range(CHUNKS):
        at = slice(chunk, chunk + 1)
        lanes = slice(chunk * 128, chunk * 128 + 128)
        for rows, index in ((slice(0, 128), inner), (slice(128, ZROWS), edge)):
            is_low, is_mid, is_high = index == to_low[at], index == cell_z[at], index == to_high[at]
            for plain, signed, (a, b, c) in (
                (w_hi, d_hi, (low_h, mid_h, high_h)),
                (w_lo, d_lo, (low_l, mid_l, high_l)),
            ):
                ends = jnp.where(is_high, c[at], 0.0)
                plain[rows, lanes] = jnp.where(
                    is_low, a[at], jnp.where(is_mid, b[at], ends)
                ).astype(BF16)
                signed[rows, lanes] = jnp.where(is_low, -a[at], ends).astype(BF16)


def cells_of(centre):
    return centre // 512, centre // 128 % 4, centre % 128


def transfer(adj, deform, affine):
    a_v, a_c, a_f = adj[0:3], adj[3:12], adj[12:21]
    b_f, b_c = [], []
    for i in range(3):
        for j in range(3):
            b_f.append(
                a_f[3 * i + j]
                + TIME_STEP * sum(affine[3 * m + i] * a_f[3 * m + j] for m in range(3))
            )
            b_c.append(
                a_c[3 * i + j]
                + TIME_STEP * sum(a_f[3 * i + m] * deform[3 * j + m] for m in range(3))
            )
    return a_v, b_c, b_f


def scatter_rows(a_v, b_c, frac, cell_x, cell_y, l0h, l0l, l2h, l2l):
    base, slope = [], []
    for c in range(3):
        base.append(a_v[c] - APIC_SCALE * sum(b_c[3 * c + j] * frac[j] for j in range(3)))
        slope.append([APIC_SCALE * b_c[3 * c + j] for j in range(3)])
    wx, wx1 = axis_tables(frac[0], cell_x, 6)
    for k in range(CHUNKS):
        at = slice(k, k + 1)
        lanes = slice(k * 128, k * 128 + 128)
        wy, wy1 = y_tables(frac[1], cell_y, k)
        for c in range(3):
            a = wy * base[c][at] + wy1 * slope[c][1][at]
            b = wy * slope[c][0][at]
            d = wy * slope[c][2][at]
            for pair in range(3):
                rows = slice(c * 48 + pair * 16, c * 48 + pair * 16 + 16)
                planes = (2 * pair, 2 * pair + 1)
                l0 = jnp.concatenate([wx[x][at] * a + wx1[x][at] * b for x in planes], axis=0)
                l2 = jnp.concatenate([wx[x][at] * d for x in planes], axis=0)
                l0h[rows, lanes], l0l[rows, lanes] = split(l0)
                l2h[rows, lanes], l2l[rows, lanes] = split(l2)


def scatter_sums(l0h, l0l, l2h, l2l, w_hi, w_lo, d_hi, d_lo):
    inner, edge = slice(0, 128), slice(128, ZROWS)
    terms = ((l0h, w_hi), (l0l, w_hi), (l0h, w_lo), (l2h, d_hi), (l2l, d_hi), (l2h, d_lo))
    core = sum(nt(a[...], b[inner]) for a, b in terms)
    ends = sum(nt(b[edge], a[...]) for a, b in terms)
    return core, ends


def write_planes(ends, width, hb, zu, zd):
    hb[...] = jnp.zeros(hb.shape, F32)
    zu[...] = jnp.zeros(zu.shape, F32)
    zd[...] = jnp.zeros(zd.shape, F32)
    hb[0:1, :width] = ends[0:1]
    hb[1:2, :width] = ends[1:2]
    zu[0:1, :width] = ends[0:1]
    zu[1:2, :width] = ends[3:4]
    zd[0:1, :width] = ends[1:2]
    zd[1:2, :width] = ends[2:3]


def first_kernel(
    live, adjoint, fractions, centers, deform, affine, mass,
    h, hb, zu, zd, bf_out, w_hi, w_lo, d_hi, d_lo,
    l0h, l0l, l2h, l2l,
):
    which = 1
    slots = iota((8, 128), 0) * 128 + iota((8, 128), 1)
    use = (slots < live[0, which]).astype(F32)
    adj = [v * use for v in dense(adjoint, None, 21)]
    frac = dense(fractions, which, 3)
    centre = centers[which : which + 1, :].reshape(CHUNKS, 128)
    cell_x, cell_y, cell_z = cells_of(centre)
    build_z(frac[2], cell_z, w_hi, w_lo, d_hi, d_lo)
    a_v, b_c, b_f = transfer(adj, dense(deform, which, 9), dense(affine, which, 9))
    for i in range(9):
        bf_out[i] = b_f[i]
    scatter_rows(a_v, b_c, frac, cell_x, cell_y, l0h, l0l, l2h, l2l)
    core, ends = scatter_sums(l0h, l0l, l2h, l2l, w_hi, w_lo, d_hi, d_lo)
    h[0:144] = core
    h[144:240] = jnp.zeros((96, 128), F32)
    for s in range(2):
        for x in range(4):
            row = 144 + s * 48 + (x + 1) * 8 + 1
            h[row : row + 4] = mass[s, x]
    lane, row = iota((16, 128), 1), iota((16, 128), 0)
    pick = (((row == 2) & (lane == 0)) | ((row == 3) & (lane == 127))).astype(F32)
    mass_ends = contract(pick, h[144:240], 1, 1, lax.Precision.HIGHEST)
    write_planes(jnp.concatenate([ends, mass_ends], axis=1), 240, hb, zu, zd)


def wide_rows(hb):
    return jnp.concatenate(
        [hb[0:1, :128], hb[0:1, 128:], hb[1:2, :128], hb[1:2, 128:], jnp.zeros((4, 128), F32)], axis=0
    )


def from_wide(rows):
    top = jnp.concatenate([rows[0:1], rows[1:2]], axis=1)
    low = jnp.concatenate([rows[2:3], rows[3:4]], axis=1)
    return jnp.concatenate([top, low, jnp.zeros((6, 256), F32)], axis=0)


def transposed(rows):
    return jnp.concatenate([rows, jnp.zeros((120, 256), F32)], axis=0).T


def z_kernel(comps, h, hb, from_low, from_high, h_out, hb_out, yu, yd):
    low, high = from_low[...], from_high[...]
    pad = jnp.zeros((6, 256), F32)
    halo = hb[...] + jnp.concatenate([high[1:2], low[1:2], pad], axis=0)
    hb_out[...] = halo
    wall = transposed(jnp.concatenate([low[0:1], high[0:1], pad], axis=0))
    lane = iota((8, 128), 1)
    row = iota((8, 128), 0)
    blocks = comps * 6
    up, down = None, None
    for q in range(blocks):
        rows = slice(q * 8, q * 8 + 8)
        tile = (
            h[rows]
            + jnp.where(lane == 0, wall[rows, 0:1], 0.0)
            + jnp.where(lane == 127, wall[rows, 1:2], 0.0)
        )
        h_out[rows] = tile
        place = 2 * (q % 4)
        chosen = (row >= place) & (row < place + 2)
        a = pltpu.roll(tile, (place - 4) % 8, 0) if place != 4 else tile
        b = pltpu.roll(tile, place, 0) if place else tile
        up = jnp.where(chosen, a, 0.0 if up is None else up)
        down = jnp.where(chosen, b, 0.0 if down is None else down)
        if q % 4 == 3 or q == blocks - 1:
            out = slice(q // 4 * 8, q // 4 * 8 + 8)
            yu[out] = up
            yd[out] = down
            up, down = None, None
    packed = (blocks + 3) // 4 * 8
    yu[packed : packed + 8] = wide_rows(halo)
    yd[packed : packed + 8] = wide_rows(halo)


def y_kernel(comps, h, hb, from_low, from_high, h_out, hb_out, xu, xd):
    row = iota((8, 128), 0)
    blocks = comps * 6
    packed = (blocks + 3) // 4 * 8
    for q in range(blocks):
        rows = slice(q * 8, q * 8 + 8)
        place = 2 * (q % 4)
        src = slice(q // 4 * 8, q // 4 * 8 + 8)
        a, b = from_low[src], from_high[src]
        a = pltpu.roll(a, (-place) % 8, 0) if place else a
        b = pltpu.roll(b, (4 - place) % 8, 0) if place != 4 else b
        tile = (
            h[rows] + jnp.where(row < 2, a, 0.0) + jnp.where((row >= 4) & (row < 6), b, 0.0)
        )
        h_out[rows] = tile
        c, x = q // 6, q % 6
        if x >= 4:
            xu[c * 16 + (x - 4) * 8 : c * 16 + (x - 4) * 8 + 8] = tile
        if x < 2:
            xd[c * 16 + x * 8 : c * 16 + x * 8 + 8] = tile
    place = iota((8, 256), 1) % 8
    a = pltpu.roll(from_wide(from_low[packed : packed + 8]), 252, 1)
    b = pltpu.roll(from_wide(from_high[packed : packed + 8]), 4, 1)
    halo = hb[...] + jnp.where(place < 2, a, 0.0) + jnp.where((place >= 4) & (place < 6), b, 0.0)
    hb_out[...] = halo
    xu[comps * 16 : comps * 16 + 8] = wide_rows(halo)
    xd[comps * 16 : comps * 16 + 8] = wide_rows(halo)


def x_fold(comps, h, hb, from_low, from_high, total):
    for c in range(comps):
        total[c * 48 : c * 48 + 16] = h[c * 48 : c * 48 + 16] + from_low[c * 16 : c * 16 + 16]
        total[c * 48 + 16 : c * 48 + 32] = h[c * 48 + 16 : c * 48 + 32]
        total[c * 48 + 32 : c * 48 + 48] = (
            h[c * 48 + 32 : c * 48 + 48] + from_high[c * 16 : c * 16 + 16]
        )
    plane = iota((8, 256), 1) % 48 // 8
    a = pltpu.roll(from_wide(from_low[comps * 16 : comps * 16 + 8]), 224, 1)
    b = pltpu.roll(from_wide(from_high[comps * 16 : comps * 16 + 8]), 32, 1)
    return hb[...] + jnp.where(plane < 2, a, 0.0) + jnp.where(plane >= 4, b, 0.0)


def node_values(spot, extents, total, halo, mass_at, mass_halo, g_hi, g_lo):
    first_x, first_y, first_z = spot[0], spot[1], spot[2]
    lane, row = iota((8, 128), 1), iota((8, 128), 0)
    node_z = first_z + lane
    node_y = first_y + row - 1
    keep_yz = (
        (node_z >= 1) & (node_z <= extents[2] - 2) & (node_y >= 1) & (node_y <= extents[1] - 2)
    )
    wide = iota((8, 256), 1)
    side = iota((8, 256), 0)
    halo_x = first_x + wide % 48 // 8 - 1
    halo_y = first_y + wide % 8 - 1
    halo_z = first_z + jnp.where(side == 0, 128, -1)
    keep = (
        (halo_x >= 1) & (halo_x <= extents[0] - 2)
        & (halo_y >= 1) & (halo_y <= extents[1] - 2)
        & (halo_z >= 1) & (halo_z <= extents[2] - 2)
        & (side < 2) & (wide < 144) & (wide % 8 < 6)
    )
    ends = jnp.where(keep, halo / jnp.where(keep, mass_halo, 1.0), 0.0)
    columns = transposed(ends)
    g_hi[:, 128:256], g_lo[:, 128:256] = split(columns[0:144])
    for x in range(6):
        node_x = first_x + x - 1
        keep_here = keep_yz & (row < 6) & (node_x >= 1) & (node_x <= extents[0] - 2)
        mass = jnp.where(keep_here, mass_at(x), 1.0)
        for c in range(3):
            rows = slice(c * 48 + x * 8, c * 48 + x * 8 + 8)
            total[rows] = jnp.where(keep_here, total[rows] / mass, 0.0)
    g_hi[:, 0:128], g_lo[:, 0:128] = split(total[0:144])


def gather(frac, cell_x, cell_y, g_hi, g_lo, w_hi, w_lo, d_hi, d_lo, s0, sz, rows12):
    a, b = g_hi[:, 0:ZROWS], g_lo[:, 0:ZROWS]
    s0[...] = nn(a, w_hi[...]) + nn(b, w_hi[...]) + nn(a, w_lo[...])
    sz[...] = nn(a, d_hi[...]) + nn(b, d_hi[...]) + nn(a, d_lo[...])
    wx, wx1 = axis_tables(frac[0], cell_x, 6)
    for k in range(CHUNKS):
        at = slice(k, k + 1)
        lanes = slice(k * 128, k * 128 + 128)
        wy, wy1 = y_tables(frac[1], cell_y, k)
        for c in range(3):
            plain = [s0[c * 48 + x * 8 : c * 48 + x * 8 + 8, lanes] for x in range(6)]
            slope = [sz[c * 48 + x * 8 : c * 48 + x * 8 + 8, lanes] for x in range(6)]
            r0 = sum(wx[x][at] * plain[x] for x in range(6))
            r1 = sum(wx1[x][at] * plain[x] for x in range(6))
            rz = sum(wx[x][at] * slope[x] for x in range(6))
            for i, v in enumerate((wy * r0, wy * r1, wy1 * r0, wy * rz)):
                rows12[c * 4 + i, at, :] = jnp.sum(v, axis=0, keepdims=True)


def particle(rows12, frac, b_f, deform, use):
    r_v = [rows12[c * 4] for c in range(3)]
    area = [rows12[c * 4 + 1 + j] - r_v[c] * frac[j] for c in range(3) for j in range(3)]
    stress = [-STRESS_SCALE * v for v in area]
    cof = []
    for i in range(3):
        for j in range(3):
            i1, i2, j1, j2 = (i + 1) % 3, (i + 2) % 3, (j + 1) % 3, (j + 2) % 3
            cof.append(
                deform[3 * i1 + j1] * deform[3 * i2 + j2] - deform[3 * i1 + j2] * deform[3 * i2 + j1]
            )
    det = sum(deform[j] * cof[j] for j in range(3))
    ratio = (stress[0] + stress[4] + stress[8]) / det
    out = r_v + area
    for i in range(3):
        for j in range(3):
            shear = sum((stress[3 * i + m] + stress[3 * m + i]) * deform[3 * m + j] for m in range(3))
            out.append(b_f[3 * i + j] + shear + ratio * cof[3 * i + j])
    return [v * use for v in out]


def gather_first_kernel(
    extents, live, spot, h, hb, from_low, from_high, fractions, centers, deform, bf,
    w_hi, w_lo, d_hi, d_lo, pick,
    second, zu, zd, mid, mass_core, mass_halo,
    total, g_hi, g_lo, s0, sz, rows12, buf, hot,
):
    which = 1
    halo = x_fold(5, h, hb, from_low, from_high, total)
    mass_core[...] = total[144:192]
    wide = iota((8, 256), 1)

    def spread(step):
        start = 144 + step * 48
        out = jnp.ones((8, 256), F32)
        for c in range(3):
            moved = pltpu.roll(halo, (c * 48 - start) % 256, 1)
            out = jnp.where((wide >= c * 48) & (wide < c * 48 + 48), moved, out)
        return out

    mass_halo[...] = spread(0)
    node_values(
        spot, extents, total, halo,
        lambda x: total[192 + x * 8 : 192 + x * 8 + 8], spread(1), g_hi, g_lo,
    )
    frac = dense(fractions, which, 3)
    cell_x, cell_y, _ = cells_of(centers[which : which + 1, :].reshape(CHUNKS, 128))
    gather(frac, cell_x, cell_y, g_hi, g_lo, w_hi, w_lo, d_hi, d_lo, s0, sz, rows12)
    slots = iota((8, 128), 0) * 128 + iota((8, 128), 1)
    use = (slots < live[0, which]).astype(F32)
    out = particle(rows12, frac, [bf[i] for i in range(9)], dense(deform, which, 9), use)
    for i in range(21):
        second[i] = out[i]
        buf[i * 8 : i * 8 + 8] = out[i]
    buf[168:176] = jnp.zeros((8, 128), F32)
    hi, lo = split(buf[...])
    low_row = iota((128, 128), 0)
    row = iota((8, 128), 0)
    for t in range(9):
        index = pick[t : t + 1]
        hot[...] = (low_row == index % 128).astype(F32).astype(BF16)
        got = nn(hi, hot[...]) + nn(lo, hot[...])
        chosen = (row == index // 128) & (index >= 0)
        got = got.reshape(22, 8, 128)[0:21]
        got = jnp.sum(jnp.where(chosen[None], got, 0.0), axis=1)
        dest, place = ((zd, t), (mid, t - 3), (zu, t - 6))[t // 3]
        dest[:, place * 128 : place * 128 + 128] = got


def pieces(groups, at, tiles):
    lane = iota((21, 128), 1)
    out = [jnp.zeros((21, 128), F32) for _ in range(tiles)]
    for i, group in enumerate(groups):
        place = 32 * (i % 4)
        moved = pltpu.roll(group, (place - at) % 128, 1) if place != at else group
        out[i // 4] = jnp.where((lane >= place) & (lane < place + 32), moved, out[i // 4])
    return out


def lane_tile(ref, i):
    return ref[:, i * 128 : i * 128 + 128]


def route_y_kernel(mid, from_low, from_high, yu, yd):
    for i, ref in enumerate((mid, from_low, from_high)):
        yd[:, i * 128 : i * 128 + 128] = lane_tile(ref, 0)
        yu[:, i * 128 : i * 128 + 128] = lane_tile(ref, 2)


def route_x_kernel(mid, z_low, z_high, y_low, y_high, xu, xd, final):
    groups = [lane_tile(mid, 1), lane_tile(z_low, 1), lane_tile(z_high, 1)]
    groups += [lane_tile(y_low, i) for i in range(3)]
    groups += [lane_tile(y_high, i) for i in range(3)]
    for ref, at in ((xd, 0), (xu, 64)):
        for i, tile in enumerate(pieces(groups, at, 3)):
            ref[:, i * 128 : i * 128 + 128] = tile
    for i, tile in enumerate(pieces(groups[1:], 32, 2)):
        final[:, i * 128 : i * 128 + 128] = tile


def second_kernel(
    live, second, final, x_low, x_high, prior, send, fractions, centers, deform, affine,
    h, hb, zu, zd, bf_out, w_hi, w_lo, d_hi, d_lo,
    lh, ll, hot, l0h, l0l, l2h, l2l,
):
    which = 0
    row = iota((8, 128), 0)
    low_row = iota((128, 128), 0)
    moved = [lane_tile(final, 0), lane_tile(final, 1)]
    moved += [lane_tile(x_low, i) for i in range(3)] + [lane_tile(x_high, i) for i in range(3)]
    for t in range(16):
        index = prior[t : t + 1] if t < 8 else send[t - 8 : t - 7]
        lanes = slice(t * 128, t * 128 + 128)
        hot[:, lanes] = (low_row == index % 128).astype(F32).astype(BF16)
        chosen = row == index // 128
        for pair in range(11):
            tiles = []
            for r in (2 * pair, 2 * pair + 1):
                if r > 20:
                    tiles.append(jnp.zeros((8, 128), F32))
                    continue
                value = second[r, t : t + 1, :] if t < 8 else moved[t - 8][r : r + 1]
                tiles.append(jnp.where(chosen, value, 0.0))
            hi, lo = split(jnp.concatenate(tiles, axis=0))
            lh[pair * 16 : pair * 16 + 16, lanes] = hi
            ll[pair * 16 : pair * 16 + 16, lanes] = lo
    carried = nt(lh[...], hot[...]) + nt(ll[...], hot[...])
    slots = iota((8, 128), 0) * 128 + iota((8, 128), 1)
    use = (slots < live[0, which]).astype(F32)
    adj = [carried[i * 8 : i * 8 + 8] * use for i in range(21)]
    frac = dense(fractions, which, 3)
    cell_x, cell_y, cell_z = cells_of(centers[which : which + 1, :].reshape(CHUNKS, 128))
    build_z(frac[2], cell_z, w_hi, w_lo, d_hi, d_lo)
    a_v, b_c, b_f = transfer(adj, dense(deform, which, 9), dense(affine, which, 9))
    for i in range(9):
        bf_out[i] = b_f[i]
    scatter_rows(a_v, b_c, frac, cell_x, cell_y, l0h, l0l, l2h, l2l)
    core, ends = scatter_sums(l0h, l0l, l2h, l2l, w_hi, w_lo, d_hi, d_lo)
    h[...] = core
    write_planes(ends, 144, hb, zu, zd)


def gather_second_kernel(
    extents, live, spot, h, hb, from_low, from_high, fractions, centers, deform, bf,
    w_hi, w_lo, d_hi, d_lo, mass_core, mass_halo,
    result,
    total, g_hi, g_lo, s0, sz, rows12, packed,
):
    which = 0
    halo = x_fold(3, h, hb, from_low, from_high, total)
    node_values(
        spot, extents, total, halo,
        lambda x: mass_core[x * 8 : x * 8 + 8], mass_halo[...], g_hi, g_lo,
    )
    frac = dense(fractions, which, 3)
    cell_x, cell_y, _ = cells_of(centers[which : which + 1, :].reshape(CHUNKS, 128))
    gather(frac, cell_x, cell_y, g_hi, g_lo, w_hi, w_lo, d_hi, d_lo, s0, sz, rows12)
    slots = iota((8, 128), 0) * 128 + iota((8, 128), 1)
    use = (slots < live[0, which]).astype(F32)
    out = particle(rows12, frac, [bf[i] for i in range(9)], dense(deform, which, 9), use)
    for i in range(21):
        packed[i] = out[i]
    for k in range(CHUNKS):
        result[:, k * 128 : k * 128 + 128] = packed[:, k, :]


def shape(*dims, dtype=F32):
    return jax.ShapeDtypeStruct(dims, dtype)


def call(kernel, name, specs, outs, scratch=()):
    return pl.pallas_call(
        kernel,
        name=name,
        in_specs=list(specs),
        out_specs=[VMEM] * len(outs),
        out_shape=list(outs),
        scratch_shapes=[pltpu.VMEM(s, d) for s, d in scratch],
        compiler_params=pltpu.CompilerParams(vmem_limit_bytes=40 * 1024 * 1024),
    )


def both_ways(up, down, axis):
    count = lax.axis_size(axis)
    low = lax.ppermute(up, axis, [(i, i + 1) for i in range(count - 1)])
    high = lax.ppermute(down, axis, [(i + 1, i) for i in range(count - 1)])
    return low, high


def body(
    fractions, centers, deform, next_affine, cell_mass, final_adjoint,
    live_count, send_slot, receive_slot, receive_count, prior_slot,
):
    spot = jnp.stack([lax.axis_index("gx") * 4, lax.axis_index("gy") * 4, lax.axis_index("gz") * 128])
    spot = spot.astype(I32)
    extents = (lax.axis_size("gx") * 4, lax.axis_size("gy") * 4, lax.axis_size("gz") * 128)

    def cube(rows, fill):
        middle = jnp.full((1, 32), fill, I32)
        return jnp.concatenate([rows[:13], middle, rows[13:]]).reshape(3, 3, 3, 32)

    order = jnp.arange(32, dtype=I32)[None]
    chosen = jnp.where(order < receive_count[0][:, None], receive_slot[0], -1)
    pick = jnp.transpose(cube(chosen, -1), (2, 1, 0, 3))
    pick = jnp.concatenate([pick, jnp.full((3, 3, 1, 32), -1, I32)], axis=2).reshape(9, 128)
    back = cube(send_slot[0], 0)[::-1, ::-1, ::-1]
    back = jnp.concatenate([back[:, 1:], back[:, :1]], axis=1)
    back = jnp.concatenate([back[:, :, 1:], back[:, :, :1]], axis=2).reshape(3, 9, 32)
    blank = jnp.zeros((3, 32), I32)
    send = jnp.concatenate([back[1, 1:], back[2], blank, back[0], blank]).reshape(8, 128)
    prior = prior_slot.reshape(8, 128)

    wide = shape(ZROWS, 1024, dtype=BF16)
    weights = [wide] * 4
    lrows = [((144, 1024), BF16)] * 4
    gscratch = [
        ((144, 256), BF16), ((144, 256), BF16),
        ((144, 1024), F32), ((144, 1024), F32), ((12, 8, 128), F32),
    ]

    def fold(comps, h, hb, zu, zd):
        low, high = both_ways(zu, zd, "gz")
        packed = (comps * 6 + 3) // 4 * 8 + 8
        h, hb, yu, yd = call(
            functools.partial(z_kernel, comps), f"fold_z{comps}", [VMEM] * 4,
            [shape(comps * 48, 128), shape(8, 256), shape(packed, 128), shape(packed, 128)],
        )(h, hb, low, high)
        low, high = both_ways(yu, yd, "gy")
        rows = comps * 16 + 8
        h, hb, xu, xd = call(
            functools.partial(y_kernel, comps), f"fold_y{comps}", [VMEM] * 4,
            [shape(comps * 48, 128), shape(8, 256), shape(rows, 128), shape(rows, 128)],
        )(h, hb, low, high)
        low, high = both_ways(xu, xd, "gx")
        return h, hb, low, high

    h, hb, zu, zd, bf, *w = call(
        first_kernel, "scatter_first", [SMEM] + [VMEM] * 6,
        [shape(240, 128), shape(8, 256), shape(2, 256), shape(2, 256), shape(9, 8, 128)] + weights,
        lrows,
    )(live_count, final_adjoint, fractions, centers, deform, next_affine, cell_mass)
    h, hb, low, high = fold(5, h, hb, zu, zd)
    second, zu, zd, mid, mass_core, mass_halo = call(
        functools.partial(gather_first_kernel, extents), "gather_first",
        [SMEM, SMEM] + [VMEM] * 13,
        [shape(21, 8, 128), shape(21, 384), shape(21, 384), shape(21, 384), shape(48, 128), shape(8, 256)],
        [((240, 128), F32)] + gscratch + [((176, 128), F32), ((128, 128), BF16)],
    )(live_count, spot, h, hb, low, high, fractions, centers, deform, bf, *w, pick)

    z_low, z_high = both_ways(zu, zd, "gz")
    yu, yd = call(route_y_kernel, "route_y", [VMEM] * 3, [shape(21, 384)] * 2)(mid, z_low, z_high)
    y_low, y_high = both_ways(yu, yd, "gy")
    xu, xd, final = call(
        route_x_kernel, "route_x", [VMEM] * 5, [shape(21, 384), shape(21, 384), shape(21, 256)]
    )(mid, z_low, z_high, y_low, y_high)
    x_low, x_high = both_ways(xu, xd, "gx")

    h, hb, zu, zd, bf, *w = call(
        second_kernel, "scatter_second", [SMEM] + [VMEM] * 10,
        [shape(144, 128), shape(8, 256), shape(2, 256), shape(2, 256), shape(9, 8, 128)] + weights,
        [((176, 2048), BF16)] * 2 + [((128, 2048), BF16)] + lrows,
    )(live_count, second, final, x_low, x_high, prior, send, fractions, centers, deform, next_affine)
    h, hb, low, high = fold(3, h, hb, zu, zd)
    (result,) = call(
        functools.partial(gather_second_kernel, extents), "gather_second",
        [SMEM, SMEM] + [VMEM] * 14,
        [shape(21, 1024)],
        [((144, 128), F32)] + gscratch + [((21, 8, 128), F32)],
    )(live_count, spot, h, hb, low, high, fractions, centers, deform, bf, *w, mass_core, mass_halo)
    return result


def solution(mesh):
    spread = AXES
    in_specs = (
        P(None, None, spread), P(None, spread), P(None, None, spread), P(None, None, spread),
        P(None, "gx", "gy", "gz"), P(None, spread), P(spread, None), P(spread, None, None),
        P(spread, None, None), P(spread, None), P(spread),
    )
    return jax.shard_map(
        body, mesh=mesh, in_specs=in_specs, out_specs=P(None, spread), check_vma=False
    )
```

time: 972 us -> 140 us (0.14)
  the two profiles are of different devices: /device:TPU:158 before, /device:TPU:105 now
where the time goes in v1:
time: 140 us; the launch traced here: 139 us
  starting transfers between devices  78.2 us (56%)
  waiting for transfers between devices  45.1 us (32%)
  Pallas kernels  10.3 us (7%)
  local copies, waits for them, and re-layouts  4.4 us (3%)
    ppermute x9, starting transfers between devices, both_ways(): low = lax.ppermute(up, axis, [(i, i + 1) for i in range(count - 1)])  53.2 us
    ppermute x9, waiting for transfers between devices, both_ways(): high = lax.ppermute(down, axis, [(i + 1, i) for i in range(count - 1)])  44.8 us
    ppermute x9, starting transfers between devices, both_ways(): high = lax.ppermute(down, axis, [(i + 1, i) for i in range(count - 1)])  25.1 us
    unnamed x25, local copies, waits for them, and re-layouts  3.15 us
    pallas_call x1, Pallas kernels, body(): call(second_kernel, 'scatter_second', [SMEM] + [VMEM] * 10, [shape(144, 1...  3.02 us
  transfers between devices with their start and end apart: 18, of which 10 were waited for; matrix products, arithmetic and copies ran while one was open for 1% of the time, Pallas kernels for 0%

profile of v1, /device:TPU:105, one launch (start us, length us, event | category | flops | bytes accessed | tf_op | source)
XLA Modules:
  0.0 138.8 jit_solution(3516682903651041273)
XLA Ops:
  0.0 0.9 copy.25.deform
  1.1 0.6 copy-done
  1.7 0.2 copy-done.1
  1.9 2.3 %scatter_first.1 = (f32[240,128]{1,0:T(8,128)S(1)}, f32[8,256]{1,0:T(8,128)S(1)}, f32[2,256]{1,0:T(2,128)S(1)}, f32[2,256]{1,0:T(2,128)S(1)}, f32[9,8,128]{2,1,0...) custom-call(s32[1,2]{1,0:T(1,128)S(1)} %copy-done.3, ...), custom_call_target="tpu_custom_call" | custom-call | tf_op jit(solution)/shard_map/scatter_first/pallas_call | solution.py:577
  4.2 12.8 %collective-permute-start = (f32[2,256]{1,0:T(2,128)S(1)}, f32[2,256]{1,0:T(2,128)S(1)}, u32[]{:S(2)}, u32[]{:S(2)}) collective-permute-start(f32[2,256]{1,0:T(2,128)S(1)} %get-tuple-element.52), channel_id=1, source_target_pairs={{0,1},{1,2},{2,3},{3,4},{4,5},{5,6},{6,7},{8,9},{9,10},{10,11},{11... | collective-permute-start | bytes 6152 | tf_op jit(solution)/shard_map/ppermute | solution.py:525
  17.0 2.1 %collective-permute-start.1 = (f32[2,256]{1,0:T(2,128)S(1)}, f32[2,256]{1,0:T(2,128)S(1)}, u32[]{:S(2)}, u32[]{:S(2)}) collective-permute-start(f32[2,256]{1,0:T(2,128)S(1)} %get-tuple-element.53), channel_id=1, source_target_pairs={{1,0},{2,1},{3,2},{4,3},{5,4},{6,5},{7,6},{9,8},{10,9},{11,10},{12... | collective-permute-start | bytes 6152 | tf_op jit(solution)/shard_map/ppermute | solution.py:526
  19.2 0.7 copy-done.9
  19.9 0.1 pad.9.clone
  20.3 0.6 copy-done.6
  20.9 0.7 slice-done
  21.6 8.4 %collective-permute-done.1.from_high = f32[2,256]{1,0:T(2,128)S(1)} collective-permute-done((f32[2,256]{1,0:T(2,128)S(1)}, f32[2,256]{1,0:T(2,128)S(1)}, u32[]{:S(2)}, u32[]{:S(2)}) %collective-permute-start.1) | collective-permute-done | bytes 2080 | tf_op jit(solution)/shard_map/ppermute | solution.py:526
  30.0 0.3 fold_z5.1
  30.3 4.6 %collective-permute-start.2 = (f32[72,128]{1,0:T(8,128)S(1)}, f32[72,128]{1,0:T(8,128)S(1)}, u32[]{:S(2)}, u32[]{:S(2)}) collective-permute-start(f32[72,128]{1,0:T(8,128)S(1)} %get-tuple-element.56), channel_id=1, source_target_pairs={{0,8},{8,16},{16,24},{24,32},{32,40},{40,48},{48,56},{56,64},{64,7... | collective-permute-start | bytes 110600 | tf_op jit(solution)/shard_map/ppermute | solution.py:525
  35.0 1.9 %collective-permute-start.3 = (f32[72,128]{1,0:T(8,128)S(1)}, f32[72,128]{1,0:T(8,128)S(1)}, u32[]{:S(2)}, u32[]{:S(2)}) collective-permute-start(f32[72,128]{1,0:T(8,128)S(1)} %get-tuple-element.57), channel_id=1, source_target_pairs={{8,0},{16,8},{24,16},{32,24},{40,32},{48,40},{56,48},{64,56},{72,6... | collective-permute-start | bytes 110600 | tf_op jit(solution)/shard_map/ppermute | solution.py:526
  36.9 4.5 %collective-permute-done.3.from_high = f32[72,128]{1,0:T(8,128)S(1)} collective-permute-done((f32[72,128]{1,0:T(8,128)S(1)}, f32[72,128]{1,0:T(8,128)S(1)}, u32[]{:S(2)}, u32[]{:S(2)}) %collective-permute-start.3) | collective-permute-done | bytes 36896 | tf_op jit(solution)/shard_map/ppermute | solution.py:526
  41.5 0.1 fold_y5.1
  41.5 3.1 %collective-permute-start.4 = (f32[88,128]{1,0:T(8,128)S(1)}, f32[88,128]{1,0:T(8,128)S(1)}, u32[]{:S(2)}, u32[]{:S(2)}) collective-permute-start(f32[88,128]{1,0:T(8,128)S(1)} %get-tuple-element.60), channel_id=1, source_target_pairs={{0,128},{128,256},{256,384},{1,129},{129,257},{257,385},{2,130},{1... | collective-permute-start | bytes 135176 | tf_op jit(solution)/shard_map/ppermute | solution.py:525
  44.7 1.3 collective-permute-start.5
  46.0 0.1 pad_add_fusion.4.spot
  46.1 0.1 reshape.26.pick
  46.2 3.3 %collective-permute-done.5.from_high = f32[88,128]{1,0:T(8,128)S(1)} collective-permute-done((f32[88,128]{1,0:T(8,128)S(1)}, f32[88,128]{1,0:T(8,128)S(1)}, u32[]{:S(2)}, u32[]{:S(2)}) %collective-permute-start.5) | collective-permute-done | bytes 45088 | tf_op jit(solution)/shard_map/ppermute | solution.py:526
  49.5 2.0 %gather_first.1 = (f32[21,8,128]{2,1,0:T(8,128)S(1)}, f32[21,384]{1,0:T(8,128)S(1)}, f32[21,384]{1,0:T(8,128)S(1)}, f32[21,384]{1,0:T(8,128)S(1)}, f32[48,128]{1,0:T(8,128)S(1)}, /*index=5*/f32[8,256]{1,0:T(8,128)S(1)}) custom-call(s32[1,2]{1,0:T(1,128)S(1)} %copy-done.3, s32[3]{0:T(128)S(1)} %pad_add_fusion.4.spot, f32[240,128]{1,0:T(8,128)S(1)} %get-tuple-element.58.h, ...), custom_call_target="tpu_custom_call" | custom-call | tf_op jit(solution)/shard_map/gather_first/pallas_call | solution.py:583
  51.5 5.3 %collective-permute-start.6 = (f32[21,384]{1,0:T(8,128)S(1)}, f32[21,384]{1,0:T(8,128)S(1)}, u32[]{:S(2)}, u32[]{:S(2)}) collective-permute-start(f32[21,384]{1,0:T(8,128)S(1)} %get-tuple-element.69), channel_id=1, source_target_pairs={{0,1},{1,2},{2,3},{3,4},{4,5},{5,6},{6,7},{8,9},{9,10},{10,11},{11... | collective-permute-start | bytes 96776 | tf_op jit(solution)/shard_map/ppermute | solution.py:525
  56.8 9.6 %collective-permute-start.7 = (f32[21,384]{1,0:T(8,128)S(1)}, f32[21,384]{1,0:T(8,128)S(1)}, u32[]{:S(2)}, u32[]{:S(2)}) collective-permute-start(f32[21,384]{1,0:T(8,128)S(1)} %get-tuple-element.70), channel_id=1, source_target_pairs={{1,0},{2,1},{3,2},{4,3},{5,4},{6,5},{7,6},{9,8},{10,9},{11,10},{12... | collective-permute-start | bytes 96776 | tf_op jit(solution)/shard_map/ppermute | solution.py:526
  66.4 0.4 collective-permute-done.6.from_low.z_low
  66.8 3.8 %collective-permute-done.7.from_high.z_high = f32[21,384]{1,0:T(8,128)S(1)} collective-permute-done((f32[21,384]{1,0:T(8,128)S(1)}, f32[21,384]{1,0:T(8,128)S(1)}, u32[]{:S(2)}, u32[]{:S(2)}) %collective-permute-start.7) | collective-permute-done | bytes 32288 | tf_op jit(solution)/shard_map/ppermute | solution.py:526
  70.6 5.4 %collective-permute-start.8 = (f32[21,384]{1,0:T(8,128)S(1)}, f32[21,384]{1,0:T(8,128)S(1)}, u32[]{:S(2)}, u32[]{:S(2)}) collective-permute-start(f32[21,384]{1,0:T(8,128)S(1)} %get-tuple-element.71), channel_id=1, source_target_pairs={{0,8},{8,16},{16,24},{24,32},{32,40},{40,48},{48,56},{56,64},{64,7... | collective-permute-start | bytes 96776 | tf_op jit(solution)/shard_map/ppermute | solution.py:525
  76.0 1.9 %collective-permute-start.9 = (f32[21,384]{1,0:T(8,128)S(1)}, f32[21,384]{1,0:T(8,128)S(1)}, u32[]{:S(2)}, u32[]{:S(2)}) collective-permute-start(f32[21,384]{1,0:T(8,128)S(1)} %get-tuple-element.72), channel_id=1, source_target_pairs={{8,0},{16,8},{24,16},{32,24},{40,32},{48,40},{56,48},{64,56},{72,6... | collective-permute-start | bytes 96776 | tf_op jit(solution)/shard_map/ppermute | solution.py:526
  78.0 4.5 %collective-permute-done.9.y_high = f32[21,384]{1,0:T(8,128)S(1)} collective-permute-done((f32[21,384]{1,0:T(8,128)S(1)}, f32[21,384]{1,0:T(8,128)S(1)}, u32[]{:S(2)}, u32[]{:S(2)}) %collective-permute-start.9) | collective-permute-done | bytes 32288 | tf_op jit(solution)/shard_map/ppermute | solution.py:526
  82.5 0.1 route_x.1
  82.6 3.1 %collective-permute-start.10 = (f32[21,384]{1,0:T(8,128)S(1)}, f32[21,384]{1,0:T(8,128)S(1)}, u32[]{:S(2)}, u32[]{:S(2)}) collective-permute-start(f32[21,384]{1,0:T(8,128)S(1)} %get-tuple-element.74), channel_id=1, source_target_pairs={{0,128},{128,256},{256,384},{1,129},{129,257},{257,385},{2,130},{1... | collective-permute-start | bytes 96776 | tf_op jit(solution)/shard_map/ppermute | solution.py:525
  85.8 1.3 collective-permute-start.11
  87.2 0.2 concatenate.23
  87.3 0.1 reshape.30.send
  87.4 3.1 %collective-permute-done.11.x_high = f32[21,384]{1,0:T(8,128)S(1)} collective-permute-done((f32[21,384]{1,0:T(8,128)S(1)}, f32[21,384]{1,0:T(8,128)S(1)}, u32[]{:S(2)}, u32[]{:S(2)}) %collective-permute-start.11) | collective-permute-done | bytes 32288 | tf_op jit(solution)/shard_map/ppermute | solution.py:526
  90.5 3.0 %scatter_second.1 = (f32[144,128]{1,0:T(8,128)S(1)}, f32[8,256]{1,0:T(8,128)S(1)}, f32[2,256]{1,0:T(2,128)S(1)}, f32[2,256]{1,0:T(2,128)S(1)}, f32[9,8,128]{2,1,...) custom-call(s32[1,2]{1,0:T(1,128)S(1)} %copy-done.3, ...), custom_call_target="tpu_custom_call" | custom-call | tf_op jit(solution)/shard_map/scatter_second/pallas_call | solution.py:598
  93.5 11.3 %collective-permute-start.12 = (f32[2,256]{1,0:T(2,128)S(1)}, f32[2,256]{1,0:T(2,128)S(1)}, u32[]{:S(2)}, u32[]{:S(2)}) collective-permute-start(f32[2,256]{1,0:T(2,128)S(1)} %get-tuple-element.78), channel_id=1, source_target_pairs={{0,1},{1,2},{2,3},{3,4},{4,5},{5,6},{6,7},{8,9},{9,10},{10,11},{11... | collective-permute-start | bytes 6152 | tf_op jit(solution)/shard_map/ppermute | solution.py:525
  104.8 3.6 %collective-permute-start.13 = (f32[2,256]{1,0:T(2,128)S(1)}, f32[2,256]{1,0:T(2,128)S(1)}, u32[]{:S(2)}, u32[]{:S(2)}) collective-permute-start(f32[2,256]{1,0:T(2,128)S(1)} %get-tuple-element.79), channel_id=1, source_target_pairs={{1,0},{2,1},{3,2},{4,3},{5,4},{6,5},{7,6},{9,8},{10,9},{11,10},{12... | collective-permute-start | bytes 6152 | tf_op jit(solution)/shard_map/ppermute | solution.py:526
  108.4 9.4 %collective-permute-done.13.from_high = f32[2,256]{1,0:T(2,128)S(1)} collective-permute-done((f32[2,256]{1,0:T(2,128)S(1)}, f32[2,256]{1,0:T(2,128)S(1)}, u32[]{:S(2)}, u32[]{:S(2)}) %collective-permute-start.13) | collective-permute-done | bytes 2080 | tf_op jit(solution)/shard_map/ppermute | solution.py:526
  117.8 0.2 fold_z3.1
  118.1 4.8 %collective-permute-start.14 = (f32[48,128]{1,0:T(8,128)S(1)}, f32[48,128]{1,0:T(8,128)S(1)}, u32[]{:S(2)}, u32[]{:S(2)}) collective-permute-start(f32[48,128]{1,0:T(8,128)S(1)} %get-tuple-element.82), channel_id=1, source_target_pairs={{0,8},{8,16},{16,24},{24,32},{32,40},{40,48},{48,56},{56,64},{64,7... | collective-permute-start | bytes 73736 | tf_op jit(solution)/shard_map/ppermute | solution.py:525
  122.8 1.9 %collective-permute-start.15 = (f32[48,128]{1,0:T(8,128)S(1)}, f32[48,128]{1,0:T(8,128)S(1)}, u32[]{:S(2)}, u32[]{:S(2)}) collective-permute-start(f32[48,128]{1,0:T(8,128)S(1)} %get-tuple-element.83), channel_id=1, source_target_pairs={{8,0},{16,8},{24,16},{32,24},{40,32},{48,40},{56,48},{64,56},{72,6... | collective-permute-start | bytes 73736 | tf_op jit(solution)/shard_map/ppermute | solution.py:526
  124.8 4.4 %collective-permute-done.15.from_high = f32[48,128]{1,0:T(8,128)S(1)} collective-permute-done((f32[48,128]{1,0:T(8,128)S(1)}, f32[48,128]{1,0:T(8,128)S(1)}, u32[]{:S(2)}, u32[]{:S(2)}) %collective-permute-start.15) | collective-permute-done | bytes 24608 | tf_op jit(solution)/shard_map/ppermute | solution.py:526
  129.2 0.1 fold_y3.1
  129.3 2.8 %collective-permute-start.16 = (f32[56,128]{1,0:T(8,128)S(1)}, f32[56,128]{1,0:T(8,128)S(1)}, u32[]{:S(2)}, u32[]{:S(2)}) collective-permute-start(f32[56,128]{1,0:T(8,128)S(1)} %get-tuple-element.86), channel_id=1, source_target_pairs={{0,128},{128,256},{256,384},{1,129},{129,257},{257,385},{2,130},{1... | collective-permute-start | bytes 86024 | tf_op jit(solution)/shard_map/ppermute | solution.py:525
  132.1 1.3 collective-permute-start.17
  133.4 3.3 %collective-permute-done.17.from_high = f32[56,128]{1,0:T(8,128)S(1)} collective-permute-done((f32[56,128]{1,0:T(8,128)S(1)}, f32[56,128]{1,0:T(8,128)S(1)}, u32[]{:S(2)}, u32[]{:S(2)}) %collective-permute-start.17) | collective-permute-done | bytes 28704 | tf_op jit(solution)/shard_map/ppermute | solution.py:526
  136.7 2.1 %gather_second.1 = f32[21,1024]{1,0:T(8,128)} custom-call(s32[1,2]{1,0:T(1,128)S(1)} %copy-done.3, s32[3]{0:T(128)S(1)} %pad_add_fusion.4.spot, f32[144,128]{1,0:T(8,128)S(1)} %get-tuple-element.84.h, f32[8,256]{1,0:T(8,128)S(1)} %get-tuple-element.85.hb, f32[56,128]{1,0:T(8,128)S(1)} %collective-permute-done.16.from_low, ...), custom_call_target="tpu_custom_call" | custom-call | tf_op jit(solution)/shard_map/gather_second/pallas_call | solution.py:604
  (53 shorter events, 0.6 us)
Async XLA Ops:
  0.0 1.0 copy-start.7
  0.0 1.0 copy-start.5
  1.0 0.7 copy-start
  1.0 0.9 copy-start.1
  1.0 0.9 copy-start.2
  1.0 0.9 copy-start.3
  1.9 17.2 %copy-start.8 = (s32[1,26,32]{2,0,1:T(1,128)S(1)}, s32[1,26,32]{2,0,1:T(1,128)}, u32[]{:S(2)}) copy-start(s32[1,26,32]{2,0,1:T(1,128)} %param.19) | copy-start | bytes 9988
  4.2 17.4 %collective-permute-start = (f32[2,256]{1,0:T(2,128)S(1)}, f32[2,256]{1,0:T(2,128)S(1)}, u32[]{:S(2)}, u32[]{:S(2)}) collective-permute-start(f32[2,256]{1,0:T(2,128)S(1)} %get-tuple-element.52), channel_id=1, source_target_pairs={{0,1},{1,2},{2,3},{3,4},{4,5},{5,6},{6,7},{8,9},{9,10},{10,11},{11... | collective-permute-start | bytes 6152 | tf_op jit(solution)/shard_map/ppermute | solution.py:525
  17.0 2.2 %copy-start.10 = (s32[1,26]{1,0:T(1,128)S(1)}, s32[1,26]{1,0:T(1,128)}, u32[]{:S(2)}) copy-start(s32[1,26]{1,0:T(1,128)} %param.20) | copy-start | bytes 316
  17.0 13.0 %collective-permute-start.1 = (f32[2,256]{1,0:T(2,128)S(1)}, f32[2,256]{1,0:T(2,128)S(1)}, u32[]{:S(2)}, u32[]{:S(2)}) collective-permute-start(f32[2,256]{1,0:T(2,128)S(1)} %get-tuple-element.53), channel_id=1, source_target_pairs={{1,0},{2,1},{3,2},{4,3},{5,4},{6,5},{7,6},{9,8},{10,9},{11,10},{12... | collective-permute-start | bytes 6152 | tf_op jit(solution)/shard_map/ppermute | solution.py:526
  19.2 0.7 copy-start.9
  20.3 0.6 copy-start.6
  20.9 0.7 slice-start
  30.3 6.6 %collective-permute-start.2 = (f32[72,128]{1,0:T(8,128)S(1)}, f32[72,128]{1,0:T(8,128)S(1)}, u32[]{:S(2)}, u32[]{:S(2)}) collective-permute-start(f32[72,128]{1,0:T(8,128)S(1)} %get-tuple-element.56), channel_id=1, source_target_pairs={{0,8},{8,16},{16,24},{24,32},{32,40},{40,48},{48,56},{56,64},{64,7... | collective-permute-start | bytes 110600 | tf_op jit(solution)/shard_map/ppermute | solution.py:525
  35.0 6.5 %collective-permute-start.3 = (f32[72,128]{1,0:T(8,128)S(1)}, f32[72,128]{1,0:T(8,128)S(1)}, u32[]{:S(2)}, u32[]{:S(2)}) collective-permute-start(f32[72,128]{1,0:T(8,128)S(1)} %get-tuple-element.57), channel_id=1, source_target_pairs={{8,0},{16,8},{24,16},{32,24},{40,32},{48,40},{56,48},{64,56},{72,6... | collective-permute-start | bytes 110600 | tf_op jit(solution)/shard_map/ppermute | solution.py:526
  41.5 4.6 %collective-permute-start.4 = (f32[88,128]{1,0:T(8,128)S(1)}, f32[88,128]{1,0:T(8,128)S(1)}, u32[]{:S(2)}, u32[]{:S(2)}) collective-permute-start(f32[88,128]{1,0:T(8,128)S(1)} %get-tuple-element.60), channel_id=1, source_target_pairs={{0,128},{128,256},{256,384},{1,129},{129,257},{257,385},{2,130},{1... | collective-permute-start | bytes 135176 | tf_op jit(solution)/shard_map/ppermute | solution.py:525
  44.7 4.8 %collective-permute-start.5 = (f32[88,128]{1,0:T(8,128)S(1)}, f32[88,128]{1,0:T(8,128)S(1)}, u32[]{:S(2)}, u32[]{:S(2)}) collective-permute-start(f32[88,128]{1,0:T(8,128)S(1)} %get-tuple-element.61), channel_id=1, source_target_pairs={{128,0},{256,128},{384,256},{129,1},{257,129},{385,257},{130,2},{2... | collective-permute-start | bytes 135176 | tf_op jit(solution)/shard_map/ppermute | solution.py:526
  51.5 15.3 %collective-permute-start.6 = (f32[21,384]{1,0:T(8,128)S(1)}, f32[21,384]{1,0:T(8,128)S(1)}, u32[]{:S(2)}, u32[]{:S(2)}) collective-permute-start(f32[21,384]{1,0:T(8,128)S(1)} %get-tuple-element.69), channel_id=1, source_target_pairs={{0,1},{1,2},{2,3},{3,4},{4,5},{5,6},{6,7},{8,9},{9,10},{10,11},{11... | collective-permute-start | bytes 96776 | tf_op jit(solution)/shard_map/ppermute | solution.py:525
  56.8 13.8 %collective-permute-start.7 = (f32[21,384]{1,0:T(8,128)S(1)}, f32[21,384]{1,0:T(8,128)S(1)}, u32[]{:S(2)}, u32[]{:S(2)}) collective-permute-start(f32[21,384]{1,0:T(8,128)S(1)} %get-tuple-element.70), channel_id=1, source_target_pairs={{1,0},{2,1},{3,2},{4,3},{5,4},{6,5},{7,6},{9,8},{10,9},{11,10},{12... | collective-permute-start | bytes 96776 | tf_op jit(solution)/shard_map/ppermute | solution.py:526
  70.6 7.4 %collective-permute-start.8 = (f32[21,384]{1,0:T(8,128)S(1)}, f32[21,384]{1,0:T(8,128)S(1)}, u32[]{:S(2)}, u32[]{:S(2)}) collective-permute-start(f32[21,384]{1,0:T(8,128)S(1)} %get-tuple-element.71), channel_id=1, source_target_pairs={{0,8},{8,16},{16,24},{24,32},{32,40},{40,48},{48,56},{56,64},{64,7... | collective-permute-start | bytes 96776 | tf_op jit(solution)/shard_map/ppermute | solution.py:525
  76.0 6.5 %collective-permute-start.9 = (f32[21,384]{1,0:T(8,128)S(1)}, f32[21,384]{1,0:T(8,128)S(1)}, u32[]{:S(2)}, u32[]{:S(2)}) collective-permute-start(f32[21,384]{1,0:T(8,128)S(1)} %get-tuple-element.72), channel_id=1, source_target_pairs={{8,0},{16,8},{24,16},{32,24},{40,32},{48,40},{56,48},{64,56},{72,6... | collective-permute-start | bytes 96776 | tf_op jit(solution)/shard_map/ppermute | solution.py:526
  82.6 4.7 %collective-permute-start.10 = (f32[21,384]{1,0:T(8,128)S(1)}, f32[21,384]{1,0:T(8,128)S(1)}, u32[]{:S(2)}, u32[]{:S(2)}) collective-permute-start(f32[21,384]{1,0:T(8,128)S(1)} %get-tuple-element.74), channel_id=1, source_target_pairs={{0,128},{128,256},{256,384},{1,129},{129,257},{257,385},{2,130},{1... | collective-permute-start | bytes 96776 | tf_op jit(solution)/shard_map/ppermute | solution.py:525
  85.8 4.7 %collective-permute-start.11 = (f32[21,384]{1,0:T(8,128)S(1)}, f32[21,384]{1,0:T(8,128)S(1)}, u32[]{:S(2)}, u32[]{:S(2)}) collective-permute-start(f32[21,384]{1,0:T(8,128)S(1)} %get-tuple-element.75), channel_id=1, source_target_pairs={{128,0},{256,128},{384,256},{129,1},{257,129},{385,257},{130,2},{2... | collective-permute-start | bytes 96776 | tf_op jit(solution)/shard_map/ppermute | solution.py:526
  87.4 3.1 %copy-start.4 = (s32[1024]{0:T(1024)S(1)}, s32[1024]{0:T(1024)}, u32[]{:S(2)}) copy-start(s32[1024]{0:T(1024)} %param.21) | copy-start | bytes 12292
  93.5 14.9 %collective-permute-start.12 = (f32[2,256]{1,0:T(2,128)S(1)}, f32[2,256]{1,0:T(2,128)S(1)}, u32[]{:S(2)}, u32[]{:S(2)}) collective-permute-start(f32[2,256]{1,0:T(2,128)S(1)} %get-tuple-element.78), channel_id=1, source_target_pairs={{0,1},{1,2},{2,3},{3,4},{4,5},{5,6},{6,7},{8,9},{9,10},{10,11},{11... | collective-permute-start | bytes 6152 | tf_op jit(solution)/shard_map/ppermute | solution.py:525
  104.8 13.0 %collective-permute-start.13 = (f32[2,256]{1,0:T(2,128)S(1)}, f32[2,256]{1,0:T(2,128)S(1)}, u32[]{:S(2)}, u32[]{:S(2)}) collective-permute-start(f32[2,256]{1,0:T(2,128)S(1)} %get-tuple-element.79), channel_id=1, source_target_pairs={{1,0},{2,1},{3,2},{4,3},{5,4},{6,5},{7,6},{9,8},{10,9},{11,10},{12... | collective-permute-start | bytes 6152 | tf_op jit(solution)/shard_map/ppermute | solution.py:526
  118.1 6.7 %collective-permute-start.14 = (f32[48,128]{1,0:T(8,128)S(1)}, f32[48,128]{1,0:T(8,128)S(1)}, u32[]{:S(2)}, u32[]{:S(2)}) collective-permute-start(f32[48,128]{1,0:T(8,128)S(1)} %get-tuple-element.82), channel_id=1, source_target_pairs={{0,8},{8,16},{16,24},{24,32},{32,40},{40,48},{48,56},{56,64},{64,7... | collective-permute-start | bytes 73736 | tf_op jit(solution)/shard_map/ppermute | solution.py:525
  122.8 6.4 %collective-permute-start.15 = (f32[48,128]{1,0:T(8,128)S(1)}, f32[48,128]{1,0:T(8,128)S(1)}, u32[]{:S(2)}, u32[]{:S(2)}) collective-permute-start(f32[48,128]{1,0:T(8,128)S(1)} %get-tuple-element.83), channel_id=1, source_target_pairs={{8,0},{16,8},{24,16},{32,24},{40,32},{48,40},{56,48},{64,56},{72,6... | collective-permute-start | bytes 73736 | tf_op jit(solution)/shard_map/ppermute | solution.py:526
  129.3 4.1 %collective-permute-start.16 = (f32[56,128]{1,0:T(8,128)S(1)}, f32[56,128]{1,0:T(8,128)S(1)}, u32[]{:S(2)}, u32[]{:S(2)}) collective-permute-start(f32[56,128]{1,0:T(8,128)S(1)} %get-tuple-element.86), channel_id=1, source_target_pairs={{0,128},{128,256},{256,384},{1,129},{129,257},{257,385},{2,130},{1... | collective-permute-start | bytes 86024 | tf_op jit(solution)/shard_map/ppermute | solution.py:525
  132.1 4.6 %collective-permute-start.17 = (f32[56,128]{1,0:T(8,128)S(1)}, f32[56,128]{1,0:T(8,128)S(1)}, u32[]{:S(2)}, u32[]{:S(2)}) collective-permute-start(f32[56,128]{1,0:T(8,128)S(1)} %get-tuple-element.87), channel_id=1, source_target_pairs={{128,0},{256,128},{384,256},{129,1},{257,129},{385,257},{130,2},{2... | collective-permute-start | bytes 86024 | tf_op jit(solution)/shard_map/ppermute | solution.py:526

commit v2 on v1

--- a/solution.py
+++ b/solution.py
@@ -76,7 +76,7 @@
     return plain, signed
 
 
-def build_z(fz, cell_z, w_hi, w_lo, d_hi, d_lo):
+def build_z(fz, cell_z, w_hi, w_lo, d_hi, d_lo, chunks=CHUNKS, edges_only=False):
     low, mid, high = spline(fz)
     low_h, low_l = rounded(low)
     mid_h, mid_l = rounded(mid)
@@ -86,10 +86,13 @@
     inner = iota((128, 128), 0)
     edge = iota((16, 128), 0)
     edge = jnp.where(edge < 2, edge + 128, jnp.where(edge == 2, 0, jnp.where(edge == 3, 127, 999)))
-    for chunk in range(CHUNKS):
+    parts = ((slice(0, 128), inner), (slice(128, ZROWS), edge))
+    if edges_only:
+        parts = ((slice(0, 16), edge),)
+    for chunk in range(chunks):
         at = slice(chunk, chunk + 1)
         lanes = slice(chunk * 128, chunk * 128 + 128)
-        for rows, index in ((slice(0, 128), inner), (slice(128, ZROWS), edge)):
+        for rows, index in parts:
             is_low, is_mid, is_high = index == to_low[at], index == cell_z[at], index == to_high[at]
             for plain, signed, (a, b, c) in (
                 (w_hi, d_hi, (low_h, mid_h, high_h)),
@@ -106,29 +109,34 @@
     return centre // 512, centre // 128 % 4, centre % 128
 
 
+def to_grid(adj, deform):
+    a_v, a_c, a_f = adj[0:3], adj[3:12], adj[12:21]
+    b_c = [
+        a_c[3 * i + j] + TIME_STEP * sum(a_f[3 * i + m] * deform[3 * j + m] for m in range(3))
+        for i in range(3)
+        for j in range(3)
+    ]
+    return a_v, b_c
+
+
 def transfer(adj, deform, affine):
-    a_v, a_c, a_f = adj[0:3], adj[3:12], adj[12:21]
-    b_f, b_c = [], []
-    for i in range(3):
-        for j in range(3):
-            b_f.append(
-                a_f[3 * i + j]
-                + TIME_STEP * sum(affine[3 * m + i] * a_f[3 * m + j] for m in range(3))
-            )
-            b_c.append(
-                a_c[3 * i + j]
-                + TIME_STEP * sum(a_f[3 * i + m] * deform[3 * j + m] for m in range(3))
-            )
+    a_v, b_c = to_grid(adj, deform)
+    a_f = adj[12:21]
+    b_f = [
+        a_f[3 * i + j] + TIME_STEP * sum(affine[3 * m + i] * a_f[3 * m + j] for m in range(3))
+        for i in range(3)
+        for j in range(3)
+    ]
     return a_v, b_c, b_f
 
 
-def scatter_rows(a_v, b_c, frac, cell_x, cell_y, l0h, l0l, l2h, l2l):
+def scatter_rows(a_v, b_c, frac, cell_x, cell_y, l0h, l0l, l2h, l2l, chunks=CHUNKS):
     base, slope = [], []
     for c in range(3):
         base.append(a_v[c] - APIC_SCALE * sum(b_c[3 * c + j] * frac[j] for j in range(3)))
         slope.append([APIC_SCALE * b_c[3 * c + j] for j in range(3)])
     wx, wx1 = axis_tables(frac[0], cell_x, 6)
-    for k in range(CHUNKS):
+    for k in range(chunks):
         at = slice(k, k + 1)
         lanes = slice(k * 128, k * 128 + 128)
         wy, wy1 = y_tables(frac[1], cell_y, k)
@@ -145,31 +153,50 @@
                 l2h[rows, lanes], l2l[rows, lanes] = split(l2)
 
 
-def scatter_sums(l0h, l0l, l2h, l2l, w_hi, w_lo, d_hi, d_lo):
-    inner, edge = slice(0, 128), slice(128, ZROWS)
-    terms = ((l0h, w_hi), (l0l, w_hi), (l0h, w_lo), (l2h, d_hi), (l2l, d_hi), (l2h, d_lo))
-    core = sum(nt(a[...], b[inner]) for a, b in terms)
-    ends = sum(nt(b[edge], a[...]) for a, b in terms)
-    return core, ends
-
-
-def write_planes(ends, width, hb, zu, zd):
-    hb[...] = jnp.zeros(hb.shape, F32)
+def paired(l, w):
+    l0h, l0l, l2h, l2l = l
+    w_hi, w_lo, d_hi, d_lo = w
+    return ((l0h, w_hi), (l0l, w_hi), (l0h, w_lo), (l2h, d_hi), (l2l, d_hi), (l2h, d_lo))
+
+
+def core_sums(l, w):
+    return sum(nt(a[...], b[0:128]) for a, b in paired(l, w))
+
+
+def edge_sums(l, w, rows=slice(128, ZROWS), lanes=slice(0, 1024)):
+    return sum(nt(b[rows, lanes], a[:, lanes]) for a, b in paired(l, w))
+
+
+def put_planes(ref, at, first, second):
+    width = first.shape[1]
+    ref[at : at + 1, :width] = first
+    ref[at + 1 : at + 2, :width] = second
+
+
+def static_rows(table, send, start, hot, dest):
+    hi, lo = split(table[...])
+    low_row, row = iota((128, 128), 0), iota((8, 128), 0)
+    for t in range(3):
+        index = send[start + t : start + t + 1]
+        hot[...] = (low_row == index % 128).astype(F32).astype(BF16)
+        got = (nn(hi, hot[...]) + nn(lo, hot[...])).reshape(14, 8, 128)
+        chosen = row == index // 128
+        dest[0:14, t * 128 : t * 128 + 128] = jnp.sum(jnp.where(chosen[None], got, 0.0), axis=1)
+
+
+def first_kernel(
+    live, adjoint, fractions, centers, deform, affine, mass, send,
+    h, hb, zu, zd, bf_out, w_hi, w_lo, d_hi, d_lo,
+    l0h, l0l, l2h, l2l, table, hot,
+):
+    table[104:112] = jnp.zeros((8, 128), F32)
+    early = dense(fractions, 0, 3) + [centers[0:1, :].reshape(CHUNKS, 128).astype(F32)]
+    for i, tile in enumerate(early + dense(deform, 0, 9)):
+        table[i * 8 : i * 8 + 8] = tile
     zu[...] = jnp.zeros(zu.shape, F32)
     zd[...] = jnp.zeros(zd.shape, F32)
-    hb[0:1, :width] = ends[0:1]
-    hb[1:2, :width] = ends[1:2]
-    zu[0:1, :width] = ends[0:1]
-    zu[1:2, :width] = ends[3:4]
-    zd[0:1, :width] = ends[1:2]
-    zd[1:2, :width] = ends[2:3]
-
-
-def first_kernel(
-    live, adjoint, fractions, centers, deform, affine, mass,
-    h, hb, zu, zd, bf_out, w_hi, w_lo, d_hi, d_lo,
-    l0h, l0l, l2h, l2l,
-):
+    static_rows(table, send, 2, hot, zd)
+    static_rows(table, send, 5, hot, zu)
     which = 1
     slots = iota((8, 128), 0) * 128 + iota((8, 128), 1)
     use = (slots < live[0, which]).astype(F32)
@@ -177,13 +204,14 @@
     frac = dense(fractions, which, 3)
     centre = centers[which : which + 1, :].reshape(CHUNKS, 128)
     cell_x, cell_y, cell_z = cells_of(centre)
-    build_z(frac[2], cell_z, w_hi, w_lo, d_hi, d_lo)
+    w = (w_hi, w_lo, d_hi, d_lo)
+    l = (l0h, l0l, l2h, l2l)
+    build_z(frac[2], cell_z, *w)
     a_v, b_c, b_f = transfer(adj, dense(deform, which, 9), dense(affine, which, 9))
     for i in range(9):
         bf_out[i] = b_f[i]
-    scatter_rows(a_v, b_c, frac, cell_x, cell_y, l0h, l0l, l2h, l2l)
-    core, ends = scatter_sums(l0h, l0l, l2h, l2l, w_hi, w_lo, d_hi, d_lo)
-    h[0:144] = core
+    scatter_rows(a_v, b_c, frac, cell_x, cell_y, *l)
+    h[0:144] = core_sums(l, w)
     h[144:240] = jnp.zeros((96, 128), F32)
     for s in range(2):
         for x in range(4):
@@ -192,7 +220,11 @@
     lane, row = iota((16, 128), 1), iota((16, 128), 0)
     pick = (((row == 2) & (lane == 0)) | ((row == 3) & (lane == 127))).astype(F32)
     mass_ends = contract(pick, h[144:240], 1, 1, lax.Precision.HIGHEST)
-    write_planes(jnp.concatenate([ends, mass_ends], axis=1), 240, hb, zu, zd)
+    ends = jnp.concatenate([edge_sums(l, w), mass_ends], axis=1)
+    hb[...] = jnp.zeros(hb.shape, F32)
+    put_planes(hb, 0, ends[0:1], ends[1:2])
+    put_planes(zu, 13, ends[0:1], ends[3:4])
+    put_planes(zd, 13, ends[1:2], ends[2:3])
 
 
 def wide_rows(hb):
@@ -212,9 +244,14 @@
 
 
 def z_kernel(comps, h, hb, from_low, from_high, h_out, hb_out, yu, yd):
-    low, high = from_low[...], from_high[...]
+    z_fold(
+        comps, h, hb[...], from_low[13:15, 0:256], from_high[13:15, 0:256], h_out, hb_out, yu, yd
+    )
+
+
+def z_fold(comps, h, halo, low, high, h_out, hb_out, yu, yd):
     pad = jnp.zeros((6, 256), F32)
-    halo = hb[...] + jnp.concatenate([high[1:2], low[1:2], pad], axis=0)
+    halo = halo + jnp.concatenate([high[1:2], low[1:2], pad], axis=0)
     hb_out[...] = halo
     wall = transposed(jnp.concatenate([low[0:1], high[0:1], pad], axis=0))
     lane = iota((8, 128), 1)
@@ -362,7 +399,7 @@
 def gather_first_kernel(
     extents, live, spot, h, hb, from_low, from_high, fractions, centers, deform, bf,
     w_hi, w_lo, d_hi, d_lo, pick,
-    second, zu, zd, mid, mass_core, mass_halo,
+    second, xu, xd, mid, mass_core, mass_halo,
     total, g_hi, g_lo, s0, sz, rows12, buf, hot,
 ):
     which = 1
@@ -403,7 +440,7 @@
         chosen = (row == index // 128) & (index >= 0)
         got = got.reshape(22, 8, 128)[0:21]
         got = jnp.sum(jnp.where(chosen[None], got, 0.0), axis=1)
-        dest, place = ((zd, t), (mid, t - 3), (zu, t - 6))[t // 3]
+        dest, place = ((xd, t), (mid, t - 3), (xu, t - 6))[t // 3]
         dest[:, place * 128 : place * 128 + 128] = got
 
 
@@ -427,57 +464,107 @@
         yu[:, i * 128 : i * 128 + 128] = lane_tile(ref, 2)
 
 
-def route_x_kernel(mid, z_low, z_high, y_low, y_high, xu, xd, final):
-    groups = [lane_tile(mid, 1), lane_tile(z_low, 1), lane_tile(z_high, 1)]
-    groups += [lane_tile(y_low, i) for i in range(3)]
-    groups += [lane_tile(y_high, i) for i in range(3)]
-    for ref, at in ((xd, 0), (xu, 64)):
-        for i, tile in enumerate(pieces(groups, at, 3)):
-            ref[:, i * 128 : i * 128 + 128] = tile
-    for i, tile in enumerate(pieces(groups[1:], 32, 2)):
-        final[:, i * 128 : i * 128 + 128] = tile
-
-
-def second_kernel(
-    live, second, final, x_low, x_high, prior, send, fractions, centers, deform, affine,
-    h, hb, zu, zd, bf_out, w_hi, w_lo, d_hi, d_lo,
-    lh, ll, hot, l0h, l0l, l2h, l2l,
-):
-    which = 0
-    row = iota((8, 128), 0)
-    low_row = iota((128, 128), 0)
-    moved = [lane_tile(final, 0), lane_tile(final, 1)]
-    moved += [lane_tile(x_low, i) for i in range(3)] + [lane_tile(x_high, i) for i in range(3)]
-    for t in range(16):
-        index = prior[t : t + 1] if t < 8 else send[t - 8 : t - 7]
+def carry(tiles, indices, lh, ll, hot):
+    row, low_row = iota((8, 128), 0), iota((128, 128), 0)
+    for t, (values, index) in enumerate(zip(tiles, indices)):
         lanes = slice(t * 128, t * 128 + 128)
         hot[:, lanes] = (low_row == index % 128).astype(F32).astype(BF16)
         chosen = row == index // 128
         for pair in range(11):
-            tiles = []
+            both = []
             for r in (2 * pair, 2 * pair + 1):
-                if r > 20:
-                    tiles.append(jnp.zeros((8, 128), F32))
-                    continue
-                value = second[r, t : t + 1, :] if t < 8 else moved[t - 8][r : r + 1]
-                tiles.append(jnp.where(chosen, value, 0.0))
-            hi, lo = split(jnp.concatenate(tiles, axis=0))
-            lh[pair * 16 : pair * 16 + 16, lanes] = hi
-            ll[pair * 16 : pair * 16 + 16, lanes] = lo
-    carried = nt(lh[...], hot[...]) + nt(ll[...], hot[...])
+                blank = jnp.zeros((8, 128), F32)
+                both.append(blank if r > 20 else jnp.where(chosen, values(r), 0.0))
+            rows = slice(pair * 16, pair * 16 + 16)
+            lh[rows, lanes], ll[rows, lanes] = split(jnp.concatenate(both, axis=0))
+    return nt(lh[...], hot[...]) + nt(ll[...], hot[...])
+
+
+def weights_kernel(fractions, centers, w_hi, w_lo, d_hi, d_lo):
+    _, _, cell_z = cells_of(centers[0:1, :].reshape(CHUNKS, 128))
+    build_z(dense(fractions, 0, 3)[2], cell_z, w_hi, w_lo, d_hi, d_lo)
+
+
+def near_kernel(
+    live, mid, x_low, x_high, y_low, y_high, second, prior, send,
+    static_low, static_high, fractions, centers, deform, w_hi, w_lo, d_hi, d_lo,
+    zu, zd, up2, dn2, own_low, own_high, carried,
+    lh, ll, hot, l0h, l0l, l2h, l2l, moved, static, e0, e1, e2, e3,
+):
+    groups = [lane_tile(mid, 1), lane_tile(x_low, 1), lane_tile(x_high, 1)]
+    groups += [lane_tile(y_low, i) for i in range(3)]
+    groups += [lane_tile(y_high, i) for i in range(3)]
+    final = pieces(groups[1:], 32, 2)
+    moved[...] = jnp.zeros(moved.shape, F32)
+    static[...] = jnp.zeros(static.shape, F32)
+    zu[...] = jnp.zeros(zu.shape, F32)
+    zd[...] = jnp.zeros(zd.shape, F32)
+    for ref, at, first, known in ((zu, 64, 0, static_high), (zd, 0, 3, static_low)):
+        for i, tile in enumerate(pieces(groups, at, 3)):
+            ref[0:21, i * 128 : i * 128 + 128] = tile
+            moved[:, first + i, :] = tile
+            static[:, first + i, :] = known[0:14, i * 128 : i * 128 + 128]
+    l = (l0h, l0l, l2h, l2l)
+    e = (e0, e1, e2, e3)
+
+    place = [static[i] for i in range(3)]
+    cell_x, cell_y, cell_z = cells_of((static[3] + 0.5).astype(I32))
+    build_z(place[2], cell_z, *e, chunks=6, edges_only=True)
+    a_v, b_c = to_grid([moved[i] for i in range(21)], [static[4 + i] for i in range(9)])
+    scatter_rows(a_v, b_c, place, cell_x, cell_y, *l, chunks=6)
+    upward = edge_sums(l, e, slice(0, 16), slice(0, 384))
+    downward = edge_sums(l, e, slice(0, 16), slice(384, 768))
+    for ref in (up2, dn2, own_low, own_high):
+        ref[...] = jnp.zeros(ref.shape, F32)
+    put_planes(up2, 0, upward[0:1], upward[3:4])
+    put_planes(own_high, 0, upward[1:2], upward[2:3])
+    put_planes(own_low, 0, downward[0:1], downward[3:4])
+    put_planes(dn2, 0, downward[1:2], downward[2:3])
+
+    tiles = [lambda r, t=t: second[r, t : t + 1, :] for t in range(8)]
+    tiles += [lambda r, t=t: final[t][r : r + 1] for t in range(2)]
+    indices = [prior[t : t + 1] for t in range(8)] + [send[t : t + 1] for t in range(2)]
+    total = carry(tiles, indices, lh, ll, hot)
     slots = iota((8, 128), 0) * 128 + iota((8, 128), 1)
-    use = (slots < live[0, which]).astype(F32)
-    adj = [carried[i * 8 : i * 8 + 8] * use for i in range(21)]
-    frac = dense(fractions, which, 3)
-    cell_x, cell_y, cell_z = cells_of(centers[which : which + 1, :].reshape(CHUNKS, 128))
-    build_z(frac[2], cell_z, w_hi, w_lo, d_hi, d_lo)
-    a_v, b_c, b_f = transfer(adj, dense(deform, which, 9), dense(affine, which, 9))
+    use = (slots < live[0, 0]).astype(F32)
+    adj = [total[i * 8 : i * 8 + 8] * use for i in range(21)]
+    for i in range(21):
+        carried[i] = adj[i]
+    frac = dense(fractions, 0, 3)
+    cell_x, cell_y, _ = cells_of(centers[0:1, :].reshape(CHUNKS, 128))
+    a_v, b_c = to_grid(adj, dense(deform, 0, 9))
+    scatter_rows(a_v, b_c, frac, cell_x, cell_y, *l)
+    ends = edge_sums(l, (w_hi, w_lo, d_hi, d_lo))
+    put_planes(zu, 21, ends[0:1], ends[3:4])
+    put_planes(zd, 21, ends[1:2], ends[2:3])
+
+
+def second_kernel(
+    live, carried, z_low, z_high, low2, high2, own_low, own_high, send,
+    fractions, centers, deform, affine, w_hi, w_lo, d_hi, d_lo,
+    h_out, hb_out, yu, yd, bf_out,
+    lh, ll, hot, l0h, l0l, l2h, l2l, h,
+):
+    tiles = [lambda r, t=t: z_low[r : r + 1, t * 128 : t * 128 + 128] for t in range(3)]
+    tiles += [lambda r, t=t: z_high[r : r + 1, t * 128 : t * 128 + 128] for t in range(3)]
+    total = carry(tiles, [send[t : t + 1] for t in range(2, 8)], lh, ll, hot)
+    slots = iota((8, 128), 0) * 128 + iota((8, 128), 1)
+    use = (slots < live[0, 0]).astype(F32)
+    adj = [(carried[i] + total[i * 8 : i * 8 + 8]) * use for i in range(21)]
+    frac = dense(fractions, 0, 3)
+    cell_x, cell_y, _ = cells_of(centers[0:1, :].reshape(CHUNKS, 128))
+    a_v, b_c, b_f = transfer(adj, dense(deform, 0, 9), dense(affine, 0, 9))
     for i in range(9):
         bf_out[i] = b_f[i]
-    scatter_rows(a_v, b_c, frac, cell_x, cell_y, l0h, l0l, l2h, l2l)
-    core, ends = scatter_sums(l0h, l0l, l2h, l2l, w_hi, w_lo, d_hi, d_lo)
-    h[...] = core
-    write_planes(ends, 144, hb, zu, zd)
+    l = (l0h, l0l, l2h, l2l)
+    w = (w_hi, w_lo, d_hi, d_lo)
+    scatter_rows(a_v, b_c, frac, cell_x, cell_y, *l)
+    h[...] = core_sums(l, w)
+    ends = jnp.concatenate([edge_sums(l, w)[0:8], jnp.zeros((8, 112), F32)], axis=1)
+    halo = jnp.where(iota((8, 256), 0) < 2, ends, 0.0)
+    low = z_low[21:23, 0:256] + low2[0:2] + own_low[0:2]
+    high = z_high[21:23, 0:256] + high2[0:2] + own_high[0:2]
+    z_fold(3, h, halo, low, high, h_out, hb_out, yu, yd)
 
 
 def gather_second_kernel(
@@ -520,10 +607,10 @@
     )
 
 
-def both_ways(up, down, axis):
+def both_ways(up, down, axis, step=1):
     count = lax.axis_size(axis)
-    low = lax.ppermute(up, axis, [(i, i + 1) for i in range(count - 1)])
-    high = lax.ppermute(down, axis, [(i + 1, i) for i in range(count - 1)])
+    low = lax.ppermute(up, axis, [(i, i + step) for i in range(count - step)])
+    high = lax.ppermute(down, axis, [(i + step, i) for i in range(count - step)])
     return low, high
 
 
@@ -541,9 +628,9 @@
 
     order = jnp.arange(32, dtype=I32)[None]
     chosen = jnp.where(order < receive_count[0][:, None], receive_slot[0], -1)
-    pick = jnp.transpose(cube(chosen, -1), (2, 1, 0, 3))
+    pick = cube(chosen, -1)
     pick = jnp.concatenate([pick, jnp.full((3, 3, 1, 32), -1, I32)], axis=2).reshape(9, 128)
-    back = cube(send_slot[0], 0)[::-1, ::-1, ::-1]
+    back = jnp.transpose(cube(send_slot[0], 0)[::-1, ::-1, ::-1], (2, 1, 0, 3))
     back = jnp.concatenate([back[:, 1:], back[:, :1]], axis=1)
     back = jnp.concatenate([back[:, :, 1:], back[:, :, :1]], axis=2).reshape(3, 9, 32)
     blank = jnp.zeros((3, 32), I32)
@@ -558,13 +645,7 @@
         ((144, 1024), F32), ((144, 1024), F32), ((12, 8, 128), F32),
     ]
 
-    def fold(comps, h, hb, zu, zd):
-        low, high = both_ways(zu, zd, "gz")
-        packed = (comps * 6 + 3) // 4 * 8 + 8
-        h, hb, yu, yd = call(
-            functools.partial(z_kernel, comps), f"fold_z{comps}", [VMEM] * 4,
-            [shape(comps * 48, 128), shape(8, 256), shape(packed, 128), shape(packed, 128)],
-        )(h, hb, low, high)
+    def fold(comps, h, hb, yu, yd):
         low, high = both_ways(yu, yd, "gy")
         rows = comps * 16 + 8
         h, hb, xu, xd = call(
@@ -575,32 +656,47 @@
         return h, hb, low, high
 
     h, hb, zu, zd, bf, *w = call(
-        first_kernel, "scatter_first", [SMEM] + [VMEM] * 6,
-        [shape(240, 128), shape(8, 256), shape(2, 256), shape(2, 256), shape(9, 8, 128)] + weights,
-        lrows,
-    )(live_count, final_adjoint, fractions, centers, deform, next_affine, cell_mass)
-    h, hb, low, high = fold(5, h, hb, zu, zd)
-    second, zu, zd, mid, mass_core, mass_halo = call(
+        first_kernel, "scatter_first", [SMEM] + [VMEM] * 7,
+        [shape(240, 128), shape(8, 256), shape(16, 384), shape(16, 384), shape(9, 8, 128)] + weights,
+        lrows + [((112, 128), F32), ((128, 128), BF16)],
+    )(live_count, final_adjoint, fractions, centers, deform, next_affine, cell_mass, send)
+    static_low, static_high = both_ways(zu, zd, "gz")
+    h, hb, yu, yd = call(
+        functools.partial(z_kernel, 5), "fold_z5", [VMEM] * 4,
+        [shape(240, 128), shape(8, 256), shape(72, 128), shape(72, 128)],
+    )(h, hb, static_low, static_high)
+    h, hb, low, high = fold(5, h, hb, yu, yd)
+    second, xu, xd, mid, mass_core, mass_halo = call(
         functools.partial(gather_first_kernel, extents), "gather_first",
         [SMEM, SMEM] + [VMEM] * 13,
         [shape(21, 8, 128), shape(21, 384), shape(21, 384), shape(21, 384), shape(48, 128), shape(8, 256)],
         [((240, 128), F32)] + gscratch + [((176, 128), F32), ((128, 128), BF16)],
     )(live_count, spot, h, hb, low, high, fractions, centers, deform, bf, *w, pick)
 
+    w = call(weights_kernel, "weights_second", [VMEM] * 2, weights)(fractions, centers)
+    x_low, x_high = both_ways(xu, xd, "gx")
+    yu, yd = call(route_y_kernel, "route_y", [VMEM] * 3, [shape(21, 384)] * 2)(mid, x_low, x_high)
+    y_low, y_high = both_ways(yu, yd, "gy")
+    zu, zd, up2, dn2, own_low, own_high, carried = call(
+        near_kernel, "scatter_near", [SMEM] + [VMEM] * 17,
+        [shape(24, 384)] * 2 + [shape(2, 256)] * 4 + [shape(21, 8, 128)],
+        [((176, 1280), BF16)] * 2 + [((128, 1280), BF16)] + lrows
+        + [((21, 8, 128), F32), ((14, 8, 128), F32)] + [((16, 768), BF16)] * 4,
+    )(
+        live_count, mid, x_low, x_high, y_low, y_high, second, prior, send,
+        static_low, static_high, fractions, centers, deform, *w,
+    )
     z_low, z_high = both_ways(zu, zd, "gz")
-    yu, yd = call(route_y_kernel, "route_y", [VMEM] * 3, [shape(21, 384)] * 2)(mid, z_low, z_high)
-    y_low, y_high = both_ways(yu, yd, "gy")
-    xu, xd, final = call(
-        route_x_kernel, "route_x", [VMEM] * 5, [shape(21, 384), shape(21, 384), shape(21, 256)]
-    )(mid, z_low, z_high, y_low, y_high)
-    x_low, x_high = both_ways(xu, xd, "gx")
-
-    h, hb, zu, zd, bf, *w = call(
-        second_kernel, "scatter_second", [SMEM] + [VMEM] * 10,
-        [shape(144, 128), shape(8, 256), shape(2, 256), shape(2, 256), shape(9, 8, 128)] + weights,
-        [((176, 2048), BF16)] * 2 + [((128, 2048), BF16)] + lrows,
-    )(live_count, second, final, x_low, x_high, prior, send, fractions, centers, deform, next_affine)
-    h, hb, low, high = fold(3, h, hb, zu, zd)
+    low2, high2 = both_ways(up2, dn2, "gz", 2)
+    h, hb, yu, yd, bf = call(
+        second_kernel, "scatter_second", [SMEM] + [VMEM] * 16,
+        [shape(144, 128), shape(8, 256), shape(48, 128), shape(48, 128), shape(9, 8, 128)],
+        [((176, 768), BF16)] * 2 + [((128, 768), BF16)] + lrows + [((144, 128), F32)],
+    )(
+        live_count, carried, z_low, z_high, low2, high2, own_low, own_high, send,
+        fractions, centers, deform, next_affine, *w,
+    )
+    h, hb, low, high = fold(3, h, hb, yu, yd)
     (result,) = call(
         functools.partial(gather_second_kernel, extents), "gather_second",
         [SMEM, SMEM] + [VMEM] * 14,

time: 140 us -> 122 us (0.87)
  starting transfers between devices: 78.2 us -> 66.7 us
  waiting for transfers between devices: 45.1 us -> 36.5 us
  Pallas kernels: 10.3 us -> 13.2 us
    ppermute x18, starting transfers between devices: 78.2 us -> 66.7 us  [the longest x9 43.4 us: both_ways(): low = lax.ppermute(up, axis, [(i, i + step) for i in range(count - step)])]
    ppermute x18, waiting for transfers between devices: 45.1 us -> 36.5 us  [the longest x9 36.5 us: both_ways(): lax.ppermute(down, axis, [(i + step, i) for i in range(count - step)])]
    pallas_call x5, Pallas kernels: 5.96 us -> 8.88 us  [the longest x1 3.25 us: body(): call(near_kernel, 'scatter_near', [SMEM] + [VMEM] * 17, [shape(24, 384)]...]
    unnamed x25 -> x23, local copies, waits for them, and re-layouts: 3.15 us -> 3.11 us
  transfers between devices with their start and end apart: 18 -> 18, of which waited for: 10 -> 8; matrix products, arithmetic and copies ran while one was open for 1% -> 0% of each run, Pallas kernels for 0% -> 0%
where the time goes in v2:
time: 122 us
  starting transfers between devices  66.7 us (55%)
  waiting for transfers between devices  36.5 us (30%)
  Pallas kernels  13.2 us (11%)
  local copies, waits for them, and re-layouts  4.4 us (4%)
    ppermute x9, starting transfers between devices, both_ways(): low = lax.ppermute(up, axis, [(i, i + step) for i in range(count - step)])  43.4 us
    ppermute x9, waiting for transfers between devices, both_ways(): lax.ppermute(down, axis, [(i + step, i) for i in range(count - step)])  36.5 us
    ppermute x9, starting transfers between devices, both_ways(): lax.ppermute(down, axis, [(i + step, i) for i in range(count - step)])  23.3 us
    pallas_call x1, Pallas kernels, body(): call(near_kernel, 'scatter_near', [SMEM] + [VMEM] * 17, [shape(24, 384)]...  3.25 us
    unnamed x23, local copies, waits for them, and re-layouts  3.11 us
  transfers between devices with their start and end apart: 18, of which 8 were waited for; matrix products, arithmetic and copies ran while one was open for 0% of the time, Pallas kernels for 0%

profile of v2, /device:TPU:105, one launch (start us, length us, event | category | flops | bytes accessed | tf_op | source)
XLA Modules:
  0.0 121.5 jit_solution(313719586491910041)
XLA Ops:
  0.0 0.7 fusion.4
  0.7 0.1 pad.9.clone
  0.8 0.1 pad_add_fusion.1
  1.1 0.2 concatenate.21
  1.3 0.1 reshape.27.send
  1.3 0.5 copy-done.7
  1.8 0.2 copy-done.5
  2.0 0.8 copy-done.6
  2.9 0.6 copy-done
  3.5 0.2 copy-done.1
  3.8 2.4 %scatter_first.1 = (f32[240,128]{1,0:T(8,128)S(1)}, f32[8,256]{1,0:T(8,128)S(1)}, f32[16,384]{1,0:T(8,128)S(1)}, f32[16,384]{1,0:T(8,128)S(1)}, f32[9,8,128]{2,1...) custom-call(s32[1,2]{1,0:T(1,128)S(1)} %copy-done.3, ...), custom_call_target="tpu_custom_call" | custom-call | tf_op jit(solution)/shard_map/scatter_first/pallas_call | solution.py:658
  6.2 12.8 %collective-permute-start = (f32[16,384]{1,0:T(8,128)S(1)}, f32[16,384]{1,0:T(8,128)S(1)}, u32[]{:S(2)}, u32[]{:S(2)}) collective-permute-start(f32[16,384]{1,0:T(8,128)S(1)} %get-tuple-element.52), channel_id=1, source_target_pairs={{0,1},{1,2},{2,3},{3,4},{4,5},{5,6},{6,7},{8,9},{9,10},{10,11},{11... | collective-permute-start | bytes 73736 | tf_op jit(solution)/shard_map/ppermute | solution.py:612
  19.0 2.1 %collective-permute-start.1 = (f32[16,384]{1,0:T(8,128)S(1)}, f32[16,384]{1,0:T(8,128)S(1)}, u32[]{:S(2)}, u32[]{:S(2)}) collective-permute-start(f32[16,384]{1,0:T(8,128)S(1)} %get-tuple-element.53), channel_id=1, source_target_pairs={{1,0},{2,1},{3,2},{4,3},{5,4},{6,5},{7,6},{9,8},{10,9},{11,10},{12... | collective-permute-start | bytes 73736 | tf_op jit(solution)/shard_map/ppermute | solution.py:613
  21.3 11.0 %collective-permute-done.1.from_high.static_high = f32[16,384]{1,0:T(8,128)S(1)} collective-permute-done((f32[16,384]{1,0:T(8,128)S(1)}, f32[16,384]{1,0:T(8,128)S(1)}, u32[]{:S(2)}, u32[]{:S(2)}) %collective-permute-start.1) | collective-permute-done | bytes 24608 | tf_op jit(solution)/shard_map/ppermute | solution.py:613
  32.3 0.3 fold_z5.1
  32.6 4.6 %collective-permute-start.2 = (f32[72,128]{1,0:T(8,128)S(1)}, f32[72,128]{1,0:T(8,128)S(1)}, u32[]{:S(2)}, u32[]{:S(2)}) collective-permute-start(f32[72,128]{1,0:T(8,128)S(1)} %get-tuple-element.56), channel_id=1, source_target_pairs={{0,8},{8,16},{16,24},{24,32},{32,40},{40,48},{48,56},{56,64},{64,7... | collective-permute-start | bytes 110600 | tf_op jit(solution)/shard_map/ppermute | solution.py:612
  37.2 1.9 %collective-permute-start.3 = (f32[72,128]{1,0:T(8,128)S(1)}, f32[72,128]{1,0:T(8,128)S(1)}, u32[]{:S(2)}, u32[]{:S(2)}) collective-permute-start(f32[72,128]{1,0:T(8,128)S(1)} %get-tuple-element.57), channel_id=1, source_target_pairs={{8,0},{16,8},{24,16},{32,24},{40,32},{48,40},{56,48},{64,56},{72,6... | collective-permute-start | bytes 110600 | tf_op jit(solution)/shard_map/ppermute | solution.py:613
  39.2 4.5 %collective-permute-done.3.from_high = f32[72,128]{1,0:T(8,128)S(1)} collective-permute-done((f32[72,128]{1,0:T(8,128)S(1)}, f32[72,128]{1,0:T(8,128)S(1)}, u32[]{:S(2)}, u32[]{:S(2)}) %collective-permute-start.3) | collective-permute-done | bytes 36896 | tf_op jit(solution)/shard_map/ppermute | solution.py:613
  43.7 0.1 fold_y5.1
  43.8 3.1 %collective-permute-start.4 = (f32[88,128]{1,0:T(8,128)S(1)}, f32[88,128]{1,0:T(8,128)S(1)}, u32[]{:S(2)}, u32[]{:S(2)}) collective-permute-start(f32[88,128]{1,0:T(8,128)S(1)} %get-tuple-element.60), channel_id=1, source_target_pairs={{0,128},{128,256},{256,384},{1,129},{129,257},{257,385},{2,130},{1... | collective-permute-start | bytes 135176 | tf_op jit(solution)/shard_map/ppermute | solution.py:612
  46.9 1.3 %collective-permute-start.5 = (f32[88,128]{1,0:T(8,128)S(1)}, f32[88,128]{1,0:T(8,128)S(1)}, u32[]{:S(2)}, u32[]{:S(2)}) collective-permute-start(f32[88,128]{1,0:T(8,128)S(1)} %get-tuple-element.61), channel_id=1, source_target_pairs={{128,0},{256,128},{384,256},{129,1},{257,129},{385,257},{130,2},{2... | collective-permute-start | bytes 135176 | tf_op jit(solution)/shard_map/ppermute | solution.py:613
  48.2 0.1 pad_add_fusion.4.spot
  48.3 0.1 reshape.29.pick
  48.4 3.3 %collective-permute-done.5.from_high = f32[88,128]{1,0:T(8,128)S(1)} collective-permute-done((f32[88,128]{1,0:T(8,128)S(1)}, f32[88,128]{1,0:T(8,128)S(1)}, u32[]{:S(2)}, u32[]{:S(2)}) %collective-permute-start.5) | collective-permute-done | bytes 45088 | tf_op jit(solution)/shard_map/ppermute | solution.py:613
  51.7 2.0 %gather_first.1 = (f32[21,8,128]{2,1,0:T(8,128)S(1)}, f32[21,384]{1,0:T(8,128)S(1)}, f32[21,384]{1,0:T(8,128)S(1)}, f32[21,384]{1,0:T(8,128)S(1)}, f32[48,128]{1,0:T(8,128)S(1)}, /*index=5*/f32[8,256]{1,0:T(8,128)S(1)}) custom-call(s32[1,2]{1,0:T(1,128)S(1)} %copy-done.3, s32[3]{0:T(128)S(1)} %pad_add_fusion.4.spot, f32[240,128]{1,0:T(8,128)S(1)} %get-tuple-element.58.h, ...), custom_call_target="tpu_custom_call" | custom-call | tf_op jit(solution)/shard_map/gather_first/pallas_call | solution.py:669
  53.8 3.1 %collective-permute-start.6 = (f32[21,384]{1,0:T(8,128)S(1)}, f32[21,384]{1,0:T(8,128)S(1)}, u32[]{:S(2)}, u32[]{:S(2)}) collective-permute-start(f32[21,384]{1,0:T(8,128)S(1)} %get-tuple-element.68), channel_id=1, source_target_pairs={{0,128},{128,256},{256,384},{1,129},{129,257},{257,385},{2,130},{1... | collective-permute-start | bytes 96776 | tf_op jit(solution)/shard_map/ppermute | solution.py:612
  56.9 1.3 %collective-permute-start.7 = (f32[21,384]{1,0:T(8,128)S(1)}, f32[21,384]{1,0:T(8,128)S(1)}, u32[]{:S(2)}, u32[]{:S(2)}) collective-permute-start(f32[21,384]{1,0:T(8,128)S(1)} %get-tuple-element.69), channel_id=1, source_target_pairs={{128,0},{256,128},{384,256},{129,1},{257,129},{385,257},{130,2},{2... | collective-permute-start | bytes 96776 | tf_op jit(solution)/shard_map/ppermute | solution.py:613
  58.2 3.7 %collective-permute-done.7.from_high.x_high = f32[21,384]{1,0:T(8,128)S(1)} collective-permute-done((f32[21,384]{1,0:T(8,128)S(1)}, f32[21,384]{1,0:T(8,128)S(1)}, u32[]{:S(2)}, u32[]{:S(2)}) %collective-permute-start.7) | collective-permute-done | bytes 32288 | tf_op jit(solution)/shard_map/ppermute | solution.py:613
  61.9 4.4 %collective-permute-start.8 = (f32[21,384]{1,0:T(8,128)S(1)}, f32[21,384]{1,0:T(8,128)S(1)}, u32[]{:S(2)}, u32[]{:S(2)}) collective-permute-start(f32[21,384]{1,0:T(8,128)S(1)} %get-tuple-element.70), channel_id=1, source_target_pairs={{0,8},{8,16},{16,24},{24,32},{32,40},{40,48},{48,56},{56,64},{64,7... | collective-permute-start | bytes 96776 | tf_op jit(solution)/shard_map/ppermute | solution.py:612
  66.4 1.9 %collective-permute-start.9 = (f32[21,384]{1,0:T(8,128)S(1)}, f32[21,384]{1,0:T(8,128)S(1)}, u32[]{:S(2)}, u32[]{:S(2)}) collective-permute-start(f32[21,384]{1,0:T(8,128)S(1)} %get-tuple-element.71), channel_id=1, source_target_pairs={{8,0},{16,8},{24,16},{32,24},{40,32},{48,40},{56,48},{64,56},{72,6... | collective-permute-start | bytes 96776 | tf_op jit(solution)/shard_map/ppermute | solution.py:613
  68.3 0.5 weights_second.1
  68.8 4.0 %collective-permute-done.9.y_high = f32[21,384]{1,0:T(8,128)S(1)} collective-permute-done((f32[21,384]{1,0:T(8,128)S(1)}, f32[21,384]{1,0:T(8,128)S(1)}, u32[]{:S(2)}, u32[]{:S(2)}) %collective-permute-start.9) | collective-permute-done | bytes 32288 | tf_op jit(solution)/shard_map/ppermute | solution.py:613
  72.8 0.7 copy-done.4
  73.5 3.3 %scatter_near.1 = (f32[24,384]{1,0:T(8,128)S(1)}, f32[24,384]{1,0:T(8,128)S(1)}, f32[2,256]{1,0:T(2,128)S(1)}, f32[2,256]{1,0:T(2,128)S(1)}, f32[2,256]{1,0:T(2,...) custom-call(s32[1,2]{1,0:T(1,128)S(1)} %copy-done.3, f32[21,384]{1,0:T(8,128)S(1)} %get-tuple-element.67.mid, ...), custom_call_target="tpu_custom_call" | custom-call | tf_op jit(solution)/shard_map/scatter_near/pallas_call | solution.py:680
  76.8 5.4 %collective-permute-start.10 = (f32[24,384]{1,0:T(8,128)S(1)}, f32[24,384]{1,0:T(8,128)S(1)}, u32[]{:S(2)}, u32[]{:S(2)}) collective-permute-start(f32[24,384]{1,0:T(8,128)S(1)} %get-tuple-element.78), channel_id=1, source_target_pairs={{0,1},{1,2},{2,3},{3,4},{4,5},{5,6},{6,7},{8,9},{9,10},{10,11},{11... | collective-permute-start | bytes 110600 | tf_op jit(solution)/shard_map/ppermute | solution.py:612
  82.2 9.5 %collective-permute-start.11 = (f32[24,384]{1,0:T(8,128)S(1)}, f32[24,384]{1,0:T(8,128)S(1)}, u32[]{:S(2)}, u32[]{:S(2)}) collective-permute-start(f32[24,384]{1,0:T(8,128)S(1)} %get-tuple-element.79), channel_id=1, source_target_pairs={{1,0},{2,1},{3,2},{4,3},{5,4},{6,5},{7,6},{9,8},{10,9},{11,10},{12... | collective-permute-start | bytes 110600 | tf_op jit(solution)/shard_map/ppermute | solution.py:613
  91.7 3.2 %collective-permute-start.12 = (f32[2,256]{1,0:T(2,128)S(1)}, f32[2,256]{1,0:T(2,128)S(1)}, u32[]{:S(2)}, u32[]{:S(2)}) collective-permute-start(f32[2,256]{1,0:T(2,128)S(1)} %get-tuple-element.80), channel_id=1, source_target_pairs={{0,2},{1,3},{2,4},{3,5},{4,6},{5,7},{8,10},{9,11},{10,12},{11,13},... | collective-permute-start | bytes 6152 | tf_op jit(solution)/shard_map/ppermute | solution.py:612
  94.9 2.1 %collective-permute-start.13 = (f32[2,256]{1,0:T(2,128)S(1)}, f32[2,256]{1,0:T(2,128)S(1)}, u32[]{:S(2)}, u32[]{:S(2)}) collective-permute-start(f32[2,256]{1,0:T(2,128)S(1)} %get-tuple-element.81), channel_id=1, source_target_pairs={{2,0},{3,1},{4,2},{5,3},{6,4},{7,5},{10,8},{11,9},{12,10},{13,11},... | collective-permute-start | bytes 6152 | tf_op jit(solution)/shard_map/ppermute | solution.py:613
  97.0 2.2 %collective-permute-done.13.high2 = f32[2,256]{1,0:T(2,128)S(1)} collective-permute-done((f32[2,256]{1,0:T(2,128)S(1)}, f32[2,256]{1,0:T(2,128)S(1)}, u32[]{:S(2)}, u32[]{:S(2)}) %collective-permute-start.13) | collective-permute-done | bytes 2080 | tf_op jit(solution)/shard_map/ppermute | solution.py:613
  99.3 2.4 %scatter_second.1 = (f32[144,128]{1,0:T(8,128)S(1)}, f32[8,256]{1,0:T(8,128)S(1)}, f32[48,128]{1,0:T(8,128)S(1)}, f32[48,128]{1,0:T(8,128)S(1)}, f32[9,8,128]{2,1,0:T(8,128)S(1)}) custom-call(s32[1,2]{1,0:T(1,128)S(1)} %copy-done.3, f32[21,8,128]{2,1,0:T(8,128)S(1)} %get-tuple-element.77.carried, f32[24,384]{1,0:T(8,128)S(1)} %collective-permute-done.10.z_low, ...), custom_call_target="tpu_custom_call" | custom-call | tf_op jit(solution)/shard_map/scatter_second/pallas_call | solution.py:691
  101.6 3.9 %collective-permute-start.14 = (f32[48,128]{1,0:T(8,128)S(1)}, f32[48,128]{1,0:T(8,128)S(1)}, u32[]{:S(2)}, u32[]{:S(2)}) collective-permute-start(f32[48,128]{1,0:T(8,128)S(1)} %get-tuple-element.86), channel_id=1, source_target_pairs={{0,8},{8,16},{16,24},{24,32},{32,40},{40,48},{48,56},{56,64},{64,7... | collective-permute-start | bytes 73736 | tf_op jit(solution)/shard_map/ppermute | solution.py:612
  105.6 1.9 %collective-permute-start.15 = (f32[48,128]{1,0:T(8,128)S(1)}, f32[48,128]{1,0:T(8,128)S(1)}, u32[]{:S(2)}, u32[]{:S(2)}) collective-permute-start(f32[48,128]{1,0:T(8,128)S(1)} %get-tuple-element.87), channel_id=1, source_target_pairs={{8,0},{16,8},{24,16},{32,24},{40,32},{48,40},{56,48},{64,56},{72,6... | collective-permute-start | bytes 73736 | tf_op jit(solution)/shard_map/ppermute | solution.py:613
  107.5 4.4 %collective-permute-done.15.from_high = f32[48,128]{1,0:T(8,128)S(1)} collective-permute-done((f32[48,128]{1,0:T(8,128)S(1)}, f32[48,128]{1,0:T(8,128)S(1)}, u32[]{:S(2)}, u32[]{:S(2)}) %collective-permute-start.15) | collective-permute-done | bytes 24608 | tf_op jit(solution)/shard_map/ppermute | solution.py:613
  111.9 0.1 fold_y3.1
  112.0 2.8 %collective-permute-start.16 = (f32[56,128]{1,0:T(8,128)S(1)}, f32[56,128]{1,0:T(8,128)S(1)}, u32[]{:S(2)}, u32[]{:S(2)}) collective-permute-start(f32[56,128]{1,0:T(8,128)S(1)} %get-tuple-element.90), channel_id=1, source_target_pairs={{0,128},{128,256},{256,384},{1,129},{129,257},{257,385},{2,130},{1... | collective-permute-start | bytes 86024 | tf_op jit(solution)/shard_map/ppermute | solution.py:612
  114.8 1.3 %collective-permute-start.17 = (f32[56,128]{1,0:T(8,128)S(1)}, f32[56,128]{1,0:T(8,128)S(1)}, u32[]{:S(2)}, u32[]{:S(2)}) collective-permute-start(f32[56,128]{1,0:T(8,128)S(1)} %get-tuple-element.91), channel_id=1, source_target_pairs={{128,0},{256,128},{384,256},{129,1},{257,129},{385,257},{130,2},{2... | collective-permute-start | bytes 86024 | tf_op jit(solution)/shard_map/ppermute | solution.py:613
  116.1 3.3 %collective-permute-done.17.from_high = f32[56,128]{1,0:T(8,128)S(1)} collective-permute-done((f32[56,128]{1,0:T(8,128)S(1)}, f32[56,128]{1,0:T(8,128)S(1)}, u32[]{:S(2)}, u32[]{:S(2)}) %collective-permute-start.17) | collective-permute-done | bytes 28704 | tf_op jit(solution)/shard_map/ppermute | solution.py:613
  119.4 2.1 %gather_second.1 = f32[21,1024]{1,0:T(8,128)} custom-call(s32[1,2]{1,0:T(1,128)S(1)} %copy-done.3, s32[3]{0:T(128)S(1)} %pad_add_fusion.4.spot, f32[144,128]{1,0:T(8,128)S(1)} %get-tuple-element.88.h, f32[8,256]{1,0:T(8,128)S(1)} %get-tuple-element.89.hb, f32[56,128]{1,0:T(8,128)S(1)} %collective-permute-done.16.from_low, ...), custom_call_target="tpu_custom_call" | custom-call | tf_op jit(solution)/shard_map/gather_second/pallas_call | solution.py:700
  (49 shorter events, 0.5 us)
Async XLA Ops:
  1.0 0.7 copy-start.7
  1.1 0.9 copy-start.5
  2.0 0.9 copy-start.6
  2.8 0.7 copy-start
  2.9 0.9 copy-start.1
  2.9 0.9 copy-start.2
  2.9 0.9 copy-start.3
  3.8 17.4 %copy-start.8 = (s32[1,26,32]{2,0,1:T(1,128)S(1)}, s32[1,26,32]{2,0,1:T(1,128)}, u32[]{:S(2)}) copy-start(s32[1,26,32]{2,0,1:T(1,128)} %param.19) | copy-start | bytes 9988
  6.2 15.1 %collective-permute-start = (f32[16,384]{1,0:T(8,128)S(1)}, f32[16,384]{1,0:T(8,128)S(1)}, u32[]{:S(2)}, u32[]{:S(2)}) collective-permute-start(f32[16,384]{1,0:T(8,128)S(1)} %get-tuple-element.52), channel_id=1, source_target_pairs={{0,1},{1,2},{2,3},{3,4},{4,5},{5,6},{6,7},{8,9},{9,10},{10,11},{11... | collective-permute-start | bytes 73736 | tf_op jit(solution)/shard_map/ppermute | solution.py:612
  19.0 2.2 %copy-start.9 = (s32[1,26]{1,0:T(1,128)S(1)}, s32[1,26]{1,0:T(1,128)}, u32[]{:S(2)}) copy-start(s32[1,26]{1,0:T(1,128)} %param.20) | copy-start | bytes 316
  19.0 13.3 %collective-permute-start.1 = (f32[16,384]{1,0:T(8,128)S(1)}, f32[16,384]{1,0:T(8,128)S(1)}, u32[]{:S(2)}, u32[]{:S(2)}) collective-permute-start(f32[16,384]{1,0:T(8,128)S(1)} %get-tuple-element.53), channel_id=1, source_target_pairs={{1,0},{2,1},{3,2},{4,3},{5,4},{6,5},{7,6},{9,8},{10,9},{11,10},{12... | collective-permute-start | bytes 73736 | tf_op jit(solution)/shard_map/ppermute | solution.py:613
  32.6 6.6 %collective-permute-start.2 = (f32[72,128]{1,0:T(8,128)S(1)}, f32[72,128]{1,0:T(8,128)S(1)}, u32[]{:S(2)}, u32[]{:S(2)}) collective-permute-start(f32[72,128]{1,0:T(8,128)S(1)} %get-tuple-element.56), channel_id=1, source_target_pairs={{0,8},{8,16},{16,24},{24,32},{32,40},{40,48},{48,56},{56,64},{64,7... | collective-permute-start | bytes 110600 | tf_op jit(solution)/shard_map/ppermute | solution.py:612
  37.2 6.5 %collective-permute-start.3 = (f32[72,128]{1,0:T(8,128)S(1)}, f32[72,128]{1,0:T(8,128)S(1)}, u32[]{:S(2)}, u32[]{:S(2)}) collective-permute-start(f32[72,128]{1,0:T(8,128)S(1)} %get-tuple-element.57), channel_id=1, source_target_pairs={{8,0},{16,8},{24,16},{32,24},{40,32},{48,40},{56,48},{64,56},{72,6... | collective-permute-start | bytes 110600 | tf_op jit(solution)/shard_map/ppermute | solution.py:613
  43.8 4.6 %collective-permute-start.4 = (f32[88,128]{1,0:T(8,128)S(1)}, f32[88,128]{1,0:T(8,128)S(1)}, u32[]{:S(2)}, u32[]{:S(2)}) collective-permute-start(f32[88,128]{1,0:T(8,128)S(1)} %get-tuple-element.60), channel_id=1, source_target_pairs={{0,128},{128,256},{256,384},{1,129},{129,257},{257,385},{2,130},{1... | collective-permute-start | bytes 135176 | tf_op jit(solution)/shard_map/ppermute | solution.py:612
  46.9 4.8 %collective-permute-start.5 = (f32[88,128]{1,0:T(8,128)S(1)}, f32[88,128]{1,0:T(8,128)S(1)}, u32[]{:S(2)}, u32[]{:S(2)}) collective-permute-start(f32[88,128]{1,0:T(8,128)S(1)} %get-tuple-element.61), channel_id=1, source_target_pairs={{128,0},{256,128},{384,256},{129,1},{257,129},{385,257},{130,2},{2... | collective-permute-start | bytes 135176 | tf_op jit(solution)/shard_map/ppermute | solution.py:613
  53.8 4.4 %collective-permute-start.6 = (f32[21,384]{1,0:T(8,128)S(1)}, f32[21,384]{1,0:T(8,128)S(1)}, u32[]{:S(2)}, u32[]{:S(2)}) collective-permute-start(f32[21,384]{1,0:T(8,128)S(1)} %get-tuple-element.68), channel_id=1, source_target_pairs={{0,128},{128,256},{256,384},{1,129},{129,257},{257,385},{2,130},{1... | collective-permute-start | bytes 96776 | tf_op jit(solution)/shard_map/ppermute | solution.py:612
  56.9 5.1 %collective-permute-start.7 = (f32[21,384]{1,0:T(8,128)S(1)}, f32[21,384]{1,0:T(8,128)S(1)}, u32[]{:S(2)}, u32[]{:S(2)}) collective-permute-start(f32[21,384]{1,0:T(8,128)S(1)} %get-tuple-element.69), channel_id=1, source_target_pairs={{128,0},{256,128},{384,256},{129,1},{257,129},{385,257},{130,2},{2... | collective-permute-start | bytes 96776 | tf_op jit(solution)/shard_map/ppermute | solution.py:613
  61.9 6.9 %collective-permute-start.8 = (f32[21,384]{1,0:T(8,128)S(1)}, f32[21,384]{1,0:T(8,128)S(1)}, u32[]{:S(2)}, u32[]{:S(2)}) collective-permute-start(f32[21,384]{1,0:T(8,128)S(1)} %get-tuple-element.70), channel_id=1, source_target_pairs={{0,8},{8,16},{16,24},{24,32},{32,40},{40,48},{48,56},{56,64},{64,7... | collective-permute-start | bytes 96776 | tf_op jit(solution)/shard_map/ppermute | solution.py:612
  66.4 6.5 %collective-permute-start.9 = (f32[21,384]{1,0:T(8,128)S(1)}, f32[21,384]{1,0:T(8,128)S(1)}, u32[]{:S(2)}, u32[]{:S(2)}) collective-permute-start(f32[21,384]{1,0:T(8,128)S(1)} %get-tuple-element.71), channel_id=1, source_target_pairs={{8,0},{16,8},{24,16},{32,24},{40,32},{48,40},{56,48},{64,56},{72,6... | collective-permute-start | bytes 96776 | tf_op jit(solution)/shard_map/ppermute | solution.py:613
  72.8 0.7 copy-start.4
  76.8 22.5 %collective-permute-start.10 = (f32[24,384]{1,0:T(8,128)S(1)}, f32[24,384]{1,0:T(8,128)S(1)}, u32[]{:S(2)}, u32[]{:S(2)}) collective-permute-start(f32[24,384]{1,0:T(8,128)S(1)} %get-tuple-element.78), channel_id=1, source_target_pairs={{0,1},{1,2},{2,3},{3,4},{4,5},{5,6},{6,7},{8,9},{9,10},{10,11},{11... | collective-permute-start | bytes 110600 | tf_op jit(solution)/shard_map/ppermute | solution.py:612
  82.2 17.1 %collective-permute-start.11 = (f32[24,384]{1,0:T(8,128)S(1)}, f32[24,384]{1,0:T(8,128)S(1)}, u32[]{:S(2)}, u32[]{:S(2)}) collective-permute-start(f32[24,384]{1,0:T(8,128)S(1)} %get-tuple-element.79), channel_id=1, source_target_pairs={{1,0},{2,1},{3,2},{4,3},{5,4},{6,5},{7,6},{9,8},{10,9},{11,10},{12... | collective-permute-start | bytes 110600 | tf_op jit(solution)/shard_map/ppermute | solution.py:613
  91.7 5.3 %collective-permute-start.12 = (f32[2,256]{1,0:T(2,128)S(1)}, f32[2,256]{1,0:T(2,128)S(1)}, u32[]{:S(2)}, u32[]{:S(2)}) collective-permute-start(f32[2,256]{1,0:T(2,128)S(1)} %get-tuple-element.80), channel_id=1, source_target_pairs={{0,2},{1,3},{2,4},{3,5},{4,6},{5,7},{8,10},{9,11},{10,12},{11,13},... | collective-permute-start | bytes 6152 | tf_op jit(solution)/shard_map/ppermute | solution.py:612
  94.9 4.3 %collective-permute-start.13 = (f32[2,256]{1,0:T(2,128)S(1)}, f32[2,256]{1,0:T(2,128)S(1)}, u32[]{:S(2)}, u32[]{:S(2)}) collective-permute-start(f32[2,256]{1,0:T(2,128)S(1)} %get-tuple-element.81), channel_id=1, source_target_pairs={{2,0},{3,1},{4,2},{5,3},{6,4},{7,5},{10,8},{11,9},{12,10},{13,11},... | collective-permute-start | bytes 6152 | tf_op jit(solution)/shard_map/ppermute | solution.py:613
  101.6 5.9 %collective-permute-start.14 = (f32[48,128]{1,0:T(8,128)S(1)}, f32[48,128]{1,0:T(8,128)S(1)}, u32[]{:S(2)}, u32[]{:S(2)}) collective-permute-start(f32[48,128]{1,0:T(8,128)S(1)} %get-tuple-element.86), channel_id=1, source_target_pairs={{0,8},{8,16},{16,24},{24,32},{32,40},{40,48},{48,56},{56,64},{64,7... | collective-permute-start | bytes 73736 | tf_op jit(solution)/shard_map/ppermute | solution.py:612
  105.6 6.4 %collective-permute-start.15 = (f32[48,128]{1,0:T(8,128)S(1)}, f32[48,128]{1,0:T(8,128)S(1)}, u32[]{:S(2)}, u32[]{:S(2)}) collective-permute-start(f32[48,128]{1,0:T(8,128)S(1)} %get-tuple-element.87), channel_id=1, source_target_pairs={{8,0},{16,8},{24,16},{32,24},{40,32},{48,40},{56,48},{64,56},{72,6... | collective-permute-start | bytes 73736 | tf_op jit(solution)/shard_map/ppermute | solution.py:613
  112.0 4.1 %collective-permute-start.16 = (f32[56,128]{1,0:T(8,128)S(1)}, f32[56,128]{1,0:T(8,128)S(1)}, u32[]{:S(2)}, u32[]{:S(2)}) collective-permute-start(f32[56,128]{1,0:T(8,128)S(1)} %get-tuple-element.90), channel_id=1, source_target_pairs={{0,128},{128,256},{256,384},{1,129},{129,257},{257,385},{2,130},{1... | collective-permute-start | bytes 86024 | tf_op jit(solution)/shard_map/ppermute | solution.py:612
  114.8 4.6 %collective-permute-start.17 = (f32[56,128]{1,0:T(8,128)S(1)}, f32[56,128]{1,0:T(8,128)S(1)}, u32[]{:S(2)}, u32[]{:S(2)}) collective-permute-start(f32[56,128]{1,0:T(8,128)S(1)} %get-tuple-element.91), channel_id=1, source_target_pairs={{128,0},{256,128},{384,256},{129,1},{257,129},{385,257},{130,2},{2... | collective-permute-start | bytes 86024 | tf_op jit(solution)/shard_map/ppermute | solution.py:613

commit v3 on v2

--- a/solution.py
+++ b/solution.py
@@ -52,8 +52,8 @@
     return lax.broadcasted_iota(I32, shape, axis)
 
 
-def dense(ref, lead, rows):
-    value = ref[lead] if lead is not None else ref[...]
+def dense(ref, step, rows):
+    value = ref[:, step, :] if step is not None else ref[...]
     value = value.reshape(rows, CHUNKS, 128)
     return [value[i] for i in range(rows)]
 
@@ -105,6 +105,46 @@
                 signed[rows, lanes] = jnp.where(is_low, -a[at], ends).astype(BF16)
 
 
+def lower_first(spot):
+    return spot[1] // 4 % 2 == 0
+
+
+def by_side(first, one, other):
+    return jnp.where(first, one, other)
+
+
+STEPS = (0, 1, -1)
+
+
+def offset_row(offset):
+    place = (offset[0] + 1) * 9 + (offset[1] + 1) * 3 + offset[2] + 1
+    return place - (place > 13)
+
+
+def fill_send(slots, send):
+    inward = [(x, y, 0) for y in STEPS for x in STEPS][1:]
+    order = inward + [(x, y, 1) for y in STEPS for x in STEPS] + [None] * 3
+    order += [(x, y, -1) for y in STEPS for x in STEPS]
+    send[...] = jnp.zeros(send.shape, I32)
+    for n, offset in enumerate(order):
+        if offset is not None:
+            lane = n % 4 * 32
+            send[n // 4 : n // 4 + 1, lane : lane + 32] = slots[25 - offset_row(offset)]
+
+
+def pick_kernel(counts, slots, pick):
+    pick[...] = jnp.full(pick.shape, -1, I32)
+    order = iota((1, 32), 1)
+    for x in (-1, 0, 1):
+        for y in (-1, 0, 1):
+            for z in (-1, 0, 1):
+                if (x, y, z) != (0, 0, 0):
+                    n, row, lane = offset_row((x, y, z)), (x + 1) * 3 + y + 1, (z + 1) * 32
+                    pick[row : row + 1, lane : lane + 32] = jnp.where(
+                        order < counts[0, n], slots[n], -1
+                    )
+
+
 def cells_of(centre):
     return centre // 512, centre // 128 % 4, centre % 128
 
@@ -185,10 +225,11 @@
 
 
 def first_kernel(
-    live, adjoint, fractions, centers, deform, affine, mass, send,
-    h, hb, zu, zd, bf_out, w_hi, w_lo, d_hi, d_lo,
+    live, adjoint, fractions, centers, deform, affine, mass, slots_back,
+    h, hb, zu, zd, bf_out, w_hi, w_lo, d_hi, d_lo, send,
     l0h, l0l, l2h, l2l, table, hot,
 ):
+    fill_send(slots_back, send)
     table[104:112] = jnp.zeros((8, 128), F32)
     early = dense(fractions, 0, 3) + [centers[0:1, :].reshape(CHUNKS, 128).astype(F32)]
     for i, tile in enumerate(early + dense(deform, 0, 9)):
@@ -243,13 +284,12 @@
     return jnp.concatenate([rows, jnp.zeros((120, 256), F32)], axis=0).T
 
 
-def z_kernel(comps, h, hb, from_low, from_high, h_out, hb_out, yu, yd):
-    z_fold(
-        comps, h, hb[...], from_low[13:15, 0:256], from_high[13:15, 0:256], h_out, hb_out, yu, yd
-    )
-
-
-def z_fold(comps, h, halo, low, high, h_out, hb_out, yu, yd):
+def z_kernel(comps, spot, h, hb, from_low, from_high, h_out, hb_out, ya, yb):
+    low, high = from_low[13:15, 0:256], from_high[13:15, 0:256]
+    z_fold(comps, lower_first(spot), h, hb[...], low, high, h_out, hb_out, ya, yb)
+
+
+def z_fold(comps, first, h, halo, low, high, h_out, hb_out, ya, yb):
     pad = jnp.zeros((6, 256), F32)
     halo = halo + jnp.concatenate([high[1:2], low[1:2], pad], axis=0)
     hb_out[...] = halo
@@ -274,15 +314,16 @@
         down = jnp.where(chosen, b, 0.0 if down is None else down)
         if q % 4 == 3 or q == blocks - 1:
             out = slice(q // 4 * 8, q // 4 * 8 + 8)
-            yu[out] = up
-            yd[out] = down
+            ya[out] = by_side(first, up, down)
+            yb[out] = by_side(first, down, up)
             up, down = None, None
     packed = (blocks + 3) // 4 * 8
-    yu[packed : packed + 8] = wide_rows(halo)
-    yd[packed : packed + 8] = wide_rows(halo)
-
-
-def y_kernel(comps, h, hb, from_low, from_high, h_out, hb_out, xu, xd):
+    ya[packed : packed + 8] = wide_rows(halo)
+    yb[packed : packed + 8] = wide_rows(halo)
+
+
+def y_kernel(comps, spot, h, hb, ra, rb, h_out, hb_out, xu, xd):
+    first = lower_first(spot)
     row = iota((8, 128), 0)
     blocks = comps * 6
     packed = (blocks + 3) // 4 * 8
@@ -290,7 +331,7 @@
         rows = slice(q * 8, q * 8 + 8)
         place = 2 * (q % 4)
         src = slice(q // 4 * 8, q // 4 * 8 + 8)
-        a, b = from_low[src], from_high[src]
+        a, b = by_side(first, rb[src], ra[src]), by_side(first, ra[src], rb[src])
         a = pltpu.roll(a, (-place) % 8, 0) if place else a
         b = pltpu.roll(b, (4 - place) % 8, 0) if place != 4 else b
         tile = (
@@ -303,8 +344,10 @@
         if x < 2:
             xd[c * 16 + x * 8 : c * 16 + x * 8 + 8] = tile
     place = iota((8, 256), 1) % 8
-    a = pltpu.roll(from_wide(from_low[packed : packed + 8]), 252, 1)
-    b = pltpu.roll(from_wide(from_high[packed : packed + 8]), 4, 1)
+    a, b = ra[packed : packed + 8], rb[packed : packed + 8]
+    a, b = by_side(first, b, a), by_side(first, a, b)
+    a = pltpu.roll(from_wide(a), 252, 1)
+    b = pltpu.roll(from_wide(b), 4, 1)
     halo = hb[...] + jnp.where(place < 2, a, 0.0) + jnp.where((place >= 4) & (place < 6), b, 0.0)
     hb_out[...] = halo
     xu[comps * 16 : comps * 16 + 8] = wide_rows(halo)
@@ -458,10 +501,12 @@
     return ref[:, i * 128 : i * 128 + 128]
 
 
-def route_y_kernel(mid, from_low, from_high, yu, yd):
+def route_y_kernel(spot, mid, from_low, from_high, ya, yb):
+    first = lower_first(spot)
     for i, ref in enumerate((mid, from_low, from_high)):
-        yd[:, i * 128 : i * 128 + 128] = lane_tile(ref, 0)
-        yu[:, i * 128 : i * 128 + 128] = lane_tile(ref, 2)
+        down, up = lane_tile(ref, 0), lane_tile(ref, 2)
+        ya[:, i * 128 : i * 128 + 128] = by_side(first, up, down)
+        yb[:, i * 128 : i * 128 + 128] = by_side(first, down, up)
 
 
 def carry(tiles, indices, lh, ll, hot):
@@ -485,15 +530,23 @@
     build_z(dense(fractions, 0, 3)[2], cell_z, w_hi, w_lo, d_hi, d_lo)
 
 
+def stay_kernel(second, prior, stayed, lh, ll, hot):
+    tiles = [lambda r, t=t: second[r, t : t + 1, :] for t in range(8)]
+    total = carry(tiles, [prior[t : t + 1] for t in range(8)], lh, ll, hot)
+    for i in range(21):
+        stayed[i] = total[i * 8 : i * 8 + 8]
+
+
 def near_kernel(
-    live, mid, x_low, x_high, y_low, y_high, second, prior, send,
+    live, spot, mid, x_low, x_high, ra, rb, stayed, send,
     static_low, static_high, fractions, centers, deform, w_hi, w_lo, d_hi, d_lo,
     zu, zd, up2, dn2, own_low, own_high, carried,
     lh, ll, hot, l0h, l0l, l2h, l2l, moved, static, e0, e1, e2, e3,
 ):
     groups = [lane_tile(mid, 1), lane_tile(x_low, 1), lane_tile(x_high, 1)]
-    groups += [lane_tile(y_low, i) for i in range(3)]
-    groups += [lane_tile(y_high, i) for i in range(3)]
+    first = lower_first(spot)
+    groups += [by_side(first, lane_tile(rb, i), lane_tile(ra, i)) for i in range(3)]
+    groups += [by_side(first, lane_tile(ra, i), lane_tile(rb, i)) for i in range(3)]
     final = pieces(groups[1:], 32, 2)
     moved[...] = jnp.zeros(moved.shape, F32)
     static[...] = jnp.zeros(static.shape, F32)
@@ -521,13 +574,11 @@
     put_planes(own_low, 0, downward[0:1], downward[3:4])
     put_planes(dn2, 0, downward[1:2], downward[2:3])
 
-    tiles = [lambda r, t=t: second[r, t : t + 1, :] for t in range(8)]
-    tiles += [lambda r, t=t: final[t][r : r + 1] for t in range(2)]
-    indices = [prior[t : t + 1] for t in range(8)] + [send[t : t + 1] for t in range(2)]
-    total = carry(tiles, indices, lh, ll, hot)
+    tiles = [lambda r, t=t: final[t][r : r + 1] for t in range(2)]
+    total = carry(tiles, [send[t : t + 1] for t in range(2)], lh, ll, hot)
     slots = iota((8, 128), 0) * 128 + iota((8, 128), 1)
     use = (slots < live[0, 0]).astype(F32)
-    adj = [total[i * 8 : i * 8 + 8] * use for i in range(21)]
+    adj = [(stayed[i] + total[i * 8 : i * 8 + 8]) * use for i in range(21)]
     for i in range(21):
         carried[i] = adj[i]
     frac = dense(fractions, 0, 3)
@@ -540,9 +591,9 @@
 
 
 def second_kernel(
-    live, carried, z_low, z_high, low2, high2, own_low, own_high, send,
+    live, spot, carried, z_low, z_high, low2, high2, own_low, own_high, send,
     fractions, centers, deform, affine, w_hi, w_lo, d_hi, d_lo,
-    h_out, hb_out, yu, yd, bf_out,
+    h_out, hb_out, ya, yb, bf_out,
     lh, ll, hot, l0h, l0l, l2h, l2l, h,
 ):
     tiles = [lambda r, t=t: z_low[r : r + 1, t * 128 : t * 128 + 128] for t in range(3)]
@@ -564,7 +615,7 @@
     halo = jnp.where(iota((8, 256), 0) < 2, ends, 0.0)
     low = z_low[21:23, 0:256] + low2[0:2] + own_low[0:2]
     high = z_high[21:23, 0:256] + high2[0:2] + own_high[0:2]
-    z_fold(3, h, halo, low, high, h_out, hb_out, yu, yd)
+    z_fold(3, lower_first(spot), h, halo, low, high, h_out, hb_out, ya, yb)
 
 
 def gather_second_kernel(
@@ -614,6 +665,15 @@
     return low, high
 
 
+def both_pairs(first, second, axis):
+    count = lax.axis_size(axis)
+    a = [(i, i ^ 1) for i in range(count) if i ^ 1 < count]
+    b = [p for i in range(1, count - 1, 2) for p in ((i, i + 1), (i + 1, i))]
+    ra = lax.ppermute(first, axis, a)
+    rb = lax.ppermute(second, axis, b) if b else jnp.zeros_like(second)
+    return ra, rb
+
+
 def body(
     fractions, centers, deform, next_affine, cell_mass, final_adjoint,
     live_count, send_slot, receive_slot, receive_count, prior_slot,
@@ -622,19 +682,11 @@
     spot = spot.astype(I32)
     extents = (lax.axis_size("gx") * 4, lax.axis_size("gy") * 4, lax.axis_size("gz") * 128)
 
-    def cube(rows, fill):
-        middle = jnp.full((1, 32), fill, I32)
-        return jnp.concatenate([rows[:13], middle, rows[13:]]).reshape(3, 3, 3, 32)
-
-    order = jnp.arange(32, dtype=I32)[None]
-    chosen = jnp.where(order < receive_count[0][:, None], receive_slot[0], -1)
-    pick = cube(chosen, -1)
-    pick = jnp.concatenate([pick, jnp.full((3, 3, 1, 32), -1, I32)], axis=2).reshape(9, 128)
-    back = jnp.transpose(cube(send_slot[0], 0)[::-1, ::-1, ::-1], (2, 1, 0, 3))
-    back = jnp.concatenate([back[:, 1:], back[:, :1]], axis=1)
-    back = jnp.concatenate([back[:, :, 1:], back[:, :, :1]], axis=2).reshape(3, 9, 32)
-    blank = jnp.zeros((3, 32), I32)
-    send = jnp.concatenate([back[1, 1:], back[2], blank, back[0], blank]).reshape(8, 128)
+    fractions, deform, next_affine = (
+        jnp.transpose(v, (1, 0, 2)) for v in (fractions, deform, next_affine)
+    )
+    slots_back = jnp.transpose(send_slot, (1, 0, 2))
+    slots_out = jnp.transpose(receive_slot, (1, 0, 2))
     prior = prior_slot.reshape(8, 128)
 
     wide = shape(ZROWS, 1024, dtype=BF16)
@@ -645,27 +697,31 @@
         ((144, 1024), F32), ((144, 1024), F32), ((12, 8, 128), F32),
     ]
 
-    def fold(comps, h, hb, yu, yd):
-        low, high = both_ways(yu, yd, "gy")
+    def fold(comps, h, hb, ya, yb):
+        ra, rb = both_pairs(ya, yb, "gy")
         rows = comps * 16 + 8
         h, hb, xu, xd = call(
-            functools.partial(y_kernel, comps), f"fold_y{comps}", [VMEM] * 4,
+            functools.partial(y_kernel, comps), f"fold_y{comps}", [SMEM] + [VMEM] * 4,
             [shape(comps * 48, 128), shape(8, 256), shape(rows, 128), shape(rows, 128)],
-        )(h, hb, low, high)
+        )(spot, h, hb, ra, rb)
         low, high = both_ways(xu, xd, "gx")
         return h, hb, low, high
 
-    h, hb, zu, zd, bf, *w = call(
+    h, hb, zu, zd, bf, *w, send = call(
         first_kernel, "scatter_first", [SMEM] + [VMEM] * 7,
-        [shape(240, 128), shape(8, 256), shape(16, 384), shape(16, 384), shape(9, 8, 128)] + weights,
+        [shape(240, 128), shape(8, 256), shape(16, 384), shape(16, 384), shape(9, 8, 128)]
+        + weights + [shape(8, 128, dtype=I32)],
         lrows + [((112, 128), F32), ((128, 128), BF16)],
-    )(live_count, final_adjoint, fractions, centers, deform, next_affine, cell_mass, send)
+    )(live_count, final_adjoint, fractions, centers, deform, next_affine, cell_mass, slots_back)
     static_low, static_high = both_ways(zu, zd, "gz")
-    h, hb, yu, yd = call(
-        functools.partial(z_kernel, 5), "fold_z5", [VMEM] * 4,
+    (pick,) = call(pick_kernel, "fill_pick", [SMEM, VMEM], [shape(9, 128, dtype=I32)])(
+        receive_count, slots_out
+    )
+    h, hb, ya, yb = call(
+        functools.partial(z_kernel, 5), "fold_z5", [SMEM] + [VMEM] * 4,
         [shape(240, 128), shape(8, 256), shape(72, 128), shape(72, 128)],
-    )(h, hb, static_low, static_high)
-    h, hb, low, high = fold(5, h, hb, yu, yd)
+    )(spot, h, hb, static_low, static_high)
+    h, hb, low, high = fold(5, h, hb, ya, yb)
     second, xu, xd, mid, mass_core, mass_halo = call(
         functools.partial(gather_first_kernel, extents), "gather_first",
         [SMEM, SMEM] + [VMEM] * 13,
@@ -675,28 +731,34 @@
 
     w = call(weights_kernel, "weights_second", [VMEM] * 2, weights)(fractions, centers)
     x_low, x_high = both_ways(xu, xd, "gx")
-    yu, yd = call(route_y_kernel, "route_y", [VMEM] * 3, [shape(21, 384)] * 2)(mid, x_low, x_high)
-    y_low, y_high = both_ways(yu, yd, "gy")
+    (stayed,) = call(
+        stay_kernel, "stay", [VMEM] * 2, [shape(21, 8, 128)],
+        [((176, 1024), BF16)] * 2 + [((128, 1024), BF16)],
+    )(second, prior)
+    ya, yb = call(route_y_kernel, "route_y", [SMEM] + [VMEM] * 3, [shape(21, 384)] * 2)(
+        spot, mid, x_low, x_high
+    )
+    ra, rb = both_pairs(ya, yb, "gy")
     zu, zd, up2, dn2, own_low, own_high, carried = call(
-        near_kernel, "scatter_near", [SMEM] + [VMEM] * 17,
+        near_kernel, "scatter_near", [SMEM] * 2 + [VMEM] * 16,
         [shape(24, 384)] * 2 + [shape(2, 256)] * 4 + [shape(21, 8, 128)],
-        [((176, 1280), BF16)] * 2 + [((128, 1280), BF16)] + lrows
+        [((176, 256), BF16)] * 2 + [((128, 256), BF16)] + lrows
         + [((21, 8, 128), F32), ((14, 8, 128), F32)] + [((16, 768), BF16)] * 4,
     )(
-        live_count, mid, x_low, x_high, y_low, y_high, second, prior, send,
+        live_count, spot, mid, x_low, x_high, ra, rb, stayed, send,
         static_low, static_high, fractions, centers, deform, *w,
     )
     z_low, z_high = both_ways(zu, zd, "gz")
     low2, high2 = both_ways(up2, dn2, "gz", 2)
-    h, hb, yu, yd, bf = call(
-        second_kernel, "scatter_second", [SMEM] + [VMEM] * 16,
+    h, hb, ya, yb, bf = call(
+        second_kernel, "scatter_second", [SMEM] * 2 + [VMEM] * 16,
         [shape(144, 128), shape(8, 256), shape(48, 128), shape(48, 128), shape(9, 8, 128)],
         [((176, 768), BF16)] * 2 + [((128, 768), BF16)] + lrows + [((144, 128), F32)],
     )(
-        live_count, carried, z_low, z_high, low2, high2, own_low, own_high, send,
+        live_count, spot, carried, z_low, z_high, low2, high2, own_low, own_high, send,
         fractions, centers, deform, next_affine, *w,
     )
-    h, hb, low, high = fold(3, h, hb, yu, yd)
+    h, hb, low, high = fold(3, h, hb, ya, yb)
     (result,) = call(
         functools.partial(gather_second_kernel, extents), "gather_second",
         [SMEM, SMEM] + [VMEM] * 14,

time: 122 us -> 126 us (1.033)
  the two profiles are of different devices: /device:TPU:105 before, /device:TPU:64 now
where the time goes in v3:
time: 126 us; the launch traced here: 125 us
  starting transfers between devices  64.3 us (51%)
  waiting for transfers between devices  36.7 us (29%)
  Pallas kernels  16.8 us (13%)
  local copies, waits for them, and re-layouts  6.33 us (5%)
    ppermute x6, starting transfers between devices, both_ways(): low = lax.ppermute(up, axis, [(i, i + step) for i in range(count - step)])  42.8 us
    ppermute x6, waiting for transfers between devices, both_ways(): lax.ppermute(down, axis, [(i + step, i) for i in range(count - step)])  29.2 us
    ppermute x3, starting transfers between devices, both_pairs(): rb = lax.ppermute(second, axis, b) if b else jnp.zeros_like(second)  7.96 us
    ppermute x6, starting transfers between devices, both_ways(): lax.ppermute(down, axis, [(i + step, i) for i in range(count - step)])  7.75 us
    ppermute x3, waiting for transfers between devices, both_pairs(): rb = lax.ppermute(second, axis, b) if b else jnp.zeros_like(second)  6.51 us
    unnamed x30, local copies, waits for them, and re-layouts  6.33 us
    ppermute x3, starting transfers between devices, both_pairs(): ra = lax.ppermute(first, axis, a)  5.78 us
    pallas_call x1, Pallas kernels, body(): call(near_kernel, 'scatter_near', [SMEM] * 2 + [VMEM] * 16, [shape(24, 38...  3.08 us
  transfers between devices with their start and end apart: 18, of which 11 were waited for; matrix products, arithmetic and copies ran while one was open for 0% of the time, Pallas kernels for 1%

profile of v3, /device:TPU:64, one launch (start us, length us, event | category | flops | bytes accessed | tf_op | source)
XLA Modules:
  0.0 124.6 jit_solution(17461648673447490472)
XLA Ops:
  0.0 0.7 copy-done.12
  0.7 0.9 copy-done
  1.5 0.7 copy-done.2
  2.3 0.7 copy-done.4
  3.0 0.9 copy-done.6
  3.9 0.9 copy-done.8
  4.8 0.7 copy-done.9
  5.5 0.7 copy-done.11
  6.2 2.6 %scatter_first.1 = (f32[240,128]{1,0:T(8,128)S(1)}, f32[8,256]{1,0:T(8,128)S(1)}, f32[16,384]{1,0:T(8,128)S(1)}, f32[16,384]{1,0:T(8,128)S(1)}, f32[9,8,128]{2,1...) custom-call(s32[1,2]{1,0:T(1,128)S(1)} %copy-done.12, ...), custom_call_target="tpu_custom_call" | custom-call | tf_op jit(solution)/shard_map/scatter_first/pallas_call | solution.py:710
  8.8 13.9 %collective-permute-start = (f32[16,384]{1,0:T(8,128)S(1)}, f32[16,384]{1,0:T(8,128)S(1)}, u32[]{:S(2)}, u32[]{:S(2)}) collective-permute-start(f32[16,384]{1,0:T(8,128)S(1)} %get-tuple-element.53), channel_id=1, source_target_pairs={{0,1},{1,2},{2,3},{3,4},{4,5},{5,6},{6,7},{8,9},{9,10},{10,11},{11... | collective-permute-start | bytes 73736 | tf_op jit(solution)/shard_map/ppermute | solution.py:663
  22.7 1.3 %collective-permute-start.1 = (f32[16,384]{1,0:T(8,128)S(1)}, f32[16,384]{1,0:T(8,128)S(1)}, u32[]{:S(2)}, u32[]{:S(2)}) collective-permute-start(f32[16,384]{1,0:T(8,128)S(1)} %get-tuple-element.54), channel_id=1, source_target_pairs={{1,0},{2,1},{3,2},{4,3},{5,4},{6,5},{7,6},{9,8},{10,9},{11,10},{12... | collective-permute-start | bytes 73736 | tf_op jit(solution)/shard_map/ppermute | solution.py:664
  24.1 0.4 collective-permute-done.from_low.static_low
  24.5 12.6 %collective-permute-done.1.from_high.static_high = f32[16,384]{1,0:T(8,128)S(1)} collective-permute-done((f32[16,384]{1,0:T(8,128)S(1)}, f32[16,384]{1,0:T(8,128)S(1)}, u32[]{:S(2)}, u32[]{:S(2)}) %collective-permute-start.1) | collective-permute-done | bytes 24608 | tf_op jit(solution)/shard_map/ppermute | solution.py:664
  37.2 0.8 fold_z5.1
  38.0 1.9 %collective-permute-start.2 = (f32[72,128]{1,0:T(8,128)S(1)}, f32[72,128]{1,0:T(8,128)S(1)}, u32[]{:S(2)}, u32[]{:S(2)}) collective-permute-start(f32[72,128]{1,0:T(8,128)S(1)} %get-tuple-element.57), channel_id=1, source_target_pairs={{0,8},{8,0},{16,24},{24,16},{32,40},{40,32},{48,56},{56,48},{64,72... | collective-permute-start | bytes 110600 | tf_op jit(solution)/shard_map/ppermute | solution.py:672
  40.0 3.0 %collective-permute-start.3 = (f32[72,128]{1,0:T(8,128)S(1)}, f32[72,128]{1,0:T(8,128)S(1)}, u32[]{:S(2)}, u32[]{:S(2)}) collective-permute-start(f32[72,128]{1,0:T(8,128)S(1)} %get-tuple-element.58), channel_id=1, source_target_pairs={{8,16},{16,8},{24,32},{32,24},{40,48},{48,40},{56,64},{64,56},{72,... | collective-permute-start | bytes 110600 | tf_op jit(solution)/shard_map/ppermute | solution.py:673
  43.0 2.2 %collective-permute-done.3.rb = f32[72,128]{1,0:T(8,128)S(1)} collective-permute-done((f32[72,128]{1,0:T(8,128)S(1)}, f32[72,128]{1,0:T(8,128)S(1)}, u32[]{:S(2)}, u32[]{:S(2)}) %collective-permute-start.3) | collective-permute-done | bytes 36896 | tf_op jit(solution)/shard_map/ppermute | solution.py:673
  45.2 0.6 fold_y5.1
  45.9 3.5 %collective-permute-start.4 = (f32[88,128]{1,0:T(8,128)S(1)}, f32[88,128]{1,0:T(8,128)S(1)}, u32[]{:S(2)}, u32[]{:S(2)}) collective-permute-start(f32[88,128]{1,0:T(8,128)S(1)} %get-tuple-element.61), channel_id=1, source_target_pairs={{0,128},{128,256},{256,384},{1,129},{129,257},{257,385},{2,130},{1... | collective-permute-start | bytes 135176 | tf_op jit(solution)/shard_map/ppermute | solution.py:663
  49.4 1.3 %collective-permute-start.5 = (f32[88,128]{1,0:T(8,128)S(1)}, f32[88,128]{1,0:T(8,128)S(1)}, u32[]{:S(2)}, u32[]{:S(2)}) collective-permute-start(f32[88,128]{1,0:T(8,128)S(1)} %get-tuple-element.62), channel_id=1, source_target_pairs={{128,0},{256,128},{384,256},{129,1},{257,129},{385,257},{130,2},{2... | collective-permute-start | bytes 135176 | tf_op jit(solution)/shard_map/ppermute | solution.py:664
  50.7 0.6 fill_pick.1.pick
  51.4 4.0 %collective-permute-done.5.from_high = f32[88,128]{1,0:T(8,128)S(1)} collective-permute-done((f32[88,128]{1,0:T(8,128)S(1)}, f32[88,128]{1,0:T(8,128)S(1)}, u32[]{:S(2)}, u32[]{:S(2)}) %collective-permute-start.5) | collective-permute-done | bytes 45088 | tf_op jit(solution)/shard_map/ppermute | solution.py:664
  55.3 2.1 %gather_first.1 = (f32[21,8,128]{2,1,0:T(8,128)S(1)}, f32[21,384]{1,0:T(8,128)S(1)}, f32[21,384]{1,0:T(8,128)S(1)}, f32[21,384]{1,0:T(8,128)S(1)}, f32[48,128]{1,0:T(8,128)S(1)}, /*index=5*/f32[8,256]{1,0:T(8,128)S(1)}) custom-call(s32[1,2]{1,0:T(1,128)S(1)} %copy-done.12, s32[3]{0:T(128)S(1)} %pad_add_fusion.spot, f32[240,128]{1,0:T(8,128)S(1)} %get-tuple-element.59.h, ...), custom_call_target="tpu_custom_call" | custom-call | tf_op jit(solution)/shard_map/gather_first/pallas_call | solution.py:725
  57.5 3.4 %collective-permute-start.6 = (f32[21,384]{1,0:T(8,128)S(1)}, f32[21,384]{1,0:T(8,128)S(1)}, u32[]{:S(2)}, u32[]{:S(2)}) collective-permute-start(f32[21,384]{1,0:T(8,128)S(1)} %get-tuple-element.69), channel_id=1, source_target_pairs={{0,128},{128,256},{256,384},{1,129},{129,257},{257,385},{2,130},{1... | collective-permute-start | bytes 96776 | tf_op jit(solution)/shard_map/ppermute | solution.py:663
  60.9 1.3 %collective-permute-start.7 = (f32[21,384]{1,0:T(8,128)S(1)}, f32[21,384]{1,0:T(8,128)S(1)}, u32[]{:S(2)}, u32[]{:S(2)}) collective-permute-start(f32[21,384]{1,0:T(8,128)S(1)} %get-tuple-element.70), channel_id=1, source_target_pairs={{128,0},{256,128},{384,256},{129,1},{257,129},{385,257},{130,2},{2... | collective-permute-start | bytes 96776 | tf_op jit(solution)/shard_map/ppermute | solution.py:664
  62.2 0.3 collective-permute-done.6.from_low.x_low
  62.5 4.2 %collective-permute-done.7.from_high.x_high = f32[21,384]{1,0:T(8,128)S(1)} collective-permute-done((f32[21,384]{1,0:T(8,128)S(1)}, f32[21,384]{1,0:T(8,128)S(1)}, u32[]{:S(2)}, u32[]{:S(2)}) %collective-permute-start.7) | collective-permute-done | bytes 32288 | tf_op jit(solution)/shard_map/ppermute | solution.py:664
  66.7 0.6 route_y.1
  67.3 1.9 %collective-permute-start.8 = (f32[21,384]{1,0:T(8,128)S(1)}, f32[21,384]{1,0:T(8,128)S(1)}, u32[]{:S(2)}, u32[]{:S(2)}) collective-permute-start(f32[21,384]{1,0:T(8,128)S(1)} %get-tuple-element.71), channel_id=1, source_target_pairs={{0,8},{8,0},{16,24},{24,16},{32,40},{40,32},{48,56},{56,48},{64,72... | collective-permute-start | bytes 96776 | tf_op jit(solution)/shard_map/ppermute | solution.py:672
  69.2 3.0 %collective-permute-start.9 = (f32[21,384]{1,0:T(8,128)S(1)}, f32[21,384]{1,0:T(8,128)S(1)}, u32[]{:S(2)}, u32[]{:S(2)}) collective-permute-start(f32[21,384]{1,0:T(8,128)S(1)} %get-tuple-element.72), channel_id=1, source_target_pairs={{8,16},{16,8},{24,32},{32,24},{40,48},{48,40},{56,64},{64,56},{72,... | collective-permute-start | bytes 96776 | tf_op jit(solution)/shard_map/ppermute | solution.py:673
  72.3 0.5 weights_second.1
  73.0 0.5 stay.1.stayed
  73.5 1.1 collective-permute-done.9.rb
  74.5 3.1 %scatter_near.1 = (f32[24,384]{1,0:T(8,128)S(1)}, f32[24,384]{1,0:T(8,128)S(1)}, f32[2,256]{1,0:T(2,128)S(1)}, f32[2,256]{1,0:T(2,128)S(1)}, f32[2,256]{1,0:T(2,...) custom-call(s32[1,2]{1,0:T(1,128)S(1)} %copy-done.12, s32[3]{0:T(128)S(1)} %pad_add_fusion.spot, ...), custom_call_target="tpu_custom_call" | custom-call | tf_op jit(solution)/shard_map/scatter_near/pallas_call | solution.py:742
  77.6 3.2 %collective-permute-start.10 = (f32[24,384]{1,0:T(8,128)S(1)}, f32[24,384]{1,0:T(8,128)S(1)}, u32[]{:S(2)}, u32[]{:S(2)}) collective-permute-start(f32[24,384]{1,0:T(8,128)S(1)} %get-tuple-element.80), channel_id=1, source_target_pairs={{0,1},{1,2},{2,3},{3,4},{4,5},{5,6},{6,7},{8,9},{9,10},{10,11},{11... | collective-permute-start | bytes 110600 | tf_op jit(solution)/shard_map/ppermute | solution.py:663
  80.8 1.3 %collective-permute-start.11 = (f32[24,384]{1,0:T(8,128)S(1)}, f32[24,384]{1,0:T(8,128)S(1)}, u32[]{:S(2)}, u32[]{:S(2)}) collective-permute-start(f32[24,384]{1,0:T(8,128)S(1)} %get-tuple-element.81), channel_id=1, source_target_pairs={{1,0},{2,1},{3,2},{4,3},{5,4},{6,5},{7,6},{9,8},{10,9},{11,10},{12... | collective-permute-start | bytes 110600 | tf_op jit(solution)/shard_map/ppermute | solution.py:664
  82.1 15.7 %collective-permute-start.12 = (f32[2,256]{1,0:T(2,128)S(1)}, f32[2,256]{1,0:T(2,128)S(1)}, u32[]{:S(2)}, u32[]{:S(2)}) collective-permute-start(f32[2,256]{1,0:T(2,128)S(1)} %get-tuple-element.82), channel_id=1, source_target_pairs={{0,2},{1,3},{2,4},{3,5},{4,6},{5,7},{8,10},{9,11},{10,12},{11,13},... | collective-permute-start | bytes 6152 | tf_op jit(solution)/shard_map/ppermute | solution.py:663
  97.8 1.3 %collective-permute-start.13 = (f32[2,256]{1,0:T(2,128)S(1)}, f32[2,256]{1,0:T(2,128)S(1)}, u32[]{:S(2)}, u32[]{:S(2)}) collective-permute-start(f32[2,256]{1,0:T(2,128)S(1)} %get-tuple-element.83), channel_id=1, source_target_pairs={{2,0},{3,1},{4,2},{5,3},{6,4},{7,5},{10,8},{11,9},{12,10},{13,11},... | collective-permute-start | bytes 6152 | tf_op jit(solution)/shard_map/ppermute | solution.py:664
  99.1 4.2 %collective-permute-done.13.high2 = f32[2,256]{1,0:T(2,128)S(1)} collective-permute-done((f32[2,256]{1,0:T(2,128)S(1)}, f32[2,256]{1,0:T(2,128)S(1)}, u32[]{:S(2)}, u32[]{:S(2)}) %collective-permute-start.13) | collective-permute-done | bytes 2080 | tf_op jit(solution)/shard_map/ppermute | solution.py:664
  103.3 2.5 %scatter_second.1 = (f32[144,128]{1,0:T(8,128)S(1)}, f32[8,256]{1,0:T(8,128)S(1)}, f32[48,128]{1,0:T(8,128)S(1)}, f32[48,128]{1,0:T(8,128)S(1)}, f32[9,8,128]{2,1,0:T(8,128)S(1)}) custom-call(s32[1,2]{1,0:T(1,128)S(1)} %copy-done.12, s32[3]{0:T(128)S(1)} %pad_add_fusion.spot, f32[21,8,128]{2,1,0:T(8,128)S(1)} %get-tuple-element.79.carried, ...), custom_call_target="tpu_custom_call" | custom-call | tf_op jit(solution)/shard_map/scatter_second/pallas_call | solution.py:753
  105.8 1.9 %collective-permute-start.14 = (f32[48,128]{1,0:T(8,128)S(1)}, f32[48,128]{1,0:T(8,128)S(1)}, u32[]{:S(2)}, u32[]{:S(2)}) collective-permute-start(f32[48,128]{1,0:T(8,128)S(1)} %get-tuple-element.88), channel_id=1, source_target_pairs={{0,8},{8,0},{16,24},{24,16},{32,40},{40,32},{48,56},{56,48},{64,72... | collective-permute-start | bytes 73736 | tf_op jit(solution)/shard_map/ppermute | solution.py:672
  107.8 1.9 %collective-permute-start.15 = (f32[48,128]{1,0:T(8,128)S(1)}, f32[48,128]{1,0:T(8,128)S(1)}, u32[]{:S(2)}, u32[]{:S(2)}) collective-permute-start(f32[48,128]{1,0:T(8,128)S(1)} %get-tuple-element.89), channel_id=1, source_target_pairs={{8,16},{16,8},{24,32},{32,24},{40,48},{48,40},{56,64},{64,56},{72,... | collective-permute-start | bytes 73736 | tf_op jit(solution)/shard_map/ppermute | solution.py:673
  109.7 3.2 %collective-permute-done.15.rb = f32[48,128]{1,0:T(8,128)S(1)} collective-permute-done((f32[48,128]{1,0:T(8,128)S(1)}, f32[48,128]{1,0:T(8,128)S(1)}, u32[]{:S(2)}, u32[]{:S(2)}) %collective-permute-start.15) | collective-permute-done | bytes 24608 | tf_op jit(solution)/shard_map/ppermute | solution.py:673
  112.9 0.6 fold_y3.1
  113.5 3.1 %collective-permute-start.16 = (f32[56,128]{1,0:T(8,128)S(1)}, f32[56,128]{1,0:T(8,128)S(1)}, u32[]{:S(2)}, u32[]{:S(2)}) collective-permute-start(f32[56,128]{1,0:T(8,128)S(1)} %get-tuple-element.92), channel_id=1, source_target_pairs={{0,128},{128,256},{256,384},{1,129},{129,257},{257,385},{2,130},{1... | collective-permute-start | bytes 86024 | tf_op jit(solution)/shard_map/ppermute | solution.py:663
  116.7 1.3 %collective-permute-start.17 = (f32[56,128]{1,0:T(8,128)S(1)}, f32[56,128]{1,0:T(8,128)S(1)}, u32[]{:S(2)}, u32[]{:S(2)}) collective-permute-start(f32[56,128]{1,0:T(8,128)S(1)} %get-tuple-element.93), channel_id=1, source_target_pairs={{128,0},{256,128},{384,256},{129,1},{257,129},{385,257},{130,2},{2... | collective-permute-start | bytes 86024 | tf_op jit(solution)/shard_map/ppermute | solution.py:664
  118.2 4.2 %collective-permute-done.17.from_high = f32[56,128]{1,0:T(8,128)S(1)} collective-permute-done((f32[56,128]{1,0:T(8,128)S(1)}, f32[56,128]{1,0:T(8,128)S(1)}, u32[]{:S(2)}, u32[]{:S(2)}) %collective-permute-start.17) | collective-permute-done | bytes 28704 | tf_op jit(solution)/shard_map/ppermute | solution.py:664
  122.4 2.2 %gather_second.1 = f32[21,1024]{1,0:T(8,128)} custom-call(s32[1,2]{1,0:T(1,128)S(1)} %copy-done.12, s32[3]{0:T(128)S(1)} %pad_add_fusion.spot, f32[144,128]{1,0:T(8,128)S(1)} %get-tuple-element.90.h, f32[8,256]{1,0:T(8,128)S(1)} %get-tuple-element.91.hb, f32[56,128]{1,0:T(8,128)S(1)} %collective-permute-done.16.from_low, ...), custom_call_target="tpu_custom_call" | custom-call | tf_op jit(solution)/shard_map/gather_second/pallas_call | solution.py:762
  (31 shorter events, 0.5 us)
Async XLA Ops:
  0.0 0.7 copy-start.12
  0.7 0.9 copy-start
  1.5 0.7 copy-start.2
  2.3 0.7 copy-start.4
  3.0 0.9 copy-start.6
  3.9 0.9 copy-start.8
  4.8 0.7 copy-start.9
  5.5 0.7 copy-start.11
  8.8 15.7 %collective-permute-start = (f32[16,384]{1,0:T(8,128)S(1)}, f32[16,384]{1,0:T(8,128)S(1)}, u32[]{:S(2)}, u32[]{:S(2)}) collective-permute-start(f32[16,384]{1,0:T(8,128)S(1)} %get-tuple-element.53), channel_id=1, source_target_pairs={{0,1},{1,2},{2,3},{3,4},{4,5},{5,6},{6,7},{8,9},{9,10},{10,11},{11... | collective-permute-start | bytes 73736 | tf_op jit(solution)/shard_map/ppermute | solution.py:663
  22.7 14.4 %collective-permute-start.1 = (f32[16,384]{1,0:T(8,128)S(1)}, f32[16,384]{1,0:T(8,128)S(1)}, u32[]{:S(2)}, u32[]{:S(2)}) collective-permute-start(f32[16,384]{1,0:T(8,128)S(1)} %get-tuple-element.54), channel_id=1, source_target_pairs={{1,0},{2,1},{3,2},{4,3},{5,4},{6,5},{7,6},{9,8},{10,9},{11,10},{12... | collective-permute-start | bytes 73736 | tf_op jit(solution)/shard_map/ppermute | solution.py:664
  38.0 5.0 %collective-permute-start.2 = (f32[72,128]{1,0:T(8,128)S(1)}, f32[72,128]{1,0:T(8,128)S(1)}, u32[]{:S(2)}, u32[]{:S(2)}) collective-permute-start(f32[72,128]{1,0:T(8,128)S(1)} %get-tuple-element.57), channel_id=1, source_target_pairs={{0,8},{8,0},{16,24},{24,16},{32,40},{40,32},{48,56},{56,48},{64,72... | collective-permute-start | bytes 110600 | tf_op jit(solution)/shard_map/ppermute | solution.py:672
  40.0 5.3 %collective-permute-start.3 = (f32[72,128]{1,0:T(8,128)S(1)}, f32[72,128]{1,0:T(8,128)S(1)}, u32[]{:S(2)}, u32[]{:S(2)}) collective-permute-start(f32[72,128]{1,0:T(8,128)S(1)} %get-tuple-element.58), channel_id=1, source_target_pairs={{8,16},{16,8},{24,32},{32,24},{40,48},{48,40},{56,64},{64,56},{72,... | collective-permute-start | bytes 110600 | tf_op jit(solution)/shard_map/ppermute | solution.py:673
  45.2 5.5 %copy-start.10 = (s32[1,26,32]{2,0,1:T(1,128)S(1)}, s32[1,26,32]{2,0,1:T(1,128)}, u32[]{:S(2)}) copy-start(s32[1,26,32]{2,0,1:T(1,128)} %param.19) | copy-start | bytes 9988
  45.2 5.5 %copy-start.14 = (s32[1,26]{1,0:T(1,128)S(1)}, s32[1,26]{1,0:T(1,128)}, u32[]{:S(2)}) copy-start(s32[1,26]{1,0:T(1,128)} %counts.1) | copy-start | bytes 316
  45.2 10.1 %copy-start.1 = (f32[2,9,1024]{2,0,1:T(2,128)S(1)}, f32[2,9,1024]{2,0,1:T(2,128)}, u32[]{:S(2)}) copy-start(f32[2,9,1024]{2,0,1:T(2,128)} %param.13) | copy-start | bytes 221188
  45.9 9.5 %copy-start.3 = (f32[2,3,1024]{2,0,1:T(2,128)S(1)}, f32[2,3,1024]{2,0,1:T(2,128)}, u32[]{:S(2)}) copy-start(f32[2,3,1024]{2,0,1:T(2,128)} %param.11) | copy-start | bytes 73732
  45.9 5.5 %collective-permute-start.4 = (f32[88,128]{1,0:T(8,128)S(1)}, f32[88,128]{1,0:T(8,128)S(1)}, u32[]{:S(2)}, u32[]{:S(2)}) collective-permute-start(f32[88,128]{1,0:T(8,128)S(1)} %get-tuple-element.61), channel_id=1, source_target_pairs={{0,128},{128,256},{256,384},{1,129},{129,257},{257,385},{2,130},{1... | collective-permute-start | bytes 135176 | tf_op jit(solution)/shard_map/ppermute | solution.py:663
  49.4 5.9 %collective-permute-start.5 = (f32[88,128]{1,0:T(8,128)S(1)}, f32[88,128]{1,0:T(8,128)S(1)}, u32[]{:S(2)}, u32[]{:S(2)}) collective-permute-start(f32[88,128]{1,0:T(8,128)S(1)} %get-tuple-element.62), channel_id=1, source_target_pairs={{128,0},{256,128},{384,256},{129,1},{257,129},{385,257},{130,2},{2... | collective-permute-start | bytes 135176 | tf_op jit(solution)/shard_map/ppermute | solution.py:664
  51.3 4.0 %copy-start.5 = (s32[2,1024]{1,0:T(2,128)S(1)}, s32[2,1024]{1,0:T(2,128)}, u32[]{:S(2)}) copy-start(s32[2,1024]{1,0:T(2,128)} %centers.11) | copy-start | bytes 24580
  57.5 5.0 %collective-permute-start.6 = (f32[21,384]{1,0:T(8,128)S(1)}, f32[21,384]{1,0:T(8,128)S(1)}, u32[]{:S(2)}, u32[]{:S(2)}) collective-permute-start(f32[21,384]{1,0:T(8,128)S(1)} %get-tuple-element.69), channel_id=1, source_target_pairs={{0,128},{128,256},{256,384},{1,129},{129,257},{257,385},{2,130},{1... | collective-permute-start | bytes 96776 | tf_op jit(solution)/shard_map/ppermute | solution.py:663
  60.9 5.9 %collective-permute-start.7 = (f32[21,384]{1,0:T(8,128)S(1)}, f32[21,384]{1,0:T(8,128)S(1)}, u32[]{:S(2)}, u32[]{:S(2)}) collective-permute-start(f32[21,384]{1,0:T(8,128)S(1)} %get-tuple-element.70), channel_id=1, source_target_pairs={{128,0},{256,128},{384,256},{129,1},{257,129},{385,257},{130,2},{2... | collective-permute-start | bytes 96776 | tf_op jit(solution)/shard_map/ppermute | solution.py:664
  67.3 6.1 %collective-permute-start.8 = (f32[21,384]{1,0:T(8,128)S(1)}, f32[21,384]{1,0:T(8,128)S(1)}, u32[]{:S(2)}, u32[]{:S(2)}) collective-permute-start(f32[21,384]{1,0:T(8,128)S(1)} %get-tuple-element.71), channel_id=1, source_target_pairs={{0,8},{8,0},{16,24},{24,16},{32,40},{40,32},{48,56},{56,48},{64,72... | collective-permute-start | bytes 96776 | tf_op jit(solution)/shard_map/ppermute | solution.py:672
  69.2 5.3 %collective-permute-start.9 = (f32[21,384]{1,0:T(8,128)S(1)}, f32[21,384]{1,0:T(8,128)S(1)}, u32[]{:S(2)}, u32[]{:S(2)}) collective-permute-start(f32[21,384]{1,0:T(8,128)S(1)} %get-tuple-element.72), channel_id=1, source_target_pairs={{8,16},{16,8},{24,32},{32,24},{40,48},{48,40},{56,64},{64,56},{72,... | collective-permute-start | bytes 96776 | tf_op jit(solution)/shard_map/ppermute | solution.py:673
  72.3 0.7 copy-start.13
  74.5 28.8 %copy-start.7 = (f32[2,9,1024]{2,0,1:T(2,128)S(1)}, f32[2,9,1024]{2,0,1:T(2,128)}, u32[]{:S(2)}) copy-start(f32[2,9,1024]{2,0,1:T(2,128)} %param.14) | copy-start | bytes 221188
  77.6 25.7 %collective-permute-start.10 = (f32[24,384]{1,0:T(8,128)S(1)}, f32[24,384]{1,0:T(8,128)S(1)}, u32[]{:S(2)}, u32[]{:S(2)}) collective-permute-start(f32[24,384]{1,0:T(8,128)S(1)} %get-tuple-element.80), channel_id=1, source_target_pairs={{0,1},{1,2},{2,3},{3,4},{4,5},{5,6},{6,7},{8,9},{9,10},{10,11},{11... | collective-permute-start | bytes 110600 | tf_op jit(solution)/shard_map/ppermute | solution.py:663
  80.8 22.5 %collective-permute-start.11 = (f32[24,384]{1,0:T(8,128)S(1)}, f32[24,384]{1,0:T(8,128)S(1)}, u32[]{:S(2)}, u32[]{:S(2)}) collective-permute-start(f32[24,384]{1,0:T(8,128)S(1)} %get-tuple-element.81), channel_id=1, source_target_pairs={{1,0},{2,1},{3,2},{4,3},{5,4},{6,5},{7,6},{9,8},{10,9},{11,10},{12... | collective-permute-start | bytes 110600 | tf_op jit(solution)/shard_map/ppermute | solution.py:664
  82.1 17.0 %collective-permute-start.12 = (f32[2,256]{1,0:T(2,128)S(1)}, f32[2,256]{1,0:T(2,128)S(1)}, u32[]{:S(2)}, u32[]{:S(2)}) collective-permute-start(f32[2,256]{1,0:T(2,128)S(1)} %get-tuple-element.82), channel_id=1, source_target_pairs={{0,2},{1,3},{2,4},{3,5},{4,6},{5,7},{8,10},{9,11},{10,12},{11,13},... | collective-permute-start | bytes 6152 | tf_op jit(solution)/shard_map/ppermute | solution.py:663
  97.8 5.5 %collective-permute-start.13 = (f32[2,256]{1,0:T(2,128)S(1)}, f32[2,256]{1,0:T(2,128)S(1)}, u32[]{:S(2)}, u32[]{:S(2)}) collective-permute-start(f32[2,256]{1,0:T(2,128)S(1)} %get-tuple-element.83), channel_id=1, source_target_pairs={{2,0},{3,1},{4,2},{5,3},{6,4},{7,5},{10,8},{11,9},{12,10},{13,11},... | collective-permute-start | bytes 6152 | tf_op jit(solution)/shard_map/ppermute | solution.py:664
  105.8 3.9 %collective-permute-start.14 = (f32[48,128]{1,0:T(8,128)S(1)}, f32[48,128]{1,0:T(8,128)S(1)}, u32[]{:S(2)}, u32[]{:S(2)}) collective-permute-start(f32[48,128]{1,0:T(8,128)S(1)} %get-tuple-element.88), channel_id=1, source_target_pairs={{0,8},{8,0},{16,24},{24,16},{32,40},{40,32},{48,56},{56,48},{64,72... | collective-permute-start | bytes 73736 | tf_op jit(solution)/shard_map/ppermute | solution.py:672
  107.8 5.1 %collective-permute-start.15 = (f32[48,128]{1,0:T(8,128)S(1)}, f32[48,128]{1,0:T(8,128)S(1)}, u32[]{:S(2)}, u32[]{:S(2)}) collective-permute-start(f32[48,128]{1,0:T(8,128)S(1)} %get-tuple-element.89), channel_id=1, source_target_pairs={{8,16},{16,8},{24,32},{32,24},{40,48},{48,40},{56,64},{64,56},{72,... | collective-permute-start | bytes 73736 | tf_op jit(solution)/shard_map/ppermute | solution.py:673
  113.5 4.6 %collective-permute-start.16 = (f32[56,128]{1,0:T(8,128)S(1)}, f32[56,128]{1,0:T(8,128)S(1)}, u32[]{:S(2)}, u32[]{:S(2)}) collective-permute-start(f32[56,128]{1,0:T(8,128)S(1)} %get-tuple-element.92), channel_id=1, source_target_pairs={{0,128},{128,256},{256,384},{1,129},{129,257},{257,385},{2,130},{1... | collective-permute-start | bytes 86024 | tf_op jit(solution)/shard_map/ppermute | solution.py:663
  116.7 5.8 %collective-permute-start.17 = (f32[56,128]{1,0:T(8,128)S(1)}, f32[56,128]{1,0:T(8,128)S(1)}, u32[]{:S(2)}, u32[]{:S(2)}) collective-permute-start(f32[56,128]{1,0:T(8,128)S(1)} %get-tuple-element.93), channel_id=1, source_target_pairs={{128,0},{256,128},{384,256},{129,1},{257,129},{385,257},{130,2},{2... | collective-permute-start | bytes 86024 | tf_op jit(solution)/shard_map/ppermute | solution.py:664

commit v4 on v3

--- a/solution.py
+++ b/solution.py
@@ -15,7 +15,7 @@
 I32 = jnp.int32
 AXES = ("gx", "gy", "gz")
 VMEM = pl.BlockSpec(memory_space=pltpu.VMEM)
-SMEM = pl.BlockSpec(memory_space=pltpu.SMEM)
+HBM = pl.BlockSpec(memory_space=pltpu.HBM)
 CHUNKS = 8
 ZROWS = 144
 
@@ -105,12 +105,17 @@
                 signed[rows, lanes] = jnp.where(is_low, -a[at], ends).astype(BF16)
 
 
-def lower_first(spot):
-    return spot[1] // 4 % 2 == 0
-
-
-def by_side(first, one, other):
-    return jnp.where(first, one, other)
+def row_of(info, i, rows=8):
+    return jnp.broadcast_to(info[i : i + 1, :], (rows, 128))
+
+
+def by_side(info, one, other):
+    return jnp.where(row_of(info, 3, one.shape[0]) == 0, one, other)
+
+
+def in_use(live, step):
+    slots = iota((8, 128), 0) * 128 + iota((8, 128), 1)
+    return (slots < jnp.broadcast_to(live[0:1, step : step + 1], (8, 128))).astype(F32)
 
 
 STEPS = (0, 1, -1)
@@ -141,7 +146,7 @@
                 if (x, y, z) != (0, 0, 0):
                     n, row, lane = offset_row((x, y, z)), (x + 1) * 3 + y + 1, (z + 1) * 32
                     pick[row : row + 1, lane : lane + 32] = jnp.where(
-                        order < counts[0, n], slots[n], -1
+                        order < jnp.broadcast_to(counts[0:1, n : n + 1], (1, 32)), slots[n], -1
                     )
 
 
@@ -225,11 +230,30 @@
 
 
 def first_kernel(
-    live, adjoint, fractions, centers, deform, affine, mass, slots_back,
+    live_at, adjoint_at, fractions_at, centers_at, deform_at, affine_at, mass_at, slots_at,
     h, hb, zu, zd, bf_out, w_hi, w_lo, d_hi, d_lo, send,
     l0h, l0l, l2h, l2l, table, hot,
+    live, adjoint, fractions, centers, deform, affine, mass, slots_back, arrived,
 ):
+    sources = (slots_at, fractions_at, centers_at, deform_at, live_at, adjoint_at, affine_at, mass_at)
+    places = (slots_back, fractions, centers, deform, live, adjoint, affine, mass)
+    copies = [
+        pltpu.make_async_copy(a, b, arrived.at[i]) for i, (a, b) in enumerate(zip(sources, places))
+    ]
+    for copy in copies:
+        copy.start()
+    w = (w_hi, w_lo, d_hi, d_lo)
+    l = (l0h, l0l, l2h, l2l)
+    for copy in copies[:3]:
+        copy.wait()
     fill_send(slots_back, send)
+    which = 1
+    frac = dense(fractions, which, 3)
+    centre = centers[which : which + 1, :].reshape(CHUNKS, 128)
+    cell_x, cell_y, cell_z = cells_of(centre)
+    build_z(frac[2], cell_z, *w)
+    for copy in copies[3:]:
+        copy.wait()
     table[104:112] = jnp.zeros((8, 128), F32)
     early = dense(fractions, 0, 3) + [centers[0:1, :].reshape(CHUNKS, 128).astype(F32)]
     for i, tile in enumerate(early + dense(deform, 0, 9)):
@@ -238,16 +262,8 @@
     zd[...] = jnp.zeros(zd.shape, F32)
     static_rows(table, send, 2, hot, zd)
     static_rows(table, send, 5, hot, zu)
-    which = 1
-    slots = iota((8, 128), 0) * 128 + iota((8, 128), 1)
-    use = (slots < live[0, which]).astype(F32)
+    use = in_use(live, which)
     adj = [v * use for v in dense(adjoint, None, 21)]
-    frac = dense(fractions, which, 3)
-    centre = centers[which : which + 1, :].reshape(CHUNKS, 128)
-    cell_x, cell_y, cell_z = cells_of(centre)
-    w = (w_hi, w_lo, d_hi, d_lo)
-    l = (l0h, l0l, l2h, l2l)
-    build_z(frac[2], cell_z, *w)
     a_v, b_c, b_f = transfer(adj, dense(deform, which, 9), dense(affine, which, 9))
     for i in range(9):
         bf_out[i] = b_f[i]
@@ -286,7 +302,7 @@
 
 def z_kernel(comps, spot, h, hb, from_low, from_high, h_out, hb_out, ya, yb):
     low, high = from_low[13:15, 0:256], from_high[13:15, 0:256]
-    z_fold(comps, lower_first(spot), h, hb[...], low, high, h_out, hb_out, ya, yb)
+    z_fold(comps, spot, h, hb[...], low, high, h_out, hb_out, ya, yb)
 
 
 def z_fold(comps, first, h, halo, low, high, h_out, hb_out, ya, yb):
@@ -323,7 +339,7 @@
 
 
 def y_kernel(comps, spot, h, hb, ra, rb, h_out, hb_out, xu, xd):
-    first = lower_first(spot)
+    first = spot
     row = iota((8, 128), 0)
     blocks = comps * 6
     packed = (blocks + 3) // 4 * 8
@@ -368,7 +384,8 @@
 
 
 def node_values(spot, extents, total, halo, mass_at, mass_halo, g_hi, g_lo):
-    first_x, first_y, first_z = spot[0], spot[1], spot[2]
+    first_x, first_y, first_z = (row_of(spot, i) for i in range(3))
+    far_x, far_y, far_z = (jnp.concatenate([v, v], axis=1) for v in (first_x, first_y, first_z))
     lane, row = iota((8, 128), 1), iota((8, 128), 0)
     node_z = first_z + lane
     node_y = first_y + row - 1
@@ -377,9 +394,9 @@
     )
     wide = iota((8, 256), 1)
     side = iota((8, 256), 0)
-    halo_x = first_x + wide % 48 // 8 - 1
-    halo_y = first_y + wide % 8 - 1
-    halo_z = first_z + jnp.where(side == 0, 128, -1)
+    halo_x = far_x + wide % 48 // 8 - 1
+    halo_y = far_y + wide % 8 - 1
+    halo_z = far_z + jnp.where(side == 0, 128, -1)
     keep = (
         (halo_x >= 1) & (halo_x <= extents[0] - 2)
         & (halo_y >= 1) & (halo_y <= extents[1] - 2)
@@ -466,8 +483,7 @@
     frac = dense(fractions, which, 3)
     cell_x, cell_y, _ = cells_of(centers[which : which + 1, :].reshape(CHUNKS, 128))
     gather(frac, cell_x, cell_y, g_hi, g_lo, w_hi, w_lo, d_hi, d_lo, s0, sz, rows12)
-    slots = iota((8, 128), 0) * 128 + iota((8, 128), 1)
-    use = (slots < live[0, which]).astype(F32)
+    use = in_use(live, which)
     out = particle(rows12, frac, [bf[i] for i in range(9)], dense(deform, which, 9), use)
     for i in range(21):
         second[i] = out[i]
@@ -502,7 +518,7 @@
 
 
 def route_y_kernel(spot, mid, from_low, from_high, ya, yb):
-    first = lower_first(spot)
+    first = spot
     for i, ref in enumerate((mid, from_low, from_high)):
         down, up = lane_tile(ref, 0), lane_tile(ref, 2)
         ya[:, i * 128 : i * 128 + 128] = by_side(first, up, down)
@@ -544,7 +560,7 @@
     lh, ll, hot, l0h, l0l, l2h, l2l, moved, static, e0, e1, e2, e3,
 ):
     groups = [lane_tile(mid, 1), lane_tile(x_low, 1), lane_tile(x_high, 1)]
-    first = lower_first(spot)
+    first = spot
     groups += [by_side(first, lane_tile(rb, i), lane_tile(ra, i)) for i in range(3)]
     groups += [by_side(first, lane_tile(ra, i), lane_tile(rb, i)) for i in range(3)]
     final = pieces(groups[1:], 32, 2)
@@ -576,8 +592,7 @@
 
     tiles = [lambda r, t=t: final[t][r : r + 1] for t in range(2)]
     total = carry(tiles, [send[t : t + 1] for t in range(2)], lh, ll, hot)
-    slots = iota((8, 128), 0) * 128 + iota((8, 128), 1)
-    use = (slots < live[0, 0]).astype(F32)
+    use = in_use(live, 0)
     adj = [(stayed[i] + total[i * 8 : i * 8 + 8]) * use for i in range(21)]
     for i in range(21):
         carried[i] = adj[i]
@@ -599,8 +614,7 @@
     tiles = [lambda r, t=t: z_low[r : r + 1, t * 128 : t * 128 + 128] for t in range(3)]
     tiles += [lambda r, t=t: z_high[r : r + 1, t * 128 : t * 128 + 128] for t in range(3)]
     total = carry(tiles, [send[t : t + 1] for t in range(2, 8)], lh, ll, hot)
-    slots = iota((8, 128), 0) * 128 + iota((8, 128), 1)
-    use = (slots < live[0, 0]).astype(F32)
+    use = in_use(live, 0)
     adj = [(carried[i] + total[i * 8 : i * 8 + 8]) * use for i in range(21)]
     frac = dense(fractions, 0, 3)
     cell_x, cell_y, _ = cells_of(centers[0:1, :].reshape(CHUNKS, 128))
@@ -615,7 +629,7 @@
     halo = jnp.where(iota((8, 256), 0) < 2, ends, 0.0)
     low = z_low[21:23, 0:256] + low2[0:2] + own_low[0:2]
     high = z_high[21:23, 0:256] + high2[0:2] + own_high[0:2]
-    z_fold(3, lower_first(spot), h, halo, low, high, h_out, hb_out, ya, yb)
+    z_fold(3, spot, h, halo, low, high, h_out, hb_out, ya, yb)
 
 
 def gather_second_kernel(
@@ -633,8 +647,7 @@
     frac = dense(fractions, which, 3)
     cell_x, cell_y, _ = cells_of(centers[which : which + 1, :].reshape(CHUNKS, 128))
     gather(frac, cell_x, cell_y, g_hi, g_lo, w_hi, w_lo, d_hi, d_lo, s0, sz, rows12)
-    slots = iota((8, 128), 0) * 128 + iota((8, 128), 1)
-    use = (slots < live[0, which]).astype(F32)
+    use = in_use(live, which)
     out = particle(rows12, frac, [bf[i] for i in range(9)], dense(deform, which, 9), use)
     for i in range(21):
         packed[i] = out[i]
@@ -653,7 +666,7 @@
         in_specs=list(specs),
         out_specs=[VMEM] * len(outs),
         out_shape=list(outs),
-        scratch_shapes=[pltpu.VMEM(s, d) for s, d in scratch],
+        scratch_shapes=[pltpu.VMEM(*v) if isinstance(v, tuple) else v for v in scratch],
         compiler_params=pltpu.CompilerParams(vmem_limit_bytes=40 * 1024 * 1024),
     )
 
@@ -678,8 +691,10 @@
     fractions, centers, deform, next_affine, cell_mass, final_adjoint,
     live_count, send_slot, receive_slot, receive_count, prior_slot,
 ):
-    spot = jnp.stack([lax.axis_index("gx") * 4, lax.axis_index("gy") * 4, lax.axis_index("gz") * 128])
-    spot = spot.astype(I32)
+    at_y = lax.axis_index("gy")
+    spot = [lax.axis_index("gx") * 4, at_y * 4, lax.axis_index("gz") * 128, at_y % 2]
+    spot = jnp.stack(spot + [jnp.zeros_like(at_y)] * 4).astype(I32)
+    spot = jnp.broadcast_to(spot[:, None], (8, 128))
     extents = (lax.axis_size("gx") * 4, lax.axis_size("gy") * 4, lax.axis_size("gz") * 128)
 
     fractions, deform, next_affine = (
@@ -701,30 +716,34 @@
         ra, rb = both_pairs(ya, yb, "gy")
         rows = comps * 16 + 8
         h, hb, xu, xd = call(
-            functools.partial(y_kernel, comps), f"fold_y{comps}", [SMEM] + [VMEM] * 4,
+            functools.partial(y_kernel, comps), f"fold_y{comps}", [VMEM] + [VMEM] * 4,
             [shape(comps * 48, 128), shape(8, 256), shape(rows, 128), shape(rows, 128)],
         )(spot, h, hb, ra, rb)
         low, high = both_ways(xu, xd, "gx")
         return h, hb, low, high
 
+    firsts = (
+        live_count, final_adjoint, fractions, centers, deform, next_affine, cell_mass, slots_back
+    )
     h, hb, zu, zd, bf, *w, send = call(
-        first_kernel, "scatter_first", [SMEM] + [VMEM] * 7,
+        first_kernel, "scatter_first", [HBM] * 8,
         [shape(240, 128), shape(8, 256), shape(16, 384), shape(16, 384), shape(9, 8, 128)]
         + weights + [shape(8, 128, dtype=I32)],
-        lrows + [((112, 128), F32), ((128, 128), BF16)],
-    )(live_count, final_adjoint, fractions, centers, deform, next_affine, cell_mass, slots_back)
+        lrows + [((112, 128), F32), ((128, 128), BF16)]
+        + [(v.shape, v.dtype) for v in firsts] + [pltpu.SemaphoreType.DMA((8,))],
+    )(*(pltpu.with_memory_space_constraint(v, pltpu.HBM) for v in firsts))
     static_low, static_high = both_ways(zu, zd, "gz")
-    (pick,) = call(pick_kernel, "fill_pick", [SMEM, VMEM], [shape(9, 128, dtype=I32)])(
+    (pick,) = call(pick_kernel, "fill_pick", [VMEM, VMEM], [shape(9, 128, dtype=I32)])(
         receive_count, slots_out
     )
     h, hb, ya, yb = call(
-        functools.partial(z_kernel, 5), "fold_z5", [SMEM] + [VMEM] * 4,
+        functools.partial(z_kernel, 5), "fold_z5", [VMEM] + [VMEM] * 4,
         [shape(240, 128), shape(8, 256), shape(72, 128), shape(72, 128)],
     )(spot, h, hb, static_low, static_high)
     h, hb, low, high = fold(5, h, hb, ya, yb)
     second, xu, xd, mid, mass_core, mass_halo = call(
         functools.partial(gather_first_kernel, extents), "gather_first",
-        [SMEM, SMEM] + [VMEM] * 13,
+        [VMEM, VMEM] + [VMEM] * 13,
         [shape(21, 8, 128), shape(21, 384), shape(21, 384), shape(21, 384), shape(48, 128), shape(8, 256)],
         [((240, 128), F32)] + gscratch + [((176, 128), F32), ((128, 128), BF16)],
     )(live_count, spot, h, hb, low, high, fractions, centers, deform, bf, *w, pick)
@@ -735,12 +754,12 @@
         stay_kernel, "stay", [VMEM] * 2, [shape(21, 8, 128)],
         [((176, 1024), BF16)] * 2 + [((128, 1024), BF16)],
     )(second, prior)
-    ya, yb = call(route_y_kernel, "route_y", [SMEM] + [VMEM] * 3, [shape(21, 384)] * 2)(
+    ya, yb = call(route_y_kernel, "route_y", [VMEM] + [VMEM] * 3, [shape(21, 384)] * 2)(
         spot, mid, x_low, x_high
     )
     ra, rb = both_pairs(ya, yb, "gy")
     zu, zd, up2, dn2, own_low, own_high, carried = call(
-        near_kernel, "scatter_near", [SMEM] * 2 + [VMEM] * 16,
+        near_kernel, "scatter_near", [VMEM] * 2 + [VMEM] * 16,
         [shape(24, 384)] * 2 + [shape(2, 256)] * 4 + [shape(21, 8, 128)],
         [((176, 256), BF16)] * 2 + [((128, 256), BF16)] + lrows
         + [((21, 8, 128), F32), ((14, 8, 128), F32)] + [((16, 768), BF16)] * 4,
@@ -751,7 +770,7 @@
     z_low, z_high = both_ways(zu, zd, "gz")
     low2, high2 = both_ways(up2, dn2, "gz", 2)
     h, hb, ya, yb, bf = call(
-        second_kernel, "scatter_second", [SMEM] * 2 + [VMEM] * 16,
+        second_kernel, "scatter_second", [VMEM] * 2 + [VMEM] * 16,
         [shape(144, 128), shape(8, 256), shape(48, 128), shape(48, 128), shape(9, 8, 128)],
         [((176, 768), BF16)] * 2 + [((128, 768), BF16)] + lrows + [((144, 128), F32)],
     )(
@@ -761,7 +780,7 @@
     h, hb, low, high = fold(3, h, hb, ya, yb)
     (result,) = call(
         functools.partial(gather_second_kernel, extents), "gather_second",
-        [SMEM, SMEM] + [VMEM] * 14,
+        [VMEM, VMEM] + [VMEM] * 14,
         [shape(21, 1024)],
         [((144, 128), F32)] + gscratch + [((21, 8, 128), F32)],
     )(live_count, spot, h, hb, low, high, fractions, centers, deform, bf, *w, mass_core, mass_halo)

time: 126 us -> 116 us (0.921)
  local copies, waits for them, and re-layouts: 6.33 us -> 0.96 us
  Pallas kernels: 16.8 us -> 12.6 us
    unnamed x30 -> x16, local copies, waits for them, and re-layouts: 6.33 us -> 0.8 us
    pallas_call x9, Pallas kernels: 13.6 us -> 9.97 us  [the longest x1 3.25 us: body(): call(first_kernel, 'scatter_first', [HBM] * 8, [shape(240, 128), shape(8,...]
  transfers between devices with their start and end apart: 18 -> 18, of which waited for: 11 -> 12; matrix products, arithmetic and copies ran while one was open for 0% -> 0% of each run, Pallas kernels for 1% -> 1%
where the time goes in v4:
time: 116 us; the launch traced here: 115 us
  starting transfers between devices  64.4 us (56%)
  waiting for transfers between devices  37.2 us (32%)
  Pallas kernels  12.6 us (11%)
    ppermute x6, starting transfers between devices, both_ways(): low = lax.ppermute(up, axis, [(i, i + step) for i in range(count - step)])  42.9 us
    ppermute x6, waiting for transfers between devices, both_ways(): lax.ppermute(down, axis, [(i + step, i) for i in range(count - step)])  29.5 us
    ppermute x3, starting transfers between devices, both_pairs(): rb = lax.ppermute(second, axis, b) if b else jnp.zeros_like(second)  7.96 us
    ppermute x6, starting transfers between devices, both_ways(): lax.ppermute(down, axis, [(i + step, i) for i in range(count - step)])  7.75 us
    ppermute x3, waiting for transfers between devices, both_pairs(): rb = lax.ppermute(second, axis, b) if b else jnp.zeros_like(second)  6.51 us
    ppermute x3, starting transfers between devices, both_pairs(): ra = lax.ppermute(first, axis, a)  5.78 us
    pallas_call x1, Pallas kernels, body(): call(first_kernel, 'scatter_first', [HBM] * 8, [shape(240, 128), shape(8,...  3.25 us
    pallas_call x1, Pallas kernels, body(): call(near_kernel, 'scatter_near', [VMEM] * 2 + [VMEM] * 16, [shape(24, 38...  2.55 us
  transfers between devices with their start and end apart: 18, of which 12 were waited for; matrix products, arithmetic and copies ran while one was open for 0% of the time, Pallas kernels for 1%

profile of v4, /device:TPU:64, one launch (start us, length us, event | category | flops | bytes accessed | tf_op | source)
XLA Modules:
  0.0 115.4 jit_solution(7517529170119352254)
XLA Ops:
  0.0 3.2 %scatter_first.1 = (f32[240,128]{1,0:T(8,128)S(1)}, f32[8,256]{1,0:T(8,128)S(1)}, f32[16,384]{1,0:T(8,128)S(1)}, f32[16,384]{1,0:T(8,128)S(1)}, f32[9,8,128]{2,1...) custom-call(s32[1,2]{1,0:T(1,128)} %live.7, ...), custom_call_target="tpu_custom_call" | custom-call | tf_op jit(solution)/shard_map/scatter_first/pallas_call | solution.py:728
  3.3 13.9 %collective-permute-start = (f32[16,384]{1,0:T(8,128)S(1)}, f32[16,384]{1,0:T(8,128)S(1)}, u32[]{:S(2)}, u32[]{:S(2)}) collective-permute-start(f32[16,384]{1,0:T(8,128)S(1)} %get-tuple-element.53), channel_id=1, source_target_pairs={{0,1},{1,2},{2,3},{3,4},{4,5},{5,6},{6,7},{8,9},{9,10},{10,11},{11... | collective-permute-start | bytes 73736 | tf_op jit(solution)/shard_map/ppermute | solution.py:676
  17.2 1.3 %collective-permute-start.1 = (f32[16,384]{1,0:T(8,128)S(1)}, f32[16,384]{1,0:T(8,128)S(1)}, u32[]{:S(2)}, u32[]{:S(2)}) collective-permute-start(f32[16,384]{1,0:T(8,128)S(1)} %get-tuple-element.54), channel_id=1, source_target_pairs={{1,0},{2,1},{3,2},{4,3},{5,4},{6,5},{7,6},{9,8},{10,9},{11,10},{12... | collective-permute-start | bytes 73736 | tf_op jit(solution)/shard_map/ppermute | solution.py:677
  18.5 0.1 stack.19
  18.6 0.4 collective-permute-done.from_low.static_low
  19.0 12.6 %collective-permute-done.1.from_high.static_high = f32[16,384]{1,0:T(8,128)S(1)} collective-permute-done((f32[16,384]{1,0:T(8,128)S(1)}, f32[16,384]{1,0:T(8,128)S(1)}, u32[]{:S(2)}, u32[]{:S(2)}) %collective-permute-start.1) | collective-permute-done | bytes 24608 | tf_op jit(solution)/shard_map/ppermute | solution.py:677
  31.6 0.1 broadcast_in_dim.2.spot
  31.7 0.3 fold_z5.1
  32.0 1.9 %collective-permute-start.2 = (f32[72,128]{1,0:T(8,128)S(1)}, f32[72,128]{1,0:T(8,128)S(1)}, u32[]{:S(2)}, u32[]{:S(2)}) collective-permute-start(f32[72,128]{1,0:T(8,128)S(1)} %get-tuple-element.57), channel_id=1, source_target_pairs={{0,8},{8,0},{16,24},{24,16},{32,40},{40,32},{48,56},{56,48},{64,72... | collective-permute-start | bytes 110600 | tf_op jit(solution)/shard_map/ppermute | solution.py:685
  34.0 3.0 %collective-permute-start.3 = (f32[72,128]{1,0:T(8,128)S(1)}, f32[72,128]{1,0:T(8,128)S(1)}, u32[]{:S(2)}, u32[]{:S(2)}) collective-permute-start(f32[72,128]{1,0:T(8,128)S(1)} %get-tuple-element.58), channel_id=1, source_target_pairs={{8,16},{16,8},{24,32},{32,24},{40,48},{48,40},{56,64},{64,56},{72,... | collective-permute-start | bytes 110600 | tf_op jit(solution)/shard_map/ppermute | solution.py:686
  37.0 2.2 %collective-permute-done.3.rb = f32[72,128]{1,0:T(8,128)S(1)} collective-permute-done((f32[72,128]{1,0:T(8,128)S(1)}, f32[72,128]{1,0:T(8,128)S(1)}, u32[]{:S(2)}, u32[]{:S(2)}) %collective-permute-start.3) | collective-permute-done | bytes 36896 | tf_op jit(solution)/shard_map/ppermute | solution.py:686
  39.2 0.1 fold_y5.1
  39.3 3.5 %collective-permute-start.4 = (f32[88,128]{1,0:T(8,128)S(1)}, f32[88,128]{1,0:T(8,128)S(1)}, u32[]{:S(2)}, u32[]{:S(2)}) collective-permute-start(f32[88,128]{1,0:T(8,128)S(1)} %get-tuple-element.61), channel_id=1, source_target_pairs={{0,128},{128,256},{256,384},{1,129},{129,257},{257,385},{2,130},{1... | collective-permute-start | bytes 135176 | tf_op jit(solution)/shard_map/ppermute | solution.py:676
  42.9 1.3 %collective-permute-start.5 = (f32[88,128]{1,0:T(8,128)S(1)}, f32[88,128]{1,0:T(8,128)S(1)}, u32[]{:S(2)}, u32[]{:S(2)}) collective-permute-start(f32[88,128]{1,0:T(8,128)S(1)} %get-tuple-element.62), channel_id=1, source_target_pairs={{128,0},{256,128},{384,256},{129,1},{257,129},{385,257},{130,2},{2... | collective-permute-start | bytes 135176 | tf_op jit(solution)/shard_map/ppermute | solution.py:677
  44.2 0.2 fill_pick.1.pick
  44.3 0.0 copy-start.2
  44.3 0.2 collective-permute-done.4.from_low
  44.5 4.2 %collective-permute-done.5.from_high = f32[88,128]{1,0:T(8,128)S(1)} collective-permute-done((f32[88,128]{1,0:T(8,128)S(1)}, f32[88,128]{1,0:T(8,128)S(1)}, u32[]{:S(2)}, u32[]{:S(2)}) %collective-permute-start.5) | collective-permute-done | bytes 45088 | tf_op jit(solution)/shard_map/ppermute | solution.py:677
  48.8 0.6 copy-done.5
  49.5 1.6 %gather_first.1 = (f32[21,8,128]{2,1,0:T(8,128)S(1)}, f32[21,384]{1,0:T(8,128)S(1)}, f32[21,384]{1,0:T(8,128)S(1)}, f32[21,384]{1,0:T(8,128)S(1)}, f32[48,128]{1,0:T(8,128)S(1)}, /*index=5*/f32[8,256]{1,0:T(8,128)S(1)}) custom-call(s32[1,2]{1,0:T(1,128)S(1)} %copy-done.5, s32[8,128]{1,0:T(8,128)S(1)} %broadcast_in_dim.2.spot, ...), custom_call_target="tpu_custom_call" | custom-call | tf_op jit(solution)/shard_map/gather_first/pallas_call | solution.py:744
  51.0 3.4 %collective-permute-start.6 = (f32[21,384]{1,0:T(8,128)S(1)}, f32[21,384]{1,0:T(8,128)S(1)}, u32[]{:S(2)}, u32[]{:S(2)}) collective-permute-start(f32[21,384]{1,0:T(8,128)S(1)} %get-tuple-element.69), channel_id=1, source_target_pairs={{0,128},{128,256},{256,384},{1,129},{129,257},{257,385},{2,130},{1... | collective-permute-start | bytes 96776 | tf_op jit(solution)/shard_map/ppermute | solution.py:676
  54.4 1.3 %collective-permute-start.7 = (f32[21,384]{1,0:T(8,128)S(1)}, f32[21,384]{1,0:T(8,128)S(1)}, u32[]{:S(2)}, u32[]{:S(2)}) collective-permute-start(f32[21,384]{1,0:T(8,128)S(1)} %get-tuple-element.70), channel_id=1, source_target_pairs={{128,0},{256,128},{384,256},{129,1},{257,129},{385,257},{130,2},{2... | collective-permute-start | bytes 96776 | tf_op jit(solution)/shard_map/ppermute | solution.py:677
  55.7 0.3 collective-permute-done.6.from_low.x_low
  56.1 4.2 %collective-permute-done.7.from_high.x_high = f32[21,384]{1,0:T(8,128)S(1)} collective-permute-done((f32[21,384]{1,0:T(8,128)S(1)}, f32[21,384]{1,0:T(8,128)S(1)}, u32[]{:S(2)}, u32[]{:S(2)}) %collective-permute-start.7) | collective-permute-done | bytes 32288 | tf_op jit(solution)/shard_map/ppermute | solution.py:677
  60.3 1.9 %collective-permute-start.8 = (f32[21,384]{1,0:T(8,128)S(1)}, f32[21,384]{1,0:T(8,128)S(1)}, u32[]{:S(2)}, u32[]{:S(2)}) collective-permute-start(f32[21,384]{1,0:T(8,128)S(1)} %get-tuple-element.71), channel_id=1, source_target_pairs={{0,8},{8,0},{16,24},{24,16},{32,40},{40,32},{48,56},{56,48},{64,72... | collective-permute-start | bytes 96776 | tf_op jit(solution)/shard_map/ppermute | solution.py:685
  62.2 3.0 %collective-permute-start.9 = (f32[21,384]{1,0:T(8,128)S(1)}, f32[21,384]{1,0:T(8,128)S(1)}, u32[]{:S(2)}, u32[]{:S(2)}) collective-permute-start(f32[21,384]{1,0:T(8,128)S(1)} %get-tuple-element.72), channel_id=1, source_target_pairs={{8,16},{16,8},{24,32},{32,24},{40,48},{48,40},{56,64},{64,56},{72,... | collective-permute-start | bytes 96776 | tf_op jit(solution)/shard_map/ppermute | solution.py:686
  65.3 0.0 copy-start.6
  65.3 0.5 weights_second.1
  65.8 0.1 copy-done.6
  66.0 0.5 stay.1.stayed
  66.4 0.0 collective-permute-done.8.ra
  66.5 1.1 collective-permute-done.9.rb
  67.5 2.5 %scatter_near.1 = (f32[24,384]{1,0:T(8,128)S(1)}, f32[24,384]{1,0:T(8,128)S(1)}, f32[2,256]{1,0:T(2,128)S(1)}, f32[2,256]{1,0:T(2,128)S(1)}, f32[2,256]{1,0:T(2,...) custom-call(s32[1,2]{1,0:T(1,128)S(1)} %copy-done.5, s32[8,128]{1,0:T(8,128)S(1)} %broadcast_in_dim.2.spot, ...), custom_call_target="tpu_custom_call" | custom-call | tf_op jit(solution)/shard_map/scatter_near/pallas_call | solution.py:761
  70.1 3.2 %collective-permute-start.10 = (f32[24,384]{1,0:T(8,128)S(1)}, f32[24,384]{1,0:T(8,128)S(1)}, u32[]{:S(2)}, u32[]{:S(2)}) collective-permute-start(f32[24,384]{1,0:T(8,128)S(1)} %get-tuple-element.80), channel_id=1, source_target_pairs={{0,1},{1,2},{2,3},{3,4},{4,5},{5,6},{6,7},{8,9},{9,10},{10,11},{11... | collective-permute-start | bytes 110600 | tf_op jit(solution)/shard_map/ppermute | solution.py:676
  73.2 1.3 %collective-permute-start.11 = (f32[24,384]{1,0:T(8,128)S(1)}, f32[24,384]{1,0:T(8,128)S(1)}, u32[]{:S(2)}, u32[]{:S(2)}) collective-permute-start(f32[24,384]{1,0:T(8,128)S(1)} %get-tuple-element.81), channel_id=1, source_target_pairs={{1,0},{2,1},{3,2},{4,3},{5,4},{6,5},{7,6},{9,8},{10,9},{11,10},{12... | collective-permute-start | bytes 110600 | tf_op jit(solution)/shard_map/ppermute | solution.py:677
  74.5 15.7 %collective-permute-start.12 = (f32[2,256]{1,0:T(2,128)S(1)}, f32[2,256]{1,0:T(2,128)S(1)}, u32[]{:S(2)}, u32[]{:S(2)}) collective-permute-start(f32[2,256]{1,0:T(2,128)S(1)} %get-tuple-element.82), channel_id=1, source_target_pairs={{0,2},{1,3},{2,4},{3,5},{4,6},{5,7},{8,10},{9,11},{10,12},{11,13},... | collective-permute-start | bytes 6152 | tf_op jit(solution)/shard_map/ppermute | solution.py:676
  90.3 1.3 %collective-permute-start.13 = (f32[2,256]{1,0:T(2,128)S(1)}, f32[2,256]{1,0:T(2,128)S(1)}, u32[]{:S(2)}, u32[]{:S(2)}) collective-permute-start(f32[2,256]{1,0:T(2,128)S(1)} %get-tuple-element.83), channel_id=1, source_target_pairs={{2,0},{3,1},{4,2},{5,3},{6,4},{7,5},{10,8},{11,9},{12,10},{13,11},... | collective-permute-start | bytes 6152 | tf_op jit(solution)/shard_map/ppermute | solution.py:677
  91.6 4.2 %collective-permute-done.13.high2 = f32[2,256]{1,0:T(2,128)S(1)} collective-permute-done((f32[2,256]{1,0:T(2,128)S(1)}, f32[2,256]{1,0:T(2,128)S(1)}, u32[]{:S(2)}, u32[]{:S(2)}) %collective-permute-start.13) | collective-permute-done | bytes 2080 | tf_op jit(solution)/shard_map/ppermute | solution.py:677
  95.8 2.0 %scatter_second.1 = (f32[144,128]{1,0:T(8,128)S(1)}, f32[8,256]{1,0:T(8,128)S(1)}, f32[48,128]{1,0:T(8,128)S(1)}, f32[48,128]{1,0:T(8,128)S(1)}, f32[9,8,128]{2,1,0:T(8,128)S(1)}) custom-call(s32[1,2]{1,0:T(1,128)S(1)} %copy-done.5, s32[8,128]{1,0:T(8,128)S(1)} %broadcast_in_dim.2.spot, f32[21,8,128]{2,1,0:T(8,128)S(1)} %get-tuple-element.79.carried, ...), custom_call_target="tpu_custom_call" | custom-call | tf_op jit(solution)/shard_map/scatter_second/pallas_call | solution.py:772
  97.7 1.9 %collective-permute-start.14 = (f32[48,128]{1,0:T(8,128)S(1)}, f32[48,128]{1,0:T(8,128)S(1)}, u32[]{:S(2)}, u32[]{:S(2)}) collective-permute-start(f32[48,128]{1,0:T(8,128)S(1)} %get-tuple-element.88), channel_id=1, source_target_pairs={{0,8},{8,0},{16,24},{24,16},{32,40},{40,32},{48,56},{56,48},{64,72... | collective-permute-start | bytes 73736 | tf_op jit(solution)/shard_map/ppermute | solution.py:685
  99.7 1.9 %collective-permute-start.15 = (f32[48,128]{1,0:T(8,128)S(1)}, f32[48,128]{1,0:T(8,128)S(1)}, u32[]{:S(2)}, u32[]{:S(2)}) collective-permute-start(f32[48,128]{1,0:T(8,128)S(1)} %get-tuple-element.89), channel_id=1, source_target_pairs={{8,16},{16,8},{24,32},{32,24},{40,48},{48,40},{56,64},{64,56},{72,... | collective-permute-start | bytes 73736 | tf_op jit(solution)/shard_map/ppermute | solution.py:686
  101.6 3.2 %collective-permute-done.15.rb = f32[48,128]{1,0:T(8,128)S(1)} collective-permute-done((f32[48,128]{1,0:T(8,128)S(1)}, f32[48,128]{1,0:T(8,128)S(1)}, u32[]{:S(2)}, u32[]{:S(2)}) %collective-permute-start.15) | collective-permute-done | bytes 24608 | tf_op jit(solution)/shard_map/ppermute | solution.py:686
  104.8 0.1 fold_y3.1
  104.9 3.1 %collective-permute-start.16 = (f32[56,128]{1,0:T(8,128)S(1)}, f32[56,128]{1,0:T(8,128)S(1)}, u32[]{:S(2)}, u32[]{:S(2)}) collective-permute-start(f32[56,128]{1,0:T(8,128)S(1)} %get-tuple-element.92), channel_id=1, source_target_pairs={{0,128},{128,256},{256,384},{1,129},{129,257},{257,385},{2,130},{1... | collective-permute-start | bytes 86024 | tf_op jit(solution)/shard_map/ppermute | solution.py:676
  108.0 1.3 %collective-permute-start.17 = (f32[56,128]{1,0:T(8,128)S(1)}, f32[56,128]{1,0:T(8,128)S(1)}, u32[]{:S(2)}, u32[]{:S(2)}) collective-permute-start(f32[56,128]{1,0:T(8,128)S(1)} %get-tuple-element.93), channel_id=1, source_target_pairs={{128,0},{256,128},{384,256},{129,1},{257,129},{385,257},{130,2},{2... | collective-permute-start | bytes 86024 | tf_op jit(solution)/shard_map/ppermute | solution.py:677
  109.3 0.2 collective-permute-done.16.from_low
  109.5 4.2 %collective-permute-done.17.from_high = f32[56,128]{1,0:T(8,128)S(1)} collective-permute-done((f32[56,128]{1,0:T(8,128)S(1)}, f32[56,128]{1,0:T(8,128)S(1)}, u32[]{:S(2)}, u32[]{:S(2)}) %collective-permute-start.17) | collective-permute-done | bytes 28704 | tf_op jit(solution)/shard_map/ppermute | solution.py:677
  113.8 1.6 %gather_second.1 = f32[21,1024]{1,0:T(8,128)} custom-call(s32[1,2]{1,0:T(1,128)S(1)} %copy-done.5, s32[8,128]{1,0:T(8,128)S(1)} %broadcast_in_dim.2.spot, f32[144,128]{1,0:T(8,128)S(1)} %get-tuple-element.90.h, f32[8,256]{1,0:T(8,128)S(1)} %get-tuple-element.91.hb, f32[56,128]{1,0:T(8,128)S(1)} %collective-permute-done.16.from_low, ...), custom_call_target="tpu_custom_call" | custom-call | tf_op jit(solution)/shard_map/gather_second/pallas_call | solution.py:781
  (19 shorter events, 0.0 us)
Async XLA Ops:
  3.3 15.8 %collective-permute-start = (f32[16,384]{1,0:T(8,128)S(1)}, f32[16,384]{1,0:T(8,128)S(1)}, u32[]{:S(2)}, u32[]{:S(2)}) collective-permute-start(f32[16,384]{1,0:T(8,128)S(1)} %get-tuple-element.53), channel_id=1, source_target_pairs={{0,1},{1,2},{2,3},{3,4},{4,5},{5,6},{6,7},{8,9},{9,10},{10,11},{11... | collective-permute-start | bytes 73736 | tf_op jit(solution)/shard_map/ppermute | solution.py:676
  17.2 14.4 %collective-permute-start.1 = (f32[16,384]{1,0:T(8,128)S(1)}, f32[16,384]{1,0:T(8,128)S(1)}, u32[]{:S(2)}, u32[]{:S(2)}) collective-permute-start(f32[16,384]{1,0:T(8,128)S(1)} %get-tuple-element.54), channel_id=1, source_target_pairs={{1,0},{2,1},{3,2},{4,3},{5,4},{6,5},{7,6},{9,8},{10,9},{11,10},{12... | collective-permute-start | bytes 73736 | tf_op jit(solution)/shard_map/ppermute | solution.py:677
  32.0 5.0 %collective-permute-start.2 = (f32[72,128]{1,0:T(8,128)S(1)}, f32[72,128]{1,0:T(8,128)S(1)}, u32[]{:S(2)}, u32[]{:S(2)}) collective-permute-start(f32[72,128]{1,0:T(8,128)S(1)} %get-tuple-element.57), channel_id=1, source_target_pairs={{0,8},{8,0},{16,24},{24,16},{32,40},{40,32},{48,56},{56,48},{64,72... | collective-permute-start | bytes 110600 | tf_op jit(solution)/shard_map/ppermute | solution.py:685
  34.0 5.3 %collective-permute-start.3 = (f32[72,128]{1,0:T(8,128)S(1)}, f32[72,128]{1,0:T(8,128)S(1)}, u32[]{:S(2)}, u32[]{:S(2)}) collective-permute-start(f32[72,128]{1,0:T(8,128)S(1)} %get-tuple-element.58), channel_id=1, source_target_pairs={{8,16},{16,8},{24,32},{32,24},{40,48},{48,40},{56,64},{64,56},{72,... | collective-permute-start | bytes 110600 | tf_op jit(solution)/shard_map/ppermute | solution.py:686
  39.2 4.9 %copy-start.4 = (s32[1,26,32]{2,0,1:T(1,128)S(1)}, s32[1,26,32]{2,0,1:T(1,128)}, u32[]{:S(2)}) copy-start(s32[1,26,32]{2,0,1:T(1,128)} %param.19) | copy-start | bytes 9988
  39.2 4.9 %copy-start.7 = (s32[1,26]{1,0:T(1,128)S(1)}, s32[1,26]{1,0:T(1,128)}, u32[]{:S(2)}) copy-start(s32[1,26]{1,0:T(1,128)} %counts.1) | copy-start | bytes 316
  39.2 9.6 %copy-start = (f32[2,9,1024]{2,0,1:T(2,128)S(1)}, f32[2,9,1024]{2,0,1:T(2,128)}, u32[]{:S(2)}) copy-start(f32[2,9,1024]{2,0,1:T(2,128)} %param.13) | copy-start | bytes 221188
  39.3 9.5 %copy-start.1 = (f32[2,3,1024]{2,0,1:T(2,128)S(1)}, f32[2,3,1024]{2,0,1:T(2,128)}, u32[]{:S(2)}) copy-start(f32[2,3,1024]{2,0,1:T(2,128)} %param.11) | copy-start | bytes 73732
  39.3 5.2 %collective-permute-start.4 = (f32[88,128]{1,0:T(8,128)S(1)}, f32[88,128]{1,0:T(8,128)S(1)}, u32[]{:S(2)}, u32[]{:S(2)}) collective-permute-start(f32[88,128]{1,0:T(8,128)S(1)} %get-tuple-element.61), channel_id=1, source_target_pairs={{0,128},{128,256},{256,384},{1,129},{129,257},{257,385},{2,130},{1... | collective-permute-start | bytes 135176 | tf_op jit(solution)/shard_map/ppermute | solution.py:676
  42.9 5.9 %collective-permute-start.5 = (f32[88,128]{1,0:T(8,128)S(1)}, f32[88,128]{1,0:T(8,128)S(1)}, u32[]{:S(2)}, u32[]{:S(2)}) collective-permute-start(f32[88,128]{1,0:T(8,128)S(1)} %get-tuple-element.62), channel_id=1, source_target_pairs={{128,0},{256,128},{384,256},{129,1},{257,129},{385,257},{130,2},{2... | collective-permute-start | bytes 135176 | tf_op jit(solution)/shard_map/ppermute | solution.py:677
  44.3 4.5 %copy-start.2 = (s32[2,1024]{1,0:T(2,128)S(1)}, s32[2,1024]{1,0:T(2,128)}, u32[]{:S(2)}) copy-start(s32[2,1024]{1,0:T(2,128)} %centers.9) | copy-start | bytes 24580
  48.8 0.7 copy-start.5
  51.0 5.0 %collective-permute-start.6 = (f32[21,384]{1,0:T(8,128)S(1)}, f32[21,384]{1,0:T(8,128)S(1)}, u32[]{:S(2)}, u32[]{:S(2)}) collective-permute-start(f32[21,384]{1,0:T(8,128)S(1)} %get-tuple-element.69), channel_id=1, source_target_pairs={{0,128},{128,256},{256,384},{1,129},{129,257},{257,385},{2,130},{1... | collective-permute-start | bytes 96776 | tf_op jit(solution)/shard_map/ppermute | solution.py:676
  54.4 5.9 %collective-permute-start.7 = (f32[21,384]{1,0:T(8,128)S(1)}, f32[21,384]{1,0:T(8,128)S(1)}, u32[]{:S(2)}, u32[]{:S(2)}) collective-permute-start(f32[21,384]{1,0:T(8,128)S(1)} %get-tuple-element.70), channel_id=1, source_target_pairs={{128,0},{256,128},{384,256},{129,1},{257,129},{385,257},{130,2},{2... | collective-permute-start | bytes 96776 | tf_op jit(solution)/shard_map/ppermute | solution.py:677
  60.3 6.1 %collective-permute-start.8 = (f32[21,384]{1,0:T(8,128)S(1)}, f32[21,384]{1,0:T(8,128)S(1)}, u32[]{:S(2)}, u32[]{:S(2)}) collective-permute-start(f32[21,384]{1,0:T(8,128)S(1)} %get-tuple-element.71), channel_id=1, source_target_pairs={{0,8},{8,0},{16,24},{24,16},{32,40},{40,32},{48,56},{56,48},{64,72... | collective-permute-start | bytes 96776 | tf_op jit(solution)/shard_map/ppermute | solution.py:685
  62.2 5.3 %collective-permute-start.9 = (f32[21,384]{1,0:T(8,128)S(1)}, f32[21,384]{1,0:T(8,128)S(1)}, u32[]{:S(2)}, u32[]{:S(2)}) collective-permute-start(f32[21,384]{1,0:T(8,128)S(1)} %get-tuple-element.72), channel_id=1, source_target_pairs={{8,16},{16,8},{24,32},{32,24},{40,48},{48,40},{56,64},{64,56},{72,... | collective-permute-start | bytes 96776 | tf_op jit(solution)/shard_map/ppermute | solution.py:686
  65.3 0.7 copy-start.6
  67.5 28.3 %copy-start.3 = (f32[2,9,1024]{2,0,1:T(2,128)S(1)}, f32[2,9,1024]{2,0,1:T(2,128)}, u32[]{:S(2)}) copy-start(f32[2,9,1024]{2,0,1:T(2,128)} %param.14) | copy-start | bytes 221188
  70.1 25.7 %collective-permute-start.10 = (f32[24,384]{1,0:T(8,128)S(1)}, f32[24,384]{1,0:T(8,128)S(1)}, u32[]{:S(2)}, u32[]{:S(2)}) collective-permute-start(f32[24,384]{1,0:T(8,128)S(1)} %get-tuple-element.80), channel_id=1, source_target_pairs={{0,1},{1,2},{2,3},{3,4},{4,5},{5,6},{6,7},{8,9},{9,10},{10,11},{11... | collective-permute-start | bytes 110600 | tf_op jit(solution)/shard_map/ppermute | solution.py:676
  73.2 22.5 %collective-permute-start.11 = (f32[24,384]{1,0:T(8,128)S(1)}, f32[24,384]{1,0:T(8,128)S(1)}, u32[]{:S(2)}, u32[]{:S(2)}) collective-permute-start(f32[24,384]{1,0:T(8,128)S(1)} %get-tuple-element.81), channel_id=1, source_target_pairs={{1,0},{2,1},{3,2},{4,3},{5,4},{6,5},{7,6},{9,8},{10,9},{11,10},{12... | collective-permute-start | bytes 110600 | tf_op jit(solution)/shard_map/ppermute | solution.py:677
  74.5 17.0 %collective-permute-start.12 = (f32[2,256]{1,0:T(2,128)S(1)}, f32[2,256]{1,0:T(2,128)S(1)}, u32[]{:S(2)}, u32[]{:S(2)}) collective-permute-start(f32[2,256]{1,0:T(2,128)S(1)} %get-tuple-element.82), channel_id=1, source_target_pairs={{0,2},{1,3},{2,4},{3,5},{4,6},{5,7},{8,10},{9,11},{10,12},{11,13},... | collective-permute-start | bytes 6152 | tf_op jit(solution)/shard_map/ppermute | solution.py:676
  90.3 5.5 %collective-permute-start.13 = (f32[2,256]{1,0:T(2,128)S(1)}, f32[2,256]{1,0:T(2,128)S(1)}, u32[]{:S(2)}, u32[]{:S(2)}) collective-permute-start(f32[2,256]{1,0:T(2,128)S(1)} %get-tuple-element.83), channel_id=1, source_target_pairs={{2,0},{3,1},{4,2},{5,3},{6,4},{7,5},{10,8},{11,9},{12,10},{13,11},... | collective-permute-start | bytes 6152 | tf_op jit(solution)/shard_map/ppermute | solution.py:677
  97.7 3.9 %collective-permute-start.14 = (f32[48,128]{1,0:T(8,128)S(1)}, f32[48,128]{1,0:T(8,128)S(1)}, u32[]{:S(2)}, u32[]{:S(2)}) collective-permute-start(f32[48,128]{1,0:T(8,128)S(1)} %get-tuple-element.88), channel_id=1, source_target_pairs={{0,8},{8,0},{16,24},{24,16},{32,40},{40,32},{48,56},{56,48},{64,72... | collective-permute-start | bytes 73736 | tf_op jit(solution)/shard_map/ppermute | solution.py:685
  99.7 5.1 %collective-permute-start.15 = (f32[48,128]{1,0:T(8,128)S(1)}, f32[48,128]{1,0:T(8,128)S(1)}, u32[]{:S(2)}, u32[]{:S(2)}) collective-permute-start(f32[48,128]{1,0:T(8,128)S(1)} %get-tuple-element.89), channel_id=1, source_target_pairs={{8,16},{16,8},{24,32},{32,24},{40,48},{48,40},{56,64},{64,56},{72,... | collective-permute-start | bytes 73736 | tf_op jit(solution)/shard_map/ppermute | solution.py:686
  104.9 4.6 %collective-permute-start.16 = (f32[56,128]{1,0:T(8,128)S(1)}, f32[56,128]{1,0:T(8,128)S(1)}, u32[]{:S(2)}, u32[]{:S(2)}) collective-permute-start(f32[56,128]{1,0:T(8,128)S(1)} %get-tuple-element.92), channel_id=1, source_target_pairs={{0,128},{128,256},{256,384},{1,129},{129,257},{257,385},{2,130},{1... | collective-permute-start | bytes 86024 | tf_op jit(solution)/shard_map/ppermute | solution.py:676
  108.0 5.8 %collective-permute-start.17 = (f32[56,128]{1,0:T(8,128)S(1)}, f32[56,128]{1,0:T(8,128)S(1)}, u32[]{:S(2)}, u32[]{:S(2)}) collective-permute-start(f32[56,128]{1,0:T(8,128)S(1)} %get-tuple-element.93), channel_id=1, source_target_pairs={{128,0},{256,128},{384,256},{129,1},{257,129},{385,257},{130,2},{2... | collective-permute-start | bytes 86024 | tf_op jit(solution)/shard_map/ppermute | solution.py:677

commit v5 on v4

--- a/solution.py
+++ b/solution.py
@@ -109,8 +109,20 @@
     return jnp.broadcast_to(info[i : i + 1, :], (rows, 128))
 
 
-def by_side(info, one, other):
-    return jnp.where(row_of(info, 3, one.shape[0]) == 0, one, other)
+def by_side(info, one, other, axis_row=3):
+    return jnp.where(row_of(info, axis_row, one.shape[0]) == 0, one, other)
+
+
+def by_z_side(info, one, other):
+    tiles = [
+        by_side(info, lane_tile(one, t), lane_tile(other, t), 4) for t in range(one.shape[1] // 128)
+    ]
+    return jnp.concatenate(tiles, axis=1)
+
+
+def fields(ref):
+    tiles = [ref[i * 8 : i * 8 + 8] for i in range(13)]
+    return tiles[0:3], cells_of((tiles[3] + 0.5).astype(I32)), tiles[4:13]
 
 
 def in_use(live, step):
@@ -218,21 +230,21 @@
     ref[at + 1 : at + 2, :width] = second
 
 
-def static_rows(table, send, start, hot, dest):
+def static_rows(table, send, rows, hot, put):
     hi, lo = split(table[...])
     low_row, row = iota((128, 128), 0), iota((8, 128), 0)
-    for t in range(3):
-        index = send[start + t : start + t + 1]
+    for t, n in enumerate(rows):
+        index = send[n : n + 1]
         hot[...] = (low_row == index % 128).astype(F32).astype(BF16)
         got = (nn(hi, hot[...]) + nn(lo, hot[...])).reshape(14, 8, 128)
         chosen = row == index // 128
-        dest[0:14, t * 128 : t * 128 + 128] = jnp.sum(jnp.where(chosen[None], got, 0.0), axis=1)
+        put(t, jnp.sum(jnp.where(chosen[None], got, 0.0), axis=1))
 
 
 def first_kernel(
-    live_at, adjoint_at, fractions_at, centers_at, deform_at, affine_at, mass_at, slots_at,
-    h, hb, zu, zd, bf_out, w_hi, w_lo, d_hi, d_lo, send,
-    l0h, l0l, l2h, l2l, table, hot,
+    spot, live_at, adjoint_at, fractions_at, centers_at, deform_at, affine_at, mass_at, slots_at,
+    h, hb, both, bf_out, w_hi, w_lo, d_hi, d_lo, send, now, early,
+    l0h, l0l, l2h, l2l, hot, zu, zd,
     live, adjoint, fractions, centers, deform, affine, mass, slots_back, arrived,
 ):
     sources = (slots_at, fractions_at, centers_at, deform_at, live_at, adjoint_at, affine_at, mass_at)
@@ -244,27 +256,33 @@
         copy.start()
     w = (w_hi, w_lo, d_hi, d_lo)
     l = (l0h, l0l, l2h, l2l)
+    zu[...] = jnp.zeros(zu.shape, F32)
+    zd[...] = jnp.zeros(zd.shape, F32)
     for copy in copies[:3]:
         copy.wait()
     fill_send(slots_back, send)
-    which = 1
-    frac = dense(fractions, which, 3)
-    centre = centers[which : which + 1, :].reshape(CHUNKS, 128)
+    frac = dense(fractions, 1, 3)
+    centre = centers[1:2, :].reshape(CHUNKS, 128)
     cell_x, cell_y, cell_z = cells_of(centre)
     build_z(frac[2], cell_z, *w)
     for copy in copies[3:]:
         copy.wait()
-    table[104:112] = jnp.zeros((8, 128), F32)
-    early = dense(fractions, 0, 3) + [centers[0:1, :].reshape(CHUNKS, 128).astype(F32)]
-    for i, tile in enumerate(early + dense(deform, 0, 9)):
-        table[i * 8 : i * 8 + 8] = tile
-    zu[...] = jnp.zeros(zu.shape, F32)
-    zd[...] = jnp.zeros(zd.shape, F32)
-    static_rows(table, send, 2, hot, zd)
-    static_rows(table, send, 5, hot, zu)
-    use = in_use(live, which)
+    deform_now = dense(deform, 1, 9)
+    for i, tile in enumerate(frac + [centre.astype(F32)] + deform_now):
+        now[i * 8 : i * 8 + 8] = tile
+    early[104:112] = jnp.zeros((8, 128), F32)
+    known = dense(fractions, 0, 3) + [centers[0:1, :].reshape(CHUNKS, 128).astype(F32)]
+    for i, tile in enumerate(known + dense(deform, 0, 9)):
+        early[i * 8 : i * 8 + 8] = tile
+
+    def put(t, got):
+        dest = (zd, zu)[t // 3]
+        dest[0:14, t % 3 * 128 : t % 3 * 128 + 128] = got
+
+    static_rows(early, send, range(2, 8), hot, put)
+    use = in_use(live, 1)
     adj = [v * use for v in dense(adjoint, None, 21)]
-    a_v, b_c, b_f = transfer(adj, dense(deform, which, 9), dense(affine, which, 9))
+    a_v, b_c, b_f = transfer(adj, deform_now, dense(affine, 1, 9))
     for i in range(9):
         bf_out[i] = b_f[i]
     scatter_rows(a_v, b_c, frac, cell_x, cell_y, *l)
@@ -282,6 +300,8 @@
     put_planes(hb, 0, ends[0:1], ends[1:2])
     put_planes(zu, 13, ends[0:1], ends[3:4])
     put_planes(zd, 13, ends[1:2], ends[2:3])
+    both[0:16] = by_z_side(spot, zu, zd)
+    both[16:32] = by_z_side(spot, zd, zu)
 
 
 def wide_rows(hb):
@@ -300,8 +320,9 @@
     return jnp.concatenate([rows, jnp.zeros((120, 256), F32)], axis=0).T
 
 
-def z_kernel(comps, spot, h, hb, from_low, from_high, h_out, hb_out, ya, yb):
-    low, high = from_low[13:15, 0:256], from_high[13:15, 0:256]
+def z_kernel(comps, spot, h, hb, both, far, h_out, hb_out, ya, yb):
+    direct, relayed = both[13:15, 0:256], far[13:15, 0:256]
+    low, high = by_z_side(spot, relayed, direct), by_z_side(spot, direct, relayed)
     z_fold(comps, spot, h, hb[...], low, high, h_out, hb_out, ya, yb)
 
 
@@ -457,8 +478,7 @@
 
 
 def gather_first_kernel(
-    extents, live, spot, h, hb, from_low, from_high, fractions, centers, deform, bf,
-    w_hi, w_lo, d_hi, d_lo, pick,
+    extents, live, spot, h, hb, from_low, from_high, now, bf, w_hi, w_lo, d_hi, d_lo, pick,
     second, xu, xd, mid, mass_core, mass_halo,
     total, g_hi, g_lo, s0, sz, rows12, buf, hot,
 ):
@@ -480,11 +500,10 @@
         spot, extents, total, halo,
         lambda x: total[192 + x * 8 : 192 + x * 8 + 8], spread(1), g_hi, g_lo,
     )
-    frac = dense(fractions, which, 3)
-    cell_x, cell_y, _ = cells_of(centers[which : which + 1, :].reshape(CHUNKS, 128))
+    frac, (cell_x, cell_y, _), deform = fields(now)
     gather(frac, cell_x, cell_y, g_hi, g_lo, w_hi, w_lo, d_hi, d_lo, s0, sz, rows12)
     use = in_use(live, which)
-    out = particle(rows12, frac, [bf[i] for i in range(9)], dense(deform, which, 9), use)
+    out = particle(rows12, frac, [bf[i] for i in range(9)], deform, use)
     for i in range(21):
         second[i] = out[i]
         buf[i * 8 : i * 8 + 8] = out[i]
@@ -525,116 +544,142 @@
         yb[:, i * 128 : i * 128 + 128] = by_side(first, down, up)
 
 
-def carry(tiles, indices, lh, ll, hot):
+def carry(tiles, indices, lh, ll, hot, count=21):
     row, low_row = iota((8, 128), 0), iota((128, 128), 0)
     for t, (values, index) in enumerate(zip(tiles, indices)):
         lanes = slice(t * 128, t * 128 + 128)
         hot[:, lanes] = (low_row == index % 128).astype(F32).astype(BF16)
         chosen = row == index // 128
-        for pair in range(11):
+        for pair in range((count + 1) // 2):
             both = []
             for r in (2 * pair, 2 * pair + 1):
                 blank = jnp.zeros((8, 128), F32)
-                both.append(blank if r > 20 else jnp.where(chosen, values(r), 0.0))
+                both.append(blank if r >= count else jnp.where(chosen, values(r), 0.0))
             rows = slice(pair * 16, pair * 16 + 16)
             lh[rows, lanes], ll[rows, lanes] = split(jnp.concatenate(both, axis=0))
     return nt(lh[...], hot[...]) + nt(ll[...], hot[...])
 
 
-def weights_kernel(fractions, centers, w_hi, w_lo, d_hi, d_lo):
-    _, _, cell_z = cells_of(centers[0:1, :].reshape(CHUNKS, 128))
-    build_z(dense(fractions, 0, 3)[2], cell_z, w_hi, w_lo, d_hi, d_lo)
-
-
-def stay_kernel(second, prior, stayed, lh, ll, hot):
+def weights_kernel(early, send, w_hi, w_lo, d_hi, d_lo, a_hi, a_lo, b_hi, b_lo, arrive, hot):
+    frac, cells, _ = fields(early)
+    build_z(frac[2], cells[2], w_hi, w_lo, d_hi, d_lo)
+
+    def put(t, got):
+        arrive[:, t, :] = got
+
+    static_rows(early, send, (2, 3, 4, 5, 6, 7, 0, 1), hot, put)
+    _, _, cell_z = cells_of((arrive[3] + 0.5).astype(I32))
+    build_z(arrive[2], cell_z, a_hi, a_lo, b_hi, b_lo)
+
+
+def stay_kernel(
+    live, second, prior, early, w_hi, w_lo, d_hi, d_lo,
+    stayed, core, ends,
+    lh, ll, hot, l0h, l0l, l2h, l2l,
+):
     tiles = [lambda r, t=t: second[r, t : t + 1, :] for t in range(8)]
     total = carry(tiles, [prior[t : t + 1] for t in range(8)], lh, ll, hot)
+    use = in_use(live, 0)
+    adj = [total[i * 8 : i * 8 + 8] * use for i in range(21)]
     for i in range(21):
-        stayed[i] = total[i * 8 : i * 8 + 8]
+        stayed[i] = adj[i]
+    frac, (cell_x, cell_y, _), deform = fields(early)
+    a_v, b_c = to_grid(adj, deform)
+    l, w = (l0h, l0l, l2h, l2l), (w_hi, w_lo, d_hi, d_lo)
+    scatter_rows(a_v, b_c, frac, cell_x, cell_y, *l)
+    core[...] = core_sums(l, w)
+    ends[...] = edge_sums(l, w)
 
 
 def near_kernel(
-    live, spot, mid, x_low, x_high, ra, rb, stayed, send,
-    static_low, static_high, fractions, centers, deform, w_hi, w_lo, d_hi, d_lo,
-    zu, zd, up2, dn2, own_low, own_high, carried,
-    lh, ll, hot, l0h, l0l, l2h, l2l, moved, static, e0, e1, e2, e3,
+    spot, mid, x_low, x_high, ra, rb, both, far, arrive, ends_stay,
+    zu, zd, up2, dn2, own_low, own_high, final,
+    l0h, l0l, l2h, l2l, moved, static, e0, e1, e2, e3,
 ):
     groups = [lane_tile(mid, 1), lane_tile(x_low, 1), lane_tile(x_high, 1)]
-    first = spot
-    groups += [by_side(first, lane_tile(rb, i), lane_tile(ra, i)) for i in range(3)]
-    groups += [by_side(first, lane_tile(ra, i), lane_tile(rb, i)) for i in range(3)]
-    final = pieces(groups[1:], 32, 2)
-    moved[...] = jnp.zeros(moved.shape, F32)
-    static[...] = jnp.zeros(static.shape, F32)
+    groups += [by_side(spot, lane_tile(rb, i), lane_tile(ra, i)) for i in range(3)]
+    groups += [by_side(spot, lane_tile(ra, i), lane_tile(rb, i)) for i in range(3)]
     zu[...] = jnp.zeros(zu.shape, F32)
     zd[...] = jnp.zeros(zd.shape, F32)
+    direct, relayed = both[0:16], far[...]
+    static_low = by_z_side(spot, relayed, direct)
+    static_high = by_z_side(spot, direct, relayed)
     for ref, at, first, known in ((zu, 64, 0, static_high), (zd, 0, 3, static_low)):
         for i, tile in enumerate(pieces(groups, at, 3)):
             ref[0:21, i * 128 : i * 128 + 128] = tile
             moved[:, first + i, :] = tile
-            static[:, first + i, :] = known[0:14, i * 128 : i * 128 + 128]
+            static[:, first + i, :] = lane_tile(known, i)[0:14]
+    for i, tile in enumerate(pieces(groups[1:], 32, 2)):
+        final[:, i * 128 : i * 128 + 128] = tile
+        moved[:, 6 + i, :] = tile
+        static[:, 6 + i, :] = arrive[:, 6 + i, :]
     l = (l0h, l0l, l2h, l2l)
     e = (e0, e1, e2, e3)
-
     place = [static[i] for i in range(3)]
     cell_x, cell_y, cell_z = cells_of((static[3] + 0.5).astype(I32))
-    build_z(place[2], cell_z, *e, chunks=6, edges_only=True)
+    build_z(place[2], cell_z, *e, edges_only=True)
     a_v, b_c = to_grid([moved[i] for i in range(21)], [static[4 + i] for i in range(9)])
-    scatter_rows(a_v, b_c, place, cell_x, cell_y, *l, chunks=6)
+    scatter_rows(a_v, b_c, place, cell_x, cell_y, *l)
     upward = edge_sums(l, e, slice(0, 16), slice(0, 384))
     downward = edge_sums(l, e, slice(0, 16), slice(384, 768))
+    ends = edge_sums(l, e, slice(0, 16), slice(768, 1024)) + ends_stay[...]
     for ref in (up2, dn2, own_low, own_high):
         ref[...] = jnp.zeros(ref.shape, F32)
     put_planes(up2, 0, upward[0:1], upward[3:4])
     put_planes(own_high, 0, upward[1:2], upward[2:3])
     put_planes(own_low, 0, downward[0:1], downward[3:4])
     put_planes(dn2, 0, downward[1:2], downward[2:3])
-
-    tiles = [lambda r, t=t: final[t][r : r + 1] for t in range(2)]
-    total = carry(tiles, [send[t : t + 1] for t in range(2)], lh, ll, hot)
-    use = in_use(live, 0)
-    adj = [(stayed[i] + total[i * 8 : i * 8 + 8]) * use for i in range(21)]
-    for i in range(21):
-        carried[i] = adj[i]
-    frac = dense(fractions, 0, 3)
-    cell_x, cell_y, _ = cells_of(centers[0:1, :].reshape(CHUNKS, 128))
-    a_v, b_c = to_grid(adj, dense(deform, 0, 9))
-    scatter_rows(a_v, b_c, frac, cell_x, cell_y, *l)
-    ends = edge_sums(l, (w_hi, w_lo, d_hi, d_lo))
     put_planes(zu, 21, ends[0:1], ends[3:4])
     put_planes(zd, 21, ends[1:2], ends[2:3])
 
 
 def second_kernel(
-    live, spot, carried, z_low, z_high, low2, high2, own_low, own_high, send,
-    fractions, centers, deform, affine, w_hi, w_lo, d_hi, d_lo,
-    h_out, hb_out, ya, yb, bf_out,
-    lh, ll, hot, l0h, l0l, l2h, l2l, h,
+    spot, z_low, z_high, low2, high2, own_low, own_high, final, arrive, a_hi, a_lo, b_hi, b_lo,
+    core_stay, ends_stay,
+    h_out, hb_out, ya, yb,
+    l0h, l0l, l2h, l2l, moved, h,
 ):
-    tiles = [lambda r, t=t: z_low[r : r + 1, t * 128 : t * 128 + 128] for t in range(3)]
-    tiles += [lambda r, t=t: z_high[r : r + 1, t * 128 : t * 128 + 128] for t in range(3)]
-    total = carry(tiles, [send[t : t + 1] for t in range(2, 8)], lh, ll, hot)
-    use = in_use(live, 0)
-    adj = [(carried[i] + total[i * 8 : i * 8 + 8]) * use for i in range(21)]
-    frac = dense(fractions, 0, 3)
-    cell_x, cell_y, _ = cells_of(centers[0:1, :].reshape(CHUNKS, 128))
-    a_v, b_c, b_f = transfer(adj, dense(deform, 0, 9), dense(affine, 0, 9))
-    for i in range(9):
-        bf_out[i] = b_f[i]
-    l = (l0h, l0l, l2h, l2l)
-    w = (w_hi, w_lo, d_hi, d_lo)
-    scatter_rows(a_v, b_c, frac, cell_x, cell_y, *l)
-    h[...] = core_sums(l, w)
-    ends = jnp.concatenate([edge_sums(l, w)[0:8], jnp.zeros((8, 112), F32)], axis=1)
+    for i in range(3):
+        moved[:, i, :] = lane_tile(z_low, i)[0:21]
+        moved[:, 3 + i, :] = lane_tile(z_high, i)[0:21]
+    for i in range(2):
+        moved[:, 6 + i, :] = lane_tile(final, i)
+    place = [arrive[i] for i in range(3)]
+    cell_x, cell_y, _ = cells_of((arrive[3] + 0.5).astype(I32))
+    a_v, b_c = to_grid([moved[i] for i in range(21)], [arrive[4 + i] for i in range(9)])
+    l, w = (l0h, l0l, l2h, l2l), (a_hi, a_lo, b_hi, b_lo)
+    scatter_rows(a_v, b_c, place, cell_x, cell_y, *l)
+    h[...] = core_sums(l, w) + core_stay[...]
+    ends = edge_sums(l, w) + ends_stay[...]
+    ends = jnp.concatenate([ends[0:8], jnp.zeros((8, 112), F32)], axis=1)
     halo = jnp.where(iota((8, 256), 0) < 2, ends, 0.0)
     low = z_low[21:23, 0:256] + low2[0:2] + own_low[0:2]
     high = z_high[21:23, 0:256] + high2[0:2] + own_high[0:2]
     z_fold(3, spot, h, halo, low, high, h_out, hb_out, ya, yb)
 
 
+def deform_kernel(live, stayed, z_low, z_high, final, send, affine, bf_out, lh, ll, hot):
+    tiles = []
+    for ref, count in ((z_low, 3), (z_high, 3), (final, 2)):
+        for t in range(count):
+            tiles.append(
+                lambda r, ref=ref, t=t: ref[12 + r : 13 + r, t * 128 : t * 128 + 128]
+            )
+    rows = [send[t : t + 1] for t in (2, 3, 4, 5, 6, 7, 0, 1)]
+    total = carry(tiles, rows, lh, ll, hot, 9)
+    use = in_use(live, 0)
+    a_f = [(stayed[12 + i] + total[i * 8 : i * 8 + 8]) * use for i in range(9)]
+    k = dense(affine, 0, 9)
+    for i in range(3):
+        for j in range(3):
+            bf_out[3 * i + j] = a_f[3 * i + j] + TIME_STEP * sum(
+                k[3 * m + i] * a_f[3 * m + j] for m in range(3)
+            )
+
+
 def gather_second_kernel(
-    extents, live, spot, h, hb, from_low, from_high, fractions, centers, deform, bf,
-    w_hi, w_lo, d_hi, d_lo, mass_core, mass_halo,
+    extents, live, spot, h, hb, from_low, from_high, early, bf, w_hi, w_lo, d_hi, d_lo,
+    mass_core, mass_halo,
     result,
     total, g_hi, g_lo, s0, sz, rows12, packed,
 ):
@@ -644,11 +689,10 @@
         spot, extents, total, halo,
         lambda x: mass_core[x * 8 : x * 8 + 8], mass_halo[...], g_hi, g_lo,
     )
-    frac = dense(fractions, which, 3)
-    cell_x, cell_y, _ = cells_of(centers[which : which + 1, :].reshape(CHUNKS, 128))
+    frac, (cell_x, cell_y, _), deform = fields(early)
     gather(frac, cell_x, cell_y, g_hi, g_lo, w_hi, w_lo, d_hi, d_lo, s0, sz, rows12)
     use = in_use(live, which)
-    out = particle(rows12, frac, [bf[i] for i in range(9)], dense(deform, which, 9), use)
+    out = particle(rows12, frac, [bf[i] for i in range(9)], deform, use)
     for i in range(21):
         packed[i] = out[i]
     for k in range(CHUNKS):
@@ -692,8 +736,9 @@
     live_count, send_slot, receive_slot, receive_count, prior_slot,
 ):
     at_y = lax.axis_index("gy")
-    spot = [lax.axis_index("gx") * 4, at_y * 4, lax.axis_index("gz") * 128, at_y % 2]
-    spot = jnp.stack(spot + [jnp.zeros_like(at_y)] * 4).astype(I32)
+    at_z = lax.axis_index("gz")
+    spot = [lax.axis_index("gx") * 4, at_y * 4, at_z * 128, at_y % 2, at_z % 2]
+    spot = jnp.stack(spot + [jnp.zeros_like(at_y)] * 3).astype(I32)
     spot = jnp.broadcast_to(spot[:, None], (8, 128))
     extents = (lax.axis_size("gx") * 4, lax.axis_size("gy") * 4, lax.axis_size("gz") * 128)
 
@@ -716,7 +761,7 @@
         ra, rb = both_pairs(ya, yb, "gy")
         rows = comps * 16 + 8
         h, hb, xu, xd = call(
-            functools.partial(y_kernel, comps), f"fold_y{comps}", [VMEM] + [VMEM] * 4,
+            functools.partial(y_kernel, comps), f"fold_y{comps}", [VMEM] * 5,
             [shape(comps * 48, 128), shape(8, 256), shape(rows, 128), shape(rows, 128)],
         )(spot, h, hb, ra, rb)
         low, high = both_ways(xu, xd, "gx")
@@ -725,65 +770,79 @@
     firsts = (
         live_count, final_adjoint, fractions, centers, deform, next_affine, cell_mass, slots_back
     )
-    h, hb, zu, zd, bf, *w, send = call(
-        first_kernel, "scatter_first", [HBM] * 8,
-        [shape(240, 128), shape(8, 256), shape(16, 384), shape(16, 384), shape(9, 8, 128)]
-        + weights + [shape(8, 128, dtype=I32)],
-        lrows + [((112, 128), F32), ((128, 128), BF16)]
+    h, hb, both, bf, *w, send, now, early = call(
+        first_kernel, "scatter_first", [VMEM] + [HBM] * 8,
+        [shape(240, 128), shape(8, 256), shape(32, 384), shape(9, 8, 128)]
+        + weights + [shape(8, 128, dtype=I32), shape(104, 128), shape(112, 128)],
+        lrows + [((128, 128), BF16), ((16, 384), F32), ((16, 384), F32)]
         + [(v.shape, v.dtype) for v in firsts] + [pltpu.SemaphoreType.DMA((8,))],
-    )(*(pltpu.with_memory_space_constraint(v, pltpu.HBM) for v in firsts))
-    static_low, static_high = both_ways(zu, zd, "gz")
+    )(spot, *(pltpu.with_memory_space_constraint(v, pltpu.HBM) for v in firsts))
+    count = lax.axis_size("gz")
+    both = lax.ppermute(both, "gz", [(i, i ^ 1) for i in range(count) if i ^ 1 < count])
+    hop = [(i, i + 2) for i in range(0, count - 2, 2)] + [(i, i - 2) for i in range(3, count, 2)]
+    far = lax.ppermute(both[16:32], "gz", hop) if hop else jnp.zeros_like(both[16:32])
     (pick,) = call(pick_kernel, "fill_pick", [VMEM, VMEM], [shape(9, 128, dtype=I32)])(
         receive_count, slots_out
     )
+    weights2 = call(
+        weights_kernel, "weights_second", [VMEM] * 2, weights + weights + [shape(14, 8, 128)],
+        [((128, 128), BF16)],
+    )(early, send)
+    w2, wa, arrive = weights2[0:4], weights2[4:8], weights2[8]
+
+    def first_z(*refs):
+        z_kernel(5, *refs[:5], *refs[6:])
+
     h, hb, ya, yb = call(
-        functools.partial(z_kernel, 5), "fold_z5", [VMEM] + [VMEM] * 4,
+        first_z, "fold_z5", [VMEM] * 5 + [pl.BlockSpec(memory_space=pl.ANY)],
         [shape(240, 128), shape(8, 256), shape(72, 128), shape(72, 128)],
-    )(spot, h, hb, static_low, static_high)
+    )(spot, h, hb, both, far, arrive)
     h, hb, low, high = fold(5, h, hb, ya, yb)
     second, xu, xd, mid, mass_core, mass_halo = call(
-        functools.partial(gather_first_kernel, extents), "gather_first",
-        [VMEM, VMEM] + [VMEM] * 13,
+        functools.partial(gather_first_kernel, extents), "gather_first", [VMEM] * 13,
         [shape(21, 8, 128), shape(21, 384), shape(21, 384), shape(21, 384), shape(48, 128), shape(8, 256)],
         [((240, 128), F32)] + gscratch + [((176, 128), F32), ((128, 128), BF16)],
-    )(live_count, spot, h, hb, low, high, fractions, centers, deform, bf, *w, pick)
-
-    w = call(weights_kernel, "weights_second", [VMEM] * 2, weights)(fractions, centers)
+    )(live_count, spot, h, hb, low, high, now, bf, *w, pick)
+
     x_low, x_high = both_ways(xu, xd, "gx")
-    (stayed,) = call(
-        stay_kernel, "stay", [VMEM] * 2, [shape(21, 8, 128)],
-        [((176, 1024), BF16)] * 2 + [((128, 1024), BF16)],
-    )(second, prior)
-    ya, yb = call(route_y_kernel, "route_y", [VMEM] + [VMEM] * 3, [shape(21, 384)] * 2)(
-        spot, mid, x_low, x_high
-    )
+    stayed, core_stay, ends_stay = call(
+        stay_kernel, "stay", [VMEM] * 8,
+        [shape(21, 8, 128), shape(144, 128), shape(16, 144)],
+        [((176, 1024), BF16)] * 2 + [((128, 1024), BF16)] + lrows,
+    )(live_count, second, prior, early, *w2)
+
+    def route(*refs):
+        route_y_kernel(*refs[:4], *refs[5:])
+
+    ya, yb = call(
+        route, "route_y", [VMEM] * 4 + [pl.BlockSpec(memory_space=pl.ANY)], [shape(21, 384)] * 2
+    )(spot, mid, x_low, x_high, ends_stay)
     ra, rb = both_pairs(ya, yb, "gy")
-    zu, zd, up2, dn2, own_low, own_high, carried = call(
-        near_kernel, "scatter_near", [VMEM] * 2 + [VMEM] * 16,
-        [shape(24, 384)] * 2 + [shape(2, 256)] * 4 + [shape(21, 8, 128)],
-        [((176, 256), BF16)] * 2 + [((128, 256), BF16)] + lrows
-        + [((21, 8, 128), F32), ((14, 8, 128), F32)] + [((16, 768), BF16)] * 4,
-    )(
-        live_count, spot, mid, x_low, x_high, ra, rb, stayed, send,
-        static_low, static_high, fractions, centers, deform, *w,
-    )
+    zu, zd, up2, dn2, own_low, own_high, final = call(
+        near_kernel, "scatter_near", [VMEM] * 10,
+        [shape(24, 384)] * 2 + [shape(2, 256)] * 4 + [shape(21, 256)],
+        lrows + [((21, 8, 128), F32), ((14, 8, 128), F32)] + [((16, 1024), BF16)] * 4,
+    )(spot, mid, x_low, x_high, ra, rb, both, far, arrive, ends_stay)
     z_low, z_high = both_ways(zu, zd, "gz")
     low2, high2 = both_ways(up2, dn2, "gz", 2)
-    h, hb, ya, yb, bf = call(
-        second_kernel, "scatter_second", [VMEM] * 2 + [VMEM] * 16,
-        [shape(144, 128), shape(8, 256), shape(48, 128), shape(48, 128), shape(9, 8, 128)],
-        [((176, 768), BF16)] * 2 + [((128, 768), BF16)] + lrows + [((144, 128), F32)],
+    h, hb, ya, yb = call(
+        second_kernel, "scatter_second", [VMEM] * 15,
+        [shape(144, 128), shape(8, 256), shape(48, 128), shape(48, 128)],
+        lrows + [((21, 8, 128), F32), ((144, 128), F32)],
     )(
-        live_count, spot, carried, z_low, z_high, low2, high2, own_low, own_high, send,
-        fractions, centers, deform, next_affine, *w,
-    )
+        spot, z_low, z_high, low2, high2, own_low, own_high, final, arrive, *wa,
+        core_stay, ends_stay,
+    )
+    (bf,) = call(
+        deform_kernel, "deform_second", [VMEM] * 7, [shape(9, 8, 128)],
+        [((80, 1024), BF16)] * 2 + [((128, 1024), BF16)],
+    )(live_count, stayed, z_low, z_high, final, send, next_affine)
     h, hb, low, high = fold(3, h, hb, ya, yb)
     (result,) = call(
-        functools.partial(gather_second_kernel, extents), "gather_second",
-        [VMEM, VMEM] + [VMEM] * 14,
+        functools.partial(gather_second_kernel, extents), "gather_second", [VMEM] * 14,
         [shape(21, 1024)],
         [((144, 128), F32)] + gscratch + [((21, 8, 128), F32)],
-    )(live_count, spot, h, hb, low, high, fractions, centers, deform, bf, *w, mass_core, mass_halo)
+    )(live_count, spot, h, hb, low, high, early, bf, *w2, mass_core, mass_halo)
     return result
 
 

time: 116 us -> 112 us (0.966)
  the two profiles are of different devices: /device:TPU:64 before, /device:TPU:105 now
where the time goes in v5:
time: 112 us; the launch traced here: 111 us
  starting transfers between devices  74.1 us (66%)
  waiting for transfers between devices  22 us (20%)
  Pallas kernels  13.3 us (12%)
  local copies, waits for them, and re-layouts  1.52 us (1%)
    ppermute x5, starting transfers between devices, both_ways(): low = lax.ppermute(up, axis, [(i, i + step) for i in range(count - step)])  24 us
    ppermute x5, waiting for transfers between devices, both_ways(): lax.ppermute(down, axis, [(i + step, i) for i in range(count - step)])  13.7 us
    ppermute x3, starting transfers between devices, both_pairs(): rb = lax.ppermute(second, axis, b) if b else jnp.zeros_like(second)  13.6 us
    ppermute x1, starting transfers between devices, body(): lax.ppermute(both, 'gz', [(i, i ^ 1) for i in range(count) if i ^ 1 < cou...  12.7 us
    ppermute x3, starting transfers between devices, both_pairs(): ra = lax.ppermute(first, axis, a)  11.5 us
    ppermute x5, starting transfers between devices, both_ways(): lax.ppermute(down, axis, [(i + step, i) for i in range(count - step)])  9.1 us
    ppermute x3, waiting for transfers between devices, both_pairs(): rb = lax.ppermute(second, axis, b) if b else jnp.zeros_like(second)  6.7 us
    pallas_call x1, Pallas kernels, body(): call(first_kernel, 'scatter_first', [VMEM] + [HBM] * 8, [shape(240, 128),...  3.24 us
  transfers between devices with their start and end apart: 18, of which 9 were waited for; matrix products, arithmetic and copies ran while one was open for 0% of the time, Pallas kernels for 4%

profile of v5, /device:TPU:105, one launch (start us, length us, event | category | flops | bytes accessed | tf_op | source)
XLA Modules:
  0.0 111.3 jit_solution(8956424193260029501)
XLA Ops:
  0.0 0.1 stack.23
  0.1 0.1 broadcast_in_dim.2.spot.refs_0_
  0.2 3.2 %scatter_first.1 = (f32[240,128]{1,0:T(8,128)S(1)}, f32[8,256]{1,0:T(8,128)S(1)}, f32[32,384]{1,0:T(8,128)S(1)}, f32[9,8,128]{2,1,0:T(8,128)S(1)}, bf16[144,1024...) custom-call(s32[8,128]{1,0:T(8,128)S(1)} %broadcast_in_dim.2.spot.re, ...), custom_call_target="tpu_custom_call" | custom-call | tf_op jit(solution)/shard_map/scatter_first/pallas_call | solution.py:773
  3.4 12.7 %collective-permute-start = (f32[32,384]{1,0:T(8,128)S(1)}, f32[32,384]{1,0:T(8,128)S(1)}, u32[]{:S(2)}, u32[]{:S(2)}) collective-permute-start(f32[32,384]{1,0:T(8,128)S(1)} %get-tuple-element.61), channel_id=1, source_target_pairs={{0,1},{1,0},{2,3},{3,2},{4,5},{5,4},{6,7},{7,6},{8,9},{9,8},{10,11... | collective-permute-start | bytes 147464 | tf_op jit(solution)/shard_map/ppermute | solution.py:781
  16.2 1.6 %collective-permute-done.refs_3_.both = f32[32,384]{1,0:T(8,128)S(1)} collective-permute-done((f32[32,384]{1,0:T(8,128)S(1)}, f32[32,384]{1,0:T(8,128)S(1)}, u32[]{:S(2)}, u32[]{:S(2)}) %collective-permute-start) | collective-permute-done | bytes 49184 | tf_op jit(solution)/shard_map/ppermute | solution.py:781
  17.7 3.2 %collective-permute-start.1 = (f32[16,384]{1,0:T(8,128)S(1)}, f32[16,384]{1,0:T(8,128)S(1)}, u32[]{:S(2)}, u32[]{:S(2)}) collective-permute-start(f32[16,384]{1,0:T(8,128)S(1)} %slice.4), channel_id=1, source_target_pairs={{0,2},{2,4},{4,6},{3,1},{5,3},{7,5},{8,10},{10,12},{12,14},{11,9},... | collective-permute-start | bytes 73736 | tf_op jit(solution)/shard_map/ppermute | solution.py:783
  20.9 1.7 %weights_second.1 = (bf16[144,1024]{1,0:T(8,128)(2,1)S(1)}, bf16[144,1024]{1,0:T(8,128)(2,1)S(1)}, bf16[144,1024]{1,0:T(8,128)(2,1)S(1)}, bf16[144,1024]{1,0:T(8...) custom-call(f32[112,128]{1,0:T(8,128)S(1)} %get-tuple-element.62.ear, ...), custom_call_target="tpu_custom_call" | custom-call | tf_op jit(solution)/shard_map/weights_second/pallas_call | solution.py:787
  22.7 0.0 collective-permute-done.1.refs_4_.far
  22.7 0.3 fold_z5.1
  23.0 5.5 %collective-permute-start.2 = (f32[72,128]{1,0:T(8,128)S(1)}, f32[72,128]{1,0:T(8,128)S(1)}, u32[]{:S(2)}, u32[]{:S(2)}) collective-permute-start(f32[72,128]{1,0:T(8,128)S(1)} %get-tuple-element.67), channel_id=1, source_target_pairs={{0,8},{8,0},{16,24},{24,16},{32,40},{40,32},{48,56},{56,48},{64,72... | collective-permute-start | bytes 110600 | tf_op jit(solution)/shard_map/ppermute | solution.py:729
  28.5 4.6 %collective-permute-start.3 = (f32[72,128]{1,0:T(8,128)S(1)}, f32[72,128]{1,0:T(8,128)S(1)}, u32[]{:S(2)}, u32[]{:S(2)}) collective-permute-start(f32[72,128]{1,0:T(8,128)S(1)} %get-tuple-element.68), channel_id=1, source_target_pairs={{8,16},{16,8},{24,32},{32,24},{40,48},{48,40},{56,64},{64,56},{72,... | collective-permute-start | bytes 110600 | tf_op jit(solution)/shard_map/ppermute | solution.py:730
  33.1 1.9 %collective-permute-done.3.rb = f32[72,128]{1,0:T(8,128)S(1)} collective-permute-done((f32[72,128]{1,0:T(8,128)S(1)}, f32[72,128]{1,0:T(8,128)S(1)}, u32[]{:S(2)}, u32[]{:S(2)}) %collective-permute-start.3) | collective-permute-done | bytes 36896 | tf_op jit(solution)/shard_map/ppermute | solution.py:730
  35.0 0.1 fold_y5.1
  35.1 3.1 %collective-permute-start.4 = (f32[88,128]{1,0:T(8,128)S(1)}, f32[88,128]{1,0:T(8,128)S(1)}, u32[]{:S(2)}, u32[]{:S(2)}) collective-permute-start(f32[88,128]{1,0:T(8,128)S(1)} %get-tuple-element.71), channel_id=1, source_target_pairs={{0,128},{128,256},{256,384},{1,129},{129,257},{257,385},{2,130},{1... | collective-permute-start | bytes 135176 | tf_op jit(solution)/shard_map/ppermute | solution.py:720
  38.2 0.0 copy-start.4
  38.2 1.3 %collective-permute-start.5 = (f32[88,128]{1,0:T(8,128)S(1)}, f32[88,128]{1,0:T(8,128)S(1)}, u32[]{:S(2)}, u32[]{:S(2)}) collective-permute-start(f32[88,128]{1,0:T(8,128)S(1)} %get-tuple-element.72), channel_id=1, source_target_pairs={{128,0},{256,128},{384,256},{129,1},{257,129},{385,257},{130,2},{2... | collective-permute-start | bytes 135176 | tf_op jit(solution)/shard_map/ppermute | solution.py:721
  39.5 0.2 fill_pick.1.pick
  39.7 0.0 collective-permute-done.4.from_low
  39.7 3.3 %collective-permute-done.5.from_high = f32[88,128]{1,0:T(8,128)S(1)} collective-permute-done((f32[88,128]{1,0:T(8,128)S(1)}, f32[88,128]{1,0:T(8,128)S(1)}, u32[]{:S(2)}, u32[]{:S(2)}) %collective-permute-start.5) | collective-permute-done | bytes 45088 | tf_op jit(solution)/shard_map/ppermute | solution.py:721
  43.0 0.7 copy-done.2
  43.7 1.5 %gather_first.1 = (f32[21,8,128]{2,1,0:T(8,128)S(1)}, f32[21,384]{1,0:T(8,128)S(1)}, f32[21,384]{1,0:T(8,128)S(1)}, f32[21,384]{1,0:T(8,128)S(1)}, f32[48,128]{1,0:T(8,128)S(1)}, /*index=5*/f32[8,256]{1,0:T(8,128)S(1)}) custom-call(s32[1,2]{1,0:T(1,128)S(1)} %copy-done.2, s32[8,128]{1,0:T(8,128)S(1)} %broadcast_in_dim.2.spot.refs_0_, ...), custom_call_target="tpu_custom_call" | custom-call | tf_op jit(solution)/shard_map/gather_first/pallas_call | solution.py:801
  45.2 3.1 %collective-permute-start.6 = (f32[21,384]{1,0:T(8,128)S(1)}, f32[21,384]{1,0:T(8,128)S(1)}, u32[]{:S(2)}, u32[]{:S(2)}) collective-permute-start(f32[21,384]{1,0:T(8,128)S(1)} %get-tuple-element.80), channel_id=1, source_target_pairs={{0,128},{128,256},{256,384},{1,129},{129,257},{257,385},{2,130},{1... | collective-permute-start | bytes 96776 | tf_op jit(solution)/shard_map/ppermute | solution.py:720
  48.3 1.3 %collective-permute-start.7 = (f32[21,384]{1,0:T(8,128)S(1)}, f32[21,384]{1,0:T(8,128)S(1)}, u32[]{:S(2)}, u32[]{:S(2)}) collective-permute-start(f32[21,384]{1,0:T(8,128)S(1)} %get-tuple-element.81), channel_id=1, source_target_pairs={{128,0},{256,128},{384,256},{129,1},{257,129},{385,257},{130,2},{2... | collective-permute-start | bytes 96776 | tf_op jit(solution)/shard_map/ppermute | solution.py:721
  49.6 0.0 copy-start.3
  49.6 0.7 copy-done.3
  50.3 1.7 %stay.1 = (f32[21,8,128]{2,1,0:T(8,128)S(1)}, f32[144,128]{1,0:T(8,128)S(1)}, f32[16,144]{1,0:T(8,128)S(1)}) custom-call(s32[1,2]{1,0:T(1,128)S(1)} %copy-done.2, f32[21,8,128]{2,1,0:T(8,128)S(1)} %get-tuple-element.82.second, s32[8,128]{1,0:T(8,128)S(1)} %bitcast.14, f32[112,128]{1,0:T(8,128)S(1)} %get-tuple-element.62.early, ...), custom_call_target="tpu_custom_call" | custom-call | tf_op jit(solution)/shard_map/stay/pallas_call | solution.py:808
  52.1 0.9 collective-permute-done.7.refs_3_.x_high
  53.0 3.6 %collective-permute-start.8 = (f32[21,384]{1,0:T(8,128)S(1)}, f32[21,384]{1,0:T(8,128)S(1)}, u32[]{:S(2)}, u32[]{:S(2)}) collective-permute-start(f32[21,384]{1,0:T(8,128)S(1)} %get-tuple-element.88), channel_id=1, source_target_pairs={{0,8},{8,0},{16,24},{24,16},{32,40},{40,32},{48,56},{56,48},{64,72... | collective-permute-start | bytes 96776 | tf_op jit(solution)/shard_map/ppermute | solution.py:729
  56.6 5.9 %collective-permute-start.9 = (f32[21,384]{1,0:T(8,128)S(1)}, f32[21,384]{1,0:T(8,128)S(1)}, u32[]{:S(2)}, u32[]{:S(2)}) collective-permute-start(f32[21,384]{1,0:T(8,128)S(1)} %get-tuple-element.89), channel_id=1, source_target_pairs={{8,16},{16,8},{24,32},{32,24},{40,48},{48,40},{56,64},{64,56},{72,... | collective-permute-start | bytes 96776 | tf_op jit(solution)/shard_map/ppermute | solution.py:730
  62.5 1.6 %collective-permute-done.9.rb = f32[21,384]{1,0:T(8,128)S(1)} collective-permute-done((f32[21,384]{1,0:T(8,128)S(1)}, f32[21,384]{1,0:T(8,128)S(1)}, u32[]{:S(2)}, u32[]{:S(2)}) %collective-permute-start.9) | collective-permute-done | bytes 32288 | tf_op jit(solution)/shard_map/ppermute | solution.py:730
  64.1 1.0 scatter_near.1
  65.2 11.7 %collective-permute-start.10 = (f32[24,384]{1,0:T(8,128)S(1)}, f32[24,384]{1,0:T(8,128)S(1)}, u32[]{:S(2)}, u32[]{:S(2)}) collective-permute-start(f32[24,384]{1,0:T(8,128)S(1)} %get-tuple-element.90), channel_id=1, source_target_pairs={{0,1},{1,2},{2,3},{3,4},{4,5},{5,6},{6,7},{8,9},{9,10},{10,11},{11... | collective-permute-start | bytes 110600 | tf_op jit(solution)/shard_map/ppermute | solution.py:720
  76.9 3.2 %collective-permute-start.11 = (f32[24,384]{1,0:T(8,128)S(1)}, f32[24,384]{1,0:T(8,128)S(1)}, u32[]{:S(2)}, u32[]{:S(2)}) collective-permute-start(f32[24,384]{1,0:T(8,128)S(1)} %get-tuple-element.91), channel_id=1, source_target_pairs={{1,0},{2,1},{3,2},{4,3},{5,4},{6,5},{7,6},{9,8},{10,9},{11,10},{12... | collective-permute-start | bytes 110600 | tf_op jit(solution)/shard_map/ppermute | solution.py:721
  80.1 3.2 %collective-permute-start.12 = (f32[2,256]{1,0:T(2,128)S(1)}, f32[2,256]{1,0:T(2,128)S(1)}, u32[]{:S(2)}, u32[]{:S(2)}) collective-permute-start(f32[2,256]{1,0:T(2,128)S(1)} %get-tuple-element.92), channel_id=1, source_target_pairs={{0,2},{1,3},{2,4},{3,5},{4,6},{5,7},{8,10},{9,11},{10,12},{11,13},... | collective-permute-start | bytes 6152 | tf_op jit(solution)/shard_map/ppermute | solution.py:720
  83.3 2.1 %collective-permute-start.13 = (f32[2,256]{1,0:T(2,128)S(1)}, f32[2,256]{1,0:T(2,128)S(1)}, u32[]{:S(2)}, u32[]{:S(2)}) collective-permute-start(f32[2,256]{1,0:T(2,128)S(1)} %get-tuple-element.93), channel_id=1, source_target_pairs={{2,0},{3,1},{4,2},{5,3},{6,4},{7,5},{10,8},{11,9},{12,10},{13,11},... | collective-permute-start | bytes 6152 | tf_op jit(solution)/shard_map/ppermute | solution.py:721
  85.4 2.5 %collective-permute-done.13.high2 = f32[2,256]{1,0:T(2,128)S(1)} collective-permute-done((f32[2,256]{1,0:T(2,128)S(1)}, f32[2,256]{1,0:T(2,128)S(1)}, u32[]{:S(2)}, u32[]{:S(2)}) %collective-permute-start.13) | collective-permute-done | bytes 2080 | tf_op jit(solution)/shard_map/ppermute | solution.py:721
  87.9 4.1 %collective-permute-done.11.z_high = f32[24,384]{1,0:T(8,128)S(1)} collective-permute-done((f32[24,384]{1,0:T(8,128)S(1)}, f32[24,384]{1,0:T(8,128)S(1)}, u32[]{:S(2)}, u32[]{:S(2)}) %collective-permute-start.11) | collective-permute-done | bytes 36896 | tf_op jit(solution)/shard_map/ppermute | solution.py:721
  92.0 1.3 %scatter_second.1 = (f32[144,128]{1,0:T(8,128)S(1)}, f32[8,256]{1,0:T(8,128)S(1)}, f32[48,128]{1,0:T(8,128)S(1)}, f32[48,128]{1,0:T(8,128)S(1)}) custom-call(s32[8,128]{1,0:T(8,128)S(1)} %broadcast_in_dim.2.spot.refs_0_, f32[24,384]{1,0:T(8,128)S(1)} %collective-permute-done.10.z_low, f32[24,384]{1,0:T(8,128)S(1)} %collective-permute-done.11.z_high, ...), custom_call_target="tpu_custom_call" | custom-call | tf_op jit(solution)/shard_map/scatter_second/pallas_call | solution.py:828
  93.4 0.0 copy-start
  93.4 2.4 %collective-permute-start.14 = (f32[48,128]{1,0:T(8,128)S(1)}, f32[48,128]{1,0:T(8,128)S(1)}, u32[]{:S(2)}, u32[]{:S(2)}) collective-permute-start(f32[48,128]{1,0:T(8,128)S(1)} %get-tuple-element.104), channel_id=1, source_target_pairs={{0,8},{8,0},{16,24},{24,16},{32,40},{40,32},{48,56},{56,48},{64,72... | collective-permute-start | bytes 73736 | tf_op jit(solution)/shard_map/ppermute | solution.py:729
  95.9 3.1 %collective-permute-start.15 = (f32[48,128]{1,0:T(8,128)S(1)}, f32[48,128]{1,0:T(8,128)S(1)}, u32[]{:S(2)}, u32[]{:S(2)}) collective-permute-start(f32[48,128]{1,0:T(8,128)S(1)} %get-tuple-element.105), channel_id=1, source_target_pairs={{8,16},{16,8},{24,32},{32,24},{40,48},{48,40},{56,64},{64,56},{72,... | collective-permute-start | bytes 73736 | tf_op jit(solution)/shard_map/ppermute | solution.py:730
  99.0 3.2 %collective-permute-done.15.rb = f32[48,128]{1,0:T(8,128)S(1)} collective-permute-done((f32[48,128]{1,0:T(8,128)S(1)}, f32[48,128]{1,0:T(8,128)S(1)}, u32[]{:S(2)}, u32[]{:S(2)}) %collective-permute-start.15) | collective-permute-done | bytes 24608 | tf_op jit(solution)/shard_map/ppermute | solution.py:730
  102.2 0.1 fold_y3.1
  102.3 2.8 %collective-permute-start.16 = (f32[56,128]{1,0:T(8,128)S(1)}, f32[56,128]{1,0:T(8,128)S(1)}, u32[]{:S(2)}, u32[]{:S(2)}) collective-permute-start(f32[56,128]{1,0:T(8,128)S(1)} %get-tuple-element.108), channel_id=1, source_target_pairs={{0,128},{128,256},{256,384},{1,129},{129,257},{257,385},{2,130},{1... | collective-permute-start | bytes 86024 | tf_op jit(solution)/shard_map/ppermute | solution.py:720
  105.1 1.3 %collective-permute-start.17 = (f32[56,128]{1,0:T(8,128)S(1)}, f32[56,128]{1,0:T(8,128)S(1)}, u32[]{:S(2)}, u32[]{:S(2)}) collective-permute-start(f32[56,128]{1,0:T(8,128)S(1)} %get-tuple-element.109), channel_id=1, source_target_pairs={{128,0},{256,128},{384,256},{129,1},{257,129},{385,257},{130,2},{2... | collective-permute-start | bytes 86024 | tf_op jit(solution)/shard_map/ppermute | solution.py:721
  106.4 0.5 deform_second.1.bf
  106.9 2.8 %collective-permute-done.17.from_high = f32[56,128]{1,0:T(8,128)S(1)} collective-permute-done((f32[56,128]{1,0:T(8,128)S(1)}, f32[56,128]{1,0:T(8,128)S(1)}, u32[]{:S(2)}, u32[]{:S(2)}) %collective-permute-start.17) | collective-permute-done | bytes 28704 | tf_op jit(solution)/shard_map/ppermute | solution.py:721
  109.7 1.6 %gather_second.1 = f32[21,1024]{1,0:T(8,128)} custom-call(s32[1,2]{1,0:T(1,128)S(1)} %copy-done.2, s32[8,128]{1,0:T(8,128)S(1)} %broadcast_in_dim.2.spot.refs_0_, f32[144,128]{1,0:T(8,128)S(1)} %get-tuple-element.106.h, f32[8,256]{1,0:T(8,128)S(1)} %get-tuple-element.107.hb, f32[56,128]{1,0:T(8,128)S(1)} %collective-permute-done.16.from_low, ...), custom_call_target="tpu_custom_call" | custom-call | tf_op jit(solution)/shard_map/gather_second/pallas_call | solution.py:841
  (15 shorter events, 0.0 us)
Async XLA Ops:
  3.4 14.3 %collective-permute-start = (f32[32,384]{1,0:T(8,128)S(1)}, f32[32,384]{1,0:T(8,128)S(1)}, u32[]{:S(2)}, u32[]{:S(2)}) collective-permute-start(f32[32,384]{1,0:T(8,128)S(1)} %get-tuple-element.61), channel_id=1, source_target_pairs={{0,1},{1,0},{2,3},{3,2},{4,5},{5,4},{6,7},{7,6},{8,9},{9,8},{10,11... | collective-permute-start | bytes 147464 | tf_op jit(solution)/shard_map/ppermute | solution.py:781
  17.7 5.0 %collective-permute-start.1 = (f32[16,384]{1,0:T(8,128)S(1)}, f32[16,384]{1,0:T(8,128)S(1)}, u32[]{:S(2)}, u32[]{:S(2)}) collective-permute-start(f32[16,384]{1,0:T(8,128)S(1)} %slice.4), channel_id=1, source_target_pairs={{0,2},{2,4},{4,6},{3,1},{5,3},{7,5},{8,10},{10,12},{12,14},{11,9},... | collective-permute-start | bytes 73736 | tf_op jit(solution)/shard_map/ppermute | solution.py:783
  23.0 10.1 %collective-permute-start.2 = (f32[72,128]{1,0:T(8,128)S(1)}, f32[72,128]{1,0:T(8,128)S(1)}, u32[]{:S(2)}, u32[]{:S(2)}) collective-permute-start(f32[72,128]{1,0:T(8,128)S(1)} %get-tuple-element.67), channel_id=1, source_target_pairs={{0,8},{8,0},{16,24},{24,16},{32,40},{40,32},{48,56},{56,48},{64,72... | collective-permute-start | bytes 110600 | tf_op jit(solution)/shard_map/ppermute | solution.py:729
  28.5 6.5 %collective-permute-start.3 = (f32[72,128]{1,0:T(8,128)S(1)}, f32[72,128]{1,0:T(8,128)S(1)}, u32[]{:S(2)}, u32[]{:S(2)}) collective-permute-start(f32[72,128]{1,0:T(8,128)S(1)} %get-tuple-element.68), channel_id=1, source_target_pairs={{8,16},{16,8},{24,32},{32,24},{40,48},{48,40},{56,64},{64,56},{72,... | collective-permute-start | bytes 110600 | tf_op jit(solution)/shard_map/ppermute | solution.py:730
  35.0 4.5 %copy-start.1 = (s32[1,26,32]{2,0,1:T(1,128)S(1)}, s32[1,26,32]{2,0,1:T(1,128)}, u32[]{:S(2)}) copy-start(s32[1,26,32]{2,0,1:T(1,128)} %param.19) | copy-start | bytes 9988
  35.1 4.6 %collective-permute-start.4 = (f32[88,128]{1,0:T(8,128)S(1)}, f32[88,128]{1,0:T(8,128)S(1)}, u32[]{:S(2)}, u32[]{:S(2)}) collective-permute-start(f32[88,128]{1,0:T(8,128)S(1)} %get-tuple-element.71), channel_id=1, source_target_pairs={{0,128},{128,256},{256,384},{1,129},{129,257},{257,385},{2,130},{1... | collective-permute-start | bytes 135176 | tf_op jit(solution)/shard_map/ppermute | solution.py:720
  38.2 1.3 %copy-start.4 = (s32[1,26]{1,0:T(1,128)S(1)}, s32[1,26]{1,0:T(1,128)}, u32[]{:S(2)}) copy-start(s32[1,26]{1,0:T(1,128)} %counts.1) | copy-start | bytes 316
  38.2 4.8 %collective-permute-start.5 = (f32[88,128]{1,0:T(8,128)S(1)}, f32[88,128]{1,0:T(8,128)S(1)}, u32[]{:S(2)}, u32[]{:S(2)}) collective-permute-start(f32[88,128]{1,0:T(8,128)S(1)} %get-tuple-element.72), channel_id=1, source_target_pairs={{128,0},{256,128},{384,256},{129,1},{257,129},{385,257},{130,2},{2... | collective-permute-start | bytes 135176 | tf_op jit(solution)/shard_map/ppermute | solution.py:721
  43.0 0.7 copy-start.2
  45.2 6.9 %collective-permute-start.6 = (f32[21,384]{1,0:T(8,128)S(1)}, f32[21,384]{1,0:T(8,128)S(1)}, u32[]{:S(2)}, u32[]{:S(2)}) collective-permute-start(f32[21,384]{1,0:T(8,128)S(1)} %get-tuple-element.80), channel_id=1, source_target_pairs={{0,128},{128,256},{256,384},{1,129},{129,257},{257,385},{2,130},{1... | collective-permute-start | bytes 96776 | tf_op jit(solution)/shard_map/ppermute | solution.py:720
  48.3 4.7 %collective-permute-start.7 = (f32[21,384]{1,0:T(8,128)S(1)}, f32[21,384]{1,0:T(8,128)S(1)}, u32[]{:S(2)}, u32[]{:S(2)}) collective-permute-start(f32[21,384]{1,0:T(8,128)S(1)} %get-tuple-element.81), channel_id=1, source_target_pairs={{128,0},{256,128},{384,256},{129,1},{257,129},{385,257},{130,2},{2... | collective-permute-start | bytes 96776 | tf_op jit(solution)/shard_map/ppermute | solution.py:721
  49.6 0.7 copy-start.3
  53.0 9.5 %collective-permute-start.8 = (f32[21,384]{1,0:T(8,128)S(1)}, f32[21,384]{1,0:T(8,128)S(1)}, u32[]{:S(2)}, u32[]{:S(2)}) collective-permute-start(f32[21,384]{1,0:T(8,128)S(1)} %get-tuple-element.88), channel_id=1, source_target_pairs={{0,8},{8,0},{16,24},{24,16},{32,40},{40,32},{48,56},{56,48},{64,72... | collective-permute-start | bytes 96776 | tf_op jit(solution)/shard_map/ppermute | solution.py:729
  56.6 7.5 %collective-permute-start.9 = (f32[21,384]{1,0:T(8,128)S(1)}, f32[21,384]{1,0:T(8,128)S(1)}, u32[]{:S(2)}, u32[]{:S(2)}) collective-permute-start(f32[21,384]{1,0:T(8,128)S(1)} %get-tuple-element.89), channel_id=1, source_target_pairs={{8,16},{16,8},{24,32},{32,24},{40,48},{48,40},{56,64},{64,56},{72,... | collective-permute-start | bytes 96776 | tf_op jit(solution)/shard_map/ppermute | solution.py:730
  65.2 22.8 %collective-permute-start.10 = (f32[24,384]{1,0:T(8,128)S(1)}, f32[24,384]{1,0:T(8,128)S(1)}, u32[]{:S(2)}, u32[]{:S(2)}) collective-permute-start(f32[24,384]{1,0:T(8,128)S(1)} %get-tuple-element.90), channel_id=1, source_target_pairs={{0,1},{1,2},{2,3},{3,4},{4,5},{5,6},{6,7},{8,9},{9,10},{10,11},{11... | collective-permute-start | bytes 110600 | tf_op jit(solution)/shard_map/ppermute | solution.py:720
  76.9 15.1 %collective-permute-start.11 = (f32[24,384]{1,0:T(8,128)S(1)}, f32[24,384]{1,0:T(8,128)S(1)}, u32[]{:S(2)}, u32[]{:S(2)}) collective-permute-start(f32[24,384]{1,0:T(8,128)S(1)} %get-tuple-element.91), channel_id=1, source_target_pairs={{1,0},{2,1},{3,2},{4,3},{5,4},{6,5},{7,6},{9,8},{10,9},{11,10},{12... | collective-permute-start | bytes 110600 | tf_op jit(solution)/shard_map/ppermute | solution.py:721
  80.1 5.3 %collective-permute-start.12 = (f32[2,256]{1,0:T(2,128)S(1)}, f32[2,256]{1,0:T(2,128)S(1)}, u32[]{:S(2)}, u32[]{:S(2)}) collective-permute-start(f32[2,256]{1,0:T(2,128)S(1)} %get-tuple-element.92), channel_id=1, source_target_pairs={{0,2},{1,3},{2,4},{3,5},{4,6},{5,7},{8,10},{9,11},{10,12},{11,13},... | collective-permute-start | bytes 6152 | tf_op jit(solution)/shard_map/ppermute | solution.py:720
  83.3 4.6 %collective-permute-start.13 = (f32[2,256]{1,0:T(2,128)S(1)}, f32[2,256]{1,0:T(2,128)S(1)}, u32[]{:S(2)}, u32[]{:S(2)}) collective-permute-start(f32[2,256]{1,0:T(2,128)S(1)} %get-tuple-element.93), channel_id=1, source_target_pairs={{2,0},{3,1},{4,2},{5,3},{6,4},{7,5},{10,8},{11,9},{12,10},{13,11},... | collective-permute-start | bytes 6152 | tf_op jit(solution)/shard_map/ppermute | solution.py:721
  93.4 13.0 %copy-start = (f32[2,9,1024]{2,0,1:T(2,128)S(1)}, f32[2,9,1024]{2,0,1:T(2,128)}, u32[]{:S(2)}) copy-start(f32[2,9,1024]{2,0,1:T(2,128)} %param.14) | copy-start | bytes 221188
  93.4 5.6 %collective-permute-start.14 = (f32[48,128]{1,0:T(8,128)S(1)}, f32[48,128]{1,0:T(8,128)S(1)}, u32[]{:S(2)}, u32[]{:S(2)}) collective-permute-start(f32[48,128]{1,0:T(8,128)S(1)} %get-tuple-element.104), channel_id=1, source_target_pairs={{0,8},{8,0},{16,24},{24,16},{32,40},{40,32},{48,56},{56,48},{64,72... | collective-permute-start | bytes 73736 | tf_op jit(solution)/shard_map/ppermute | solution.py:729
  95.9 6.4 %collective-permute-start.15 = (f32[48,128]{1,0:T(8,128)S(1)}, f32[48,128]{1,0:T(8,128)S(1)}, u32[]{:S(2)}, u32[]{:S(2)}) collective-permute-start(f32[48,128]{1,0:T(8,128)S(1)} %get-tuple-element.105), channel_id=1, source_target_pairs={{8,16},{16,8},{24,32},{32,24},{40,48},{48,40},{56,64},{64,56},{72,... | collective-permute-start | bytes 73736 | tf_op jit(solution)/shard_map/ppermute | solution.py:730
  102.3 4.6 %collective-permute-start.16 = (f32[56,128]{1,0:T(8,128)S(1)}, f32[56,128]{1,0:T(8,128)S(1)}, u32[]{:S(2)}, u32[]{:S(2)}) collective-permute-start(f32[56,128]{1,0:T(8,128)S(1)} %get-tuple-element.108), channel_id=1, source_target_pairs={{0,128},{128,256},{256,384},{1,129},{129,257},{257,385},{2,130},{1... | collective-permute-start | bytes 86024 | tf_op jit(solution)/shard_map/ppermute | solution.py:720
  105.1 4.6 %collective-permute-start.17 = (f32[56,128]{1,0:T(8,128)S(1)}, f32[56,128]{1,0:T(8,128)S(1)}, u32[]{:S(2)}, u32[]{:S(2)}) collective-permute-start(f32[56,128]{1,0:T(8,128)S(1)} %get-tuple-element.109), channel_id=1, source_target_pairs={{128,0},{256,128},{384,256},{129,1},{257,129},{385,257},{130,2},{2... | collective-permute-start | bytes 86024 | tf_op jit(solution)/shard_map/ppermute | solution.py:721

commit v6 on v5

--- a/solution.py
+++ b/solution.py
@@ -271,6 +271,9 @@
     for i, tile in enumerate(frac + [centre.astype(F32)] + deform_now):
         now[i * 8 : i * 8 + 8] = tile
     early[104:112] = jnp.zeros((8, 128), F32)
+    use = in_use(live, 1)
+    now[104:112] = use
+    now[112:120] = in_use(live, 0)
     known = dense(fractions, 0, 3) + [centers[0:1, :].reshape(CHUNKS, 128).astype(F32)]
     for i, tile in enumerate(known + dense(deform, 0, 9)):
         early[i * 8 : i * 8 + 8] = tile
@@ -280,7 +283,6 @@
         dest[0:14, t % 3 * 128 : t % 3 * 128 + 128] = got
 
     static_rows(early, send, range(2, 8), hot, put)
-    use = in_use(live, 1)
     adj = [v * use for v in dense(adjoint, None, 21)]
     a_v, b_c, b_f = transfer(adj, deform_now, dense(affine, 1, 9))
     for i in range(9):
@@ -478,11 +480,10 @@
 
 
 def gather_first_kernel(
-    extents, live, spot, h, hb, from_low, from_high, now, bf, w_hi, w_lo, d_hi, d_lo, pick,
+    extents, spot, h, hb, from_low, from_high, now, bf, w_hi, w_lo, d_hi, d_lo, pick,
     second, xu, xd, mid, mass_core, mass_halo,
     total, g_hi, g_lo, s0, sz, rows12, buf, hot,
 ):
-    which = 1
     halo = x_fold(5, h, hb, from_low, from_high, total)
     mass_core[...] = total[144:192]
     wide = iota((8, 256), 1)
@@ -502,7 +503,7 @@
     )
     frac, (cell_x, cell_y, _), deform = fields(now)
     gather(frac, cell_x, cell_y, g_hi, g_lo, w_hi, w_lo, d_hi, d_lo, s0, sz, rows12)
-    use = in_use(live, which)
+    use = now[104:112]
     out = particle(rows12, frac, [bf[i] for i in range(9)], deform, use)
     for i in range(21):
         second[i] = out[i]
@@ -573,13 +574,13 @@
 
 
 def stay_kernel(
-    live, second, prior, early, w_hi, w_lo, d_hi, d_lo,
+    now, second, prior, early, w_hi, w_lo, d_hi, d_lo,
     stayed, core, ends,
     lh, ll, hot, l0h, l0l, l2h, l2l,
 ):
     tiles = [lambda r, t=t: second[r, t : t + 1, :] for t in range(8)]
     total = carry(tiles, [prior[t : t + 1] for t in range(8)], lh, ll, hot)
-    use = in_use(live, 0)
+    use = now[112:120]
     adj = [total[i * 8 : i * 8 + 8] * use for i in range(21)]
     for i in range(21):
         stayed[i] = adj[i]
@@ -593,8 +594,8 @@
 
 def near_kernel(
     spot, mid, x_low, x_high, ra, rb, both, far, arrive, ends_stay,
-    zu, zd, up2, dn2, own_low, own_high, final,
-    l0h, l0l, l2h, l2l, moved, static, e0, e1, e2, e3,
+    swap, along, against, own_low, own_high, final,
+    l0h, l0l, l2h, l2l, moved, static, e0, e1, e2, e3, zu, zd, up2, dn2,
 ):
     groups = [lane_tile(mid, 1), lane_tile(x_low, 1), lane_tile(x_high, 1)]
     groups += [by_side(spot, lane_tile(rb, i), lane_tile(ra, i)) for i in range(3)]
@@ -631,17 +632,22 @@
     put_planes(dn2, 0, downward[1:2], downward[2:3])
     put_planes(zu, 21, ends[0:1], ends[3:4])
     put_planes(zd, 21, ends[1:2], ends[2:3])
+    swap[0:24] = by_z_side(spot, zu, zd)
+    swap[24:48] = by_z_side(spot, zd, zu)
+    along[...] = by_z_side(spot, up2, dn2)
+    against[...] = by_z_side(spot, dn2, up2)
 
 
 def second_kernel(
-    spot, z_low, z_high, low2, high2, own_low, own_high, final, arrive, a_hi, a_lo, b_hi, b_lo,
+    spot, both, far, against, own_low, own_high, final, arrive, a_hi, a_lo, b_hi, b_lo,
     core_stay, ends_stay,
-    h_out, hb_out, ya, yb,
-    l0h, l0l, l2h, l2l, moved, h,
+    h_out, hb_out, ya, yb, moved,
+    l0h, l0l, l2h, l2l, h,
 ):
     for i in range(3):
-        moved[:, i, :] = lane_tile(z_low, i)[0:21]
-        moved[:, 3 + i, :] = lane_tile(z_high, i)[0:21]
+        near, relayed = lane_tile(both, i)[0:24], lane_tile(far, i)
+        moved[:, i, :] = by_side(spot, relayed, near, 4)[0:21]
+        moved[:, 3 + i, :] = by_side(spot, near, relayed, 4)[0:21]
     for i in range(2):
         moved[:, 6 + i, :] = lane_tile(final, i)
     place = [arrive[i] for i in range(3)]
@@ -653,21 +659,22 @@
     ends = edge_sums(l, w) + ends_stay[...]
     ends = jnp.concatenate([ends[0:8], jnp.zeros((8, 112), F32)], axis=1)
     halo = jnp.where(iota((8, 256), 0) < 2, ends, 0.0)
-    low = z_low[21:23, 0:256] + low2[0:2] + own_low[0:2]
-    high = z_high[21:23, 0:256] + high2[0:2] + own_high[0:2]
+    near, relayed = both[21:23, 0:256] + against[0:2], far[21:23, 0:256]
+    low = by_z_side(spot, relayed, near) + own_low[0:2]
+    high = by_z_side(spot, near, relayed) + own_high[0:2]
     z_fold(3, spot, h, halo, low, high, h_out, hb_out, ya, yb)
 
 
-def deform_kernel(live, stayed, z_low, z_high, final, send, affine, bf_out, lh, ll, hot):
-    tiles = []
-    for ref, count in ((z_low, 3), (z_high, 3), (final, 2)):
-        for t in range(count):
-            tiles.append(
-                lambda r, ref=ref, t=t: ref[12 + r : 13 + r, t * 128 : t * 128 + 128]
-            )
+def relay_kernel(both, along, _, out):
+    out[...] = both[24:48]
+    out[21:23, 0:256] = both[45:47, 0:256] + along[0:2]
+
+
+def deform_kernel(now, stayed, moved, send, affine, bf_out, lh, ll, hot):
+    tiles = [lambda r, t=t: moved[12 + r, t : t + 1, :] for t in range(8)]
     rows = [send[t : t + 1] for t in (2, 3, 4, 5, 6, 7, 0, 1)]
     total = carry(tiles, rows, lh, ll, hot, 9)
-    use = in_use(live, 0)
+    use = now[112:120]
     a_f = [(stayed[12 + i] + total[i * 8 : i * 8 + 8]) * use for i in range(9)]
     k = dense(affine, 0, 9)
     for i in range(3):
@@ -678,12 +685,11 @@
 
 
 def gather_second_kernel(
-    extents, live, spot, h, hb, from_low, from_high, early, bf, w_hi, w_lo, d_hi, d_lo,
+    extents, spot, h, hb, from_low, from_high, now, early, bf, w_hi, w_lo, d_hi, d_lo,
     mass_core, mass_halo,
     result,
     total, g_hi, g_lo, s0, sz, rows12, packed,
 ):
-    which = 0
     halo = x_fold(3, h, hb, from_low, from_high, total)
     node_values(
         spot, extents, total, halo,
@@ -691,7 +697,7 @@
     )
     frac, (cell_x, cell_y, _), deform = fields(early)
     gather(frac, cell_x, cell_y, g_hi, g_lo, w_hi, w_lo, d_hi, d_lo, s0, sz, rows12)
-    use = in_use(live, which)
+    use = now[112:120]
     out = particle(rows12, frac, [bf[i] for i in range(9)], deform, use)
     for i in range(21):
         packed[i] = out[i]
@@ -773,14 +779,15 @@
     h, hb, both, bf, *w, send, now, early = call(
         first_kernel, "scatter_first", [VMEM] + [HBM] * 8,
         [shape(240, 128), shape(8, 256), shape(32, 384), shape(9, 8, 128)]
-        + weights + [shape(8, 128, dtype=I32), shape(104, 128), shape(112, 128)],
+        + weights + [shape(8, 128, dtype=I32), shape(120, 128), shape(112, 128)],
         lrows + [((128, 128), BF16), ((16, 384), F32), ((16, 384), F32)]
         + [(v.shape, v.dtype) for v in firsts] + [pltpu.SemaphoreType.DMA((8,))],
     )(spot, *(pltpu.with_memory_space_constraint(v, pltpu.HBM) for v in firsts))
     count = lax.axis_size("gz")
-    both = lax.ppermute(both, "gz", [(i, i ^ 1) for i in range(count) if i ^ 1 < count])
+    pairs = [(i, i ^ 1) for i in range(count) if i ^ 1 < count]
     hop = [(i, i + 2) for i in range(0, count - 2, 2)] + [(i, i - 2) for i in range(3, count, 2)]
-    far = lax.ppermute(both[16:32], "gz", hop) if hop else jnp.zeros_like(both[16:32])
+    both = lax.ppermute(both, "gz", pairs)
+    far = lax.ppermute(both[16:32], "gz", hop)
     (pick,) = call(pick_kernel, "fill_pick", [VMEM, VMEM], [shape(9, 128, dtype=I32)])(
         receive_count, slots_out
     )
@@ -799,17 +806,17 @@
     )(spot, h, hb, both, far, arrive)
     h, hb, low, high = fold(5, h, hb, ya, yb)
     second, xu, xd, mid, mass_core, mass_halo = call(
-        functools.partial(gather_first_kernel, extents), "gather_first", [VMEM] * 13,
+        functools.partial(gather_first_kernel, extents), "gather_first", [VMEM] * 12,
         [shape(21, 8, 128), shape(21, 384), shape(21, 384), shape(21, 384), shape(48, 128), shape(8, 256)],
         [((240, 128), F32)] + gscratch + [((176, 128), F32), ((128, 128), BF16)],
-    )(live_count, spot, h, hb, low, high, now, bf, *w, pick)
+    )(spot, h, hb, low, high, now, bf, *w, pick)
 
     x_low, x_high = both_ways(xu, xd, "gx")
     stayed, core_stay, ends_stay = call(
         stay_kernel, "stay", [VMEM] * 8,
         [shape(21, 8, 128), shape(144, 128), shape(16, 144)],
         [((176, 1024), BF16)] * 2 + [((128, 1024), BF16)] + lrows,
-    )(live_count, second, prior, early, *w2)
+    )(now, second, prior, early, *w2)
 
     def route(*refs):
         route_y_kernel(*refs[:4], *refs[5:])
@@ -818,31 +825,35 @@
         route, "route_y", [VMEM] * 4 + [pl.BlockSpec(memory_space=pl.ANY)], [shape(21, 384)] * 2
     )(spot, mid, x_low, x_high, ends_stay)
     ra, rb = both_pairs(ya, yb, "gy")
-    zu, zd, up2, dn2, own_low, own_high, final = call(
+    swap, along, against, own_low, own_high, final = call(
         near_kernel, "scatter_near", [VMEM] * 10,
-        [shape(24, 384)] * 2 + [shape(2, 256)] * 4 + [shape(21, 256)],
-        lrows + [((21, 8, 128), F32), ((14, 8, 128), F32)] + [((16, 1024), BF16)] * 4,
+        [shape(48, 384)] + [shape(2, 256)] * 4 + [shape(21, 256)],
+        lrows + [((21, 8, 128), F32), ((14, 8, 128), F32)] + [((16, 1024), BF16)] * 4
+        + [((24, 384), F32)] * 2 + [((2, 256), F32)] * 2,
     )(spot, mid, x_low, x_high, ra, rb, both, far, arrive, ends_stay)
-    z_low, z_high = both_ways(zu, zd, "gz")
-    low2, high2 = both_ways(up2, dn2, "gz", 2)
-    h, hb, ya, yb = call(
-        second_kernel, "scatter_second", [VMEM] * 15,
-        [shape(144, 128), shape(8, 256), shape(48, 128), shape(48, 128)],
-        lrows + [((21, 8, 128), F32), ((144, 128), F32)],
+    both = lax.ppermute(swap, "gz", pairs)
+    against = lax.ppermute(against, "gz", [(b, a) for a, b in hop])
+    (far,) = call(
+        relay_kernel, "relay", [VMEM] * 2 + [pl.BlockSpec(memory_space=pl.ANY)], [shape(24, 384)]
+    )(both, along, against)
+    far = lax.ppermute(far, "gz", hop)
+    h, hb, ya, yb, moved = call(
+        second_kernel, "scatter_second", [VMEM] * 14,
+        [shape(144, 128), shape(8, 256), shape(48, 128), shape(48, 128), shape(21, 8, 128)],
+        lrows + [((144, 128), F32)],
     )(
-        spot, z_low, z_high, low2, high2, own_low, own_high, final, arrive, *wa,
-        core_stay, ends_stay,
+        spot, both, far, against, own_low, own_high, final, arrive, *wa, core_stay, ends_stay
     )
     (bf,) = call(
-        deform_kernel, "deform_second", [VMEM] * 7, [shape(9, 8, 128)],
+        deform_kernel, "deform_second", [VMEM] * 5, [shape(9, 8, 128)],
         [((80, 1024), BF16)] * 2 + [((128, 1024), BF16)],
-    )(live_count, stayed, z_low, z_high, final, send, next_affine)
+    )(now, stayed, moved, send, next_affine)
     h, hb, low, high = fold(3, h, hb, ya, yb)
     (result,) = call(
         functools.partial(gather_second_kernel, extents), "gather_second", [VMEM] * 14,
         [shape(21, 1024)],
         [((144, 128), F32)] + gscratch + [((21, 8, 128), F32)],
-    )(live_count, spot, h, hb, low, high, early, bf, *w2, mass_core, mass_halo)
+    )(spot, h, hb, low, high, now, early, bf, *w2, mass_core, mass_halo)
     return result
 
 

time: 112 us -> 107 us (0.955)
  the two profiles are of different devices: /device:TPU:105 before, /device:TPU:144 now
where the time goes in v6:
time: 107 us
  starting transfers between devices  55.5 us (52%)
  waiting for transfers between devices  36.6 us (34%)
  Pallas kernels  13.3 us (12%)
    ppermute x3, waiting for transfers between devices, both_pairs(): rb = lax.ppermute(second, axis, b) if b else jnp.zeros_like(second)  12.8 us
    ppermute x1, starting transfers between devices, body(): both = lax.ppermute(both, 'gz', pairs)  10.9 us
    ppermute x1, starting transfers between devices, body(): both = lax.ppermute(swap, 'gz', pairs)  10.6 us
    ppermute x3, waiting for transfers between devices, both_ways(): lax.ppermute(down, axis, [(i + step, i) for i in range(count - step)])  10.3 us
    ppermute x3, starting transfers between devices, both_ways(): low = lax.ppermute(up, axis, [(i, i + step) for i in range(count - step)])  10.1 us
    ppermute x3, starting transfers between devices, both_pairs(): rb = lax.ppermute(second, axis, b) if b else jnp.zeros_like(second)  6.64 us
    ppermute x3, starting transfers between devices, both_pairs(): ra = lax.ppermute(first, axis, a)  5.76 us
    ppermute x1, waiting for transfers between devices, body(): both = lax.ppermute(both, 'gz', pairs)  5.6 us
  transfers between devices with their start and end apart: 17, of which 11 were waited for; matrix products, arithmetic and copies ran while one was open for 0% of the time, Pallas kernels for 4%

profile of v6, /device:TPU:144, one launch (start us, length us, event | category | flops | bytes accessed | tf_op | source)
XLA Modules:
  0.0 106.6 jit_solution(1663806868475765029)
XLA Ops:
  0.0 0.1 stack.23
  0.1 0.1 broadcast_in_dim.2.spot.refs_0_
  0.2 3.3 %scatter_first.1 = (f32[240,128]{1,0:T(8,128)S(1)}, f32[8,256]{1,0:T(8,128)S(1)}, f32[32,384]{1,0:T(8,128)S(1)}, f32[9,8,128]{2,1,0:T(8,128)S(1)}, bf16[144,1024...) custom-call(s32[8,128]{1,0:T(8,128)S(1)} %broadcast_in_dim.2.spot.re, ...), custom_call_target="tpu_custom_call" | custom-call | tf_op jit(solution)/shard_map/scatter_first/pallas_call | solution.py:779
  3.4 10.9 %collective-permute-start = (f32[32,384]{1,0:T(8,128)S(1)}, f32[32,384]{1,0:T(8,128)S(1)}, u32[]{:S(2)}, u32[]{:S(2)}) collective-permute-start(f32[32,384]{1,0:T(8,128)S(1)} %get-tuple-element.61), channel_id=1, source_target_pairs={{0,1},{1,0},{2,3},{3,2},{4,5},{5,4},{6,7},{7,6},{8,9},{9,8},{10,11... | collective-permute-start | bytes 147464 | tf_op jit(solution)/shard_map/ppermute | solution.py:789
  14.4 5.6 %collective-permute-done.refs_3_.both = f32[32,384]{1,0:T(8,128)S(1)} collective-permute-done((f32[32,384]{1,0:T(8,128)S(1)}, f32[32,384]{1,0:T(8,128)S(1)}, u32[]{:S(2)}, u32[]{:S(2)}) %collective-permute-start) | collective-permute-done | bytes 49184 | tf_op jit(solution)/shard_map/ppermute | solution.py:789
  20.0 3.2 %collective-permute-start.1 = (f32[16,384]{1,0:T(8,128)S(1)}, f32[16,384]{1,0:T(8,128)S(1)}, u32[]{:S(2)}, u32[]{:S(2)}) collective-permute-start(f32[16,384]{1,0:T(8,128)S(1)} %slice.4), channel_id=1, source_target_pairs={{0,2},{2,4},{4,6},{3,1},{5,3},{7,5},{8,10},{10,12},{12,14},{11,9},... | collective-permute-start | bytes 73736 | tf_op jit(solution)/shard_map/ppermute | solution.py:790
  23.2 1.7 %weights_second.1 = (bf16[144,1024]{1,0:T(8,128)(2,1)S(1)}, bf16[144,1024]{1,0:T(8,128)(2,1)S(1)}, bf16[144,1024]{1,0:T(8,128)(2,1)S(1)}, bf16[144,1024]{1,0:T(8...) custom-call(f32[112,128]{1,0:T(8,128)S(1)} %get-tuple-element.62.ear, ...), custom_call_target="tpu_custom_call" | custom-call | tf_op jit(solution)/shard_map/weights_second/pallas_call | solution.py:794
  24.9 0.8 collective-permute-done.1.refs_4_.far
  25.7 0.3 fold_z5.1
  26.0 1.9 %collective-permute-start.2 = (f32[72,128]{1,0:T(8,128)S(1)}, f32[72,128]{1,0:T(8,128)S(1)}, u32[]{:S(2)}, u32[]{:S(2)}) collective-permute-start(f32[72,128]{1,0:T(8,128)S(1)} %get-tuple-element.67), channel_id=1, source_target_pairs={{0,8},{8,0},{16,24},{24,16},{32,40},{40,32},{48,56},{56,48},{64,72... | collective-permute-start | bytes 110600 | tf_op jit(solution)/shard_map/ppermute | solution.py:735
  27.9 2.1 %collective-permute-start.3 = (f32[72,128]{1,0:T(8,128)S(1)}, f32[72,128]{1,0:T(8,128)S(1)}, u32[]{:S(2)}, u32[]{:S(2)}) collective-permute-start(f32[72,128]{1,0:T(8,128)S(1)} %get-tuple-element.68), channel_id=1, source_target_pairs={{8,16},{16,8},{24,32},{32,24},{40,48},{48,40},{56,64},{64,56},{72,... | collective-permute-start | bytes 110600 | tf_op jit(solution)/shard_map/ppermute | solution.py:736
  30.0 0.0 collective-permute-done.2.ra
  30.0 4.4 %collective-permute-done.3.rb = f32[72,128]{1,0:T(8,128)S(1)} collective-permute-done((f32[72,128]{1,0:T(8,128)S(1)}, f32[72,128]{1,0:T(8,128)S(1)}, u32[]{:S(2)}, u32[]{:S(2)}) %collective-permute-start.3) | collective-permute-done | bytes 36896 | tf_op jit(solution)/shard_map/ppermute | solution.py:736
  34.4 0.1 fold_y5.1
  34.5 3.3 %collective-permute-start.4 = (f32[88,128]{1,0:T(8,128)S(1)}, f32[88,128]{1,0:T(8,128)S(1)}, u32[]{:S(2)}, u32[]{:S(2)}) collective-permute-start(f32[88,128]{1,0:T(8,128)S(1)} %get-tuple-element.71), channel_id=1, source_target_pairs={{0,128},{128,256},{256,384},{1,129},{129,257},{257,385},{2,130},{1... | collective-permute-start | bytes 135176 | tf_op jit(solution)/shard_map/ppermute | solution.py:726
  37.8 0.0 copy-start.3
  37.8 1.3 %collective-permute-start.5 = (f32[88,128]{1,0:T(8,128)S(1)}, f32[88,128]{1,0:T(8,128)S(1)}, u32[]{:S(2)}, u32[]{:S(2)}) collective-permute-start(f32[88,128]{1,0:T(8,128)S(1)} %get-tuple-element.72), channel_id=1, source_target_pairs={{128,0},{256,128},{384,256},{129,1},{257,129},{385,257},{130,2},{2... | collective-permute-start | bytes 135176 | tf_op jit(solution)/shard_map/ppermute | solution.py:727
  39.1 0.2 fill_pick.1.pick
  39.3 0.2 collective-permute-done.4.from_low
  39.5 4.3 %collective-permute-done.5.from_high = f32[88,128]{1,0:T(8,128)S(1)} collective-permute-done((f32[88,128]{1,0:T(8,128)S(1)}, f32[88,128]{1,0:T(8,128)S(1)}, u32[]{:S(2)}, u32[]{:S(2)}) %collective-permute-start.5) | collective-permute-done | bytes 45088 | tf_op jit(solution)/shard_map/ppermute | solution.py:727
  43.8 1.5 %gather_first.1 = (f32[21,8,128]{2,1,0:T(8,128)S(1)}, f32[21,384]{1,0:T(8,128)S(1)}, f32[21,384]{1,0:T(8,128)S(1)}, f32[21,384]{1,0:T(8,128)S(1)}, f32[48,128]{1,0:T(8,128)S(1)}, /*index=5*/f32[8,256]{1,0:T(8,128)S(1)}) custom-call(s32[8,128]{1,0:T(8,128)S(1)} %broadcast_in_dim.2.spot.refs_0_, f32[240,128]{1,0:T(8,128)S(1)} %get-tuple-element.69.h, ...), custom_call_target="tpu_custom_call" | custom-call | tf_op jit(solution)/shard_map/gather_first/pallas_call | solution.py:808
  45.3 3.5 %collective-permute-start.6 = (f32[21,384]{1,0:T(8,128)S(1)}, f32[21,384]{1,0:T(8,128)S(1)}, u32[]{:S(2)}, u32[]{:S(2)}) collective-permute-start(f32[21,384]{1,0:T(8,128)S(1)} %get-tuple-element.80), channel_id=1, source_target_pairs={{0,128},{128,256},{256,384},{1,129},{129,257},{257,385},{2,130},{1... | collective-permute-start | bytes 96776 | tf_op jit(solution)/shard_map/ppermute | solution.py:726
  48.8 1.3 %collective-permute-start.7 = (f32[21,384]{1,0:T(8,128)S(1)}, f32[21,384]{1,0:T(8,128)S(1)}, u32[]{:S(2)}, u32[]{:S(2)}) collective-permute-start(f32[21,384]{1,0:T(8,128)S(1)} %get-tuple-element.81), channel_id=1, source_target_pairs={{128,0},{256,128},{384,256},{129,1},{257,129},{385,257},{130,2},{2... | collective-permute-start | bytes 96776 | tf_op jit(solution)/shard_map/ppermute | solution.py:727
  50.1 0.0 copy-start.2
  50.1 0.7 copy-done.2
  50.8 1.7 %stay.1 = (f32[21,8,128]{2,1,0:T(8,128)S(1)}, f32[144,128]{1,0:T(8,128)S(1)}, f32[16,144]{1,0:T(8,128)S(1)}) custom-call(f32[120,128]{1,0:T(8,128)S(1)} %get-tuple-element.73.now, f32[21,8,128]{2,1,0:T(8,128)S(1)} %get-tuple-element.82.second, s32[8,128]{1,0:T(8,128)S(1)} %bitcast.14, f32[112,128]{1,0:T(8,128)S(1)} %get-tuple-element.62.early, ...), custom_call_target="tpu_custom_call" | custom-call | tf_op jit(solution)/shard_map/stay/pallas_call | solution.py:815
  52.5 0.0 collective-permute-done.6.refs_2_.x_low
  52.5 2.1 %collective-permute-done.7.refs_3_.x_high = f32[21,384]{1,0:T(8,128)S(1)} collective-permute-done((f32[21,384]{1,0:T(8,128)S(1)}, f32[21,384]{1,0:T(8,128)S(1)}, u32[]{:S(2)}, u32[]{:S(2)}) %collective-permute-start.7) | collective-permute-done | bytes 32288 | tf_op jit(solution)/shard_map/ppermute | solution.py:727
  54.6 1.9 %collective-permute-start.8 = (f32[21,384]{1,0:T(8,128)S(1)}, f32[21,384]{1,0:T(8,128)S(1)}, u32[]{:S(2)}, u32[]{:S(2)}) collective-permute-start(f32[21,384]{1,0:T(8,128)S(1)} %get-tuple-element.88), channel_id=1, source_target_pairs={{0,8},{8,0},{16,24},{24,16},{32,40},{40,32},{48,56},{56,48},{64,72... | collective-permute-start | bytes 96776 | tf_op jit(solution)/shard_map/ppermute | solution.py:735
  56.6 1.9 %collective-permute-start.9 = (f32[21,384]{1,0:T(8,128)S(1)}, f32[21,384]{1,0:T(8,128)S(1)}, u32[]{:S(2)}, u32[]{:S(2)}) collective-permute-start(f32[21,384]{1,0:T(8,128)S(1)} %get-tuple-element.89), channel_id=1, source_target_pairs={{8,16},{16,8},{24,32},{32,24},{40,48},{48,40},{56,64},{64,56},{72,... | collective-permute-start | bytes 96776 | tf_op jit(solution)/shard_map/ppermute | solution.py:736
  58.5 4.5 %collective-permute-done.9.rb = f32[21,384]{1,0:T(8,128)S(1)} collective-permute-done((f32[21,384]{1,0:T(8,128)S(1)}, f32[21,384]{1,0:T(8,128)S(1)}, u32[]{:S(2)}, u32[]{:S(2)}) %collective-permute-start.9) | collective-permute-done | bytes 32288 | tf_op jit(solution)/shard_map/ppermute | solution.py:736
  63.1 1.0 scatter_near.1
  64.1 10.6 %collective-permute-start.10 = (f32[48,384]{1,0:T(8,128)S(1)}, f32[48,384]{1,0:T(8,128)S(1)}, u32[]{:S(2)}, u32[]{:S(2)}) collective-permute-start(f32[48,384]{1,0:T(8,128)S(1)} %get-tuple-element.90), channel_id=1, source_target_pairs={{0,1},{1,0},{2,3},{3,2},{4,5},{5,4},{6,7},{7,6},{8,9},{9,8},{10,11... | collective-permute-start | bytes 221192 | tf_op jit(solution)/shard_map/ppermute | solution.py:834
  74.7 2.4 %collective-permute-start.11 = (f32[2,256]{1,0:T(2,128)S(1)}, f32[2,256]{1,0:T(2,128)S(1)}, u32[]{:S(2)}, u32[]{:S(2)}) collective-permute-start(f32[2,256]{1,0:T(2,128)S(1)} %get-tuple-element.92), channel_id=1, source_target_pairs={{2,0},{4,2},{6,4},{1,3},{3,5},{5,7},{10,8},{12,10},{14,12},{9,11},... | collective-permute-start | bytes 6152 | tf_op jit(solution)/shard_map/ppermute | solution.py:835
  77.0 3.1 %collective-permute-done.11._.against = f32[2,256]{1,0:T(2,128)S(1)} collective-permute-done((f32[2,256]{1,0:T(2,128)S(1)}, f32[2,256]{1,0:T(2,128)S(1)}, u32[]{:S(2)}, u32[]{:S(2)}) %collective-permute-start.11) | collective-permute-done | bytes 2080 | tf_op jit(solution)/shard_map/ppermute | solution.py:835
  80.2 2.1 %collective-permute-start.12 = (f32[24,384]{1,0:T(8,128)S(1)}, f32[24,384]{1,0:T(8,128)S(1)}, u32[]{:S(2)}, u32[]{:S(2)}) collective-permute-start(f32[24,384]{1,0:T(8,128)S(1)} %relay.1), channel_id=1, source_target_pairs={{0,2},{2,4},{4,6},{3,1},{5,3},{7,5},{8,10},{10,12},{12,14},{11,9},... | collective-permute-start | bytes 110600 | tf_op jit(solution)/shard_map/ppermute | solution.py:839
  82.2 3.8 %collective-permute-done.12.far = f32[24,384]{1,0:T(8,128)S(1)} collective-permute-done((f32[24,384]{1,0:T(8,128)S(1)}, f32[24,384]{1,0:T(8,128)S(1)}, u32[]{:S(2)}, u32[]{:S(2)}) %collective-permute-start.12) | collective-permute-done | bytes 36896 | tf_op jit(solution)/shard_map/ppermute | solution.py:839
  86.0 1.4 %scatter_second.1 = (f32[144,128]{1,0:T(8,128)S(1)}, f32[8,256]{1,0:T(8,128)S(1)}, f32[48,128]{1,0:T(8,128)S(1)}, f32[48,128]{1,0:T(8,128)S(1)}, f32[21,8,128]{2,1,0:T(8,128)S(1)}) custom-call(s32[8,128]{1,0:T(8,128)S(1)} %broadcast_in_dim.2.spot.refs_0_, f32[48,384]{1,0:T(8,128)S(1)} %collective-permute-done.10.both, ...), custom_call_target="tpu_custom_call" | custom-call | tf_op jit(solution)/shard_map/scatter_second/pallas_call | solution.py:840
  87.4 1.9 %collective-permute-start.13 = (f32[48,128]{1,0:T(8,128)S(1)}, f32[48,128]{1,0:T(8,128)S(1)}, u32[]{:S(2)}, u32[]{:S(2)}) collective-permute-start(f32[48,128]{1,0:T(8,128)S(1)} %get-tuple-element.103), channel_id=1, source_target_pairs={{0,8},{8,0},{16,24},{24,16},{32,40},{40,32},{48,56},{56,48},{64,72... | collective-permute-start | bytes 73736 | tf_op jit(solution)/shard_map/ppermute | solution.py:735
  89.3 0.0 copy-start
  89.3 2.6 %collective-permute-start.14 = (f32[48,128]{1,0:T(8,128)S(1)}, f32[48,128]{1,0:T(8,128)S(1)}, u32[]{:S(2)}, u32[]{:S(2)}) collective-permute-start(f32[48,128]{1,0:T(8,128)S(1)} %get-tuple-element.104), channel_id=1, source_target_pairs={{8,16},{16,8},{24,32},{32,24},{40,48},{48,40},{56,64},{64,56},{72,... | collective-permute-start | bytes 73736 | tf_op jit(solution)/shard_map/ppermute | solution.py:736
  92.0 3.8 %collective-permute-done.14.rb = f32[48,128]{1,0:T(8,128)S(1)} collective-permute-done((f32[48,128]{1,0:T(8,128)S(1)}, f32[48,128]{1,0:T(8,128)S(1)}, u32[]{:S(2)}, u32[]{:S(2)}) %collective-permute-start.14) | collective-permute-done | bytes 24608 | tf_op jit(solution)/shard_map/ppermute | solution.py:736
  95.8 0.1 fold_y3.1
  95.9 3.3 %collective-permute-start.15 = (f32[56,128]{1,0:T(8,128)S(1)}, f32[56,128]{1,0:T(8,128)S(1)}, u32[]{:S(2)}, u32[]{:S(2)}) collective-permute-start(f32[56,128]{1,0:T(8,128)S(1)} %get-tuple-element.107), channel_id=1, source_target_pairs={{0,128},{128,256},{256,384},{1,129},{129,257},{257,385},{2,130},{1... | collective-permute-start | bytes 86024 | tf_op jit(solution)/shard_map/ppermute | solution.py:726
  99.2 1.3 %collective-permute-start.16 = (f32[56,128]{1,0:T(8,128)S(1)}, f32[56,128]{1,0:T(8,128)S(1)}, u32[]{:S(2)}, u32[]{:S(2)}) collective-permute-start(f32[56,128]{1,0:T(8,128)S(1)} %get-tuple-element.108), channel_id=1, source_target_pairs={{128,0},{256,128},{384,256},{129,1},{257,129},{385,257},{130,2},{2... | collective-permute-start | bytes 86024 | tf_op jit(solution)/shard_map/ppermute | solution.py:727
  100.5 0.5 deform_second.1.bf
  101.1 3.9 %collective-permute-done.16.from_high = f32[56,128]{1,0:T(8,128)S(1)} collective-permute-done((f32[56,128]{1,0:T(8,128)S(1)}, f32[56,128]{1,0:T(8,128)S(1)}, u32[]{:S(2)}, u32[]{:S(2)}) %collective-permute-start.16) | collective-permute-done | bytes 28704 | tf_op jit(solution)/shard_map/ppermute | solution.py:727
  105.0 1.6 %gather_second.1 = f32[21,1024]{1,0:T(8,128)} custom-call(s32[8,128]{1,0:T(8,128)S(1)} %broadcast_in_dim.2.spot.refs_0_, f32[144,128]{1,0:T(8,128)S(1)} %get-tuple-element.105.h, f32[8,256]{1,0:T(8,128)S(1)} %get-tuple-element.106.hb, f32[56,128]{1,0:T(8,128)S(1)} %collective-permute-done.15.from_low, f32[56,128]{1,0:T(8,128)S(1)} %collective-permute-done.16.from_high, ...), custom_call_target="tpu_custom_call" | custom-call | tf_op jit(solution)/shard_map/gather_second/pallas_call | solution.py:852
  (12 shorter events, 0.0 us)
Async XLA Ops:
  3.4 16.5 %collective-permute-start = (f32[32,384]{1,0:T(8,128)S(1)}, f32[32,384]{1,0:T(8,128)S(1)}, u32[]{:S(2)}, u32[]{:S(2)}) collective-permute-start(f32[32,384]{1,0:T(8,128)S(1)} %get-tuple-element.61), channel_id=1, source_target_pairs={{0,1},{1,0},{2,3},{3,2},{4,5},{5,4},{6,7},{7,6},{8,9},{9,8},{10,11... | collective-permute-start | bytes 147464 | tf_op jit(solution)/shard_map/ppermute | solution.py:789
  20.0 5.7 %collective-permute-start.1 = (f32[16,384]{1,0:T(8,128)S(1)}, f32[16,384]{1,0:T(8,128)S(1)}, u32[]{:S(2)}, u32[]{:S(2)}) collective-permute-start(f32[16,384]{1,0:T(8,128)S(1)} %slice.4), channel_id=1, source_target_pairs={{0,2},{2,4},{4,6},{3,1},{5,3},{7,5},{8,10},{10,12},{12,14},{11,9},... | collective-permute-start | bytes 73736 | tf_op jit(solution)/shard_map/ppermute | solution.py:790
  26.0 4.0 %collective-permute-start.2 = (f32[72,128]{1,0:T(8,128)S(1)}, f32[72,128]{1,0:T(8,128)S(1)}, u32[]{:S(2)}, u32[]{:S(2)}) collective-permute-start(f32[72,128]{1,0:T(8,128)S(1)} %get-tuple-element.67), channel_id=1, source_target_pairs={{0,8},{8,0},{16,24},{24,16},{32,40},{40,32},{48,56},{56,48},{64,72... | collective-permute-start | bytes 110600 | tf_op jit(solution)/shard_map/ppermute | solution.py:735
  27.9 6.5 %collective-permute-start.3 = (f32[72,128]{1,0:T(8,128)S(1)}, f32[72,128]{1,0:T(8,128)S(1)}, u32[]{:S(2)}, u32[]{:S(2)}) collective-permute-start(f32[72,128]{1,0:T(8,128)S(1)} %get-tuple-element.68), channel_id=1, source_target_pairs={{8,16},{16,8},{24,32},{32,24},{40,48},{48,40},{56,64},{64,56},{72,... | collective-permute-start | bytes 110600 | tf_op jit(solution)/shard_map/ppermute | solution.py:736
  34.4 4.7 %copy-start.1 = (s32[1,26,32]{2,0,1:T(1,128)S(1)}, s32[1,26,32]{2,0,1:T(1,128)}, u32[]{:S(2)}) copy-start(s32[1,26,32]{2,0,1:T(1,128)} %param.19) | copy-start | bytes 9988
  34.5 5.0 %collective-permute-start.4 = (f32[88,128]{1,0:T(8,128)S(1)}, f32[88,128]{1,0:T(8,128)S(1)}, u32[]{:S(2)}, u32[]{:S(2)}) collective-permute-start(f32[88,128]{1,0:T(8,128)S(1)} %get-tuple-element.71), channel_id=1, source_target_pairs={{0,128},{128,256},{256,384},{1,129},{129,257},{257,385},{2,130},{1... | collective-permute-start | bytes 135176 | tf_op jit(solution)/shard_map/ppermute | solution.py:726
  37.8 1.3 %copy-start.3 = (s32[1,26]{1,0:T(1,128)S(1)}, s32[1,26]{1,0:T(1,128)}, u32[]{:S(2)}) copy-start(s32[1,26]{1,0:T(1,128)} %counts.1) | copy-start | bytes 316
  37.8 5.9 %collective-permute-start.5 = (f32[88,128]{1,0:T(8,128)S(1)}, f32[88,128]{1,0:T(8,128)S(1)}, u32[]{:S(2)}, u32[]{:S(2)}) collective-permute-start(f32[88,128]{1,0:T(8,128)S(1)} %get-tuple-element.72), channel_id=1, source_target_pairs={{128,0},{256,128},{384,256},{129,1},{257,129},{385,257},{130,2},{2... | collective-permute-start | bytes 135176 | tf_op jit(solution)/shard_map/ppermute | solution.py:727
  45.3 7.3 %collective-permute-start.6 = (f32[21,384]{1,0:T(8,128)S(1)}, f32[21,384]{1,0:T(8,128)S(1)}, u32[]{:S(2)}, u32[]{:S(2)}) collective-permute-start(f32[21,384]{1,0:T(8,128)S(1)} %get-tuple-element.80), channel_id=1, source_target_pairs={{0,128},{128,256},{256,384},{1,129},{129,257},{257,385},{2,130},{1... | collective-permute-start | bytes 96776 | tf_op jit(solution)/shard_map/ppermute | solution.py:726
  48.8 5.9 %collective-permute-start.7 = (f32[21,384]{1,0:T(8,128)S(1)}, f32[21,384]{1,0:T(8,128)S(1)}, u32[]{:S(2)}, u32[]{:S(2)}) collective-permute-start(f32[21,384]{1,0:T(8,128)S(1)} %get-tuple-element.81), channel_id=1, source_target_pairs={{128,0},{256,128},{384,256},{129,1},{257,129},{385,257},{130,2},{2... | collective-permute-start | bytes 96776 | tf_op jit(solution)/shard_map/ppermute | solution.py:727
  50.1 0.7 copy-start.2
  54.6 3.9 %collective-permute-start.8 = (f32[21,384]{1,0:T(8,128)S(1)}, f32[21,384]{1,0:T(8,128)S(1)}, u32[]{:S(2)}, u32[]{:S(2)}) collective-permute-start(f32[21,384]{1,0:T(8,128)S(1)} %get-tuple-element.88), channel_id=1, source_target_pairs={{0,8},{8,0},{16,24},{24,16},{32,40},{40,32},{48,56},{56,48},{64,72... | collective-permute-start | bytes 96776 | tf_op jit(solution)/shard_map/ppermute | solution.py:735
  56.6 6.5 %collective-permute-start.9 = (f32[21,384]{1,0:T(8,128)S(1)}, f32[21,384]{1,0:T(8,128)S(1)}, u32[]{:S(2)}, u32[]{:S(2)}) collective-permute-start(f32[21,384]{1,0:T(8,128)S(1)} %get-tuple-element.89), channel_id=1, source_target_pairs={{8,16},{16,8},{24,32},{32,24},{40,48},{48,40},{56,64},{64,56},{72,... | collective-permute-start | bytes 96776 | tf_op jit(solution)/shard_map/ppermute | solution.py:736
  64.1 16.1 %collective-permute-start.10 = (f32[48,384]{1,0:T(8,128)S(1)}, f32[48,384]{1,0:T(8,128)S(1)}, u32[]{:S(2)}, u32[]{:S(2)}) collective-permute-start(f32[48,384]{1,0:T(8,128)S(1)} %get-tuple-element.90), channel_id=1, source_target_pairs={{0,1},{1,0},{2,3},{3,2},{4,5},{5,4},{6,7},{7,6},{8,9},{9,8},{10,11... | collective-permute-start | bytes 221192 | tf_op jit(solution)/shard_map/ppermute | solution.py:834
  74.7 5.5 %collective-permute-start.11 = (f32[2,256]{1,0:T(2,128)S(1)}, f32[2,256]{1,0:T(2,128)S(1)}, u32[]{:S(2)}, u32[]{:S(2)}) collective-permute-start(f32[2,256]{1,0:T(2,128)S(1)} %get-tuple-element.92), channel_id=1, source_target_pairs={{2,0},{4,2},{6,4},{1,3},{3,5},{5,7},{10,8},{12,10},{14,12},{9,11},... | collective-permute-start | bytes 6152 | tf_op jit(solution)/shard_map/ppermute | solution.py:835
  80.2 5.9 %collective-permute-start.12 = (f32[24,384]{1,0:T(8,128)S(1)}, f32[24,384]{1,0:T(8,128)S(1)}, u32[]{:S(2)}, u32[]{:S(2)}) collective-permute-start(f32[24,384]{1,0:T(8,128)S(1)} %relay.1), channel_id=1, source_target_pairs={{0,2},{2,4},{4,6},{3,1},{5,3},{7,5},{8,10},{10,12},{12,14},{11,9},... | collective-permute-start | bytes 110600 | tf_op jit(solution)/shard_map/ppermute | solution.py:839
  87.4 4.6 %collective-permute-start.13 = (f32[48,128]{1,0:T(8,128)S(1)}, f32[48,128]{1,0:T(8,128)S(1)}, u32[]{:S(2)}, u32[]{:S(2)}) collective-permute-start(f32[48,128]{1,0:T(8,128)S(1)} %get-tuple-element.103), channel_id=1, source_target_pairs={{0,8},{8,0},{16,24},{24,16},{32,40},{40,32},{48,56},{56,48},{64,72... | collective-permute-start | bytes 73736 | tf_op jit(solution)/shard_map/ppermute | solution.py:735
  89.3 11.2 %copy-start = (f32[2,9,1024]{2,0,1:T(2,128)S(1)}, f32[2,9,1024]{2,0,1:T(2,128)}, u32[]{:S(2)}) copy-start(f32[2,9,1024]{2,0,1:T(2,128)} %param.14) | copy-start | bytes 221188
  89.3 6.5 %collective-permute-start.14 = (f32[48,128]{1,0:T(8,128)S(1)}, f32[48,128]{1,0:T(8,128)S(1)}, u32[]{:S(2)}, u32[]{:S(2)}) collective-permute-start(f32[48,128]{1,0:T(8,128)S(1)} %get-tuple-element.104), channel_id=1, source_target_pairs={{8,16},{16,8},{24,32},{32,24},{40,48},{48,40},{56,64},{64,56},{72,... | collective-permute-start | bytes 73736 | tf_op jit(solution)/shard_map/ppermute | solution.py:736
  95.9 5.2 %collective-permute-start.15 = (f32[56,128]{1,0:T(8,128)S(1)}, f32[56,128]{1,0:T(8,128)S(1)}, u32[]{:S(2)}, u32[]{:S(2)}) collective-permute-start(f32[56,128]{1,0:T(8,128)S(1)} %get-tuple-element.107), channel_id=1, source_target_pairs={{0,128},{128,256},{256,384},{1,129},{129,257},{257,385},{2,130},{1... | collective-permute-start | bytes 86024 | tf_op jit(solution)/shard_map/ppermute | solution.py:726
  99.2 5.8 %collective-permute-start.16 = (f32[56,128]{1,0:T(8,128)S(1)}, f32[56,128]{1,0:T(8,128)S(1)}, u32[]{:S(2)}, u32[]{:S(2)}) collective-permute-start(f32[56,128]{1,0:T(8,128)S(1)} %get-tuple-element.108), channel_id=1, source_target_pairs={{128,0},{256,128},{384,256},{129,1},{257,129},{385,257},{130,2},{2... | collective-permute-start | bytes 86024 | tf_op jit(solution)/shard_map/ppermute | solution.py:727

commit v7 on v6

--- a/solution.py
+++ b/solution.py
@@ -163,7 +163,7 @@
 
 
 def cells_of(centre):
-    return centre // 512, centre // 128 % 4, centre % 128
+    return centre >> 9, (centre >> 7) & 3, centre & 127
 
 
 def to_grid(adj, deform):
@@ -216,8 +216,11 @@
     return ((l0h, w_hi), (l0l, w_hi), (l0h, w_lo), (l2h, d_hi), (l2l, d_hi), (l2h, d_lo))
 
 
-def core_sums(l, w):
-    return sum(nt(a[...], b[0:128]) for a, b in paired(l, w))
+def all_sums(l, w):
+    full = sum(nt(a[...], b[...]) for a, b in paired(l, w))
+    tail = jnp.concatenate([full[:, 128:ZROWS], jnp.zeros((144, 112), F32)], axis=1)
+    tail = jnp.concatenate([tail, jnp.zeros((112, 128), F32)], axis=0).T
+    return full[:, 0:128], tail[0:16, 0:144]
 
 
 def edge_sums(l, w, rows=slice(128, ZROWS), lanes=slice(0, 1024)):
@@ -235,9 +238,9 @@
     low_row, row = iota((128, 128), 0), iota((8, 128), 0)
     for t, n in enumerate(rows):
         index = send[n : n + 1]
-        hot[...] = (low_row == index % 128).astype(F32).astype(BF16)
+        hot[...] = (low_row == (index & 127)).astype(F32).astype(BF16)
         got = (nn(hi, hot[...]) + nn(lo, hot[...])).reshape(14, 8, 128)
-        chosen = row == index // 128
+        chosen = row == (index >> 7)
         put(t, jnp.sum(jnp.where(chosen[None], got, 0.0), axis=1))
 
 
@@ -288,7 +291,8 @@
     for i in range(9):
         bf_out[i] = b_f[i]
     scatter_rows(a_v, b_c, frac, cell_x, cell_y, *l)
-    h[0:144] = core_sums(l, w)
+    core, ends = all_sums(l, w)
+    h[0:144] = core
     h[144:240] = jnp.zeros((96, 128), F32)
     for s in range(2):
         for x in range(4):
@@ -297,7 +301,7 @@
     lane, row = iota((16, 128), 1), iota((16, 128), 0)
     pick = (((row == 2) & (lane == 0)) | ((row == 3) & (lane == 127))).astype(F32)
     mass_ends = contract(pick, h[144:240], 1, 1, lax.Precision.HIGHEST)
-    ends = jnp.concatenate([edge_sums(l, w), mass_ends], axis=1)
+    ends = jnp.concatenate([ends, mass_ends], axis=1)
     hb[...] = jnp.zeros(hb.shape, F32)
     put_planes(hb, 0, ends[0:1], ends[1:2])
     put_planes(zu, 13, ends[0:1], ends[3:4])
@@ -514,9 +518,9 @@
     row = iota((8, 128), 0)
     for t in range(9):
         index = pick[t : t + 1]
-        hot[...] = (low_row == index % 128).astype(F32).astype(BF16)
+        hot[...] = (low_row == (index & 127)).astype(F32).astype(BF16)
         got = nn(hi, hot[...]) + nn(lo, hot[...])
-        chosen = (row == index // 128) & (index >= 0)
+        chosen = (row == (index >> 7)) & (index >= 0)
         got = got.reshape(22, 8, 128)[0:21]
         got = jnp.sum(jnp.where(chosen[None], got, 0.0), axis=1)
         dest, place = ((xd, t), (mid, t - 3), (xu, t - 6))[t // 3]
@@ -549,8 +553,8 @@
     row, low_row = iota((8, 128), 0), iota((128, 128), 0)
     for t, (values, index) in enumerate(zip(tiles, indices)):
         lanes = slice(t * 128, t * 128 + 128)
-        hot[:, lanes] = (low_row == index % 128).astype(F32).astype(BF16)
-        chosen = row == index // 128
+        hot[:, lanes] = (low_row == (index & 127)).astype(F32).astype(BF16)
+        chosen = row == (index >> 7)
         for pair in range((count + 1) // 2):
             both = []
             for r in (2 * pair, 2 * pair + 1):
@@ -588,8 +592,7 @@
     a_v, b_c = to_grid(adj, deform)
     l, w = (l0h, l0l, l2h, l2l), (w_hi, w_lo, d_hi, d_lo)
     scatter_rows(a_v, b_c, frac, cell_x, cell_y, *l)
-    core[...] = core_sums(l, w)
-    ends[...] = edge_sums(l, w)
+    core[...], ends[...] = all_sums(l, w)
 
 
 def near_kernel(
@@ -655,8 +658,9 @@
     a_v, b_c = to_grid([moved[i] for i in range(21)], [arrive[4 + i] for i in range(9)])
     l, w = (l0h, l0l, l2h, l2l), (a_hi, a_lo, b_hi, b_lo)
     scatter_rows(a_v, b_c, place, cell_x, cell_y, *l)
-    h[...] = core_sums(l, w) + core_stay[...]
-    ends = edge_sums(l, w) + ends_stay[...]
+    core, ends = all_sums(l, w)
+    h[...] = core + core_stay[...]
+    ends = ends + ends_stay[...]
     ends = jnp.concatenate([ends[0:8], jnp.zeros((8, 112), F32)], axis=1)
     halo = jnp.where(iota((8, 256), 0) < 2, ends, 0.0)
     near, relayed = both[21:23, 0:256] + against[0:2], far[21:23, 0:256]
@@ -763,13 +767,17 @@
         ((144, 1024), F32), ((144, 1024), F32), ((12, 8, 128), F32),
     ]
 
-    def fold(comps, h, hb, ya, yb):
+    def fold(comps, h, hb, ya, yb, after=()):
         ra, rb = both_pairs(ya, yb, "gy")
         rows = comps * 16 + 8
+
+        def kernel(*refs):
+            y_kernel(comps, *refs[:5], *refs[5 + len(after) :])
+
         h, hb, xu, xd = call(
-            functools.partial(y_kernel, comps), f"fold_y{comps}", [VMEM] * 5,
+            kernel, f"fold_y{comps}", [VMEM] * 5 + [pl.BlockSpec(memory_space=pl.ANY)] * len(after),
             [shape(comps * 48, 128), shape(8, 256), shape(rows, 128), shape(rows, 128)],
-        )(spot, h, hb, ra, rb)
+        )(spot, h, hb, ra, rb, *after)
         low, high = both_ways(xu, xd, "gx")
         return h, hb, low, high
 
@@ -796,15 +804,11 @@
         [((128, 128), BF16)],
     )(early, send)
     w2, wa, arrive = weights2[0:4], weights2[4:8], weights2[8]
-
-    def first_z(*refs):
-        z_kernel(5, *refs[:5], *refs[6:])
-
     h, hb, ya, yb = call(
-        first_z, "fold_z5", [VMEM] * 5 + [pl.BlockSpec(memory_space=pl.ANY)],
+        functools.partial(z_kernel, 5), "fold_z5", [VMEM] * 5,
         [shape(240, 128), shape(8, 256), shape(72, 128), shape(72, 128)],
-    )(spot, h, hb, both, far, arrive)
-    h, hb, low, high = fold(5, h, hb, ya, yb)
+    )(spot, h, hb, both, far)
+    h, hb, low, high = fold(5, h, hb, ya, yb, (arrive,))
     second, xu, xd, mid, mass_core, mass_halo = call(
         functools.partial(gather_first_kernel, extents), "gather_first", [VMEM] * 12,
         [shape(21, 8, 128), shape(21, 384), shape(21, 384), shape(21, 384), shape(48, 128), shape(8, 256)],

time: 107 us -> 106 us (level)
    ppermute x1, waiting for transfers between devices: 0.81 us -> 2.52 us  [body(): far = lax.ppermute(both[16:32], 'gz', hop)]
    ppermute x3, waiting for transfers between devices: 12.8 us -> 11.1 us  [both_pairs(): rb = lax.ppermute(second, axis, b) if b else jnp.zeros_like(second)]
where the time goes in v7:
time: 106 us
  starting transfers between devices  55.3 us (52%)
  waiting for transfers between devices  36.8 us (35%)
  Pallas kernels  12.5 us (12%)
    ppermute x3, waiting for transfers between devices, both_pairs(): rb = lax.ppermute(second, axis, b) if b else jnp.zeros_like(second)  11.1 us
    ppermute x1, starting transfers between devices, body(): both = lax.ppermute(both, 'gz', pairs)  10.9 us
    ppermute x1, starting transfers between devices, body(): both = lax.ppermute(swap, 'gz', pairs)  10.6 us
    ppermute x3, waiting for transfers between devices, both_ways(): lax.ppermute(down, axis, [(i + step, i) for i in range(count - step)])  10.5 us
    ppermute x3, starting transfers between devices, both_ways(): low = lax.ppermute(up, axis, [(i, i + step) for i in range(count - step)])  9.95 us
    ppermute x3, starting transfers between devices, both_pairs(): rb = lax.ppermute(second, axis, b) if b else jnp.zeros_like(second)  6.6 us
    ppermute x3, starting transfers between devices, both_pairs(): ra = lax.ppermute(first, axis, a)  5.76 us
    ppermute x1, waiting for transfers between devices, body(): both = lax.ppermute(both, 'gz', pairs)  5.6 us
  transfers between devices with their start and end apart: 17, of which 11 were waited for; matrix products, arithmetic and copies ran while one was open for 0% of the time, Pallas kernels for 4%

profile of v7, /device:TPU:144, one launch (start us, length us, event | category | flops | bytes accessed | tf_op | source)
XLA Modules:
  0.0 105.8 jit_solution(8166281065868095563)
XLA Ops:
  0.0 0.1 stack.23
  0.1 0.1 broadcast_in_dim.2.spot.refs_0_
  0.2 3.0 %scatter_first.1 = (f32[240,128]{1,0:T(8,128)S(1)}, f32[8,256]{1,0:T(8,128)S(1)}, f32[32,384]{1,0:T(8,128)S(1)}, f32[9,8,128]{2,1,0:T(8,128)S(1)}, bf16[144,1024...) custom-call(s32[8,128]{1,0:T(8,128)S(1)} %broadcast_in_dim.2.spot.re, ...), custom_call_target="tpu_custom_call" | custom-call | tf_op jit(solution)/shard_map/scatter_first/pallas_call | solution.py:787
  3.2 10.9 %collective-permute-start = (f32[32,384]{1,0:T(8,128)S(1)}, f32[32,384]{1,0:T(8,128)S(1)}, u32[]{:S(2)}, u32[]{:S(2)}) collective-permute-start(f32[32,384]{1,0:T(8,128)S(1)} %get-tuple-element.61), channel_id=1, source_target_pairs={{0,1},{1,0},{2,3},{3,2},{4,5},{5,4},{6,7},{7,6},{8,9},{9,8},{10,11... | collective-permute-start | bytes 147464 | tf_op jit(solution)/shard_map/ppermute | solution.py:797
  14.1 5.6 %collective-permute-done.both = f32[32,384]{1,0:T(8,128)S(1)} collective-permute-done((f32[32,384]{1,0:T(8,128)S(1)}, f32[32,384]{1,0:T(8,128)S(1)}, u32[]{:S(2)}, u32[]{:S(2)}) %collective-permute-start) | collective-permute-done | bytes 49184 | tf_op jit(solution)/shard_map/ppermute | solution.py:797
  19.7 3.2 %collective-permute-start.1 = (f32[16,384]{1,0:T(8,128)S(1)}, f32[16,384]{1,0:T(8,128)S(1)}, u32[]{:S(2)}, u32[]{:S(2)}) collective-permute-start(f32[16,384]{1,0:T(8,128)S(1)} %slice.4), channel_id=1, source_target_pairs={{0,2},{2,4},{4,6},{3,1},{5,3},{7,5},{8,10},{10,12},{12,14},{11,9},... | collective-permute-start | bytes 73736 | tf_op jit(solution)/shard_map/ppermute | solution.py:798
  22.9 2.5 %collective-permute-done.1.far = f32[16,384]{1,0:T(8,128)S(1)} collective-permute-done((f32[16,384]{1,0:T(8,128)S(1)}, f32[16,384]{1,0:T(8,128)S(1)}, u32[]{:S(2)}, u32[]{:S(2)}) %collective-permute-start.1) | collective-permute-done | bytes 24608 | tf_op jit(solution)/shard_map/ppermute | solution.py:798
  25.4 0.3 fold_z5.1
  25.7 1.9 %collective-permute-start.2 = (f32[72,128]{1,0:T(8,128)S(1)}, f32[72,128]{1,0:T(8,128)S(1)}, u32[]{:S(2)}, u32[]{:S(2)}) collective-permute-start(f32[72,128]{1,0:T(8,128)S(1)} %get-tuple-element.64), channel_id=1, source_target_pairs={{0,8},{8,0},{16,24},{24,16},{32,40},{40,32},{48,56},{56,48},{64,72... | collective-permute-start | bytes 110600 | tf_op jit(solution)/shard_map/ppermute | solution.py:739
  27.6 2.1 %collective-permute-start.3 = (f32[72,128]{1,0:T(8,128)S(1)}, f32[72,128]{1,0:T(8,128)S(1)}, u32[]{:S(2)}, u32[]{:S(2)}) collective-permute-start(f32[72,128]{1,0:T(8,128)S(1)} %get-tuple-element.65), channel_id=1, source_target_pairs={{8,16},{16,8},{24,32},{32,24},{40,48},{48,40},{56,64},{64,56},{72,... | collective-permute-start | bytes 110600 | tf_op jit(solution)/shard_map/ppermute | solution.py:740
  29.7 1.7 %weights_second.1 = (bf16[144,1024]{1,0:T(8,128)(2,1)S(1)}, bf16[144,1024]{1,0:T(8,128)(2,1)S(1)}, bf16[144,1024]{1,0:T(8,128)(2,1)S(1)}, bf16[144,1024]{1,0:T(8...) custom-call(f32[112,128]{1,0:T(8,128)S(1)} %get-tuple-element.66.ear, ...), custom_call_target="tpu_custom_call" | custom-call | tf_op jit(solution)/shard_map/weights_second/pallas_call | solution.py:802
  31.4 0.0 collective-permute-done.2.refs_3_
  31.4 2.7 %collective-permute-done.3.refs_4_ = f32[72,128]{1,0:T(8,128)S(1)} collective-permute-done((f32[72,128]{1,0:T(8,128)S(1)}, f32[72,128]{1,0:T(8,128)S(1)}, u32[]{:S(2)}, u32[]{:S(2)}) %collective-permute-start.3) | collective-permute-done | bytes 36896 | tf_op jit(solution)/shard_map/ppermute | solution.py:740
  34.1 0.1 fold_y5.1
  34.2 3.3 %collective-permute-start.4 = (f32[88,128]{1,0:T(8,128)S(1)}, f32[88,128]{1,0:T(8,128)S(1)}, u32[]{:S(2)}, u32[]{:S(2)}) collective-permute-start(f32[88,128]{1,0:T(8,128)S(1)} %get-tuple-element.71), channel_id=1, source_target_pairs={{0,128},{128,256},{256,384},{1,129},{129,257},{257,385},{2,130},{1... | collective-permute-start | bytes 135176 | tf_op jit(solution)/shard_map/ppermute | solution.py:730
  37.5 0.0 copy-start.3
  37.5 1.3 %collective-permute-start.5 = (f32[88,128]{1,0:T(8,128)S(1)}, f32[88,128]{1,0:T(8,128)S(1)}, u32[]{:S(2)}, u32[]{:S(2)}) collective-permute-start(f32[88,128]{1,0:T(8,128)S(1)} %get-tuple-element.72), channel_id=1, source_target_pairs={{128,0},{256,128},{384,256},{129,1},{257,129},{385,257},{130,2},{2... | collective-permute-start | bytes 135176 | tf_op jit(solution)/shard_map/ppermute | solution.py:731
  38.8 0.2 fill_pick.1.pick
  39.0 0.2 collective-permute-done.4.from_low
  39.2 4.3 %collective-permute-done.5.from_high = f32[88,128]{1,0:T(8,128)S(1)} collective-permute-done((f32[88,128]{1,0:T(8,128)S(1)}, f32[88,128]{1,0:T(8,128)S(1)}, u32[]{:S(2)}, u32[]{:S(2)}) %collective-permute-start.5) | collective-permute-done | bytes 45088 | tf_op jit(solution)/shard_map/ppermute | solution.py:731
  43.5 1.5 %gather_first.1 = (f32[21,8,128]{2,1,0:T(8,128)S(1)}, f32[21,384]{1,0:T(8,128)S(1)}, f32[21,384]{1,0:T(8,128)S(1)}, f32[21,384]{1,0:T(8,128)S(1)}, f32[48,128]{1,0:T(8,128)S(1)}, /*index=5*/f32[8,256]{1,0:T(8,128)S(1)}) custom-call(s32[8,128]{1,0:T(8,128)S(1)} %broadcast_in_dim.2.spot.refs_0_, f32[240,128]{1,0:T(8,128)S(1)} %get-tuple-element.69.h, ...), custom_call_target="tpu_custom_call" | custom-call | tf_op jit(solution)/shard_map/gather_first/pallas_call | solution.py:812
  45.0 3.5 %collective-permute-start.6 = (f32[21,384]{1,0:T(8,128)S(1)}, f32[21,384]{1,0:T(8,128)S(1)}, u32[]{:S(2)}, u32[]{:S(2)}) collective-permute-start(f32[21,384]{1,0:T(8,128)S(1)} %get-tuple-element.80), channel_id=1, source_target_pairs={{0,128},{128,256},{256,384},{1,129},{129,257},{257,385},{2,130},{1... | collective-permute-start | bytes 96776 | tf_op jit(solution)/shard_map/ppermute | solution.py:730
  48.5 1.3 %collective-permute-start.7 = (f32[21,384]{1,0:T(8,128)S(1)}, f32[21,384]{1,0:T(8,128)S(1)}, u32[]{:S(2)}, u32[]{:S(2)}) collective-permute-start(f32[21,384]{1,0:T(8,128)S(1)} %get-tuple-element.81), channel_id=1, source_target_pairs={{128,0},{256,128},{384,256},{129,1},{257,129},{385,257},{130,2},{2... | collective-permute-start | bytes 96776 | tf_op jit(solution)/shard_map/ppermute | solution.py:731
  49.8 0.0 copy-start.2
  49.8 0.7 copy-done.2
  50.5 1.6 %stay.1 = (f32[21,8,128]{2,1,0:T(8,128)S(1)}, f32[144,128]{1,0:T(8,128)S(1)}, f32[16,144]{1,0:T(8,128)S(1)}) custom-call(f32[120,128]{1,0:T(8,128)S(1)} %get-tuple-element.73.now, f32[21,8,128]{2,1,0:T(8,128)S(1)} %get-tuple-element.82.second, s32[8,128]{1,0:T(8,128)S(1)} %bitcast.14, f32[112,128]{1,0:T(8,128)S(1)} %get-tuple-element.66.early, ...), custom_call_target="tpu_custom_call" | custom-call | tf_op jit(solution)/shard_map/stay/pallas_call | solution.py:819
  52.1 2.3 %collective-permute-done.7.refs_3_.x_high = f32[21,384]{1,0:T(8,128)S(1)} collective-permute-done((f32[21,384]{1,0:T(8,128)S(1)}, f32[21,384]{1,0:T(8,128)S(1)}, u32[]{:S(2)}, u32[]{:S(2)}) %collective-permute-start.7) | collective-permute-done | bytes 32288 | tf_op jit(solution)/shard_map/ppermute | solution.py:731
  54.3 1.9 %collective-permute-start.8 = (f32[21,384]{1,0:T(8,128)S(1)}, f32[21,384]{1,0:T(8,128)S(1)}, u32[]{:S(2)}, u32[]{:S(2)}) collective-permute-start(f32[21,384]{1,0:T(8,128)S(1)} %get-tuple-element.88), channel_id=1, source_target_pairs={{0,8},{8,0},{16,24},{24,16},{32,40},{40,32},{48,56},{56,48},{64,72... | collective-permute-start | bytes 96776 | tf_op jit(solution)/shard_map/ppermute | solution.py:739
  56.3 1.9 %collective-permute-start.9 = (f32[21,384]{1,0:T(8,128)S(1)}, f32[21,384]{1,0:T(8,128)S(1)}, u32[]{:S(2)}, u32[]{:S(2)}) collective-permute-start(f32[21,384]{1,0:T(8,128)S(1)} %get-tuple-element.89), channel_id=1, source_target_pairs={{8,16},{16,8},{24,32},{32,24},{40,48},{48,40},{56,64},{64,56},{72,... | collective-permute-start | bytes 96776 | tf_op jit(solution)/shard_map/ppermute | solution.py:740
  58.2 4.5 %collective-permute-done.9.rb = f32[21,384]{1,0:T(8,128)S(1)} collective-permute-done((f32[21,384]{1,0:T(8,128)S(1)}, f32[21,384]{1,0:T(8,128)S(1)}, u32[]{:S(2)}, u32[]{:S(2)}) %collective-permute-start.9) | collective-permute-done | bytes 32288 | tf_op jit(solution)/shard_map/ppermute | solution.py:740
  62.8 1.0 scatter_near.1
  63.8 10.6 %collective-permute-start.10 = (f32[48,384]{1,0:T(8,128)S(1)}, f32[48,384]{1,0:T(8,128)S(1)}, u32[]{:S(2)}, u32[]{:S(2)}) collective-permute-start(f32[48,384]{1,0:T(8,128)S(1)} %get-tuple-element.90), channel_id=1, source_target_pairs={{0,1},{1,0},{2,3},{3,2},{4,5},{5,4},{6,7},{7,6},{8,9},{9,8},{10,11... | collective-permute-start | bytes 221192 | tf_op jit(solution)/shard_map/ppermute | solution.py:838
  74.4 2.4 %collective-permute-start.11 = (f32[2,256]{1,0:T(2,128)S(1)}, f32[2,256]{1,0:T(2,128)S(1)}, u32[]{:S(2)}, u32[]{:S(2)}) collective-permute-start(f32[2,256]{1,0:T(2,128)S(1)} %get-tuple-element.92), channel_id=1, source_target_pairs={{2,0},{4,2},{6,4},{1,3},{3,5},{5,7},{10,8},{12,10},{14,12},{9,11},... | collective-permute-start | bytes 6152 | tf_op jit(solution)/shard_map/ppermute | solution.py:839
  76.8 3.1 %collective-permute-done.11._.against = f32[2,256]{1,0:T(2,128)S(1)} collective-permute-done((f32[2,256]{1,0:T(2,128)S(1)}, f32[2,256]{1,0:T(2,128)S(1)}, u32[]{:S(2)}, u32[]{:S(2)}) %collective-permute-start.11) | collective-permute-done | bytes 2080 | tf_op jit(solution)/shard_map/ppermute | solution.py:839
  79.9 0.0 collective-permute-done.10.both
  79.9 2.1 %collective-permute-start.12 = (f32[24,384]{1,0:T(8,128)S(1)}, f32[24,384]{1,0:T(8,128)S(1)}, u32[]{:S(2)}, u32[]{:S(2)}) collective-permute-start(f32[24,384]{1,0:T(8,128)S(1)} %relay.1), channel_id=1, source_target_pairs={{0,2},{2,4},{4,6},{3,1},{5,3},{7,5},{8,10},{10,12},{12,14},{11,9},... | collective-permute-start | bytes 110600 | tf_op jit(solution)/shard_map/ppermute | solution.py:843
  82.0 3.8 %collective-permute-done.12.far = f32[24,384]{1,0:T(8,128)S(1)} collective-permute-done((f32[24,384]{1,0:T(8,128)S(1)}, f32[24,384]{1,0:T(8,128)S(1)}, u32[]{:S(2)}, u32[]{:S(2)}) %collective-permute-start.12) | collective-permute-done | bytes 36896 | tf_op jit(solution)/shard_map/ppermute | solution.py:843
  85.7 1.0 scatter_second.1
  86.8 1.9 %collective-permute-start.13 = (f32[48,128]{1,0:T(8,128)S(1)}, f32[48,128]{1,0:T(8,128)S(1)}, u32[]{:S(2)}, u32[]{:S(2)}) collective-permute-start(f32[48,128]{1,0:T(8,128)S(1)} %get-tuple-element.103), channel_id=1, source_target_pairs={{0,8},{8,0},{16,24},{24,16},{32,40},{40,32},{48,56},{56,48},{64,72... | collective-permute-start | bytes 73736 | tf_op jit(solution)/shard_map/ppermute | solution.py:739
  88.7 0.0 copy-start
  88.7 2.6 %collective-permute-start.14 = (f32[48,128]{1,0:T(8,128)S(1)}, f32[48,128]{1,0:T(8,128)S(1)}, u32[]{:S(2)}, u32[]{:S(2)}) collective-permute-start(f32[48,128]{1,0:T(8,128)S(1)} %get-tuple-element.104), channel_id=1, source_target_pairs={{8,16},{16,8},{24,32},{32,24},{40,48},{48,40},{56,64},{64,56},{72,... | collective-permute-start | bytes 73736 | tf_op jit(solution)/shard_map/ppermute | solution.py:740
  91.3 3.9 %collective-permute-done.14.refs_4_ = f32[48,128]{1,0:T(8,128)S(1)} collective-permute-done((f32[48,128]{1,0:T(8,128)S(1)}, f32[48,128]{1,0:T(8,128)S(1)}, u32[]{:S(2)}, u32[]{:S(2)}) %collective-permute-start.14) | collective-permute-done | bytes 24608 | tf_op jit(solution)/shard_map/ppermute | solution.py:740
  95.2 0.1 fold_y3.1
  95.3 3.2 %collective-permute-start.15 = (f32[56,128]{1,0:T(8,128)S(1)}, f32[56,128]{1,0:T(8,128)S(1)}, u32[]{:S(2)}, u32[]{:S(2)}) collective-permute-start(f32[56,128]{1,0:T(8,128)S(1)} %get-tuple-element.107), channel_id=1, source_target_pairs={{0,128},{128,256},{256,384},{1,129},{129,257},{257,385},{2,130},{1... | collective-permute-start | bytes 86024 | tf_op jit(solution)/shard_map/ppermute | solution.py:730
  98.4 1.3 %collective-permute-start.16 = (f32[56,128]{1,0:T(8,128)S(1)}, f32[56,128]{1,0:T(8,128)S(1)}, u32[]{:S(2)}, u32[]{:S(2)}) collective-permute-start(f32[56,128]{1,0:T(8,128)S(1)} %get-tuple-element.108), channel_id=1, source_target_pairs={{128,0},{256,128},{384,256},{129,1},{257,129},{385,257},{130,2},{2... | collective-permute-start | bytes 86024 | tf_op jit(solution)/shard_map/ppermute | solution.py:731
  99.8 0.5 deform_second.1.bf
  100.2 4.0 %collective-permute-done.16.from_high = f32[56,128]{1,0:T(8,128)S(1)} collective-permute-done((f32[56,128]{1,0:T(8,128)S(1)}, f32[56,128]{1,0:T(8,128)S(1)}, u32[]{:S(2)}, u32[]{:S(2)}) %collective-permute-start.16) | collective-permute-done | bytes 28704 | tf_op jit(solution)/shard_map/ppermute | solution.py:731
  104.2 1.5 %gather_second.1 = f32[21,1024]{1,0:T(8,128)} custom-call(s32[8,128]{1,0:T(8,128)S(1)} %broadcast_in_dim.2.spot.refs_0_, f32[144,128]{1,0:T(8,128)S(1)} %get-tuple-element.105.h, f32[8,256]{1,0:T(8,128)S(1)} %get-tuple-element.106.hb, f32[56,128]{1,0:T(8,128)S(1)} %collective-permute-done.15.from_low, f32[56,128]{1,0:T(8,128)S(1)} %collective-permute-done.16.from_high, ...), custom_call_target="tpu_custom_call" | custom-call | tf_op jit(solution)/shard_map/gather_second/pallas_call | solution.py:856
  (12 shorter events, 0.0 us)
Async XLA Ops:
  3.2 16.5 %collective-permute-start = (f32[32,384]{1,0:T(8,128)S(1)}, f32[32,384]{1,0:T(8,128)S(1)}, u32[]{:S(2)}, u32[]{:S(2)}) collective-permute-start(f32[32,384]{1,0:T(8,128)S(1)} %get-tuple-element.61), channel_id=1, source_target_pairs={{0,1},{1,0},{2,3},{3,2},{4,5},{5,4},{6,7},{7,6},{8,9},{9,8},{10,11... | collective-permute-start | bytes 147464 | tf_op jit(solution)/shard_map/ppermute | solution.py:797
  19.7 5.7 %collective-permute-start.1 = (f32[16,384]{1,0:T(8,128)S(1)}, f32[16,384]{1,0:T(8,128)S(1)}, u32[]{:S(2)}, u32[]{:S(2)}) collective-permute-start(f32[16,384]{1,0:T(8,128)S(1)} %slice.4), channel_id=1, source_target_pairs={{0,2},{2,4},{4,6},{3,1},{5,3},{7,5},{8,10},{10,12},{12,14},{11,9},... | collective-permute-start | bytes 73736 | tf_op jit(solution)/shard_map/ppermute | solution.py:798
  25.7 5.7 %collective-permute-start.2 = (f32[72,128]{1,0:T(8,128)S(1)}, f32[72,128]{1,0:T(8,128)S(1)}, u32[]{:S(2)}, u32[]{:S(2)}) collective-permute-start(f32[72,128]{1,0:T(8,128)S(1)} %get-tuple-element.64), channel_id=1, source_target_pairs={{0,8},{8,0},{16,24},{24,16},{32,40},{40,32},{48,56},{56,48},{64,72... | collective-permute-start | bytes 110600 | tf_op jit(solution)/shard_map/ppermute | solution.py:739
  27.6 6.5 %collective-permute-start.3 = (f32[72,128]{1,0:T(8,128)S(1)}, f32[72,128]{1,0:T(8,128)S(1)}, u32[]{:S(2)}, u32[]{:S(2)}) collective-permute-start(f32[72,128]{1,0:T(8,128)S(1)} %get-tuple-element.65), channel_id=1, source_target_pairs={{8,16},{16,8},{24,32},{32,24},{40,48},{48,40},{56,64},{64,56},{72,... | collective-permute-start | bytes 110600 | tf_op jit(solution)/shard_map/ppermute | solution.py:740
  34.1 4.7 %copy-start.1 = (s32[1,26,32]{2,0,1:T(1,128)S(1)}, s32[1,26,32]{2,0,1:T(1,128)}, u32[]{:S(2)}) copy-start(s32[1,26,32]{2,0,1:T(1,128)} %param.19) | copy-start | bytes 9988
  34.2 5.0 %collective-permute-start.4 = (f32[88,128]{1,0:T(8,128)S(1)}, f32[88,128]{1,0:T(8,128)S(1)}, u32[]{:S(2)}, u32[]{:S(2)}) collective-permute-start(f32[88,128]{1,0:T(8,128)S(1)} %get-tuple-element.71), channel_id=1, source_target_pairs={{0,128},{128,256},{256,384},{1,129},{129,257},{257,385},{2,130},{1... | collective-permute-start | bytes 135176 | tf_op jit(solution)/shard_map/ppermute | solution.py:730
  37.5 1.3 %copy-start.3 = (s32[1,26]{1,0:T(1,128)S(1)}, s32[1,26]{1,0:T(1,128)}, u32[]{:S(2)}) copy-start(s32[1,26]{1,0:T(1,128)} %counts.1) | copy-start | bytes 316
  37.5 5.9 %collective-permute-start.5 = (f32[88,128]{1,0:T(8,128)S(1)}, f32[88,128]{1,0:T(8,128)S(1)}, u32[]{:S(2)}, u32[]{:S(2)}) collective-permute-start(f32[88,128]{1,0:T(8,128)S(1)} %get-tuple-element.72), channel_id=1, source_target_pairs={{128,0},{256,128},{384,256},{129,1},{257,129},{385,257},{130,2},{2... | collective-permute-start | bytes 135176 | tf_op jit(solution)/shard_map/ppermute | solution.py:731
  45.0 7.1 %collective-permute-start.6 = (f32[21,384]{1,0:T(8,128)S(1)}, f32[21,384]{1,0:T(8,128)S(1)}, u32[]{:S(2)}, u32[]{:S(2)}) collective-permute-start(f32[21,384]{1,0:T(8,128)S(1)} %get-tuple-element.80), channel_id=1, source_target_pairs={{0,128},{128,256},{256,384},{1,129},{129,257},{257,385},{2,130},{1... | collective-permute-start | bytes 96776 | tf_op jit(solution)/shard_map/ppermute | solution.py:730
  48.5 5.9 %collective-permute-start.7 = (f32[21,384]{1,0:T(8,128)S(1)}, f32[21,384]{1,0:T(8,128)S(1)}, u32[]{:S(2)}, u32[]{:S(2)}) collective-permute-start(f32[21,384]{1,0:T(8,128)S(1)} %get-tuple-element.81), channel_id=1, source_target_pairs={{128,0},{256,128},{384,256},{129,1},{257,129},{385,257},{130,2},{2... | collective-permute-start | bytes 96776 | tf_op jit(solution)/shard_map/ppermute | solution.py:731
  49.8 0.7 copy-start.2
  54.3 3.9 %collective-permute-start.8 = (f32[21,384]{1,0:T(8,128)S(1)}, f32[21,384]{1,0:T(8,128)S(1)}, u32[]{:S(2)}, u32[]{:S(2)}) collective-permute-start(f32[21,384]{1,0:T(8,128)S(1)} %get-tuple-element.88), channel_id=1, source_target_pairs={{0,8},{8,0},{16,24},{24,16},{32,40},{40,32},{48,56},{56,48},{64,72... | collective-permute-start | bytes 96776 | tf_op jit(solution)/shard_map/ppermute | solution.py:739
  56.3 6.5 %collective-permute-start.9 = (f32[21,384]{1,0:T(8,128)S(1)}, f32[21,384]{1,0:T(8,128)S(1)}, u32[]{:S(2)}, u32[]{:S(2)}) collective-permute-start(f32[21,384]{1,0:T(8,128)S(1)} %get-tuple-element.89), channel_id=1, source_target_pairs={{8,16},{16,8},{24,32},{32,24},{40,48},{48,40},{56,64},{64,56},{72,... | collective-permute-start | bytes 96776 | tf_op jit(solution)/shard_map/ppermute | solution.py:740
  63.8 16.1 %collective-permute-start.10 = (f32[48,384]{1,0:T(8,128)S(1)}, f32[48,384]{1,0:T(8,128)S(1)}, u32[]{:S(2)}, u32[]{:S(2)}) collective-permute-start(f32[48,384]{1,0:T(8,128)S(1)} %get-tuple-element.90), channel_id=1, source_target_pairs={{0,1},{1,0},{2,3},{3,2},{4,5},{5,4},{6,7},{7,6},{8,9},{9,8},{10,11... | collective-permute-start | bytes 221192 | tf_op jit(solution)/shard_map/ppermute | solution.py:838
  74.4 5.5 %collective-permute-start.11 = (f32[2,256]{1,0:T(2,128)S(1)}, f32[2,256]{1,0:T(2,128)S(1)}, u32[]{:S(2)}, u32[]{:S(2)}) collective-permute-start(f32[2,256]{1,0:T(2,128)S(1)} %get-tuple-element.92), channel_id=1, source_target_pairs={{2,0},{4,2},{6,4},{1,3},{3,5},{5,7},{10,8},{12,10},{14,12},{9,11},... | collective-permute-start | bytes 6152 | tf_op jit(solution)/shard_map/ppermute | solution.py:839
  79.9 5.9 %collective-permute-start.12 = (f32[24,384]{1,0:T(8,128)S(1)}, f32[24,384]{1,0:T(8,128)S(1)}, u32[]{:S(2)}, u32[]{:S(2)}) collective-permute-start(f32[24,384]{1,0:T(8,128)S(1)} %relay.1), channel_id=1, source_target_pairs={{0,2},{2,4},{4,6},{3,1},{5,3},{7,5},{8,10},{10,12},{12,14},{11,9},... | collective-permute-start | bytes 110600 | tf_op jit(solution)/shard_map/ppermute | solution.py:843
  86.8 4.6 %collective-permute-start.13 = (f32[48,128]{1,0:T(8,128)S(1)}, f32[48,128]{1,0:T(8,128)S(1)}, u32[]{:S(2)}, u32[]{:S(2)}) collective-permute-start(f32[48,128]{1,0:T(8,128)S(1)} %get-tuple-element.103), channel_id=1, source_target_pairs={{0,8},{8,0},{16,24},{24,16},{32,40},{40,32},{48,56},{56,48},{64,72... | collective-permute-start | bytes 73736 | tf_op jit(solution)/shard_map/ppermute | solution.py:739
  88.7 11.1 %copy-start = (f32[2,9,1024]{2,0,1:T(2,128)S(1)}, f32[2,9,1024]{2,0,1:T(2,128)}, u32[]{:S(2)}) copy-start(f32[2,9,1024]{2,0,1:T(2,128)} %param.14) | copy-start | bytes 221188
  88.7 6.5 %collective-permute-start.14 = (f32[48,128]{1,0:T(8,128)S(1)}, f32[48,128]{1,0:T(8,128)S(1)}, u32[]{:S(2)}, u32[]{:S(2)}) collective-permute-start(f32[48,128]{1,0:T(8,128)S(1)} %get-tuple-element.104), channel_id=1, source_target_pairs={{8,16},{16,8},{24,32},{32,24},{40,48},{48,40},{56,64},{64,56},{72,... | collective-permute-start | bytes 73736 | tf_op jit(solution)/shard_map/ppermute | solution.py:740
  95.3 5.0 %collective-permute-start.15 = (f32[56,128]{1,0:T(8,128)S(1)}, f32[56,128]{1,0:T(8,128)S(1)}, u32[]{:S(2)}, u32[]{:S(2)}) collective-permute-start(f32[56,128]{1,0:T(8,128)S(1)} %get-tuple-element.107), channel_id=1, source_target_pairs={{0,128},{128,256},{256,384},{1,129},{129,257},{257,385},{2,130},{1... | collective-permute-start | bytes 86024 | tf_op jit(solution)/shard_map/ppermute | solution.py:730
  98.4 5.8 %collective-permute-start.16 = (f32[56,128]{1,0:T(8,128)S(1)}, f32[56,128]{1,0:T(8,128)S(1)}, u32[]{:S(2)}, u32[]{:S(2)}) collective-permute-start(f32[56,128]{1,0:T(8,128)S(1)} %get-tuple-element.108), channel_id=1, source_target_pairs={{128,0},{256,128},{384,256},{129,1},{257,129},{385,257},{130,2},{2... | collective-permute-start | bytes 86024 | tf_op jit(solution)/shard_map/ppermute | solution.py:731

commit v8 on v7

--- a/solution.py
+++ b/solution.py
@@ -113,11 +113,14 @@
     return jnp.where(row_of(info, axis_row, one.shape[0]) == 0, one, other)
 
 
+def by_sides(info, one, other, axis_row=3):
+    count = one.shape[1] // 128
+    tiles = [by_side(info, lane_tile(one, t), lane_tile(other, t), axis_row) for t in range(count)]
+    return jnp.concatenate(tiles, axis=1)
+
+
 def by_z_side(info, one, other):
-    tiles = [
-        by_side(info, lane_tile(one, t), lane_tile(other, t), 4) for t in range(one.shape[1] // 128)
-    ]
-    return jnp.concatenate(tiles, axis=1)
+    return by_sides(info, one, other, 4)
 
 
 def fields(ref):
@@ -365,7 +368,7 @@
     yb[packed : packed + 8] = wide_rows(halo)
 
 
-def y_kernel(comps, spot, h, hb, ra, rb, h_out, hb_out, xu, xd):
+def y_kernel(comps, spot, h, hb, ra, rb, h_out, hb_out, xa, xb, xu, xd):
     first = spot
     row = iota((8, 128), 0)
     blocks = comps * 6
@@ -395,9 +398,12 @@
     hb_out[...] = halo
     xu[comps * 16 : comps * 16 + 8] = wide_rows(halo)
     xd[comps * 16 : comps * 16 + 8] = wide_rows(halo)
-
-
-def x_fold(comps, h, hb, from_low, from_high, total):
+    xa[...] = by_side(spot, xu[...], xd[...])
+    xb[...] = by_side(spot, xd[...], xu[...])
+
+
+def x_fold(comps, spot, h, hb, ra, rb, total):
+    from_low, from_high = by_side(spot, ra[...], rb[...]), by_side(spot, rb[...], ra[...])
     for c in range(comps):
         total[c * 48 : c * 48 + 16] = h[c * 48 : c * 48 + 16] + from_low[c * 16 : c * 16 + 16]
         total[c * 48 + 16 : c * 48 + 32] = h[c * 48 + 16 : c * 48 + 32]
@@ -485,10 +491,10 @@
 
 def gather_first_kernel(
     extents, spot, h, hb, from_low, from_high, now, bf, w_hi, w_lo, d_hi, d_lo, pick,
-    second, xu, xd, mid, mass_core, mass_halo,
-    total, g_hi, g_lo, s0, sz, rows12, buf, hot,
+    second, xa, xb, mid, mass_core, mass_halo,
+    xu, xd, total, g_hi, g_lo, s0, sz, rows12, buf, hot,
 ):
-    halo = x_fold(5, h, hb, from_low, from_high, total)
+    halo = x_fold(5, spot, h, hb, from_low, from_high, total)
     mass_core[...] = total[144:192]
     wide = iota((8, 256), 1)
 
@@ -525,6 +531,8 @@
         got = jnp.sum(jnp.where(chosen[None], got, 0.0), axis=1)
         dest, place = ((xd, t), (mid, t - 3), (xu, t - 6))[t // 3]
         dest[:, place * 128 : place * 128 + 128] = got
+    xa[...] = by_sides(spot, xu, xd)
+    xb[...] = by_sides(spot, xd, xu)
 
 
 def pieces(groups, at, tiles):
@@ -541,9 +549,10 @@
     return ref[:, i * 128 : i * 128 + 128]
 
 
-def route_y_kernel(spot, mid, from_low, from_high, ya, yb):
+def route_y_kernel(spot, mid, xa, xb, ya, yb):
     first = spot
-    for i, ref in enumerate((mid, from_low, from_high)):
+    parts = (mid, by_sides(spot, xa, xb), by_sides(spot, xb, xa))
+    for i, ref in enumerate(parts):
         down, up = lane_tile(ref, 0), lane_tile(ref, 2)
         ya[:, i * 128 : i * 128 + 128] = by_side(first, up, down)
         yb[:, i * 128 : i * 128 + 128] = by_side(first, down, up)
@@ -600,7 +609,8 @@
     swap, along, against, own_low, own_high, final,
     l0h, l0l, l2h, l2l, moved, static, e0, e1, e2, e3, zu, zd, up2, dn2,
 ):
-    groups = [lane_tile(mid, 1), lane_tile(x_low, 1), lane_tile(x_high, 1)]
+    xa, xb = lane_tile(x_low, 1), lane_tile(x_high, 1)
+    groups = [lane_tile(mid, 1), by_side(spot, xa, xb), by_side(spot, xb, xa)]
     groups += [by_side(spot, lane_tile(rb, i), lane_tile(ra, i)) for i in range(3)]
     groups += [by_side(spot, lane_tile(ra, i), lane_tile(rb, i)) for i in range(3)]
     zu[...] = jnp.zeros(zu.shape, F32)
@@ -694,7 +704,7 @@
     result,
     total, g_hi, g_lo, s0, sz, rows12, packed,
 ):
-    halo = x_fold(3, h, hb, from_low, from_high, total)
+    halo = x_fold(3, spot, h, hb, from_low, from_high, total)
     node_values(
         spot, extents, total, halo,
         lambda x: mass_core[x * 8 : x * 8 + 8], mass_halo[...], g_hi, g_lo,
@@ -725,11 +735,12 @@
     )
 
 
-def both_ways(up, down, axis, step=1):
-    count = lax.axis_size(axis)
-    low = lax.ppermute(up, axis, [(i, i + step) for i in range(count - step)])
-    high = lax.ppermute(down, axis, [(i + step, i) for i in range(count - step)])
-    return low, high
+def crossed(first, second):
+    wide, tall = lax.axis_size("gx"), lax.axis_size("gy")
+    up = [(x * tall + y, (x + 1) * tall + y) for x in range(wide - 1) for y in range(tall)]
+    a = [p if p[0] % tall % 2 == 0 else p[::-1] for p in up]
+    b = [p[::-1] for p in a]
+    return lax.ppermute(first, ("gx", "gy"), a), lax.ppermute(second, ("gx", "gy"), b)
 
 
 def both_pairs(first, second, axis):
@@ -777,8 +788,9 @@
         h, hb, xu, xd = call(
             kernel, f"fold_y{comps}", [VMEM] * 5 + [pl.BlockSpec(memory_space=pl.ANY)] * len(after),
             [shape(comps * 48, 128), shape(8, 256), shape(rows, 128), shape(rows, 128)],
+            [((rows, 128), F32)] * 2,
         )(spot, h, hb, ra, rb, *after)
-        low, high = both_ways(xu, xd, "gx")
+        low, high = crossed(xu, xd)
         return h, hb, low, high
 
     firsts = (
@@ -812,10 +824,10 @@
     second, xu, xd, mid, mass_core, mass_halo = call(
         functools.partial(gather_first_kernel, extents), "gather_first", [VMEM] * 12,
         [shape(21, 8, 128), shape(21, 384), shape(21, 384), shape(21, 384), shape(48, 128), shape(8, 256)],
-        [((240, 128), F32)] + gscratch + [((176, 128), F32), ((128, 128), BF16)],
+        [((21, 384), F32)] * 2 + [((240, 128), F32)] + gscratch + [((176, 128), F32), ((128, 128), BF16)],
     )(spot, h, hb, low, high, now, bf, *w, pick)
 
-    x_low, x_high = both_ways(xu, xd, "gx")
+    x_low, x_high = crossed(xu, xd)
     stayed, core_stay, ends_stay = call(
         stay_kernel, "stay", [VMEM] * 8,
         [shape(21, 8, 128), shape(144, 128), shape(16, 144)],

time: 106 us -> 106 us (level)
  the two profiles are of different devices: /device:TPU:144 before, /device:TPU:400 now
where the time goes in v8:
time: 106 us
  starting transfers between devices  46.8 us (44%)
  waiting for transfers between devices  45.4 us (43%)
  Pallas kernels  12.5 us (12%)
    ppermute x3, starting transfers between devices, both_pairs(): rb = lax.ppermute(second, axis, b) if b else jnp.zeros_like(second)  11.6 us
    ppermute x1, waiting for transfers between devices, body(): both = lax.ppermute(both, 'gz', pairs)  11 us
    ppermute x3, waiting for transfers between devices, crossed(): lax.ppermute(second, ('gx', 'gy'), b)  10.5 us
    ppermute x3, starting transfers between devices, crossed(): lax.ppermute(first, ('gx', 'gy'), a)  9.88 us
    ppermute x3, waiting for transfers between devices, both_pairs(): rb = lax.ppermute(second, axis, b) if b else jnp.zeros_like(second)  7.38 us
    ppermute x1, waiting for transfers between devices, body(): both = lax.ppermute(swap, 'gz', pairs)  7.11 us
    ppermute x3, starting transfers between devices, both_pairs(): ra = lax.ppermute(first, axis, a)  5.76 us
    ppermute x1, starting transfers between devices, body(): both = lax.ppermute(swap, 'gz', pairs)  4.14 us
  transfers between devices with their start and end apart: 17, of which 11 were waited for; matrix products, arithmetic and copies ran while one was open for 0% of the time, Pallas kernels for 4%

profile of v8, /device:TPU:400, one launch (start us, length us, event | category | flops | bytes accessed | tf_op | source)
XLA Modules:
  0.0 105.8 jit_solution(11226515756410105670)
XLA Ops:
  0.0 0.1 stack.23
  0.1 0.1 broadcast_in_dim.2.spot.refs_0_
  0.2 3.0 %scatter_first.1 = (f32[240,128]{1,0:T(8,128)S(1)}, f32[8,256]{1,0:T(8,128)S(1)}, f32[32,384]{1,0:T(8,128)S(1)}, f32[9,8,128]{2,1,0:T(8,128)S(1)}, bf16[144,1024...) custom-call(s32[8,128]{1,0:T(8,128)S(1)} %broadcast_in_dim.2.spot.re, ...), custom_call_target="tpu_custom_call" | custom-call | tf_op jit(solution)/shard_map/scatter_first/pallas_call | solution.py:799
  3.2 3.6 %collective-permute-start = (f32[32,384]{1,0:T(8,128)S(1)}, f32[32,384]{1,0:T(8,128)S(1)}, u32[]{:S(2)}, u32[]{:S(2)}) collective-permute-start(f32[32,384]{1,0:T(8,128)S(1)} %get-tuple-element.61), channel_id=1, source_target_pairs={{0,1},{1,0},{2,3},{3,2},{4,5},{5,4},{6,7},{7,6},{8,9},{9,8},{10,11... | collective-permute-start | bytes 147464 | tf_op jit(solution)/shard_map/ppermute | solution.py:809
  6.8 11.0 %collective-permute-done.both = f32[32,384]{1,0:T(8,128)S(1)} collective-permute-done((f32[32,384]{1,0:T(8,128)S(1)}, f32[32,384]{1,0:T(8,128)S(1)}, u32[]{:S(2)}, u32[]{:S(2)}) %collective-permute-start) | collective-permute-done | bytes 49184 | tf_op jit(solution)/shard_map/ppermute | solution.py:809
  17.9 2.3 %collective-permute-start.1 = (f32[16,384]{1,0:T(8,128)S(1)}, f32[16,384]{1,0:T(8,128)S(1)}, u32[]{:S(2)}, u32[]{:S(2)}) collective-permute-start(f32[16,384]{1,0:T(8,128)S(1)} %slice.4), channel_id=1, source_target_pairs={{0,2},{2,4},{4,6},{3,1},{5,3},{7,5},{8,10},{10,12},{12,14},{11,9},... | collective-permute-start | bytes 73736 | tf_op jit(solution)/shard_map/ppermute | solution.py:810
  20.2 3.4 %collective-permute-done.1.far = f32[16,384]{1,0:T(8,128)S(1)} collective-permute-done((f32[16,384]{1,0:T(8,128)S(1)}, f32[16,384]{1,0:T(8,128)S(1)}, u32[]{:S(2)}, u32[]{:S(2)}) %collective-permute-start.1) | collective-permute-done | bytes 24608 | tf_op jit(solution)/shard_map/ppermute | solution.py:810
  23.6 0.3 fold_z5.1
  23.9 1.9 %collective-permute-start.2 = (f32[72,128]{1,0:T(8,128)S(1)}, f32[72,128]{1,0:T(8,128)S(1)}, u32[]{:S(2)}, u32[]{:S(2)}) collective-permute-start(f32[72,128]{1,0:T(8,128)S(1)} %get-tuple-element.64), channel_id=1, source_target_pairs={{0,8},{8,0},{16,24},{24,16},{32,40},{40,32},{48,56},{56,48},{64,72... | collective-permute-start | bytes 110600 | tf_op jit(solution)/shard_map/ppermute | solution.py:750
  25.8 6.1 %collective-permute-start.3 = (f32[72,128]{1,0:T(8,128)S(1)}, f32[72,128]{1,0:T(8,128)S(1)}, u32[]{:S(2)}, u32[]{:S(2)}) collective-permute-start(f32[72,128]{1,0:T(8,128)S(1)} %get-tuple-element.65), channel_id=1, source_target_pairs={{8,16},{16,8},{24,32},{32,24},{40,48},{48,40},{56,64},{64,56},{72,... | collective-permute-start | bytes 110600 | tf_op jit(solution)/shard_map/ppermute | solution.py:751
  31.9 1.7 %weights_second.1 = (bf16[144,1024]{1,0:T(8,128)(2,1)S(1)}, bf16[144,1024]{1,0:T(8,128)(2,1)S(1)}, bf16[144,1024]{1,0:T(8,128)(2,1)S(1)}, bf16[144,1024]{1,0:T(8...) custom-call(f32[112,128]{1,0:T(8,128)S(1)} %get-tuple-element.66.ear, ...), custom_call_target="tpu_custom_call" | custom-call | tf_op jit(solution)/shard_map/weights_second/pallas_call | solution.py:814
  33.6 0.0 collective-permute-done.3.refs_4_
  33.6 0.0 copy-start.1
  33.6 0.1 fold_y5.1
  33.7 3.4 %collective-permute-start.4 = (f32[88,128]{1,0:T(8,128)S(1)}, f32[88,128]{1,0:T(8,128)S(1)}, u32[]{:S(2)}, u32[]{:S(2)}) collective-permute-start(f32[88,128]{1,0:T(8,128)S(1)} %get-tuple-element.71), channel_id=1, source_target_pairs={{0,128},{136,8},{16,144},{152,24},{32,160},{168,40},{48,176},{184,... | collective-permute-start | bytes 135176 | tf_op jit(solution)/shard_map/ppermute | solution.py:743
  37.1 0.0 copy-start.3
  37.1 1.3 %collective-permute-start.5 = (f32[88,128]{1,0:T(8,128)S(1)}, f32[88,128]{1,0:T(8,128)S(1)}, u32[]{:S(2)}, u32[]{:S(2)}) collective-permute-start(f32[88,128]{1,0:T(8,128)S(1)} %get-tuple-element.72), channel_id=1, source_target_pairs={{128,0},{8,136},{144,16},{24,152},{160,32},{40,168},{176,48},{56,1... | collective-permute-start | bytes 135176 | tf_op jit(solution)/shard_map/ppermute | solution.py:743
  38.4 0.2 fill_pick.1.pick
  38.6 0.2 collective-permute-done.4.from_low
  38.8 4.3 %collective-permute-done.5.from_high = f32[88,128]{1,0:T(8,128)S(1)} collective-permute-done((f32[88,128]{1,0:T(8,128)S(1)}, f32[88,128]{1,0:T(8,128)S(1)}, u32[]{:S(2)}, u32[]{:S(2)}) %collective-permute-start.5) | collective-permute-done | bytes 45088 | tf_op jit(solution)/shard_map/ppermute | solution.py:743
  43.0 1.5 %gather_first.1 = (f32[21,8,128]{2,1,0:T(8,128)S(1)}, f32[21,384]{1,0:T(8,128)S(1)}, f32[21,384]{1,0:T(8,128)S(1)}, f32[21,384]{1,0:T(8,128)S(1)}, f32[48,128]{1,0:T(8,128)S(1)}, /*index=5*/f32[8,256]{1,0:T(8,128)S(1)}) custom-call(s32[8,128]{1,0:T(8,128)S(1)} %broadcast_in_dim.2.spot.refs_0_, f32[240,128]{1,0:T(8,128)S(1)} %get-tuple-element.69.h, ...), custom_call_target="tpu_custom_call" | custom-call | tf_op jit(solution)/shard_map/gather_first/pallas_call | solution.py:824
  44.6 3.4 %collective-permute-start.6 = (f32[21,384]{1,0:T(8,128)S(1)}, f32[21,384]{1,0:T(8,128)S(1)}, u32[]{:S(2)}, u32[]{:S(2)}) collective-permute-start(f32[21,384]{1,0:T(8,128)S(1)} %get-tuple-element.80), channel_id=1, source_target_pairs={{0,128},{136,8},{16,144},{152,24},{32,160},{168,40},{48,176},{184,... | collective-permute-start | bytes 96776 | tf_op jit(solution)/shard_map/ppermute | solution.py:743
  48.0 1.3 %collective-permute-start.7 = (f32[21,384]{1,0:T(8,128)S(1)}, f32[21,384]{1,0:T(8,128)S(1)}, u32[]{:S(2)}, u32[]{:S(2)}) collective-permute-start(f32[21,384]{1,0:T(8,128)S(1)} %get-tuple-element.81), channel_id=1, source_target_pairs={{128,0},{8,136},{144,16},{24,152},{160,32},{40,168},{176,48},{56,1... | collective-permute-start | bytes 96776 | tf_op jit(solution)/shard_map/ppermute | solution.py:743
  49.3 0.0 copy-start.2
  49.3 0.7 copy-done.2
  50.0 1.6 %stay.1 = (f32[21,8,128]{2,1,0:T(8,128)S(1)}, f32[144,128]{1,0:T(8,128)S(1)}, f32[16,144]{1,0:T(8,128)S(1)}) custom-call(f32[120,128]{1,0:T(8,128)S(1)} %get-tuple-element.73.now, f32[21,8,128]{2,1,0:T(8,128)S(1)} %get-tuple-element.82.second, s32[8,128]{1,0:T(8,128)S(1)} %bitcast.14, f32[112,128]{1,0:T(8,128)S(1)} %get-tuple-element.66.early, ...), custom_call_target="tpu_custom_call" | custom-call | tf_op jit(solution)/shard_map/stay/pallas_call | solution.py:831
  51.6 2.3 %collective-permute-done.7.refs_3_.x_high = f32[21,384]{1,0:T(8,128)S(1)} collective-permute-done((f32[21,384]{1,0:T(8,128)S(1)}, f32[21,384]{1,0:T(8,128)S(1)}, u32[]{:S(2)}, u32[]{:S(2)}) %collective-permute-start.7) | collective-permute-done | bytes 32288 | tf_op jit(solution)/shard_map/ppermute | solution.py:743
  53.8 1.9 %collective-permute-start.8 = (f32[21,384]{1,0:T(8,128)S(1)}, f32[21,384]{1,0:T(8,128)S(1)}, u32[]{:S(2)}, u32[]{:S(2)}) collective-permute-start(f32[21,384]{1,0:T(8,128)S(1)} %get-tuple-element.88), channel_id=1, source_target_pairs={{0,8},{8,0},{16,24},{24,16},{32,40},{40,32},{48,56},{56,48},{64,72... | collective-permute-start | bytes 96776 | tf_op jit(solution)/shard_map/ppermute | solution.py:750
  55.8 3.5 %collective-permute-start.9 = (f32[21,384]{1,0:T(8,128)S(1)}, f32[21,384]{1,0:T(8,128)S(1)}, u32[]{:S(2)}, u32[]{:S(2)}) collective-permute-start(f32[21,384]{1,0:T(8,128)S(1)} %get-tuple-element.89), channel_id=1, source_target_pairs={{8,16},{16,8},{24,32},{32,24},{40,48},{48,40},{56,64},{64,56},{72,... | collective-permute-start | bytes 96776 | tf_op jit(solution)/shard_map/ppermute | solution.py:751
  59.3 3.0 %collective-permute-done.9.rb = f32[21,384]{1,0:T(8,128)S(1)} collective-permute-done((f32[21,384]{1,0:T(8,128)S(1)}, f32[21,384]{1,0:T(8,128)S(1)}, u32[]{:S(2)}, u32[]{:S(2)}) %collective-permute-start.9) | collective-permute-done | bytes 32288 | tf_op jit(solution)/shard_map/ppermute | solution.py:751
  62.3 1.0 scatter_near.1
  63.3 4.1 %collective-permute-start.10 = (f32[48,384]{1,0:T(8,128)S(1)}, f32[48,384]{1,0:T(8,128)S(1)}, u32[]{:S(2)}, u32[]{:S(2)}) collective-permute-start(f32[48,384]{1,0:T(8,128)S(1)} %get-tuple-element.90), channel_id=1, source_target_pairs={{0,1},{1,0},{2,3},{3,2},{4,5},{5,4},{6,7},{7,6},{8,9},{9,8},{10,11... | collective-permute-start | bytes 221192 | tf_op jit(solution)/shard_map/ppermute | solution.py:850
  67.5 3.2 %collective-permute-start.11 = (f32[2,256]{1,0:T(2,128)S(1)}, f32[2,256]{1,0:T(2,128)S(1)}, u32[]{:S(2)}, u32[]{:S(2)}) collective-permute-start(f32[2,256]{1,0:T(2,128)S(1)} %get-tuple-element.92), channel_id=1, source_target_pairs={{2,0},{4,2},{6,4},{1,3},{3,5},{5,7},{10,8},{12,10},{14,12},{9,11},... | collective-permute-start | bytes 6152 | tf_op jit(solution)/shard_map/ppermute | solution.py:851
  70.7 2.3 %collective-permute-done.11._.against = f32[2,256]{1,0:T(2,128)S(1)} collective-permute-done((f32[2,256]{1,0:T(2,128)S(1)}, f32[2,256]{1,0:T(2,128)S(1)}, u32[]{:S(2)}, u32[]{:S(2)}) %collective-permute-start.11) | collective-permute-done | bytes 2080 | tf_op jit(solution)/shard_map/ppermute | solution.py:851
  72.9 7.1 %collective-permute-done.10.both = f32[48,384]{1,0:T(8,128)S(1)} collective-permute-done((f32[48,384]{1,0:T(8,128)S(1)}, f32[48,384]{1,0:T(8,128)S(1)}, u32[]{:S(2)}, u32[]{:S(2)}) %collective-permute-start.10) | collective-permute-done | bytes 73760 | tf_op jit(solution)/shard_map/ppermute | solution.py:850
  80.0 2.3 %collective-permute-start.12 = (f32[24,384]{1,0:T(8,128)S(1)}, f32[24,384]{1,0:T(8,128)S(1)}, u32[]{:S(2)}, u32[]{:S(2)}) collective-permute-start(f32[24,384]{1,0:T(8,128)S(1)} %relay.1), channel_id=1, source_target_pairs={{0,2},{2,4},{4,6},{3,1},{5,3},{7,5},{8,10},{10,12},{12,14},{11,9},... | collective-permute-start | bytes 110600 | tf_op jit(solution)/shard_map/ppermute | solution.py:855
  82.4 3.5 %collective-permute-done.12.far = f32[24,384]{1,0:T(8,128)S(1)} collective-permute-done((f32[24,384]{1,0:T(8,128)S(1)}, f32[24,384]{1,0:T(8,128)S(1)}, u32[]{:S(2)}, u32[]{:S(2)}) %collective-permute-start.12) | collective-permute-done | bytes 36896 | tf_op jit(solution)/shard_map/ppermute | solution.py:855
  85.9 1.0 scatter_second.1
  86.9 1.9 %collective-permute-start.13 = (f32[48,128]{1,0:T(8,128)S(1)}, f32[48,128]{1,0:T(8,128)S(1)}, u32[]{:S(2)}, u32[]{:S(2)}) collective-permute-start(f32[48,128]{1,0:T(8,128)S(1)} %get-tuple-element.103), channel_id=1, source_target_pairs={{0,8},{8,0},{16,24},{24,16},{32,40},{40,32},{48,56},{56,48},{64,72... | collective-permute-start | bytes 73736 | tf_op jit(solution)/shard_map/ppermute | solution.py:750
  88.8 0.0 copy-start
  88.9 2.1 %collective-permute-start.14 = (f32[48,128]{1,0:T(8,128)S(1)}, f32[48,128]{1,0:T(8,128)S(1)}, u32[]{:S(2)}, u32[]{:S(2)}) collective-permute-start(f32[48,128]{1,0:T(8,128)S(1)} %get-tuple-element.104), channel_id=1, source_target_pairs={{8,16},{16,8},{24,32},{32,24},{40,48},{48,40},{56,64},{64,56},{72,... | collective-permute-start | bytes 73736 | tf_op jit(solution)/shard_map/ppermute | solution.py:751
  90.9 4.4 %collective-permute-done.14.refs_4_ = f32[48,128]{1,0:T(8,128)S(1)} collective-permute-done((f32[48,128]{1,0:T(8,128)S(1)}, f32[48,128]{1,0:T(8,128)S(1)}, u32[]{:S(2)}, u32[]{:S(2)}) %collective-permute-start.14) | collective-permute-done | bytes 24608 | tf_op jit(solution)/shard_map/ppermute | solution.py:751
  95.3 0.1 fold_y3.1
  95.4 3.1 %collective-permute-start.15 = (f32[56,128]{1,0:T(8,128)S(1)}, f32[56,128]{1,0:T(8,128)S(1)}, u32[]{:S(2)}, u32[]{:S(2)}) collective-permute-start(f32[56,128]{1,0:T(8,128)S(1)} %get-tuple-element.107), channel_id=1, source_target_pairs={{0,128},{136,8},{16,144},{152,24},{32,160},{168,40},{48,176},{184,... | collective-permute-start | bytes 86024 | tf_op jit(solution)/shard_map/ppermute | solution.py:743
  98.5 1.3 %collective-permute-start.16 = (f32[56,128]{1,0:T(8,128)S(1)}, f32[56,128]{1,0:T(8,128)S(1)}, u32[]{:S(2)}, u32[]{:S(2)}) collective-permute-start(f32[56,128]{1,0:T(8,128)S(1)} %get-tuple-element.108), channel_id=1, source_target_pairs={{128,0},{8,136},{144,16},{24,152},{160,32},{40,168},{176,48},{56,1... | collective-permute-start | bytes 86024 | tf_op jit(solution)/shard_map/ppermute | solution.py:743
  99.8 0.5 deform_second.1.bf
  100.3 4.0 %collective-permute-done.16.from_high = f32[56,128]{1,0:T(8,128)S(1)} collective-permute-done((f32[56,128]{1,0:T(8,128)S(1)}, f32[56,128]{1,0:T(8,128)S(1)}, u32[]{:S(2)}, u32[]{:S(2)}) %collective-permute-start.16) | collective-permute-done | bytes 28704 | tf_op jit(solution)/shard_map/ppermute | solution.py:743
  104.3 1.6 %gather_second.1 = f32[21,1024]{1,0:T(8,128)} custom-call(s32[8,128]{1,0:T(8,128)S(1)} %broadcast_in_dim.2.spot.refs_0_, f32[144,128]{1,0:T(8,128)S(1)} %get-tuple-element.105.h, f32[8,256]{1,0:T(8,128)S(1)} %get-tuple-element.106.hb, f32[56,128]{1,0:T(8,128)S(1)} %collective-permute-done.15.from_low, f32[56,128]{1,0:T(8,128)S(1)} %collective-permute-done.16.from_high, ...), custom_call_target="tpu_custom_call" | custom-call | tf_op jit(solution)/shard_map/gather_second/pallas_call | solution.py:868
  (12 shorter events, 0.0 us)
Async XLA Ops:
  3.2 14.7 %collective-permute-start = (f32[32,384]{1,0:T(8,128)S(1)}, f32[32,384]{1,0:T(8,128)S(1)}, u32[]{:S(2)}, u32[]{:S(2)}) collective-permute-start(f32[32,384]{1,0:T(8,128)S(1)} %get-tuple-element.61), channel_id=1, source_target_pairs={{0,1},{1,0},{2,3},{3,2},{4,5},{5,4},{6,7},{7,6},{8,9},{9,8},{10,11... | collective-permute-start | bytes 147464 | tf_op jit(solution)/shard_map/ppermute | solution.py:809
  17.9 5.7 %collective-permute-start.1 = (f32[16,384]{1,0:T(8,128)S(1)}, f32[16,384]{1,0:T(8,128)S(1)}, u32[]{:S(2)}, u32[]{:S(2)}) collective-permute-start(f32[16,384]{1,0:T(8,128)S(1)} %slice.4), channel_id=1, source_target_pairs={{0,2},{2,4},{4,6},{3,1},{5,3},{7,5},{8,10},{10,12},{12,14},{11,9},... | collective-permute-start | bytes 73736 | tf_op jit(solution)/shard_map/ppermute | solution.py:810
  23.9 9.7 %collective-permute-start.2 = (f32[72,128]{1,0:T(8,128)S(1)}, f32[72,128]{1,0:T(8,128)S(1)}, u32[]{:S(2)}, u32[]{:S(2)}) collective-permute-start(f32[72,128]{1,0:T(8,128)S(1)} %get-tuple-element.64), channel_id=1, source_target_pairs={{0,8},{8,0},{16,24},{24,16},{32,40},{40,32},{48,56},{56,48},{64,72... | collective-permute-start | bytes 110600 | tf_op jit(solution)/shard_map/ppermute | solution.py:750
  25.8 7.8 %collective-permute-start.3 = (f32[72,128]{1,0:T(8,128)S(1)}, f32[72,128]{1,0:T(8,128)S(1)}, u32[]{:S(2)}, u32[]{:S(2)}) collective-permute-start(f32[72,128]{1,0:T(8,128)S(1)} %get-tuple-element.65), channel_id=1, source_target_pairs={{8,16},{16,8},{24,32},{32,24},{40,48},{48,40},{56,64},{64,56},{72,... | collective-permute-start | bytes 110600 | tf_op jit(solution)/shard_map/ppermute | solution.py:751
  33.6 4.8 %copy-start.1 = (s32[1,26,32]{2,0,1:T(1,128)S(1)}, s32[1,26,32]{2,0,1:T(1,128)}, u32[]{:S(2)}) copy-start(s32[1,26,32]{2,0,1:T(1,128)} %param.19) | copy-start | bytes 9988
  33.7 5.1 %collective-permute-start.4 = (f32[88,128]{1,0:T(8,128)S(1)}, f32[88,128]{1,0:T(8,128)S(1)}, u32[]{:S(2)}, u32[]{:S(2)}) collective-permute-start(f32[88,128]{1,0:T(8,128)S(1)} %get-tuple-element.71), channel_id=1, source_target_pairs={{0,128},{136,8},{16,144},{152,24},{32,160},{168,40},{48,176},{184,... | collective-permute-start | bytes 135176 | tf_op jit(solution)/shard_map/ppermute | solution.py:743
  37.1 1.3 %copy-start.3 = (s32[1,26]{1,0:T(1,128)S(1)}, s32[1,26]{1,0:T(1,128)}, u32[]{:S(2)}) copy-start(s32[1,26]{1,0:T(1,128)} %counts.1) | copy-start | bytes 316
  37.1 5.9 %collective-permute-start.5 = (f32[88,128]{1,0:T(8,128)S(1)}, f32[88,128]{1,0:T(8,128)S(1)}, u32[]{:S(2)}, u32[]{:S(2)}) collective-permute-start(f32[88,128]{1,0:T(8,128)S(1)} %get-tuple-element.72), channel_id=1, source_target_pairs={{128,0},{8,136},{144,16},{24,152},{160,32},{40,168},{176,48},{56,1... | collective-permute-start | bytes 135176 | tf_op jit(solution)/shard_map/ppermute | solution.py:743
  44.6 7.0 %collective-permute-start.6 = (f32[21,384]{1,0:T(8,128)S(1)}, f32[21,384]{1,0:T(8,128)S(1)}, u32[]{:S(2)}, u32[]{:S(2)}) collective-permute-start(f32[21,384]{1,0:T(8,128)S(1)} %get-tuple-element.80), channel_id=1, source_target_pairs={{0,128},{136,8},{16,144},{152,24},{32,160},{168,40},{48,176},{184,... | collective-permute-start | bytes 96776 | tf_op jit(solution)/shard_map/ppermute | solution.py:743
  48.0 5.9 %collective-permute-start.7 = (f32[21,384]{1,0:T(8,128)S(1)}, f32[21,384]{1,0:T(8,128)S(1)}, u32[]{:S(2)}, u32[]{:S(2)}) collective-permute-start(f32[21,384]{1,0:T(8,128)S(1)} %get-tuple-element.81), channel_id=1, source_target_pairs={{128,0},{8,136},{144,16},{24,152},{160,32},{40,168},{176,48},{56,1... | collective-permute-start | bytes 96776 | tf_op jit(solution)/shard_map/ppermute | solution.py:743
  49.3 0.7 copy-start.2
  53.8 5.5 %collective-permute-start.8 = (f32[21,384]{1,0:T(8,128)S(1)}, f32[21,384]{1,0:T(8,128)S(1)}, u32[]{:S(2)}, u32[]{:S(2)}) collective-permute-start(f32[21,384]{1,0:T(8,128)S(1)} %get-tuple-element.88), channel_id=1, source_target_pairs={{0,8},{8,0},{16,24},{24,16},{32,40},{40,32},{48,56},{56,48},{64,72... | collective-permute-start | bytes 96776 | tf_op jit(solution)/shard_map/ppermute | solution.py:750
  55.8 6.5 %collective-permute-start.9 = (f32[21,384]{1,0:T(8,128)S(1)}, f32[21,384]{1,0:T(8,128)S(1)}, u32[]{:S(2)}, u32[]{:S(2)}) collective-permute-start(f32[21,384]{1,0:T(8,128)S(1)} %get-tuple-element.89), channel_id=1, source_target_pairs={{8,16},{16,8},{24,32},{32,24},{40,48},{48,40},{56,64},{64,56},{72,... | collective-permute-start | bytes 96776 | tf_op jit(solution)/shard_map/ppermute | solution.py:751
  63.3 16.7 %collective-permute-start.10 = (f32[48,384]{1,0:T(8,128)S(1)}, f32[48,384]{1,0:T(8,128)S(1)}, u32[]{:S(2)}, u32[]{:S(2)}) collective-permute-start(f32[48,384]{1,0:T(8,128)S(1)} %get-tuple-element.90), channel_id=1, source_target_pairs={{0,1},{1,0},{2,3},{3,2},{4,5},{5,4},{6,7},{7,6},{8,9},{9,8},{10,11... | collective-permute-start | bytes 221192 | tf_op jit(solution)/shard_map/ppermute | solution.py:850
  67.5 5.5 %collective-permute-start.11 = (f32[2,256]{1,0:T(2,128)S(1)}, f32[2,256]{1,0:T(2,128)S(1)}, u32[]{:S(2)}, u32[]{:S(2)}) collective-permute-start(f32[2,256]{1,0:T(2,128)S(1)} %get-tuple-element.92), channel_id=1, source_target_pairs={{2,0},{4,2},{6,4},{1,3},{3,5},{5,7},{10,8},{12,10},{14,12},{9,11},... | collective-permute-start | bytes 6152 | tf_op jit(solution)/shard_map/ppermute | solution.py:851
  80.0 5.8 %collective-permute-start.12 = (f32[24,384]{1,0:T(8,128)S(1)}, f32[24,384]{1,0:T(8,128)S(1)}, u32[]{:S(2)}, u32[]{:S(2)}) collective-permute-start(f32[24,384]{1,0:T(8,128)S(1)} %relay.1), channel_id=1, source_target_pairs={{0,2},{2,4},{4,6},{3,1},{5,3},{7,5},{8,10},{10,12},{12,14},{11,9},... | collective-permute-start | bytes 110600 | tf_op jit(solution)/shard_map/ppermute | solution.py:855
  86.9 4.0 %collective-permute-start.13 = (f32[48,128]{1,0:T(8,128)S(1)}, f32[48,128]{1,0:T(8,128)S(1)}, u32[]{:S(2)}, u32[]{:S(2)}) collective-permute-start(f32[48,128]{1,0:T(8,128)S(1)} %get-tuple-element.103), channel_id=1, source_target_pairs={{0,8},{8,0},{16,24},{24,16},{32,40},{40,32},{48,56},{56,48},{64,72... | collective-permute-start | bytes 73736 | tf_op jit(solution)/shard_map/ppermute | solution.py:750
  88.8 11.0 %copy-start = (f32[2,9,1024]{2,0,1:T(2,128)S(1)}, f32[2,9,1024]{2,0,1:T(2,128)}, u32[]{:S(2)}) copy-start(f32[2,9,1024]{2,0,1:T(2,128)} %param.14) | copy-start | bytes 221188
  88.9 6.5 %collective-permute-start.14 = (f32[48,128]{1,0:T(8,128)S(1)}, f32[48,128]{1,0:T(8,128)S(1)}, u32[]{:S(2)}, u32[]{:S(2)}) collective-permute-start(f32[48,128]{1,0:T(8,128)S(1)} %get-tuple-element.104), channel_id=1, source_target_pairs={{8,16},{16,8},{24,32},{32,24},{40,48},{48,40},{56,64},{64,56},{72,... | collective-permute-start | bytes 73736 | tf_op jit(solution)/shard_map/ppermute | solution.py:751
  95.4 4.9 %collective-permute-start.15 = (f32[56,128]{1,0:T(8,128)S(1)}, f32[56,128]{1,0:T(8,128)S(1)}, u32[]{:S(2)}, u32[]{:S(2)}) collective-permute-start(f32[56,128]{1,0:T(8,128)S(1)} %get-tuple-element.107), channel_id=1, source_target_pairs={{0,128},{136,8},{16,144},{152,24},{32,160},{168,40},{48,176},{184,... | collective-permute-start | bytes 86024 | tf_op jit(solution)/shard_map/ppermute | solution.py:743
  98.5 5.8 %collective-permute-start.16 = (f32[56,128]{1,0:T(8,128)S(1)}, f32[56,128]{1,0:T(8,128)S(1)}, u32[]{:S(2)}, u32[]{:S(2)}) collective-permute-start(f32[56,128]{1,0:T(8,128)S(1)} %get-tuple-element.108), channel_id=1, source_target_pairs={{128,0},{8,136},{144,16},{24,152},{160,32},{40,168},{176,48},{56,1... | collective-permute-start | bytes 86024 | tf_op jit(solution)/shard_map/ppermute | solution.py:743

commit v9 on v7

--- a/solution.py
+++ b/solution.py
@@ -83,26 +83,34 @@
     high_h, high_l = rounded(high)
     to_low = jnp.where(cell_z == 0, 129, cell_z - 1)
     to_high = cell_z + 1
-    inner = iota((128, 128), 0)
-    edge = iota((16, 128), 0)
-    edge = jnp.where(edge < 2, edge + 128, jnp.where(edge == 2, 0, jnp.where(edge == 3, 127, 999)))
-    parts = ((slice(0, 128), inner), (slice(128, ZROWS), edge))
-    if edges_only:
-        parts = ((slice(0, 16), edge),)
+    rows16 = iota((16, 128), 0)
+    edge = jnp.where(rows16 == 2, 0, jnp.where(rows16 == 3, 127, 999))
+    edge = jnp.where(rows16 < 2, rows16 + 128, edge)
+    groups = [] if edges_only else [(g * 16, rows16 + g * 16) for g in range(8)]
+    groups.append((0 if edges_only else 128, edge))
+    groups = [(at, index.astype(F32).astype(BF16)) for at, index in groups]
+    nothing = jnp.zeros((16, 128), BF16)
+
+    def wide(row):
+        return jnp.broadcast_to(row.astype(F32), (16, 128)).astype(BF16)
+
     for chunk in range(chunks):
         at = slice(chunk, chunk + 1)
         lanes = slice(chunk * 128, chunk * 128 + 128)
-        for rows, index in parts:
-            is_low, is_mid, is_high = index == to_low[at], index == cell_z[at], index == to_high[at]
-            for plain, signed, (a, b, c) in (
-                (w_hi, d_hi, (low_h, mid_h, high_h)),
-                (w_lo, d_lo, (low_l, mid_l, high_l)),
-            ):
-                ends = jnp.where(is_high, c[at], 0.0)
-                plain[rows, lanes] = jnp.where(
-                    is_low, a[at], jnp.where(is_mid, b[at], ends)
-                ).astype(BF16)
-                signed[rows, lanes] = jnp.where(is_low, -a[at], ends).astype(BF16)
+        targets = [wide(v[at]) for v in (to_low, cell_z, to_high)]
+        sets = []
+        for plain, signed, parts in (
+            (w_hi, d_hi, (low_h, mid_h, high_h)),
+            (w_lo, d_lo, (low_l, mid_l, high_l)),
+        ):
+            sets.append((plain, signed, [wide(v[at]) for v in parts + (-parts[0],)]))
+        for first, index in groups:
+            rows = slice(first, first + 16)
+            is_low, is_mid, is_high = (index == v for v in targets)
+            for plain, signed, (a, b, c, d) in sets:
+                ends = jnp.where(is_high, c, nothing)
+                plain[rows, lanes] = jnp.where(is_low, a, jnp.where(is_mid, b, ends))
+                signed[rows, lanes] = jnp.where(is_low, d, ends)
 
 
 def row_of(info, i, rows=8):

time: 106 us -> 106 us (level)
  the two profiles are of different devices: /device:TPU:144 before, /device:TPU:136 now
where the time goes in v9:
time: 106 us; the launch traced here: 105 us
  starting transfers between devices  57 us (54%)
  waiting for transfers between devices  35.8 us (34%)
  Pallas kernels  11.5 us (11%)
    ppermute x3, waiting for transfers between devices, both_pairs(): rb = lax.ppermute(second, axis, b) if b else jnp.zeros_like(second)  11.8 us
    ppermute x1, starting transfers between devices, body(): both = lax.ppermute(both, 'gz', pairs)  10.9 us
    ppermute x1, starting transfers between devices, body(): both = lax.ppermute(swap, 'gz', pairs)  10.6 us
    ppermute x3, waiting for transfers between devices, both_ways(): lax.ppermute(down, axis, [(i + step, i) for i in range(count - step)])  10.5 us
    ppermute x3, starting transfers between devices, both_ways(): low = lax.ppermute(up, axis, [(i, i + step) for i in range(count - step)])  9.94 us
    ppermute x3, starting transfers between devices, both_pairs(): rb = lax.ppermute(second, axis, b) if b else jnp.zeros_like(second)  6.63 us
    ppermute x3, starting transfers between devices, both_pairs(): ra = lax.ppermute(first, axis, a)  5.76 us
    ppermute x1, waiting for transfers between devices, body(): both = lax.ppermute(both, 'gz', pairs)  5.61 us
  transfers between devices with their start and end apart: 17, of which 11 were waited for; matrix products, arithmetic and copies ran while one was open for 0% of the time, Pallas kernels for 3%

profile of v9, /device:TPU:136, one launch (start us, length us, event | category | flops | bytes accessed | tf_op | source)
XLA Modules:
  0.0 105.4 jit_solution(11631440360388110470)
XLA Ops:
  0.0 0.1 stack.23
  0.1 0.1 broadcast_in_dim.2.spot.refs_0_
  0.2 2.7 %scatter_first.1 = (f32[240,128]{1,0:T(8,128)S(1)}, f32[8,256]{1,0:T(8,128)S(1)}, f32[32,384]{1,0:T(8,128)S(1)}, f32[9,8,128]{2,1,0:T(8,128)S(1)}, bf16[144,1024...) custom-call(s32[8,128]{1,0:T(8,128)S(1)} %broadcast_in_dim.2.spot.re, ...), custom_call_target="tpu_custom_call" | custom-call | tf_op jit(solution)/shard_map/scatter_first/pallas_call | solution.py:795
  2.9 10.9 %collective-permute-start = (f32[32,384]{1,0:T(8,128)S(1)}, f32[32,384]{1,0:T(8,128)S(1)}, u32[]{:S(2)}, u32[]{:S(2)}) collective-permute-start(f32[32,384]{1,0:T(8,128)S(1)} %get-tuple-element.61), channel_id=1, source_target_pairs={{0,1},{1,0},{2,3},{3,2},{4,5},{5,4},{6,7},{7,6},{8,9},{9,8},{10,11... | collective-permute-start | bytes 147464 | tf_op jit(solution)/shard_map/ppermute | solution.py:805
  13.8 5.6 %collective-permute-done.both = f32[32,384]{1,0:T(8,128)S(1)} collective-permute-done((f32[32,384]{1,0:T(8,128)S(1)}, f32[32,384]{1,0:T(8,128)S(1)}, u32[]{:S(2)}, u32[]{:S(2)}) %collective-permute-start) | collective-permute-done | bytes 49184 | tf_op jit(solution)/shard_map/ppermute | solution.py:805
  19.4 3.5 %collective-permute-start.1 = (f32[16,384]{1,0:T(8,128)S(1)}, f32[16,384]{1,0:T(8,128)S(1)}, u32[]{:S(2)}, u32[]{:S(2)}) collective-permute-start(f32[16,384]{1,0:T(8,128)S(1)} %slice.4), channel_id=1, source_target_pairs={{0,2},{2,4},{4,6},{3,1},{5,3},{7,5},{8,10},{10,12},{12,14},{11,9},... | collective-permute-start | bytes 73736 | tf_op jit(solution)/shard_map/ppermute | solution.py:806
  22.9 2.2 %collective-permute-done.1.far = f32[16,384]{1,0:T(8,128)S(1)} collective-permute-done((f32[16,384]{1,0:T(8,128)S(1)}, f32[16,384]{1,0:T(8,128)S(1)}, u32[]{:S(2)}, u32[]{:S(2)}) %collective-permute-start.1) | collective-permute-done | bytes 24608 | tf_op jit(solution)/shard_map/ppermute | solution.py:806
  25.1 0.3 fold_z5.1
  25.4 1.9 %collective-permute-start.2 = (f32[72,128]{1,0:T(8,128)S(1)}, f32[72,128]{1,0:T(8,128)S(1)}, u32[]{:S(2)}, u32[]{:S(2)}) collective-permute-start(f32[72,128]{1,0:T(8,128)S(1)} %get-tuple-element.64), channel_id=1, source_target_pairs={{0,8},{8,0},{16,24},{24,16},{32,40},{40,32},{48,56},{56,48},{64,72... | collective-permute-start | bytes 110600 | tf_op jit(solution)/shard_map/ppermute | solution.py:747
  27.3 2.1 %collective-permute-start.3 = (f32[72,128]{1,0:T(8,128)S(1)}, f32[72,128]{1,0:T(8,128)S(1)}, u32[]{:S(2)}, u32[]{:S(2)}) collective-permute-start(f32[72,128]{1,0:T(8,128)S(1)} %get-tuple-element.65), channel_id=1, source_target_pairs={{8,16},{16,8},{24,32},{32,24},{40,48},{48,40},{56,64},{64,56},{72,... | collective-permute-start | bytes 110600 | tf_op jit(solution)/shard_map/ppermute | solution.py:748
  29.4 1.0 weights_second.1
  30.4 0.0 collective-permute-done.2.refs_3_
  30.5 3.4 %collective-permute-done.3.refs_4_ = f32[72,128]{1,0:T(8,128)S(1)} collective-permute-done((f32[72,128]{1,0:T(8,128)S(1)}, f32[72,128]{1,0:T(8,128)S(1)}, u32[]{:S(2)}, u32[]{:S(2)}) %collective-permute-start.3) | collective-permute-done | bytes 36896 | tf_op jit(solution)/shard_map/ppermute | solution.py:748
  33.8 0.1 fold_y5.1
  33.9 3.4 %collective-permute-start.4 = (f32[88,128]{1,0:T(8,128)S(1)}, f32[88,128]{1,0:T(8,128)S(1)}, u32[]{:S(2)}, u32[]{:S(2)}) collective-permute-start(f32[88,128]{1,0:T(8,128)S(1)} %get-tuple-element.71), channel_id=1, source_target_pairs={{0,128},{128,256},{256,384},{1,129},{129,257},{257,385},{2,130},{1... | collective-permute-start | bytes 135176 | tf_op jit(solution)/shard_map/ppermute | solution.py:738
  37.3 0.0 copy-start.3
  37.3 1.3 %collective-permute-start.5 = (f32[88,128]{1,0:T(8,128)S(1)}, f32[88,128]{1,0:T(8,128)S(1)}, u32[]{:S(2)}, u32[]{:S(2)}) collective-permute-start(f32[88,128]{1,0:T(8,128)S(1)} %get-tuple-element.72), channel_id=1, source_target_pairs={{128,0},{256,128},{384,256},{129,1},{257,129},{385,257},{130,2},{2... | collective-permute-start | bytes 135176 | tf_op jit(solution)/shard_map/ppermute | solution.py:739
  38.6 0.2 fill_pick.1.pick
  38.8 0.2 collective-permute-done.4.from_low
  39.0 4.3 %collective-permute-done.5.from_high = f32[88,128]{1,0:T(8,128)S(1)} collective-permute-done((f32[88,128]{1,0:T(8,128)S(1)}, f32[88,128]{1,0:T(8,128)S(1)}, u32[]{:S(2)}, u32[]{:S(2)}) %collective-permute-start.5) | collective-permute-done | bytes 45088 | tf_op jit(solution)/shard_map/ppermute | solution.py:739
  43.3 1.5 %gather_first.1 = (f32[21,8,128]{2,1,0:T(8,128)S(1)}, f32[21,384]{1,0:T(8,128)S(1)}, f32[21,384]{1,0:T(8,128)S(1)}, f32[21,384]{1,0:T(8,128)S(1)}, f32[48,128]{1,0:T(8,128)S(1)}, /*index=5*/f32[8,256]{1,0:T(8,128)S(1)}) custom-call(s32[8,128]{1,0:T(8,128)S(1)} %broadcast_in_dim.2.spot.refs_0_, f32[240,128]{1,0:T(8,128)S(1)} %get-tuple-element.69.h, ...), custom_call_target="tpu_custom_call" | custom-call | tf_op jit(solution)/shard_map/gather_first/pallas_call | solution.py:820
  44.8 3.4 %collective-permute-start.6 = (f32[21,384]{1,0:T(8,128)S(1)}, f32[21,384]{1,0:T(8,128)S(1)}, u32[]{:S(2)}, u32[]{:S(2)}) collective-permute-start(f32[21,384]{1,0:T(8,128)S(1)} %get-tuple-element.80), channel_id=1, source_target_pairs={{0,128},{128,256},{256,384},{1,129},{129,257},{257,385},{2,130},{1... | collective-permute-start | bytes 96776 | tf_op jit(solution)/shard_map/ppermute | solution.py:738
  48.2 1.3 %collective-permute-start.7 = (f32[21,384]{1,0:T(8,128)S(1)}, f32[21,384]{1,0:T(8,128)S(1)}, u32[]{:S(2)}, u32[]{:S(2)}) collective-permute-start(f32[21,384]{1,0:T(8,128)S(1)} %get-tuple-element.81), channel_id=1, source_target_pairs={{128,0},{256,128},{384,256},{129,1},{257,129},{385,257},{130,2},{2... | collective-permute-start | bytes 96776 | tf_op jit(solution)/shard_map/ppermute | solution.py:739
  49.5 0.0 copy-start.2
  49.5 0.7 copy-done.2
  50.2 1.6 %stay.1 = (f32[21,8,128]{2,1,0:T(8,128)S(1)}, f32[144,128]{1,0:T(8,128)S(1)}, f32[16,144]{1,0:T(8,128)S(1)}) custom-call(f32[120,128]{1,0:T(8,128)S(1)} %get-tuple-element.73.now, f32[21,8,128]{2,1,0:T(8,128)S(1)} %get-tuple-element.82.second, s32[8,128]{1,0:T(8,128)S(1)} %bitcast.14, f32[112,128]{1,0:T(8,128)S(1)} %get-tuple-element.66.early, ...), custom_call_target="tpu_custom_call" | custom-call | tf_op jit(solution)/shard_map/stay/pallas_call | solution.py:827
  51.8 2.3 %collective-permute-done.7.refs_3_.x_high = f32[21,384]{1,0:T(8,128)S(1)} collective-permute-done((f32[21,384]{1,0:T(8,128)S(1)}, f32[21,384]{1,0:T(8,128)S(1)}, u32[]{:S(2)}, u32[]{:S(2)}) %collective-permute-start.7) | collective-permute-done | bytes 32288 | tf_op jit(solution)/shard_map/ppermute | solution.py:739
  54.0 1.9 %collective-permute-start.8 = (f32[21,384]{1,0:T(8,128)S(1)}, f32[21,384]{1,0:T(8,128)S(1)}, u32[]{:S(2)}, u32[]{:S(2)}) collective-permute-start(f32[21,384]{1,0:T(8,128)S(1)} %get-tuple-element.88), channel_id=1, source_target_pairs={{0,8},{8,0},{16,24},{24,16},{32,40},{40,32},{48,56},{56,48},{64,72... | collective-permute-start | bytes 96776 | tf_op jit(solution)/shard_map/ppermute | solution.py:747
  56.0 1.9 %collective-permute-start.9 = (f32[21,384]{1,0:T(8,128)S(1)}, f32[21,384]{1,0:T(8,128)S(1)}, u32[]{:S(2)}, u32[]{:S(2)}) collective-permute-start(f32[21,384]{1,0:T(8,128)S(1)} %get-tuple-element.89), channel_id=1, source_target_pairs={{8,16},{16,8},{24,32},{32,24},{40,48},{48,40},{56,64},{64,56},{72,... | collective-permute-start | bytes 96776 | tf_op jit(solution)/shard_map/ppermute | solution.py:748
  57.9 4.5 %collective-permute-done.9.rb = f32[21,384]{1,0:T(8,128)S(1)} collective-permute-done((f32[21,384]{1,0:T(8,128)S(1)}, f32[21,384]{1,0:T(8,128)S(1)}, u32[]{:S(2)}, u32[]{:S(2)}) %collective-permute-start.9) | collective-permute-done | bytes 32288 | tf_op jit(solution)/shard_map/ppermute | solution.py:748
  62.5 1.0 scatter_near.1
  63.5 10.6 %collective-permute-start.10 = (f32[48,384]{1,0:T(8,128)S(1)}, f32[48,384]{1,0:T(8,128)S(1)}, u32[]{:S(2)}, u32[]{:S(2)}) collective-permute-start(f32[48,384]{1,0:T(8,128)S(1)} %get-tuple-element.90), channel_id=1, source_target_pairs={{0,1},{1,0},{2,3},{3,2},{4,5},{5,4},{6,7},{7,6},{8,9},{9,8},{10,11... | collective-permute-start | bytes 221192 | tf_op jit(solution)/shard_map/ppermute | solution.py:846
  74.1 2.4 %collective-permute-start.11 = (f32[2,256]{1,0:T(2,128)S(1)}, f32[2,256]{1,0:T(2,128)S(1)}, u32[]{:S(2)}, u32[]{:S(2)}) collective-permute-start(f32[2,256]{1,0:T(2,128)S(1)} %get-tuple-element.92), channel_id=1, source_target_pairs={{2,0},{4,2},{6,4},{1,3},{3,5},{5,7},{10,8},{12,10},{14,12},{9,11},... | collective-permute-start | bytes 6152 | tf_op jit(solution)/shard_map/ppermute | solution.py:847
  76.4 3.1 %collective-permute-done.11._.against = f32[2,256]{1,0:T(2,128)S(1)} collective-permute-done((f32[2,256]{1,0:T(2,128)S(1)}, f32[2,256]{1,0:T(2,128)S(1)}, u32[]{:S(2)}, u32[]{:S(2)}) %collective-permute-start.11) | collective-permute-done | bytes 2080 | tf_op jit(solution)/shard_map/ppermute | solution.py:847
  79.5 0.0 collective-permute-done.10.both
  79.6 3.5 %collective-permute-start.12 = (f32[24,384]{1,0:T(8,128)S(1)}, f32[24,384]{1,0:T(8,128)S(1)}, u32[]{:S(2)}, u32[]{:S(2)}) collective-permute-start(f32[24,384]{1,0:T(8,128)S(1)} %relay.1), channel_id=1, source_target_pairs={{0,2},{2,4},{4,6},{3,1},{5,3},{7,5},{8,10},{10,12},{12,14},{11,9},... | collective-permute-start | bytes 110600 | tf_op jit(solution)/shard_map/ppermute | solution.py:851
  83.1 2.4 %collective-permute-done.12.far = f32[24,384]{1,0:T(8,128)S(1)} collective-permute-done((f32[24,384]{1,0:T(8,128)S(1)}, f32[24,384]{1,0:T(8,128)S(1)}, u32[]{:S(2)}, u32[]{:S(2)}) %collective-permute-start.12) | collective-permute-done | bytes 36896 | tf_op jit(solution)/shard_map/ppermute | solution.py:851
  85.4 1.0 scatter_second.1
  86.4 1.9 %collective-permute-start.13 = (f32[48,128]{1,0:T(8,128)S(1)}, f32[48,128]{1,0:T(8,128)S(1)}, u32[]{:S(2)}, u32[]{:S(2)}) collective-permute-start(f32[48,128]{1,0:T(8,128)S(1)} %get-tuple-element.103), channel_id=1, source_target_pairs={{0,8},{8,0},{16,24},{24,16},{32,40},{40,32},{48,56},{56,48},{64,72... | collective-permute-start | bytes 73736 | tf_op jit(solution)/shard_map/ppermute | solution.py:747
  88.4 0.0 copy-start
  88.4 2.6 %collective-permute-start.14 = (f32[48,128]{1,0:T(8,128)S(1)}, f32[48,128]{1,0:T(8,128)S(1)}, u32[]{:S(2)}, u32[]{:S(2)}) collective-permute-start(f32[48,128]{1,0:T(8,128)S(1)} %get-tuple-element.104), channel_id=1, source_target_pairs={{8,16},{16,8},{24,32},{32,24},{40,48},{48,40},{56,64},{64,56},{72,... | collective-permute-start | bytes 73736 | tf_op jit(solution)/shard_map/ppermute | solution.py:748
  91.0 3.8 %collective-permute-done.14.refs_4_ = f32[48,128]{1,0:T(8,128)S(1)} collective-permute-done((f32[48,128]{1,0:T(8,128)S(1)}, f32[48,128]{1,0:T(8,128)S(1)}, u32[]{:S(2)}, u32[]{:S(2)}) %collective-permute-start.14) | collective-permute-done | bytes 24608 | tf_op jit(solution)/shard_map/ppermute | solution.py:748
  94.9 0.1 fold_y3.1
  94.9 3.2 %collective-permute-start.15 = (f32[56,128]{1,0:T(8,128)S(1)}, f32[56,128]{1,0:T(8,128)S(1)}, u32[]{:S(2)}, u32[]{:S(2)}) collective-permute-start(f32[56,128]{1,0:T(8,128)S(1)} %get-tuple-element.107), channel_id=1, source_target_pairs={{0,128},{128,256},{256,384},{1,129},{129,257},{257,385},{2,130},{1... | collective-permute-start | bytes 86024 | tf_op jit(solution)/shard_map/ppermute | solution.py:738
  98.1 1.3 %collective-permute-start.16 = (f32[56,128]{1,0:T(8,128)S(1)}, f32[56,128]{1,0:T(8,128)S(1)}, u32[]{:S(2)}, u32[]{:S(2)}) collective-permute-start(f32[56,128]{1,0:T(8,128)S(1)} %get-tuple-element.108), channel_id=1, source_target_pairs={{128,0},{256,128},{384,256},{129,1},{257,129},{385,257},{130,2},{2... | collective-permute-start | bytes 86024 | tf_op jit(solution)/shard_map/ppermute | solution.py:739
  99.4 0.5 deform_second.1.bf
  99.9 4.0 %collective-permute-done.16.from_high = f32[56,128]{1,0:T(8,128)S(1)} collective-permute-done((f32[56,128]{1,0:T(8,128)S(1)}, f32[56,128]{1,0:T(8,128)S(1)}, u32[]{:S(2)}, u32[]{:S(2)}) %collective-permute-start.16) | collective-permute-done | bytes 28704 | tf_op jit(solution)/shard_map/ppermute | solution.py:739
  103.9 1.5 %gather_second.1 = f32[21,1024]{1,0:T(8,128)} custom-call(s32[8,128]{1,0:T(8,128)S(1)} %broadcast_in_dim.2.spot.refs_0_, f32[144,128]{1,0:T(8,128)S(1)} %get-tuple-element.105.h, f32[8,256]{1,0:T(8,128)S(1)} %get-tuple-element.106.hb, f32[56,128]{1,0:T(8,128)S(1)} %collective-permute-done.15.from_low, f32[56,128]{1,0:T(8,128)S(1)} %collective-permute-done.16.from_high, ...), custom_call_target="tpu_custom_call" | custom-call | tf_op jit(solution)/shard_map/gather_second/pallas_call | solution.py:864
  (12 shorter events, 0.0 us)
Async XLA Ops:
  2.9 16.5 %collective-permute-start = (f32[32,384]{1,0:T(8,128)S(1)}, f32[32,384]{1,0:T(8,128)S(1)}, u32[]{:S(2)}, u32[]{:S(2)}) collective-permute-start(f32[32,384]{1,0:T(8,128)S(1)} %get-tuple-element.61), channel_id=1, source_target_pairs={{0,1},{1,0},{2,3},{3,2},{4,5},{5,4},{6,7},{7,6},{8,9},{9,8},{10,11... | collective-permute-start | bytes 147464 | tf_op jit(solution)/shard_map/ppermute | solution.py:805
  19.4 5.7 %collective-permute-start.1 = (f32[16,384]{1,0:T(8,128)S(1)}, f32[16,384]{1,0:T(8,128)S(1)}, u32[]{:S(2)}, u32[]{:S(2)}) collective-permute-start(f32[16,384]{1,0:T(8,128)S(1)} %slice.4), channel_id=1, source_target_pairs={{0,2},{2,4},{4,6},{3,1},{5,3},{7,5},{8,10},{10,12},{12,14},{11,9},... | collective-permute-start | bytes 73736 | tf_op jit(solution)/shard_map/ppermute | solution.py:806
  25.4 5.0 %collective-permute-start.2 = (f32[72,128]{1,0:T(8,128)S(1)}, f32[72,128]{1,0:T(8,128)S(1)}, u32[]{:S(2)}, u32[]{:S(2)}) collective-permute-start(f32[72,128]{1,0:T(8,128)S(1)} %get-tuple-element.64), channel_id=1, source_target_pairs={{0,8},{8,0},{16,24},{24,16},{32,40},{40,32},{48,56},{56,48},{64,72... | collective-permute-start | bytes 110600 | tf_op jit(solution)/shard_map/ppermute | solution.py:747
  27.3 6.5 %collective-permute-start.3 = (f32[72,128]{1,0:T(8,128)S(1)}, f32[72,128]{1,0:T(8,128)S(1)}, u32[]{:S(2)}, u32[]{:S(2)}) collective-permute-start(f32[72,128]{1,0:T(8,128)S(1)} %get-tuple-element.65), channel_id=1, source_target_pairs={{8,16},{16,8},{24,32},{32,24},{40,48},{48,40},{56,64},{64,56},{72,... | collective-permute-start | bytes 110600 | tf_op jit(solution)/shard_map/ppermute | solution.py:748
  33.8 4.8 %copy-start.1 = (s32[1,26,32]{2,0,1:T(1,128)S(1)}, s32[1,26,32]{2,0,1:T(1,128)}, u32[]{:S(2)}) copy-start(s32[1,26,32]{2,0,1:T(1,128)} %param.19) | copy-start | bytes 9988
  33.9 5.1 %collective-permute-start.4 = (f32[88,128]{1,0:T(8,128)S(1)}, f32[88,128]{1,0:T(8,128)S(1)}, u32[]{:S(2)}, u32[]{:S(2)}) collective-permute-start(f32[88,128]{1,0:T(8,128)S(1)} %get-tuple-element.71), channel_id=1, source_target_pairs={{0,128},{128,256},{256,384},{1,129},{129,257},{257,385},{2,130},{1... | collective-permute-start | bytes 135176 | tf_op jit(solution)/shard_map/ppermute | solution.py:738
  37.3 1.3 %copy-start.3 = (s32[1,26]{1,0:T(1,128)S(1)}, s32[1,26]{1,0:T(1,128)}, u32[]{:S(2)}) copy-start(s32[1,26]{1,0:T(1,128)} %counts.1) | copy-start | bytes 316
  37.3 5.9 %collective-permute-start.5 = (f32[88,128]{1,0:T(8,128)S(1)}, f32[88,128]{1,0:T(8,128)S(1)}, u32[]{:S(2)}, u32[]{:S(2)}) collective-permute-start(f32[88,128]{1,0:T(8,128)S(1)} %get-tuple-element.72), channel_id=1, source_target_pairs={{128,0},{256,128},{384,256},{129,1},{257,129},{385,257},{130,2},{2... | collective-permute-start | bytes 135176 | tf_op jit(solution)/shard_map/ppermute | solution.py:739
  44.8 7.0 %collective-permute-start.6 = (f32[21,384]{1,0:T(8,128)S(1)}, f32[21,384]{1,0:T(8,128)S(1)}, u32[]{:S(2)}, u32[]{:S(2)}) collective-permute-start(f32[21,384]{1,0:T(8,128)S(1)} %get-tuple-element.80), channel_id=1, source_target_pairs={{0,128},{128,256},{256,384},{1,129},{129,257},{257,385},{2,130},{1... | collective-permute-start | bytes 96776 | tf_op jit(solution)/shard_map/ppermute | solution.py:738
  48.2 5.9 %collective-permute-start.7 = (f32[21,384]{1,0:T(8,128)S(1)}, f32[21,384]{1,0:T(8,128)S(1)}, u32[]{:S(2)}, u32[]{:S(2)}) collective-permute-start(f32[21,384]{1,0:T(8,128)S(1)} %get-tuple-element.81), channel_id=1, source_target_pairs={{128,0},{256,128},{384,256},{129,1},{257,129},{385,257},{130,2},{2... | collective-permute-start | bytes 96776 | tf_op jit(solution)/shard_map/ppermute | solution.py:739
  49.5 0.7 copy-start.2
  54.0 3.9 %collective-permute-start.8 = (f32[21,384]{1,0:T(8,128)S(1)}, f32[21,384]{1,0:T(8,128)S(1)}, u32[]{:S(2)}, u32[]{:S(2)}) collective-permute-start(f32[21,384]{1,0:T(8,128)S(1)} %get-tuple-element.88), channel_id=1, source_target_pairs={{0,8},{8,0},{16,24},{24,16},{32,40},{40,32},{48,56},{56,48},{64,72... | collective-permute-start | bytes 96776 | tf_op jit(solution)/shard_map/ppermute | solution.py:747
  56.0 6.5 %collective-permute-start.9 = (f32[21,384]{1,0:T(8,128)S(1)}, f32[21,384]{1,0:T(8,128)S(1)}, u32[]{:S(2)}, u32[]{:S(2)}) collective-permute-start(f32[21,384]{1,0:T(8,128)S(1)} %get-tuple-element.89), channel_id=1, source_target_pairs={{8,16},{16,8},{24,32},{32,24},{40,48},{48,40},{56,64},{64,56},{72,... | collective-permute-start | bytes 96776 | tf_op jit(solution)/shard_map/ppermute | solution.py:748
  63.5 16.1 %collective-permute-start.10 = (f32[48,384]{1,0:T(8,128)S(1)}, f32[48,384]{1,0:T(8,128)S(1)}, u32[]{:S(2)}, u32[]{:S(2)}) collective-permute-start(f32[48,384]{1,0:T(8,128)S(1)} %get-tuple-element.90), channel_id=1, source_target_pairs={{0,1},{1,0},{2,3},{3,2},{4,5},{5,4},{6,7},{7,6},{8,9},{9,8},{10,11... | collective-permute-start | bytes 221192 | tf_op jit(solution)/shard_map/ppermute | solution.py:846
  74.1 5.5 %collective-permute-start.11 = (f32[2,256]{1,0:T(2,128)S(1)}, f32[2,256]{1,0:T(2,128)S(1)}, u32[]{:S(2)}, u32[]{:S(2)}) collective-permute-start(f32[2,256]{1,0:T(2,128)S(1)} %get-tuple-element.92), channel_id=1, source_target_pairs={{2,0},{4,2},{6,4},{1,3},{3,5},{5,7},{10,8},{12,10},{14,12},{9,11},... | collective-permute-start | bytes 6152 | tf_op jit(solution)/shard_map/ppermute | solution.py:847
  79.6 5.9 %collective-permute-start.12 = (f32[24,384]{1,0:T(8,128)S(1)}, f32[24,384]{1,0:T(8,128)S(1)}, u32[]{:S(2)}, u32[]{:S(2)}) collective-permute-start(f32[24,384]{1,0:T(8,128)S(1)} %relay.1), channel_id=1, source_target_pairs={{0,2},{2,4},{4,6},{3,1},{5,3},{7,5},{8,10},{10,12},{12,14},{11,9},... | collective-permute-start | bytes 110600 | tf_op jit(solution)/shard_map/ppermute | solution.py:851
  86.4 4.6 %collective-permute-start.13 = (f32[48,128]{1,0:T(8,128)S(1)}, f32[48,128]{1,0:T(8,128)S(1)}, u32[]{:S(2)}, u32[]{:S(2)}) collective-permute-start(f32[48,128]{1,0:T(8,128)S(1)} %get-tuple-element.103), channel_id=1, source_target_pairs={{0,8},{8,0},{16,24},{24,16},{32,40},{40,32},{48,56},{56,48},{64,72... | collective-permute-start | bytes 73736 | tf_op jit(solution)/shard_map/ppermute | solution.py:747
  88.4 11.0 %copy-start = (f32[2,9,1024]{2,0,1:T(2,128)S(1)}, f32[2,9,1024]{2,0,1:T(2,128)}, u32[]{:S(2)}) copy-start(f32[2,9,1024]{2,0,1:T(2,128)} %param.14) | copy-start | bytes 221188
  88.4 6.5 %collective-permute-start.14 = (f32[48,128]{1,0:T(8,128)S(1)}, f32[48,128]{1,0:T(8,128)S(1)}, u32[]{:S(2)}, u32[]{:S(2)}) collective-permute-start(f32[48,128]{1,0:T(8,128)S(1)} %get-tuple-element.104), channel_id=1, source_target_pairs={{8,16},{16,8},{24,32},{32,24},{40,48},{48,40},{56,64},{64,56},{72,... | collective-permute-start | bytes 73736 | tf_op jit(solution)/shard_map/ppermute | solution.py:748
  94.9 4.9 %collective-permute-start.15 = (f32[56,128]{1,0:T(8,128)S(1)}, f32[56,128]{1,0:T(8,128)S(1)}, u32[]{:S(2)}, u32[]{:S(2)}) collective-permute-start(f32[56,128]{1,0:T(8,128)S(1)} %get-tuple-element.107), channel_id=1, source_target_pairs={{0,128},{128,256},{256,384},{1,129},{129,257},{257,385},{2,130},{1... | collective-permute-start | bytes 86024 | tf_op jit(solution)/shard_map/ppermute | solution.py:738
  98.1 5.8 %collective-permute-start.16 = (f32[56,128]{1,0:T(8,128)S(1)}, f32[56,128]{1,0:T(8,128)S(1)}, u32[]{:S(2)}, u32[]{:S(2)}) collective-permute-start(f32[56,128]{1,0:T(8,128)S(1)} %get-tuple-element.108), channel_id=1, source_target_pairs={{128,0},{256,128},{384,256},{129,1},{257,129},{385,257},{130,2},{2... | collective-permute-start | bytes 86024 | tf_op jit(solution)/shard_map/ppermute | solution.py:739
